TPU v7x, 256 devices: a whole 4x4x8 slice. The times are simulated.
256 devices in a mesh: slab: 4 (over y), row: 4 (over x), col: 16 (over z, core).
Axes of the slice: x: 4, y: 4, z: 8, core: 2. Of those that a mesh axis runs over, the one named last changes fastest.
Arguments:
- right_sides: float32 [4, 32, 65536], P('slab', None, ('col', 'row')), may hold values from -6 to 6
- front_tiles: bfloat16 [4, 8192, 128, 128], P('slab', ('col', 'row'))
- tile_rows: int32 [4, 8192], P('slab', ('col', 'row')), may hold values from 0 to 511, as said below
- tile_cols: int32 [4, 8192], P('slab', ('col', 'row')), may hold values from 0 to 511, as said below
- section_blocks: int32 [4], P('slab'), may hold values from 4 to 8, as said below
- plane_map: int32 [4, 16384], P('slab', ('col', 'row')), may hold values from 0 to 511
- interface_coef: float32 [4, 16384], P('slab', ('col', 'row')), may hold values from 0.5 to 1
Outputs:
- solution: float32 [4, 32, 65536], P('slab', None, ('col', 'row'))
Inputs may be any that keep to these rules, and one draw needn't show every extreme that they name: `tile_rows`: tile t of a section lies on the device of piece t // 128, which is col index c and row index r with piece c * 4 + r; its row block lies among the 32 blocks of pieces c * 4 to c * 4 + 3, and its column block lies in a piece whose index is r modulo 4. Every block of a device's own piece has a tile with equal row and column block on that device. Several tiles may share a row block and a column block. `tile_cols`: see tile_rows. `section_blocks`: some slab section has all 8 blocks of every piece.
All inputs are finite; a program needn't handle non-finite values.
Results may differ from a plain program's by a relative error of at most 0.0039.
Values may be sent and summed in bfloat16 or wider, within the bound.
No kernel may reach another device: no remote copies, remote signals or barrier semaphores. Data moves between devices by JAX's collectives and lax.ppermute only.
A program may use at most 64 MiB of HBM per device.

v0:
```python
import jax
import jax.numpy as jnp
from jax import lax
from jax.sharding import PartitionSpec as P

MICRO = 2


def from_behind(block, axis, distance):
    devices = range(lax.axis_size(axis))
    route = [(i - distance, i) for i in devices if i - distance in devices]
    return lax.ppermute(block, axis, route)


def joined_along(pieces, dim):
    pieces = jnp.moveaxis(pieces, 0, dim)
    shape = pieces.shape
    return pieces.reshape(*shape[:dim], shape[dim] * shape[dim + 1], *shape[dim + 2 :])


def from_everyone(value, axis):
    devices = lax.axis_size(axis)
    return lax.all_to_all(
        jnp.broadcast_to(value[None], (devices, *value.shape)), axis, 0, 0, tiled=True
    )


def gather_directly(value, axis, dim):
    return joined_along(from_everyone(value, axis), dim)


def in_blocks(value, dim, devices):
    before, after = (value.shape[:dim], value.shape[dim + 1 :])
    return jnp.moveaxis(value.reshape(*before, devices, -1, *after), dim, 0)


def summed_on_arrival(value, axis, dim):
    devices = lax.axis_size(axis)
    pieces = lax.all_to_all(in_blocks(value, dim, devices), axis, 0, 0, tiled=True)
    return jnp.sum(pieces, axis=0)


def body(right_sides, front_tiles, tile_rows, tile_cols, section_blocks, plane_map, interface_coef):
    row_count = lax.axis_size("row")
    col_count = lax.axis_size("col")
    slab_count = lax.axis_size("slab")
    col_index = lax.axis_index("col")
    slab_index = lax.axis_index("slab")
    front = front_tiles[0]
    block_len = front.shape[1]
    piece_len = right_sides.shape[2]
    blocks_dev = piece_len // block_len
    plane_len = plane_map.shape[1]
    local_rows = tile_rows[0] - col_index * (row_count * blocks_dev)
    global_cols = tile_cols[0]
    local_cols = global_cols // blocks_dev // row_count * blocks_dev + global_cols % blocks_dev
    active = (jnp.arange(piece_len, dtype=jnp.int32) < section_blocks[0] * block_len).astype(
        jnp.float32
    )
    coef_own = interface_coef[0]
    map_next = from_behind(plane_map, "slab", -1)[0]

    def front_apply(vector):
        batch_rows = vector.shape[0]
        panel = gather_directly(vector, "col", 1)
        blocks = panel.reshape(batch_rows, col_count * blocks_dev, block_len)
        picked = jnp.take(blocks, local_cols, axis=1)
        products = jnp.einsum("wtk,tjk->wtj", picked, front, preferred_element_type=jnp.float32)
        partial_sum = (
            jnp.zeros((batch_rows, row_count * blocks_dev, block_len), jnp.float32)
            .at[:, local_rows]
            .add(products)
        )
        summed = summed_on_arrival(partial_sum.reshape(batch_rows, row_count * piece_len), "row", 1)
        return summed * active[None, :]

    part_count = MICRO
    batch_width = right_sides.shape[1] // part_count
    segment_count = slab_count + part_count - 1
    sources = right_sides[0].reshape(part_count, batch_width, piece_len)
    stored = jnp.zeros((part_count, batch_width, piece_len), jnp.float32)
    incoming = jnp.zeros((batch_width, plane_len), jnp.float32)
    for segment in range(segment_count):
        micro_part = segment - slab_index
        usable = (micro_part >= 0) & (micro_part < part_count)
        clipped = jnp.clip(micro_part, 0, part_count - 1)
        source = sources[clipped]
        pulled = incoming * coef_own[None, :]
        coupled = source.at[:, :plane_len].add(-pulled)
        current = front_apply((active[None, :] * coupled).astype(jnp.bfloat16))
        stored = jnp.where(usable, stored.at[clipped].set(current), stored)
        if segment + 1 < segment_count:
            incoming = from_behind(jnp.take(current, map_next, axis=1), "slab", 1)
    results = stored
    incoming = jnp.zeros((batch_width, plane_len), jnp.float32)
    for segment in range(segment_count):
        micro_part = segment - (slab_count - 1 - slab_index)
        usable = (micro_part >= 0) & (micro_part < part_count)
        clipped = jnp.clip(micro_part, 0, part_count - 1)
        swept_part = stored[clipped]
        lifted = jnp.zeros((batch_width, piece_len), jnp.float32).at[:, map_next].add(incoming)
        current = swept_part - front_apply(lifted.astype(jnp.bfloat16))
        results = jnp.where(usable, results.at[clipped].set(current), results)
        if segment + 1 < segment_count:
            outgoing = current[:, :plane_len] * coef_own[None, :]
            incoming = from_behind(outgoing, "slab", -1)
    return results.reshape(1, part_count * batch_width, piece_len)


def solution(mesh):
    placed = (
        P("slab", None, ("col", "row")),
        P("slab", ("col", "row"), None, None),
        P("slab", ("col", "row")),
        P("slab", ("col", "row")),
        P("slab"),
        P("slab", ("col", "row")),
        P("slab", ("col", "row")),
    )
    return jax.shard_map(
        body, mesh=mesh, in_specs=placed, out_specs=P("slab", None, ("col", "row")), check_vma=False
    )
```

profile of v0, /device:TPU:1, one launch (start us, length us, event | category | flops | bytes accessed | tf_op | source)
XLA Modules:
  0.0 486.6 jit_solution(6091967282237412339)
XLA Ops:
  5.3 10.0 %all-to-all-start = ((bf16[16,16,1024]{2,1,0:T(8,128)(2,1)}), bf16[16,16,1024]{2,1,0:T(8,128)(2,1)S(1)}, u32[]{:S(2)}, u32[]{:S(2)}) async-start(bf16[16,16,1024]{2,1,0:T(8,128)(2,1)} %broadcast_in_dim.41), calls=%async_computation | async-start | bytes 1048576 | tf_op jit(solution)/shard_map/all_to_all | solution.py:23
  19.8 12.7 %all-to-all-done = bf16[16,16,1024]{2,1,0:T(8,128)(2,1)S(1)} async-done(((bf16[16,16,1024]{2,1,0:T(8,128)(2,1)}), bf16[16,16,1024]{2,1,0:T(8,128)(2,1)S(1)}, u32[]{:S(2)}, u32[]{:S(2)}) %all-to-all-start) | async-done | bytes 524320 | tf_op jit(solution)/shard_map/all_to_all | solution.py:23
  38.6 5.2 %scatter_fusion = f32[16,32,128]{2,0,1:T(8,128)S(1)} fusion(f32[16,32,128]{2,0,1:T(8,128)S(1)} %broadcast.512.clone, s32[128]{0:T(128)S(1)} %fusion.98, f32[128,16,128]{2,1,0:T(8,128)S(1)} %fusion.18), kind=kCustom, calls=%fused_computation.14 | custom fusion | flops 262144 | bytes 3146240 | tf_op jit(solution)/shard_map/scatter-add | solution.py:72
  48.9 6.5 %all-to-all-done.1 = f32[4,16,1024]{2,1,0:T(8,128)S(1)} async-done(((f32[4,16,1024]{2,1,0:T(8,128)}), f32[4,16,1024]{2,1,0:T(8,128)S(1)}, u32[]{:S(2)}, u32[]{:S(2)}) %all-to-all-start.1) | async-done | bytes 262176 | tf_op jit(solution)/shard_map/all_to_all | solution.py:39
  61.2 21.5 %all_to_all.100 = bf16[16,16,1024]{2,1,0:T(8,128)(2,1)S(1)} all-to-all(bf16[16,16,1024]{2,1,0:T(8,128)(2,1)S(1)} %broadcast_in_dim.42), channel_id=1, replica_groups=mesh['slab'=4,'row'=4,'col'=16] {'col'}, dimensions={0} | all-to-all | bytes 1048576 | tf_op jit(solution)/shard_map/all_to_all | solution.py:23
  88.9 5.2 %scatter_fusion.1 = f32[16,32,128]{2,0,1:T(8,128)S(1)} fusion(f32[16,32,128]{2,0,1:T(8,128)S(1)} %broadcast.512.clone.1, s32[128]{0:T(128)S(1)} %fusion.98, f32[128,16,128]{2,1,0:T(8,128)S(1)} %fusion.16), kind=kCustom, calls=%fused_computation.15 | custom fusion | flops 262144 | bytes 3146240 | tf_op jit(solution)/shard_map/scatter-add | solution.py:72
  94.5 8.6 %all_to_all.105 = f32[4,16,1024]{2,1,0:T(8,128)S(1)} all-to-all(f32[4,16,1024]{2,1,0:T(8,128)S(1)} %copy.169), channel_id=1, replica_groups=mesh['slab'=4,'row'=4,'col'=16] {'row'}, dimensions={0} | all-to-all | bytes 524288 | tf_op jit(solution)/shard_map/all_to_all | solution.py:39
  109.7 22.3 %all_to_all.101 = bf16[16,16,1024]{2,1,0:T(8,128)(2,1)S(1)} all-to-all(bf16[16,16,1024]{2,1,0:T(8,128)(2,1)S(1)} %broadcast_in_dim.43), channel_id=1, replica_groups=mesh['slab'=4,'row'=4,'col'=16] {'col'}, dimensions={0} | all-to-all | bytes 1048576 | tf_op jit(solution)/shard_map/all_to_all | solution.py:23
  143.7 8.6 %all_to_all.106 = f32[4,16,1024]{2,1,0:T(8,128)S(1)} all-to-all(f32[4,16,1024]{2,1,0:T(8,128)S(1)} %copy.176), channel_id=1, replica_groups=mesh['slab'=4,'row'=4,'col'=16] {'row'}, dimensions={0} | all-to-all | bytes 524288 | tf_op jit(solution)/shard_map/all_to_all | solution.py:39
  166.2 15.5 %all-to-all-done.6 = bf16[16,16,1024]{2,1,0:T(8,128)(2,1)S(1)} async-done(((bf16[16,16,1024]{2,1,0:T(8,128)(2,1)}), bf16[16,16,1024]{2,1,0:T(8,128)(2,1)S(1)}, u32[]{:S(2)}, u32[]{:S(2)}) %all-to-all-start.6) | async-done | bytes 524320 | tf_op jit(solution)/shard_map/all_to_all | solution.py:23
  192.2 5.2 %scatter_fusion.3 = f32[16,32,128]{2,0,1:T(8,128)S(1)} fusion(f32[16,32,128]{2,0,1:T(8,128)S(1)} %broadcast.512.clone.3, s32[128]{0:T(128)S(1)} %fusion.98, f32[128,16,128]{2,1,0:T(8,128)S(1)} %fusion.12), kind=kCustom, calls=%fused_computation.17 | custom fusion | flops 262144 | bytes 3146240 | tf_op jit(solution)/shard_map/scatter-add | solution.py:72
  222.3 5.2 %scatter_fusion.5 = f32[16,32,128]{2,0,1:T(8,128)S(1)} fusion(f32[16,32,128]{2,0,1:T(8,128)S(1)} %broadcast.512.clone.5, s32[128]{0:T(128)S(1)} %fusion.98, f32[128,16,128]{2,1,0:T(8,128)S(1)} %fusion.8), kind=kCustom, calls=%fused_computation.20 | custom fusion | flops 262144 | bytes 3146240 | tf_op jit(solution)/shard_map/scatter-add | solution.py:72
  232.6 5.3 %all-to-all-done.11 = f32[4,16,1024]{2,1,0:T(8,128)S(1)} async-done(((f32[4,16,1024]{2,1,0:T(8,128)}), f32[4,16,1024]{2,1,0:T(8,128)S(1)}, u32[]{:S(2)}, u32[]{:S(2)}) %all-to-all-start.11) | async-done | bytes 262176 | tf_op jit(solution)/shard_map/all_to_all | solution.py:39
  247.4 13.7 %all-to-all-done.8 = bf16[16,16,1024]{2,1,0:T(8,128)(2,1)S(1)} async-done(((bf16[16,16,1024]{2,1,0:T(8,128)(2,1)}), bf16[16,16,1024]{2,1,0:T(8,128)(2,1)S(1)}, u32[]{:S(2)}, u32[]{:S(2)}) %all-to-all-start.8) | async-done | bytes 524320 | tf_op jit(solution)/shard_map/all_to_all | solution.py:23
  277.5 5.5 %all-to-all-done.9 = f32[4,16,1024]{2,1,0:T(8,128)S(1)} async-done(((f32[4,16,1024]{2,1,0:T(8,128)}), f32[4,16,1024]{2,1,0:T(8,128)S(1)}, u32[]{:S(2)}, u32[]{:S(2)}) %all-to-all-start.9) | async-done | bytes 262176 | tf_op jit(solution)/shard_map/all_to_all | solution.py:39
  290.7 22.1 %all_to_all.102 = bf16[16,16,1024]{2,1,0:T(8,128)(2,1)S(1)} all-to-all(bf16[16,16,1024]{2,1,0:T(8,128)(2,1)S(1)} %broadcast_in_dim.47), channel_id=1, replica_groups=mesh['slab'=4,'row'=4,'col'=16] {'col'}, dimensions={0} | all-to-all | bytes 1048576 | tf_op jit(solution)/shard_map/all_to_all | solution.py:23
  329.4 5.4 %all-to-all-done.13 = f32[4,16,1024]{2,1,0:T(8,128)S(1)} async-done(((f32[4,16,1024]{2,1,0:T(8,128)}), f32[4,16,1024]{2,1,0:T(8,128)S(1)}, u32[]{:S(2)}, u32[]{:S(2)}) %all-to-all-start.13) | async-done | bytes 262176 | tf_op jit(solution)/shard_map/all_to_all | solution.py:39
  341.8 22.1 %all_to_all.103 = bf16[16,16,1024]{2,1,0:T(8,128)(2,1)S(1)} all-to-all(bf16[16,16,1024]{2,1,0:T(8,128)(2,1)S(1)} %broadcast_in_dim.48), channel_id=1, replica_groups=mesh['slab'=4,'row'=4,'col'=16] {'col'}, dimensions={0} | all-to-all | bytes 1048576 | tf_op jit(solution)/shard_map/all_to_all | solution.py:23
  375.7 8.6 %all_to_all.107 = f32[4,16,1024]{2,1,0:T(8,128)S(1)} all-to-all(f32[4,16,1024]{2,1,0:T(8,128)S(1)} %copy.210), channel_id=1, replica_groups=mesh['slab'=4,'row'=4,'col'=16] {'row'}, dimensions={0} | all-to-all | bytes 524288 | tf_op jit(solution)/shard_map/all_to_all | solution.py:39
  390.6 22.1 %all_to_all.104 = bf16[16,16,1024]{2,1,0:T(8,128)(2,1)S(1)} all-to-all(bf16[16,16,1024]{2,1,0:T(8,128)(2,1)S(1)} %broadcast_in_dim.49), channel_id=1, replica_groups=mesh['slab'=4,'row'=4,'col'=16] {'col'}, dimensions={0} | all-to-all | bytes 1048576 | tf_op jit(solution)/shard_map/all_to_all | solution.py:23
  424.5 8.6 %all_to_all.108 = f32[4,16,1024]{2,1,0:T(8,128)S(1)} all-to-all(f32[4,16,1024]{2,1,0:T(8,128)S(1)} %copy.217), channel_id=1, replica_groups=mesh['slab'=4,'row'=4,'col'=16] {'row'}, dimensions={0} | all-to-all | bytes 524288 | tf_op jit(solution)/shard_map/all_to_all | solution.py:39
  440.3 5.5 %all-to-all-start.18 = ((bf16[16,16,1024]{2,1,0:T(8,128)(2,1)}), bf16[16,16,1024]{2,1,0:T(8,128)(2,1)S(1)}, u32[]{:S(2)}, u32[]{:S(2)}) async-start(bf16[16,16,1024]{2,1,0:T(8,128)(2,1)} %broadcast_in_dim.50), calls=%async_computation.18 | async-start | bytes 1048576 | tf_op jit(solution)/shard_map/all_to_all | solution.py:23
  446.4 16.5 %all-to-all-done.18 = bf16[16,16,1024]{2,1,0:T(8,128)(2,1)S(1)} async-done(((bf16[16,16,1024]{2,1,0:T(8,128)(2,1)}), bf16[16,16,1024]{2,1,0:T(8,128)(2,1)S(1)}, u32[]{:S(2)}, u32[]{:S(2)}) %all-to-all-start.18) | async-done | bytes 524320 | tf_op jit(solution)/shard_map/all_to_all | solution.py:23
  479.3 5.6 %all-to-all-done.19 = f32[4,16,1024]{2,1,0:T(8,128)S(1)} async-done(((f32[4,16,1024]{2,1,0:T(8,128)}), f32[4,16,1024]{2,1,0:T(8,128)S(1)}, u32[]{:S(2)}, u32[]{:S(2)}) %all-to-all-start.19) | async-done | bytes 262176 | tf_op jit(solution)/shard_map/all_to_all | solution.py:39
  (228 shorter events, 216.5 us)
Async XLA Ops:
  5.3 27.2 %all-to-all-start = ((bf16[16,16,1024]{2,1,0:T(8,128)(2,1)}), bf16[16,16,1024]{2,1,0:T(8,128)(2,1)S(1)}, u32[]{:S(2)}, u32[]{:S(2)}) async-start(bf16[16,16,1024]{2,1,0:T(8,128)(2,1)} %broadcast_in_dim.41), calls=%async_computation | async-start | bytes 1048576 | tf_op jit(solution)/shard_map/all_to_all | solution.py:23
  15.2 4.5 collective-permute-start
  38.5 22.0 %copy-start.1 = (f32[1,32,1024]{2,1,0:T(8,128)S(1)}, f32[1,32,1024]{2,1,0:T(8,128)}, u32[]{:S(2)}) copy-start(f32[1,32,1024]{2,1,0:T(8,128)} %param.41) | copy-start | bytes 393220
  38.5 22.0 %copy-start.2 = (f32[1,256]{1,0:T(1,128)S(1)}, f32[1,256]{1,0:T(1,128)}, u32[]{:S(2)}) copy-start(f32[1,256]{1,0:T(1,128)} %param.47) | copy-start | bytes 3076
  44.8 10.5 %all-to-all-start.1 = ((f32[4,16,1024]{2,1,0:T(8,128)}), f32[4,16,1024]{2,1,0:T(8,128)S(1)}, u32[]{:S(2)}, u32[]{:S(2)}) async-start(f32[4,16,1024]{2,1,0:T(8,128)} %copy.162), calls=%async_computation.1 | async-start | bytes 524288 | tf_op jit(solution)/shard_map/all_to_all | solution.py:39
  56.4 4.1 collective-permute-start.1
  104.2 4.8 collective-permute-start.2
  153.4 4.8 collective-permute-start.3
  159.7 22.0 %all-to-all-start.6 = ((bf16[16,16,1024]{2,1,0:T(8,128)(2,1)}), bf16[16,16,1024]{2,1,0:T(8,128)(2,1)S(1)}, u32[]{:S(2)}, u32[]{:S(2)}) async-start(bf16[16,16,1024]{2,1,0:T(8,128)(2,1)} %broadcast_in_dim.44), calls=%async_computation.6 | async-start | bytes 1048576 | tf_op jit(solution)/shard_map/all_to_all | solution.py:23
  182.6 20.2 %all-to-all-start.10 = ((bf16[16,16,1024]{2,1,0:T(8,128)(2,1)}), bf16[16,16,1024]{2,1,0:T(8,128)(2,1)S(1)}, u32[]{:S(2)}, u32[]{:S(2)}) async-start(bf16[16,16,1024]{2,1,0:T(8,128)(2,1)} %broadcast_in_dim.46), calls=%async_computation.10 | async-start | bytes 1048576 | tf_op jit(solution)/shard_map/all_to_all | solution.py:23
  202.7 9.8 %all-to-all-start.7 = ((f32[4,16,1024]{2,1,0:T(8,128)}), f32[4,16,1024]{2,1,0:T(8,128)S(1)}, u32[]{:S(2)}, u32[]{:S(2)}) async-start(f32[4,16,1024]{2,1,0:T(8,128)} %copy.183), calls=%async_computation.7 | async-start | bytes 524288 | tf_op jit(solution)/shard_map/all_to_all | solution.py:39
  213.6 18.3 %collective-permute-start.4 = (f32[16,256]{1,0:T(8,128)S(1)}, f32[16,256]{1,0:T(8,128)S(1)}, u32[]{:S(2)}, u32[]{:S(2)}) collective-permute-start(f32[16,256]{1,0:T(8,128)S(1)} %select_bitcast_fusion), channel_id=1, source_target_pairs={{0,64},{64,128},{128,192},{1,65},{65,129},{129,193},{2,66},{66,130... | collective-permute-start | bytes 49160 | tf_op jit(solution)/shard_map/ppermute | solution.py:12
  222.2 21.6 %copy-start.3 = (s32[3]{0:T(128)S(1)}, s32[3]{0:T(128)}, u32[]{:S(2)}) copy-start(s32[3]{0:T(128)} %constant.488.clone.1) | copy-start | bytes 40
  228.5 9.4 %all-to-all-start.11 = ((f32[4,16,1024]{2,1,0:T(8,128)}), f32[4,16,1024]{2,1,0:T(8,128)S(1)}, u32[]{:S(2)}, u32[]{:S(2)}) async-start(f32[4,16,1024]{2,1,0:T(8,128)} %copy.196), calls=%async_computation.11 | async-start | bytes 524288 | tf_op jit(solution)/shard_map/all_to_all | solution.py:39
  238.7 22.3 %all-to-all-start.8 = ((bf16[16,16,1024]{2,1,0:T(8,128)(2,1)}), bf16[16,16,1024]{2,1,0:T(8,128)(2,1)S(1)}, u32[]{:S(2)}, u32[]{:S(2)}) async-start(bf16[16,16,1024]{2,1,0:T(8,128)(2,1)} %broadcast_in_dim.45), calls=%async_computation.8 | async-start | bytes 1048576 | tf_op jit(solution)/shard_map/all_to_all | solution.py:23
  273.5 9.6 %all-to-all-start.9 = ((f32[4,16,1024]{2,1,0:T(8,128)}), f32[4,16,1024]{2,1,0:T(8,128)S(1)}, u32[]{:S(2)}, u32[]{:S(2)}) async-start(f32[4,16,1024]{2,1,0:T(8,128)} %copy.190), calls=%async_computation.9 | async-start | bytes 524288 | tf_op jit(solution)/shard_map/all_to_all | solution.py:39
  284.4 4.5 collective-permute-start.5
  325.2 9.6 %all-to-all-start.13 = ((f32[4,16,1024]{2,1,0:T(8,128)}), f32[4,16,1024]{2,1,0:T(8,128)S(1)}, u32[]{:S(2)}, u32[]{:S(2)}) async-start(f32[4,16,1024]{2,1,0:T(8,128)} %copy.203), calls=%async_computation.13 | async-start | bytes 524288 | tf_op jit(solution)/shard_map/all_to_all | solution.py:39
  335.5 4.5 collective-permute-start.6
  384.3 4.5 collective-permute-start.7
  433.2 4.5 collective-permute-start.8
  440.3 22.6 %all-to-all-start.18 = ((bf16[16,16,1024]{2,1,0:T(8,128)(2,1)}), bf16[16,16,1024]{2,1,0:T(8,128)(2,1)S(1)}, u32[]{:S(2)}, u32[]{:S(2)}) async-start(bf16[16,16,1024]{2,1,0:T(8,128)(2,1)} %broadcast_in_dim.50), calls=%async_computation.18 | async-start | bytes 1048576 | tf_op jit(solution)/shard_map/all_to_all | solution.py:23
  475.2 9.6 %all-to-all-start.19 = ((f32[4,16,1024]{2,1,0:T(8,128)}), f32[4,16,1024]{2,1,0:T(8,128)S(1)}, u32[]{:S(2)}, u32[]{:S(2)}) async-start(f32[4,16,1024]{2,1,0:T(8,128)} %copy.224), calls=%async_computation.19 | async-start | bytes 524288 | tf_op jit(solution)/shard_map/all_to_all | solution.py:39
  485.5 0.7 copy-start
where the time goes:
time: 495 us; the launch traced here: 487 us
  blocking collectives  145 us (29%)
  waiting for transfers between devices  113 us (23%)
  other arithmetic  75.5 us (15%)
  starting transfers between devices  71.6 us (14%)
  matrix products  45 us (9%)
  local copies, waits for them, and re-layouts  34.6 us (7%)
    all_to_all x5, blocking collectives, from_everyone(): lax.all_to_all(jnp.broadcast_to(value[None], (devices, *value.shape)), ax...  110 us
    all_to_all x5, waiting for transfers between devices, from_everyone(): lax.all_to_all(jnp.broadcast_to(value[None], (devices, *value.shape)), ax...  62.7 us
    scatter-add x10, other arithmetic, front_apply(): partial_sum = jnp.zeros((batch_rows, row_count * blocks_dev, block_len),...  52.2 us
    dot_general x10, matrix products, front_apply(): jnp.einsum('wtk,tjk->wtj', picked, front, preferred_element_type=jnp.floa...  45 us
    all_to_all x4, blocking collectives, summed_on_arrival(): lax.all_to_all(in_blocks(value, dim, devices), axis, 0, 0, tiled=True)  34.5 us
    all_to_all x6, waiting for transfers between devices, summed_on_arrival(): lax.all_to_all(in_blocks(value, dim, devices), axis, 0, 0, tiled=True)  33.1 us
    all_to_all x5, starting transfers between devices, from_everyone(): lax.all_to_all(jnp.broadcast_to(value[None], (devices, *value.shape)), ax...  28.7 us
    ppermute x9, starting transfers between devices, from_behind(): return lax.ppermute(block, axis, route)  21.8 us
  transfers between devices with their start and end apart: 20, of which 19 were waited for; matrix products, arithmetic and copies ran while one was open for 7% of the time, Pallas kernels for 0%

commit v1 on v0

v1 whole, which is shorter than its diff:
```python
import functools

import jax
import jax.numpy as jnp
from jax import lax
from jax.experimental import pallas as pl
from jax.experimental.pallas import tpu as pltpu
from jax.sharding import PartitionSpec as P

B = 128
BLK = 8
NROW = 4
NCOL = 16
NSLAB = 4
W = 32
NT = 128
UNROLL = 8
TGT = 2
PRT = 4
LST = NT + UNROLL
BF = jnp.bfloat16
F32 = jnp.float32


def whole(shape):
    return pl.BlockSpec(shape, lambda *_: (0,) * len(shape))


def smem():
    return pl.BlockSpec(memory_space=pltpu.SMEM)


def lists_kernel(rows_ref, cols_ref, pos_ref, out_ref):
    base = pos_ref[0] * (NROW * BLK)

    def clear(i, _):
        for k in range(2):
            out_ref[3 * k, i] = 0
            out_ref[3 * k + 1, i] = NROW * BLK
            out_ref[3 * k + 2, i] = 0
        return 0

    lax.fori_loop(0, LST, clear, 0)

    def step(t, counts):
        row = rows_ref[0, t] - base
        col = cols_ref[0, t]
        part = col // (BLK * NROW)
        blk = col % BLK
        slot = (part % 2) * (NCOL // 2) + part // 2
        out_ref[7, t] = row
        out_ref[8, t] = slot * BLK + blk
        new = []
        for k, width in ((0, TGT), (1, PRT)):
            n = counts[k]
            out_ref[3 * k, n] = t
            out_ref[3 * k + 1, n] = row
            out_ref[3 * k + 2, n] = part * width + blk
            new.append(n + (blk < width).astype(jnp.int32))
        return tuple(new)

    counts = lax.fori_loop(0, NT, step, (0, 0))
    for k in range(2):
        n = counts[k]
        out_ref[3 * k, n] = 0
        out_ref[3 * k + 1, n] = NROW * BLK
        out_ref[3 * k + 2, n] = 0
        out_ref[6, k] = (n + UNROLL - 1) // UNROLL


def make_lists(tile_rows, tile_cols, col_index):
    return pl.pallas_call(
        lists_kernel,
        out_shape=jax.ShapeDtypeStruct((9, LST), jnp.int32),
        in_specs=[smem(), smem(), smem()],
        out_specs=smem(),
        name="lists",
    )(tile_rows, tile_cols, col_index)


def product(v, tile):
    return lax.dot_general(v, tile, (((1,), (1,)), ((), ())), preferred_element_type=F32)


def write_message(acc, msg_ref, kind):
    for r in range(NROW):
        if kind == "final":
            for b in range(BLK):
                msg_ref[r, b] = acc[r * BLK + b]
        else:
            for b in range(PRT if kind == "down" else TGT):
                part = acc[r * BLK + b].astype(BF)
                for s in range(NSLAB):
                    msg_ref[s * NROW + r, b] = part


def message_shape(kind):
    if kind == "final":
        return (NROW, BLK, W, B), F32
    return (NSLAB * NROW, PRT if kind == "down" else TGT, W, B), BF


def first_kernel(lst, v_ref, tiles_ref, acc_out, msg_ref, *, kind):
    acc_out[...] = jnp.zeros_like(acc_out)

    def group(g, _):
        base = g * UNROLL
        done = []
        for u in range(UNROLL):
            done.append(product(v_ref[lst[8, base + u]], tiles_ref[base + u]))
        for u in range(UNROLL):
            acc_out[lst[7, base + u]] += done[u]
        return 0

    lax.fori_loop(0, NT // UNROLL, group, 0)
    write_message(acc_out, msg_ref, kind)


def first_apply(lst, gathered, tiles, kind):
    shape, dtype = message_shape(kind)
    return pl.pallas_call(
        functools.partial(first_kernel, kind=kind),
        out_shape=(
            jax.ShapeDtypeStruct((NROW * BLK, W, B), F32),
            jax.ShapeDtypeStruct(shape, dtype),
        ),
        in_specs=[smem(), whole(gathered.shape), whole(tiles.shape)],
        out_specs=(whole((NROW * BLK, W, B)), whole(shape)),
        grid=(1,),
        name="first",
    )(lst, gathered, tiles)


def step_kernel(lst, flag, v_ref, tiles_ref, acc_in, acc_out, msg_ref, acc, buf, sems, *, which, kind):
    groups = lst[6, which] * flag[0]
    count = groups * UNROLL
    first = 3 * which

    def copy(i):
        return pltpu.make_async_copy(tiles_ref.at[lst[first, i]], buf.at[i], sems.at[i])

    def start(i, _):
        copy(i).start()
        return 0

    lax.fori_loop(0, count, start, 0)
    acc[: NROW * BLK] = acc_in[...]

    def group(g, _):
        base = g * UNROLL
        done = []
        for u in range(UNROLL):
            copy(base + u).wait()
        for u in range(UNROLL):
            done.append(product(v_ref[lst[first + 2, base + u]], buf[base + u]))
        for u in range(UNROLL):
            acc[lst[first + 1, base + u]] += done[u]
        return 0

    lax.fori_loop(0, groups, group, 0)
    if kind != "final":
        acc_out[...] = acc[: NROW * BLK]
    write_message(acc, msg_ref, kind)


def step_apply(lst, flag, gathered, tiles, acc, which, kind):
    shape, dtype = message_shape(kind)
    return pl.pallas_call(
        functools.partial(step_kernel, which=which, kind=kind),
        out_shape=(
            jax.ShapeDtypeStruct((NROW * BLK, W, B), F32),
            jax.ShapeDtypeStruct(shape, dtype),
        ),
        in_specs=[
            smem(),
            smem(),
            whole(gathered.shape),
            pl.BlockSpec(memory_space=pl.ANY),
            whole((NROW * BLK, W, B)),
        ],
        out_specs=(whole((NROW * BLK, W, B)), whole(shape)),
        grid=(1,),
        scratch_shapes=[
            pltpu.VMEM((NROW * BLK + 1, W, B), F32),
            pltpu.VMEM((LST, B, B), BF),
            pltpu.SemaphoreType.DMA((LST,)),
        ],
        input_output_aliases={4: 0},
        name="step_" + kind,
    )(lst, flag, gathered, tiles, acc)


def split3(x):
    high = x.astype(BF)
    rest = x - high.astype(F32)
    mid = rest.astype(BF)
    low = (rest - mid.astype(F32)).astype(BF)
    return jnp.concatenate([high, mid, low], axis=0)


def down_kernel(pos, rcv_ref, rhs_ref, coef_ref, hot_ref, out_ref):
    total = jnp.zeros((3 * W, TGT * B), F32)
    for b in range(PRT):
        part = rcv_ref[0, b].astype(F32)
        for r in range(1, NROW):
            part = part + rcv_ref[r, b].astype(F32)
        total = total + jnp.dot(
            split3(part), hot_ref[b * B : (b + 1) * B, :], preferred_element_type=F32
        )
    picked = total[:W] + total[W : 2 * W] + total[2 * W :]
    for b in range(TGT):
        cols = slice(b * B, (b + 1) * B)
        out_ref[b] = (rhs_ref[b] - picked[:, cols] * coef_ref[:, cols]).astype(BF)


def up_kernel(pos, rcv_ref, coef_ref, hot_ref, out_ref):
    total = jnp.zeros((3 * W, PRT * B), F32)
    for b in range(TGT):
        part = rcv_ref[0, b].astype(F32)
        for r in range(1, NROW):
            part = part + rcv_ref[r, b].astype(F32)
        part = part * coef_ref[:, b * B : (b + 1) * B]
        total = total + jnp.dot(
            split3(part), hot_ref[b * B : (b + 1) * B, :], preferred_element_type=F32
        )
    lifted = total[:W] + total[W : 2 * W] + total[2 * W :]
    for b in range(PRT):
        out_ref[b] = (-lifted[:, b * B : (b + 1) * B]).astype(BF)


def combine(kernel, pos, received, others, blocks, name):
    tail = received.shape[1:]
    return pl.pallas_call(
        kernel,
        out_shape=jax.ShapeDtypeStruct((blocks, W, B), BF),
        grid_spec=pltpu.PrefetchScalarGridSpec(
            num_scalar_prefetch=1,
            grid=(1,),
            in_specs=[pl.BlockSpec((NROW, *tail), lambda i, p: (p[0], 0, 0, 0))]
            + [whole(o.shape) for o in others],
            out_specs=whole((blocks, W, B)),
        ),
        name=name,
    )(pos, received, *others)


Z_GROUPS = [[2 * z + k for z in range(NCOL // 2)] for k in range(2)]
CORE_GROUPS = [[2 * z, 2 * z + 1] for z in range(NCOL // 2)]


def gather_first(value):
    copies = jnp.broadcast_to(value[None], (NCOL // 2, *value.shape))
    along = lax.all_to_all(copies, "col", 0, 0, tiled=True, axis_index_groups=Z_GROUPS)
    both = lax.all_gather(along, "col", axis_index_groups=CORE_GROUPS)
    return both.reshape(NCOL * value.shape[0], W, B)


def gather_step(value):
    return lax.all_gather(value, "col").reshape(NCOL * value.shape[0], W, B)


def exchange(message):
    return lax.all_to_all(message, ("slab", "row"), 0, 0, tiled=True)


def body(right_sides, front_tiles, tile_rows, tile_cols, section_blocks, plane_map, interface_coef):
    slab = lax.axis_index("slab").astype(jnp.int32)
    col = lax.axis_index("col").astype(jnp.int32)
    tiles = front_tiles[0]
    pack = jnp.concatenate([interface_coef, plane_map.astype(F32)], axis=0)
    pack_next = lax.ppermute(pack, "slab", [(s + 1, s) for s in range(NSLAB - 1)])
    coef_next = pack_next[0:1]
    map_next = pack_next[1].astype(jnp.int32)
    lst = make_lists(tile_rows, tile_cols, col.reshape(1))

    source = right_sides[0].reshape(W, BLK, B).transpose(1, 0, 2)
    blk = jnp.arange(BLK, dtype=jnp.int32)
    keep = (blk < section_blocks[0]) & ((slab == 0) | (blk >= TGT))
    v0 = jnp.where(keep[:, None, None], source, 0.0).astype(BF)
    rhs_target = source[:TGT]
    partner = jnp.arange(PRT * B, dtype=jnp.int32)
    hot_own = (partner[:, None] == plane_map[0][None, :]).astype(BF)
    hot_next = (map_next[:, None] == partner[None, :]).astype(BF)

    acc, msg = first_apply(lst, gather_first(v0), tiles, "down")
    before = jnp.maximum(slab - 1, 0).reshape(1)
    after = jnp.minimum(slab + 1, NSLAB - 1).reshape(1)
    for s in range(1, NSLAB):
        rcv = exchange(msg)
        v = combine(down_kernel, before, rcv, (rhs_target, interface_coef, hot_own), TGT, "down")
        flag = (slab == s).astype(jnp.int32).reshape(1)
        kind = "down" if s < NSLAB - 1 else "up"
        acc, msg = step_apply(lst, flag, gather_step(v), tiles, acc, 0, kind)
    for s in range(NSLAB - 2, -1, -1):
        rcv = exchange(msg)
        v = combine(up_kernel, after, rcv, (coef_next, hot_next), PRT, "up")
        flag = (slab == s).astype(jnp.int32).reshape(1)
        kind = "up" if s > 0 else "final"
        acc, msg = step_apply(lst, flag, gather_step(v), tiles, acc, 1, kind)
    parts = lax.all_to_all(msg, "row", 0, 0, tiled=True)
    total = jnp.sum(parts, axis=0)
    total = jnp.where((blk < section_blocks[0])[:, None, None], total, 0.0)
    return total.transpose(1, 0, 2).reshape(1, W, BLK * B)


def solution(mesh):
    placed = (
        P("slab", None, ("col", "row")),
        P("slab", ("col", "row"), None, None),
        P("slab", ("col", "row")),
        P("slab", ("col", "row")),
        P("slab"),
        P("slab", ("col", "row")),
        P("slab", ("col", "row")),
    )
    return jax.shard_map(
        body, mesh=mesh, in_specs=placed, out_specs=P("slab", None, ("col", "row")), check_vma=False
    )
```

time: 495 us -> 321 us (0.65); the launches traced: 487 us -> 319 us
  other arithmetic: 75.5 us -> 2.41 us
  waiting for transfers between devices: 113 us -> 61.7 us
  Pallas kernels: 0 us -> 48.7 us
  matrix products: 45 us -> 0 us
  starting transfers between devices: 71.6 us -> 30.2 us
  local copies, waits for them, and re-layouts: 34.6 us -> 6.3 us
  between operations: 2.31 us -> 14.3 us
  blocking collectives: 145 us -> 156 us
    all_gather x0 -> x6, blocking collectives: none -> 116 us  [gather_step(): return lax.all_gather(value, 'col').reshape(NCOL * value.shape[0], W, B)]
    all_to_all x9 -> x2, blocking collectives: 145 us -> 39.7 us  [the longest x1 25 us: gather_first(): lax.all_to_all(copies, 'col', 0, 0, tiled=True, axis_index_groups=Z_GROUPS)]
    scatter-add x20 -> x0, other arithmetic: 63.9 us -> none  [the longest x10 52.2 us: front_apply(): partial_sum = jnp.zeros((batch_rows, row_count * blocks_dev, block_len),...]
    pallas_call x0 -> x14, Pallas kernels: none -> 48.7 us  [the longest x6 23.6 us: step_apply(): pl.pallas_call(functools.partial(step_kernel, which=which, kind=kind), ou...]
    dot_general x10 -> x0, matrix products: 45 us -> none  [front_apply(): jnp.einsum('wtk,tjk->wtj', picked, front, preferred_element_type=jnp.floa...]
    all_to_all x11 -> x6, waiting for transfers between devices: 95.8 us -> 55 us  [the longest x5 45.6 us: exchange(): return lax.all_to_all(message, ('slab', 'row'), 0, 0, tiled=True)]
    all_to_all x11 -> x6, starting transfers between devices: 49.8 us -> 28.9 us  [the longest x5 25.4 us: exchange(): return lax.all_to_all(message, ('slab', 'row'), 0, 0, tiled=True)]
    ppermute x9 -> x1, starting transfers between devices: 21.8 us -> 1.29 us  [body(): lax.ppermute(pack, 'slab', [(s + 1, s) for s in range(NSLAB - 1)])]
  transfers between devices with their start and end apart: 20 -> 8, of which waited for: 19 -> 7; matrix products, arithmetic and copies ran while one was open for 7% -> 1% of each run, Pallas kernels for 0% -> 4%
where the time goes in v1:
time: 321 us; the launch traced here: 319 us
  blocking collectives  156 us (49%)
  waiting for transfers between devices  61.7 us (19%)
  Pallas kernels  48.7 us (15%)
  starting transfers between devices  30.2 us (9%)
  between operations  14.3 us (4%)
  local copies, waits for them, and re-layouts  6.3 us (2%)
    all_gather x6, blocking collectives, gather_step(): return lax.all_gather(value, 'col').reshape(NCOL * value.shape[0], W, B)  116 us
    all_to_all x5, waiting for transfers between devices, exchange(): return lax.all_to_all(message, ('slab', 'row'), 0, 0, tiled=True)  45.6 us
    all_to_all x5, starting transfers between devices, exchange(): return lax.all_to_all(message, ('slab', 'row'), 0, 0, tiled=True)  25.4 us
    all_to_all x1, blocking collectives, gather_first(): lax.all_to_all(copies, 'col', 0, 0, tiled=True, axis_index_groups=Z_GROUPS)  25 us
    pallas_call x6, Pallas kernels, step_apply(): pl.pallas_call(functools.partial(step_kernel, which=which, kind=kind), ou...  23.6 us
    all_to_all x1, blocking collectives, exchange(): return lax.all_to_all(message, ('slab', 'row'), 0, 0, tiled=True)  14.7 us
    pallas_call x6, Pallas kernels, combine(): pl.pallas_call(kernel, out_shape=jax.ShapeDtypeStruct((blocks, W, B), BF)...  11 us
    all_to_all x1, waiting for transfers between devices, body(): parts = lax.all_to_all(msg, 'row', 0, 0, tiled=True)  9.36 us
  transfers between devices with their start and end apart: 8, of which 7 were waited for; matrix products, arithmetic and copies ran while one was open for 1% of the time, Pallas kernels for 4%

profile of v1, /device:TPU:1, one launch (start us, length us, event | category | flops | bytes accessed | tf_op | source)
XLA Modules:
  0.0 319.1 jit_solution(14778072211674983041)
XLA Ops:
  8.3 25.0 %all_to_all.40 = bf16[8,8,32,128]{3,2,1,0:T(8,128)(2,1)} all-to-all(bf16[8,8,32,128]{3,2,1,0:T(8,128)(2,1)S(1)} %broadcast_in_dim.32), channel_id=1, replica_groups={{0,2,4,6,8,10,12,14},{1,3,5,7,9,11,13,15},{16,18,20,22,24,26,28,30},{17..., dimensions={0} | all-to-all | bytes 1048576 | tf_op jit(solution)/shard_map/all_to_all | solution.py:253
  33.4 6.5 %lists.1.lst = s32[9,136]{1,0:T(8,128)} custom-call(s32[1,128]{1,0:T(1,128)} %rows_ref.1, s32[1,128]{1,0:T(1,128)} %cols_ref.1, s32[1]{0:T(128)} %bitcast.1.pos_ref), custom_call_target="tpu_custom_call" | custom-call | tf_op jit(solution)/shard_map/lists/pallas_call | solution.py:72
  39.9 6.7 %all-gather.9.cloned.1.call-done = bf16[16,8,32,128]{3,2,1,0:T(8,128)(2,1)} async-done(((bf16[8,8,32,128]{3,2,1,0:T(8,128)(2,1)}), bf16[16,8,32,128]{3,2,1,0:T(8,128)(2,1)}) %all-gather.9.cloned.1.call-update) | async-done | bytes 1048592 | tf_op jit(solution)/shard_map/all_gather | solution.py:254
  46.6 7.6 %first.1 = (f32[32,32,128]{2,1,0:T(8,128)}, bf16[16,4,32,128]{3,2,1,0:T(8,128)(2,1)}) custom-call(s32[9,136]{1,0:T(8,128)} %lists.1.lst, bf16[128,32,128]{2,1,0:T(8,128)(2,1)} %bitcast.33, bf16[128,128,128]{2,1,0:T(8,128)(2,1)} %bitcast.24), custom_call_target="tpu_custom_call" | custom-call | tf_op jit(solution)/shard_map/first/pallas_call | solution.py:121
  54.2 6.3 %all-to-all-start.1 = ((bf16[16,4,32,128]{3,2,1,0:T(8,128)(2,1)}), bf16[16,4,32,128]{3,2,1,0:T(8,128)(2,1)S(1)}, u32[]{:S(2)}, u32[]{:S(2)}) async-start(bf16[16,4,32,128]{3,2,1,0:T(8,128)(2,1)} %get-tuple-element.18), calls=%async_computation.1 | async-start | bytes 1048576 | tf_op jit(solution)/shard_map/all_to_all | solution.py:263
  61.9 9.4 %all-to-all-done.1.rcv_ref = bf16[16,4,32,128]{3,2,1,0:T(8,128)(2,1)S(1)} async-done(((bf16[16,4,32,128]{3,2,1,0:T(8,128)(2,1)}), bf16[16,4,32,128]{3,2,1,0:T(8,128)(2,1)S(1)}, u32[]{:S(2)}, u32[]{:S(2)}) %all-to-all-start.1) | async-done | bytes 524320 | tf_op jit(solution)/shard_map/all_to_all | solution.py:263
  74.0 21.2 %all-gather.1.v_ref = bf16[32,32,128]{2,1,0:T(8,128)(2,1)} all-gather(bf16[2,32,128]{2,1,0:T(8,128)(2,1)} %down.3), channel_id=3, replica_groups=mesh['slab'=4,'row'=4,'col'=16] {'col'}, dimensions={0}, use_global_device_ids=true | all-gather | bytes 278528 | tf_op jit(solution)/shard_map/all_gather | solution.py:259
  98.7 4.2 %all-to-all-start.2 = ((bf16[16,4,32,128]{3,2,1,0:T(8,128)(2,1)}), bf16[16,4,32,128]{3,2,1,0:T(8,128)(2,1)S(1)}, u32[]{:S(2)}, u32[]{:S(2)}) async-start(bf16[16,4,32,128]{3,2,1,0:T(8,128)(2,1)} %get-tuple-element.20), calls=%async_computation.2 | async-start | bytes 1048576 | tf_op jit(solution)/shard_map/all_to_all | solution.py:263
  102.9 11.2 %all-to-all-done.2.rcv_ref = bf16[16,4,32,128]{3,2,1,0:T(8,128)(2,1)S(1)} async-done(((bf16[16,4,32,128]{3,2,1,0:T(8,128)(2,1)}), bf16[16,4,32,128]{3,2,1,0:T(8,128)(2,1)S(1)}, u32[]{:S(2)}, u32[]{:S(2)}) %all-to-all-start.2) | async-done | bytes 524320 | tf_op jit(solution)/shard_map/all_to_all | solution.py:263
  116.7 18.4 %all-gather.2.v_ref = bf16[32,32,128]{2,1,0:T(8,128)(2,1)} all-gather(bf16[2,32,128]{2,1,0:T(8,128)(2,1)} %down.4), channel_id=4, replica_groups=mesh['slab'=4,'row'=4,'col'=16] {'col'}, dimensions={0}, use_global_device_ids=true | all-gather | bytes 278528 | tf_op jit(solution)/shard_map/all_gather | solution.py:259
  138.6 4.8 %all-to-all-start.3 = ((bf16[16,4,32,128]{3,2,1,0:T(8,128)(2,1)}), bf16[16,4,32,128]{3,2,1,0:T(8,128)(2,1)S(1)}, u32[]{:S(2)}, u32[]{:S(2)}) async-start(bf16[16,4,32,128]{3,2,1,0:T(8,128)(2,1)} %get-tuple-element.22), calls=%async_computation.3 | async-start | bytes 1048576 | tf_op jit(solution)/shard_map/all_to_all | solution.py:263
  144.7 9.5 %all-to-all-done.3.rcv_ref = bf16[16,4,32,128]{3,2,1,0:T(8,128)(2,1)S(1)} async-done(((bf16[16,4,32,128]{3,2,1,0:T(8,128)(2,1)}), bf16[16,4,32,128]{3,2,1,0:T(8,128)(2,1)S(1)}, u32[]{:S(2)}, u32[]{:S(2)}) %all-to-all-start.3) | async-done | bytes 524320 | tf_op jit(solution)/shard_map/all_to_all | solution.py:263
  156.9 19.0 %all-gather.3.v_ref = bf16[32,32,128]{2,1,0:T(8,128)(2,1)} all-gather(bf16[2,32,128]{2,1,0:T(8,128)(2,1)} %down.5), channel_id=5, replica_groups=mesh['slab'=4,'row'=4,'col'=16] {'col'}, dimensions={0}, use_global_device_ids=true | all-gather | bytes 278528 | tf_op jit(solution)/shard_map/all_gather | solution.py:259
  179.3 4.6 %all-to-all-start.4 = ((bf16[16,2,32,128]{3,2,1,0:T(8,128)(2,1)}), bf16[16,2,32,128]{3,2,1,0:T(8,128)(2,1)S(1)}, u32[]{:S(2)}, u32[]{:S(2)}) async-start(bf16[16,2,32,128]{3,2,1,0:T(8,128)(2,1)} %get-tuple-element.24), calls=%async_computation.4 | async-start | bytes 524288 | tf_op jit(solution)/shard_map/all_to_all | solution.py:263
  185.4 6.9 %all-to-all-done.4.rcv_ref = bf16[16,2,32,128]{3,2,1,0:T(8,128)(2,1)S(1)} async-done(((bf16[16,2,32,128]{3,2,1,0:T(8,128)(2,1)}), bf16[16,2,32,128]{3,2,1,0:T(8,128)(2,1)S(1)}, u32[]{:S(2)}, u32[]{:S(2)}) %all-to-all-start.4) | async-done | bytes 262176 | tf_op jit(solution)/shard_map/all_to_all | solution.py:263
  194.9 19.0 %all-gather.4.v_ref = bf16[64,32,128]{2,1,0:T(8,128)(2,1)} all-gather(bf16[4,32,128]{2,1,0:T(8,128)(2,1)} %up.3), channel_id=6, replica_groups=mesh['slab'=4,'row'=4,'col'=16] {'col'}, dimensions={0}, use_global_device_ids=true | all-gather | bytes 557056 | tf_op jit(solution)/shard_map/all_gather | solution.py:259
  217.3 14.7 %all_to_all.41.rcv_ref = bf16[16,2,32,128]{3,2,1,0:T(8,128)(2,1)} all-to-all(bf16[16,2,32,128]{3,2,1,0:T(8,128)(2,1)} %get-tuple-element.26), channel_id=1, replica_groups=mesh['slab'=4,'row'=4,'col'=16] {'slab','row'}, dimensions={0} | all-to-all | bytes 524288 | tf_op jit(solution)/shard_map/all_to_all | solution.py:263
  233.8 19.4 %all-gather.5.v_ref = bf16[64,32,128]{2,1,0:T(8,128)(2,1)} all-gather(bf16[4,32,128]{2,1,0:T(8,128)(2,1)} %up.4), channel_id=7, replica_groups=mesh['slab'=4,'row'=4,'col'=16] {'col'}, dimensions={0}, use_global_device_ids=true | all-gather | bytes 557056 | tf_op jit(solution)/shard_map/all_gather | solution.py:259
  256.7 5.6 %all-to-all-start.6 = ((bf16[16,2,32,128]{3,2,1,0:T(8,128)(2,1)}), bf16[16,2,32,128]{3,2,1,0:T(8,128)(2,1)S(1)}, u32[]{:S(2)}, u32[]{:S(2)}) async-start(bf16[16,2,32,128]{3,2,1,0:T(8,128)(2,1)} %get-tuple-element.28), calls=%async_computation.6 | async-start | bytes 524288 | tf_op jit(solution)/shard_map/all_to_all | solution.py:263
  262.3 8.6 %all-to-all-done.6.rcv_ref = bf16[16,2,32,128]{3,2,1,0:T(8,128)(2,1)S(1)} async-done(((bf16[16,2,32,128]{3,2,1,0:T(8,128)(2,1)}), bf16[16,2,32,128]{3,2,1,0:T(8,128)(2,1)S(1)}, u32[]{:S(2)}, u32[]{:S(2)}) %all-to-all-start.6) | async-done | bytes 262176 | tf_op jit(solution)/shard_map/all_to_all | solution.py:263
  273.4 18.7 %all-gather.6.v_ref = bf16[64,32,128]{2,1,0:T(8,128)(2,1)} all-gather(bf16[4,32,128]{2,1,0:T(8,128)(2,1)} %up.5), channel_id=8, replica_groups=mesh['slab'=4,'row'=4,'col'=16] {'col'}, dimensions={0}, use_global_device_ids=true | all-gather | bytes 557056 | tf_op jit(solution)/shard_map/all_gather | solution.py:259
  292.1 6.4 %step_final.1 = (f32[32,32,128]{2,1,0:T(8,128)}, f32[4,8,32,128]{3,2,1,0:T(8,128)}) custom-call(s32[9,136]{1,0:T(8,128)} %lists.1.lst, s32[1]{0:T(128)} %bitcast.2.flag, bf16[64,32,128]{2,1,0:T(8,128)(2,1)} %all-gather.6.v_ref, bf16[128,128,128]{2,1,0:T(8,128)(2,1)} %bitcast.30, f32[32,32,128]{2,1,0:T(8,128)} %get-tuple-element.29.acc_in), custom_call_target="tpu_custom_call", output_to_operand_aliasing={{0}: (4, {})} | custom-call | tf_op jit(solution)/shard_map/step_final/pallas_call | solution.py:168
  298.5 3.5 %all-to-all-start.7 = ((f32[4,8,32,128]{3,2,1,0:T(8,128)}), f32[4,8,32,128]{3,2,1,0:T(8,128)S(1)}, u32[]{:S(2)}, u32[]{:S(2)}) async-start(f32[4,8,32,128]{3,2,1,0:T(8,128)} %get-tuple-element.30), calls=%async_computation.7 | async-start | bytes 1048576 | tf_op jit(solution)/shard_map/all_to_all | solution.py:300
  302.0 9.4 %all-to-all-done.7 = f32[4,8,32,128]{3,2,1,0:T(8,128)S(1)} async-done(((f32[4,8,32,128]{3,2,1,0:T(8,128)}), f32[4,8,32,128]{3,2,1,0:T(8,128)S(1)}, u32[]{:S(2)}, u32[]{:S(2)}) %all-to-all-start.7) | async-done | bytes 524320 | tf_op jit(solution)/shard_map/all_to_all | solution.py:300
  (45 shorter events, 38.1 us)
Async XLA Ops:
  6.5 40.1 %all-gather.9.cloned.1.call-start = ((), (), s32[]{:S(2)}) async-start(), calls=%async_computation.8 | async-start | bytes 1572864 | tf_op jit(solution)/shard_map/all_gather | solution.py:254
  8.3 52.8 %copy-start.6 = (s32[1,256]{1,0:T(1,128)S(1)}, s32[1,256]{1,0:T(1,128)}, u32[]{:S(2)}) copy-start(s32[1,256]{1,0:T(1,128)} %param.12) | copy-start | bytes 3076
  54.2 17.1 %all-to-all-start.1 = ((bf16[16,4,32,128]{3,2,1,0:T(8,128)(2,1)}), bf16[16,4,32,128]{3,2,1,0:T(8,128)(2,1)S(1)}, u32[]{:S(2)}, u32[]{:S(2)}) async-start(bf16[16,4,32,128]{3,2,1,0:T(8,128)(2,1)} %get-tuple-element.18), calls=%async_computation.1 | async-start | bytes 1048576 | tf_op jit(solution)/shard_map/all_to_all | solution.py:263
  71.3 0.8 copy-start.1
  98.7 44.7 %copy-start.5 = (f32[1,256]{1,0:T(1,128)S(1)}, f32[1,256]{1,0:T(1,128)}, u32[]{:S(2)}) copy-start(f32[1,256]{1,0:T(1,128)} %coef_ref.5) | copy-start | bytes 3076
  98.7 15.3 %all-to-all-start.2 = ((bf16[16,4,32,128]{3,2,1,0:T(8,128)(2,1)}), bf16[16,4,32,128]{3,2,1,0:T(8,128)(2,1)S(1)}, u32[]{:S(2)}, u32[]{:S(2)}) async-start(bf16[16,4,32,128]{3,2,1,0:T(8,128)(2,1)} %get-tuple-element.20), calls=%async_computation.2 | async-start | bytes 1048576 | tf_op jit(solution)/shard_map/all_to_all | solution.py:263
  114.0 0.8 copy-start.2
  138.6 15.7 %all-to-all-start.3 = ((bf16[16,4,32,128]{3,2,1,0:T(8,128)(2,1)}), bf16[16,4,32,128]{3,2,1,0:T(8,128)(2,1)S(1)}, u32[]{:S(2)}, u32[]{:S(2)}) async-start(bf16[16,4,32,128]{3,2,1,0:T(8,128)(2,1)} %get-tuple-element.22), calls=%async_computation.3 | async-start | bytes 1048576 | tf_op jit(solution)/shard_map/all_to_all | solution.py:263
  143.4 40.6 %collective-permute-start = (f32[2,256]{1,0:T(2,128)S(1)}, f32[2,256]{1,0:T(2,128)S(1)}, u32[]{:S(2)}, u32[]{:S(2)}) collective-permute-start(f32[2,256]{1,0:T(2,128)S(1)} %pad_maximum_fusion), channel_id=1, source_target_pairs={{64,0},{128,64},{192,128},{65,1},{129,65},{193,129},{66,2},{130,66... | collective-permute-start | bytes 6152 | tf_op jit(solution)/shard_map/ppermute | solution.py:271
  154.3 0.8 copy-start
  179.3 13.0 %all-to-all-start.4 = ((bf16[16,2,32,128]{3,2,1,0:T(8,128)(2,1)}), bf16[16,2,32,128]{3,2,1,0:T(8,128)(2,1)S(1)}, u32[]{:S(2)}, u32[]{:S(2)}) async-start(bf16[16,2,32,128]{3,2,1,0:T(8,128)(2,1)} %get-tuple-element.24), calls=%async_computation.4 | async-start | bytes 524288 | tf_op jit(solution)/shard_map/all_to_all | solution.py:263
  192.3 0.7 copy-start.3
  256.7 14.1 %all-to-all-start.6 = ((bf16[16,2,32,128]{3,2,1,0:T(8,128)(2,1)}), bf16[16,2,32,128]{3,2,1,0:T(8,128)(2,1)S(1)}, u32[]{:S(2)}, u32[]{:S(2)}) async-start(bf16[16,2,32,128]{3,2,1,0:T(8,128)(2,1)} %get-tuple-element.28), calls=%async_computation.6 | async-start | bytes 524288 | tf_op jit(solution)/shard_map/all_to_all | solution.py:263
  270.8 0.7 copy-start.4
  298.5 12.9 %all-to-all-start.7 = ((f32[4,8,32,128]{3,2,1,0:T(8,128)}), f32[4,8,32,128]{3,2,1,0:T(8,128)S(1)}, u32[]{:S(2)}, u32[]{:S(2)}) async-start(f32[4,8,32,128]{3,2,1,0:T(8,128)} %get-tuple-element.30), calls=%async_computation.7 | async-start | bytes 1048576 | tf_op jit(solution)/shard_map/all_to_all | solution.py:300
Sparse Core Ops, SparseCore 0:
  33.5 13.0 all-gather.8

commit v2 on v1

v2 whole, which is shorter than its diff:
```python
import functools

import jax
import jax.numpy as jnp
from jax import lax
from jax.experimental import pallas as pl
from jax.experimental.pallas import tpu as pltpu
from jax.sharding import PartitionSpec as P

B = 128
BLK = 8
NROW = 4
NCOL = 16
NSLAB = 4
W = 32
NT = 128
UNROLL = 8
TGT = 2
PRT = 4
LST = NT + UNROLL
BF = jnp.bfloat16
F32 = jnp.float32


def smem():
    return pl.BlockSpec(memory_space=pltpu.SMEM)


def vmem():
    return pl.BlockSpec(memory_space=pltpu.VMEM)


PARAMS = pltpu.CompilerParams(vmem_limit_bytes=24 * 2**20)
ACC = (NROW * BLK + 1, W, B)
LISTS = 4
TAB, TC, LA, LALL = range(LISTS)


def lists_kernel(rows_ref, cols_ref, pos_ref, out_ref):
    base = pos_ref[0] * (NROW * BLK)

    def step(t, counts):
        row = rows_ref[0, t] - base
        col = cols_ref[0, t]
        part = col // (BLK * NROW)
        blk = col % BLK
        out = row % BLK
        head = t + row * NT
        wide = head + (part * PRT + blk) * (64 * NT)
        narrow = head + (part * TGT + blk) * (64 * NT)
        target = blk < TGT
        low = blk < PRT
        member = (
            (narrow, target & (out < PRT)),
            (narrow, target & (out >= PRT)),
            (wide, low & (out < TGT)),
            (wide, low),
        )
        for k in range(LISTS):
            out_ref[k, counts[k]] = member[k][0]
        return tuple(counts[k] + member[k][1].astype(jnp.int32) for k in range(LISTS))

    counts = lax.fori_loop(0, NT, step, (0,) * LISTS)
    for k in range(LISTS):
        for u in range(UNROLL):
            out_ref[k, counts[k] + u] = NROW * BLK * NT
        out_ref[LISTS, k] = (counts[k] + UNROLL - 1) // UNROLL


def make_lists(tile_rows, tile_cols, col_index):
    return pl.pallas_call(
        lists_kernel,
        out_shape=jax.ShapeDtypeStruct((LISTS + 1, LST), jnp.int32),
        in_specs=[smem(), smem(), smem()],
        out_specs=smem(),
        name="lists",
    )(tile_rows, tile_cols, col_index)


def product(v, tile):
    return lax.dot_general(v, tile, (((1,), (1,)), ((), ())), preferred_element_type=F32)


def apply_list(lst, which, v_ref, tiles_ref, acc):
    def group(g, _):
        entries = [lst[which, g * UNROLL + u] for u in range(UNROLL)]
        done = [product(v_ref[e // (64 * NT)], tiles_ref[e % NT]) for e in entries]
        for e, d in zip(entries, done):
            acc[e // NT % 64] += d
        return 0

    lax.fori_loop(0, lst[LISTS, which], group, 0)


def write_message(acc, msg_ref, kind):
    for r in range(NROW):
        if kind == "final":
            for b in range(BLK):
                msg_ref[r, b] = acc[r * BLK + b]
        else:
            for b in range(PRT if kind == "down" else TGT):
                part = acc[r * BLK + b].astype(BF)
                for s in range(NSLAB):
                    msg_ref[s * NROW + r, b] = part


def message_shape(kind):
    if kind == "final":
        return jax.ShapeDtypeStruct((NROW, BLK, W, B), F32)
    return jax.ShapeDtypeStruct((NSLAB * NROW, PRT if kind == "down" else TGT, W, B), BF)


def first_kernel(rows_ref, cols_ref, pos, own_ref, other_ref, tiles_ref, acc, msg_ref):
    acc[...] = jnp.zeros(ACC, F32)
    base = pos[0] * (NROW * BLK)
    core = pos[0] % 2

    def group(g, _):
        rows, done = [], []
        for u in range(UNROLL):
            t = g * UNROLL + u
            col = cols_ref[0, t]
            part = col // (BLK * NROW)
            at = part // 2 * BLK + col % BLK
            v = jnp.where(part % 2 == core, own_ref[at], other_ref[at])
            rows.append(rows_ref[0, t] - base)
            done.append(product(v, tiles_ref[t]))
        for r, d in zip(rows, done):
            acc[r] += d
        return 0

    lax.fori_loop(0, NT // UNROLL, group, 0)
    write_message(acc, msg_ref, "down")


def first_apply(tile_rows, tile_cols, pos, own, other, tiles):
    return pl.pallas_call(
        first_kernel,
        out_shape=(jax.ShapeDtypeStruct(ACC, F32), message_shape("down")),
        in_specs=[smem(), smem(), smem(), vmem(), vmem(), vmem()],
        out_specs=(vmem(), vmem()),
        compiler_params=PARAMS,
        name="first",
    )(tile_rows, tile_cols, pos, own, other, tiles)


def down_step_kernel(lst, flag, v_ref, tiles_ref, acc_in, acc, msg_ref, *, kind):
    @pl.when(flag[0] == 1)
    def _():
        apply_list(lst, TAB, v_ref, tiles_ref, acc)

    write_message(acc, msg_ref, kind)


def down_step(lst, flag, gathered, tiles, acc, kind):
    return pl.pallas_call(
        functools.partial(down_step_kernel, kind=kind),
        out_shape=(jax.ShapeDtypeStruct(ACC, F32), message_shape(kind)),
        in_specs=[smem(), smem(), vmem(), vmem(), vmem()],
        out_specs=(vmem(), vmem()),
        input_output_aliases={4: 0},
        compiler_params=PARAMS,
        name="down_step",
    )(lst, flag, gathered, tiles, acc)


def up_step_kernel(lst, flag, v_ref, tiles_ref, acc_in, msg_ref, acc):
    for r in range(NROW):
        for b in range(TGT):
            acc[r * BLK + b] = acc_in[r * BLK + b]

    @pl.when(flag[0] == 1)
    def _():
        apply_list(lst, LA, v_ref, tiles_ref, acc)

    write_message(acc, msg_ref, "up")


def up_step(lst, flag, gathered, tiles, acc):
    return pl.pallas_call(
        up_step_kernel,
        out_shape=message_shape("up"),
        in_specs=[smem(), smem(), vmem(), vmem(), vmem()],
        out_specs=vmem(),
        scratch_shapes=[pltpu.VMEM(ACC, F32)],
        compiler_params=PARAMS,
        name="up_step",
    )(lst, flag, gathered, tiles, acc)


def last_kernel(lst, pos, tiles_ref, v1, v2, v3, l2, l1, l0, acc_in, acc, msg_ref):
    for s, v_ref in ((1, v1), (2, v2), (3, v3)):
        @pl.when(pos[0] == s)
        def _(v_ref=v_ref):
            apply_list(lst, TC, v_ref, tiles_ref, acc)

    for s, v_ref in ((2, l2), (1, l1), (0, l0)):
        @pl.when(pos[0] == s)
        def _(v_ref=v_ref):
            apply_list(lst, LALL, v_ref, tiles_ref, acc)

    write_message(acc, msg_ref, "final")


def last_apply(lst, slab, tiles, downs, ups, acc):
    return pl.pallas_call(
        last_kernel,
        out_shape=(jax.ShapeDtypeStruct(ACC, F32), message_shape("final")),
        in_specs=[smem(), smem()] + [vmem()] * 8,
        out_specs=(vmem(), vmem()),
        input_output_aliases={9: 0},
        compiler_params=PARAMS,
        name="last",
    )(lst, slab, tiles, *downs, *ups, acc)[1]


def split(x):
    high = x.astype(BF)
    rest = x - high.astype(F32)
    return jnp.concatenate([high, rest.astype(BF)], axis=0)


def row_total(rcv_ref, pos, b):
    part = rcv_ref[pos[0] * NROW, b].astype(F32)
    for r in range(1, NROW):
        part = part + rcv_ref[pos[0] * NROW + r, b].astype(F32)
    return part


def down_kernel(pos, rcv_ref, rhs_ref, coef_ref, hot_ref, out_ref):
    values = jnp.concatenate([split(row_total(rcv_ref, pos, b)) for b in range(PRT)], axis=1)
    total = jnp.dot(values, hot_ref[...], preferred_element_type=F32)
    picked = total[:W] + total[W:]
    for b in range(TGT):
        cols = slice(b * B, (b + 1) * B)
        out_ref[b] = (rhs_ref[b] - picked[:, cols] * coef_ref[:, cols]).astype(BF)


def up_kernel(pos, rcv_ref, coef_ref, hot_ref, out_ref):
    values = jnp.concatenate(
        [
            split(row_total(rcv_ref, pos, b) * coef_ref[:, b * B : (b + 1) * B])
            for b in range(TGT)
        ],
        axis=1,
    )
    total = jnp.dot(values, hot_ref[...], preferred_element_type=F32)
    lifted = total[:W] + total[W:]
    for b in range(PRT):
        out_ref[b] = (-lifted[:, b * B : (b + 1) * B]).astype(BF)


def combine(kernel, pos, received, others, blocks, name):
    return pl.pallas_call(
        kernel,
        out_shape=jax.ShapeDtypeStruct((blocks, W, B), BF),
        in_specs=[smem()] + [vmem()] * (1 + len(others)),
        out_specs=vmem(),
        compiler_params=PARAMS,
        name=name,
    )(pos, received, *others)


Z_GROUPS = [[2 * z + k for z in range(NCOL // 2)] for k in range(2)]


def gather_first(value):
    copies = jnp.broadcast_to(value[None], (NCOL // 2, *value.shape))
    along = lax.all_to_all(copies, "col", 0, 0, tiled=True, axis_index_groups=Z_GROUPS)
    along = along.reshape(NCOL // 2 * value.shape[0], W, B)
    return along, lax.ppermute(along, "col", [(c, c ^ 1) for c in range(NCOL)])


def gather_step(value):
    return lax.all_gather(value, "col").reshape(NCOL * value.shape[0], W, B)


def exchange(message):
    return lax.all_to_all(message, ("slab", "row"), 0, 0, tiled=True)


def body(right_sides, front_tiles, tile_rows, tile_cols, section_blocks, plane_map, interface_coef):
    slab = lax.axis_index("slab").astype(jnp.int32)
    col = lax.axis_index("col").astype(jnp.int32)
    tiles = front_tiles[0]
    pack = jnp.concatenate([interface_coef, plane_map.astype(F32)], axis=0)
    pack_next = lax.ppermute(pack, "slab", [(s + 1, s) for s in range(NSLAB - 1)])
    coef_next = pack_next[0:1]
    map_next = pack_next[1].astype(jnp.int32)
    lst = make_lists(tile_rows, tile_cols, col.reshape(1))

    source = right_sides[0].reshape(W, BLK, B).transpose(1, 0, 2)
    blk = jnp.arange(BLK, dtype=jnp.int32)
    keep = (blk < section_blocks[0]) & ((slab == 0) | (blk >= TGT))
    v0 = jnp.where(keep[:, None, None], source, 0.0).astype(BF)
    rhs_target = source[:TGT]
    partner = jnp.arange(PRT * B, dtype=jnp.int32)
    hot_own = (partner[:, None] == plane_map[0][None, :]).astype(BF)
    hot_next = (map_next[:, None] == partner[None, :]).astype(BF)

    own, other = gather_first(v0)
    acc, msg = first_apply(tile_rows, tile_cols, col.reshape(1), own, other, tiles)
    before = jnp.maximum(slab - 1, 0).reshape(1)
    after = jnp.minimum(slab + 1, NSLAB - 1).reshape(1)
    downs, ups = [], []
    for s in range(1, NSLAB):
        rcv = exchange(msg)
        v = combine(down_kernel, before, rcv, (rhs_target, interface_coef, hot_own), TGT, "down")
        downs.append(gather_step(v))
        flag = (slab == s).astype(jnp.int32).reshape(1)
        kind = "down" if s < NSLAB - 1 else "up"
        acc, msg = down_step(lst, flag, downs[-1], tiles, acc, kind)
    for s in range(NSLAB - 2, -1, -1):
        rcv = exchange(msg)
        v = combine(up_kernel, after, rcv, (coef_next, hot_next), PRT, "up")
        ups.append(gather_step(v))
        if s > 0:
            flag = (slab == s).astype(jnp.int32).reshape(1)
            msg = up_step(lst, flag, ups[-1], tiles, acc)
    msg = last_apply(lst, slab.reshape(1), tiles, downs, ups, acc)
    parts = lax.all_to_all(msg, "row", 0, 0, tiled=True)
    total = jnp.sum(parts, axis=0)
    total = jnp.where((blk < section_blocks[0])[:, None, None], total, 0.0)
    return total.transpose(1, 0, 2).reshape(1, W, BLK * B)


def solution(mesh):
    placed = (
        P("slab", None, ("col", "row")),
        P("slab", ("col", "row"), None, None),
        P("slab", ("col", "row")),
        P("slab", ("col", "row")),
        P("slab"),
        P("slab", ("col", "row")),
        P("slab", ("col", "row")),
    )
    return jax.shard_map(
        body, mesh=mesh, in_specs=placed, out_specs=P("slab", None, ("col", "row")), check_vma=False
    )
```

time: 321 us -> 260 us (0.81)
  Pallas kernels: 48.7 us -> 21 us
  waiting for transfers between devices: 61.7 us -> 45.4 us
  between operations: 14.3 us -> 0.93 us
  local copies, waits for them, and re-layouts: 6.3 us -> 14.8 us
  starting transfers between devices: 30.2 us -> 24.6 us
  blocking collectives: 156 us -> 152 us
    pallas_call x8, Pallas kernels: 37.7 us -> 20.1 us  [the longest x1 5.5 us: first_apply(): pl.pallas_call(first_kernel, out_shape=(jax.ShapeDtypeStruct(ACC, F32), m...]
    all_gather x6, blocking collectives: 116 us -> 105 us  [gather_step(): return lax.all_gather(value, 'col').reshape(NCOL * value.shape[0], W, B)]
    all_to_all x5 -> x4, waiting for transfers between devices: 45.6 us -> 34.5 us  [exchange(): return lax.all_to_all(message, ('slab', 'row'), 0, 0, tiled=True)]
    pallas_call x6, Pallas kernels: 11 us -> 0.95 us  [combine(): pl.pallas_call(kernel, out_shape=jax.ShapeDtypeStruct((blocks, W, B), BF)...]
    unnamed x15 -> x25, local copies, waits for them, and re-layouts: 4.81 us -> 13.9 us
    all_to_all x5 -> x4, starting transfers between devices: 25.4 us -> 17.5 us  [exchange(): return lax.all_to_all(message, ('slab', 'row'), 0, 0, tiled=True)]
    all_to_all x1 -> x2, blocking collectives: 14.7 us -> 22.5 us  [exchange(): return lax.all_to_all(message, ('slab', 'row'), 0, 0, tiled=True)]
    all_gather x1 -> x0, waiting for transfers between devices: 6.71 us -> none  [gather_first(): both = lax.all_gather(along, 'col', axis_index_groups=CORE_GROUPS)]
  transfers between devices with their start and end apart: 8 -> 7, of which waited for: 7 -> 6; matrix products, arithmetic and copies ran while one was open for 1% -> 0% of each run, Pallas kernels for 4% -> 3%
where the time goes in v2:
time: 260 us; the launch traced here: 259 us
  blocking collectives  152 us (58%)
  waiting for transfers between devices  45.4 us (17%)
  starting transfers between devices  24.6 us (9%)
  Pallas kernels  21 us (8%)
  local copies, waits for them, and re-layouts  14.8 us (6%)
    all_gather x6, blocking collectives, gather_step(): return lax.all_gather(value, 'col').reshape(NCOL * value.shape[0], W, B)  105 us
    all_to_all x4, waiting for transfers between devices, exchange(): return lax.all_to_all(message, ('slab', 'row'), 0, 0, tiled=True)  34.5 us
    all_to_all x1, blocking collectives, gather_first(): lax.all_to_all(copies, 'col', 0, 0, tiled=True, axis_index_groups=Z_GROUPS)  24.9 us
    all_to_all x2, blocking collectives, exchange(): return lax.all_to_all(message, ('slab', 'row'), 0, 0, tiled=True)  22.5 us
    all_to_all x4, starting transfers between devices, exchange(): return lax.all_to_all(message, ('slab', 'row'), 0, 0, tiled=True)  17.5 us
    unnamed x25, local copies, waits for them, and re-layouts  13.9 us
    all_to_all x1, waiting for transfers between devices, body(): parts = lax.all_to_all(msg, 'row', 0, 0, tiled=True)  9.36 us
    pallas_call x1, Pallas kernels, first_apply(): pl.pallas_call(first_kernel, out_shape=(jax.ShapeDtypeStruct(ACC, F32), m...  5.5 us
  transfers between devices with their start and end apart: 7, of which 6 were waited for; matrix products, arithmetic and copies ran while one was open for 0% of the time, Pallas kernels for 3%

profile of v2, /device:TPU:1, one launch (start us, length us, event | category | flops | bytes accessed | tf_op | source)
XLA Modules:
  0.0 259.0 jit_solution(15164132072687833092)
XLA Ops:
  1.8 24.9 %all_to_all.40 = bf16[8,8,32,128]{3,2,1,0:T(8,128)(2,1)S(1)} all-to-all(bf16[8,8,32,128]{3,2,1,0:T(8,128)(2,1)S(1)} %broadcast_in_dim.32), channel_id=1, replica_groups={{0,2,4,6,8,10,12,14},{1,3,5,7,9,11,13,15},{16,18,20,22,24,26,28,30},{17..., dimensions={0} | all-to-all | bytes 1048576 | tf_op jit(solution)/shard_map/all_to_all | solution.py:269
  26.7 2.3 collective-permute-start
  34.1 5.5 %first.1 = (f32[33,32,128]{2,1,0:T(8,128)S(1)}, bf16[16,4,32,128]{3,2,1,0:T(8,128)(2,1)}) custom-call(s32[1,128]{1,0:T(1,128)S(1)} %copy-done.9, s32[1,128]{1,0:T(1,128)S(1)} %copy-done.10, s32[1]{0:T(128)} %bitcast.1.pos_ref.pos, bf16[64,32,128]{2,1,0:T(8,128)(2,1)S(1)} %bitcast.32, bf16[64,32,128]{2,1,0:T(8,128)(2,1)S(1)} %collective-permute-done.other_ref, ...), custom_call_target="tpu_custom_call" | custom-call | tf_op jit(solution)/shard_map/first/pallas_call | solution.py:137
  39.6 6.8 %all-to-all-start.1 = ((bf16[16,4,32,128]{3,2,1,0:T(8,128)(2,1)}), bf16[16,4,32,128]{3,2,1,0:T(8,128)(2,1)S(1)}, u32[]{:S(2)}, u32[]{:S(2)}) async-start(bf16[16,4,32,128]{3,2,1,0:T(8,128)(2,1)} %get-tuple-element.14), calls=%async_computation.1 | async-start | bytes 1048576 | tf_op jit(solution)/shard_map/all_to_all | solution.py:279
  46.4 5.4 %lists.1.lst = s32[5,136]{1,0:T(8,128)} custom-call(s32[1,128]{1,0:T(1,128)} %rows_ref.3, s32[1,128]{1,0:T(1,128)} %cols_ref.3, s32[1]{0:T(128)} %bitcast.1.pos_ref.pos), custom_call_target="tpu_custom_call" | custom-call | tf_op jit(solution)/shard_map/lists/pallas_call | solution.py:71
  51.9 5.2 %all-to-all-done.1.rcv_ref = bf16[16,4,32,128]{3,2,1,0:T(8,128)(2,1)S(1)} async-done(((bf16[16,4,32,128]{3,2,1,0:T(8,128)(2,1)}), bf16[16,4,32,128]{3,2,1,0:T(8,128)(2,1)S(1)}, u32[]{:S(2)}, u32[]{:S(2)}) %all-to-all-start.1) | async-done | bytes 524320 | tf_op jit(solution)/shard_map/all_to_all | solution.py:279
  57.3 17.0 %all-gather.v_ref.v1 = bf16[32,32,128]{2,1,0:T(8,128)(2,1)S(1)} all-gather(bf16[2,32,128]{2,1,0:T(8,128)(2,1)S(1)} %down.3), channel_id=2, replica_groups=mesh['slab'=4,'row'=4,'col'=16] {'col'}, dimensions={0}, use_global_device_ids=true | all-gather | bytes 278528 | tf_op jit(solution)/shard_map/all_gather | solution.py:275
  78.7 3.6 %all-to-all-start.2 = ((bf16[16,4,32,128]{3,2,1,0:T(8,128)(2,1)}), bf16[16,4,32,128]{3,2,1,0:T(8,128)(2,1)S(1)}, u32[]{:S(2)}, u32[]{:S(2)}) async-start(bf16[16,4,32,128]{3,2,1,0:T(8,128)(2,1)} %get-tuple-element.16), calls=%async_computation.2 | async-start | bytes 1048576 | tf_op jit(solution)/shard_map/all_to_all | solution.py:279
  82.2 11.1 %all-to-all-done.2.rcv_ref = bf16[16,4,32,128]{3,2,1,0:T(8,128)(2,1)S(1)} async-done(((bf16[16,4,32,128]{3,2,1,0:T(8,128)(2,1)}), bf16[16,4,32,128]{3,2,1,0:T(8,128)(2,1)S(1)}, u32[]{:S(2)}, u32[]{:S(2)}) %all-to-all-start.2) | async-done | bytes 524320 | tf_op jit(solution)/shard_map/all_to_all | solution.py:279
  93.5 17.4 %all-gather.1.v_ref.v2 = bf16[32,32,128]{2,1,0:T(8,128)(2,1)S(1)} all-gather(bf16[2,32,128]{2,1,0:T(8,128)(2,1)S(1)} %down.4), channel_id=3, replica_groups=mesh['slab'=4,'row'=4,'col'=16] {'col'}, dimensions={0}, use_global_device_ids=true | all-gather | bytes 278528 | tf_op jit(solution)/shard_map/all_gather | solution.py:275
  111.0 2.2 copy-done.2
  114.7 3.6 %all-to-all-start.3 = ((bf16[16,4,32,128]{3,2,1,0:T(8,128)(2,1)}), bf16[16,4,32,128]{3,2,1,0:T(8,128)(2,1)S(1)}, u32[]{:S(2)}, u32[]{:S(2)}) async-start(bf16[16,4,32,128]{3,2,1,0:T(8,128)(2,1)} %get-tuple-element.18), calls=%async_computation.3 | async-start | bytes 1048576 | tf_op jit(solution)/shard_map/all_to_all | solution.py:279
  119.7 9.8 %all-to-all-done.3.rcv_ref = bf16[16,4,32,128]{3,2,1,0:T(8,128)(2,1)S(1)} async-done(((bf16[16,4,32,128]{3,2,1,0:T(8,128)(2,1)}), bf16[16,4,32,128]{3,2,1,0:T(8,128)(2,1)S(1)}, u32[]{:S(2)}, u32[]{:S(2)}) %all-to-all-start.3) | async-done | bytes 524320 | tf_op jit(solution)/shard_map/all_to_all | solution.py:279
  129.7 16.8 %all-gather.2.v_ref.v3 = bf16[32,32,128]{2,1,0:T(8,128)(2,1)S(1)} all-gather(bf16[2,32,128]{2,1,0:T(8,128)(2,1)S(1)} %down.5), channel_id=4, replica_groups=mesh['slab'=4,'row'=4,'col'=16] {'col'}, dimensions={0}, use_global_device_ids=true | all-gather | bytes 278528 | tf_op jit(solution)/shard_map/all_gather | solution.py:275
  150.1 3.5 %all-to-all-start.4 = ((bf16[16,2,32,128]{3,2,1,0:T(8,128)(2,1)}), bf16[16,2,32,128]{3,2,1,0:T(8,128)(2,1)S(1)}, u32[]{:S(2)}, u32[]{:S(2)}) async-start(bf16[16,2,32,128]{3,2,1,0:T(8,128)(2,1)} %get-tuple-element.20), calls=%async_computation.4 | async-start | bytes 524288 | tf_op jit(solution)/shard_map/all_to_all | solution.py:279
  153.7 8.3 %all-to-all-done.4.rcv_ref = bf16[16,2,32,128]{3,2,1,0:T(8,128)(2,1)S(1)} async-done(((bf16[16,2,32,128]{3,2,1,0:T(8,128)(2,1)}), bf16[16,2,32,128]{3,2,1,0:T(8,128)(2,1)S(1)}, u32[]{:S(2)}, u32[]{:S(2)}) %all-to-all-start.4) | async-done | bytes 262176 | tf_op jit(solution)/shard_map/all_to_all | solution.py:279
  162.2 17.7 %all-gather.3.v_ref.l2 = bf16[64,32,128]{2,1,0:T(8,128)(2,1)S(1)} all-gather(bf16[4,32,128]{2,1,0:T(8,128)(2,1)S(1)} %up.3), channel_id=5, replica_groups=mesh['slab'=4,'row'=4,'col'=16] {'col'}, dimensions={0}, use_global_device_ids=true | all-gather | bytes 557056 | tf_op jit(solution)/shard_map/all_gather | solution.py:275
  182.9 11.5 %all_to_all.41.rcv_ref = bf16[16,2,32,128]{3,2,1,0:T(8,128)(2,1)S(1)} all-to-all(bf16[16,2,32,128]{3,2,1,0:T(8,128)(2,1)S(1)} %up_step.2), channel_id=1, replica_groups=mesh['slab'=4,'row'=4,'col'=16] {'slab','row'}, dimensions={0} | all-to-all | bytes 524288 | tf_op jit(solution)/shard_map/all_to_all | solution.py:279
  194.5 17.8 %all-gather.4.v_ref.l1 = bf16[64,32,128]{2,1,0:T(8,128)(2,1)S(1)} all-gather(bf16[4,32,128]{2,1,0:T(8,128)(2,1)S(1)} %up.4), channel_id=6, replica_groups=mesh['slab'=4,'row'=4,'col'=16] {'col'}, dimensions={0}, use_global_device_ids=true | all-gather | bytes 557056 | tf_op jit(solution)/shard_map/all_gather | solution.py:275
  213.0 11.0 %all_to_all.42.rcv_ref = bf16[16,2,32,128]{3,2,1,0:T(8,128)(2,1)S(1)} all-to-all(bf16[16,2,32,128]{3,2,1,0:T(8,128)(2,1)S(1)} %up_step.3), channel_id=1, replica_groups=mesh['slab'=4,'row'=4,'col'=16] {'slab','row'}, dimensions={0} | all-to-all | bytes 524288 | tf_op jit(solution)/shard_map/all_to_all | solution.py:279
  224.1 17.8 %all-gather.5.l0 = bf16[64,32,128]{2,1,0:T(8,128)(2,1)S(1)} all-gather(bf16[4,32,128]{2,1,0:T(8,128)(2,1)S(1)} %up.5), channel_id=7, replica_groups=mesh['slab'=4,'row'=4,'col'=16] {'col'}, dimensions={0}, use_global_device_ids=true | all-gather | bytes 557056 | tf_op jit(solution)/shard_map/all_gather | solution.py:275
  241.9 3.4 %last.1 = (f32[33,32,128]{2,1,0:T(8,128)S(1)}, f32[4,8,32,128]{3,2,1,0:T(8,128)}) custom-call(s32[5,136]{1,0:T(8,128)S(1)} %copy-done.7, s32[1]{0:T(128)} %bitcast.2.pos, bf16[128,128,128]{2,1,0:T(8,128)(2,1)S(1)} %bitcast.30, bf16[32,32,128]{2,1,0:T(8,128)(2,1)S(1)} %all-gather.v_ref.v1, ...), custom_call_target="tpu_custom_call", output_to_operand_aliasing={{0}: (9, {})} | custom-call | tf_op jit(solution)/shard_map/last/pallas_call | solution.py:206
  245.2 3.5 %all-to-all-start.7 = ((f32[4,8,32,128]{3,2,1,0:T(8,128)}), f32[4,8,32,128]{3,2,1,0:T(8,128)S(1)}, u32[]{:S(2)}, u32[]{:S(2)}) async-start(f32[4,8,32,128]{3,2,1,0:T(8,128)} %get-tuple-element.22), calls=%async_computation.7 | async-start | bytes 1048576 | tf_op jit(solution)/shard_map/all_to_all | solution.py:321
  248.7 9.4 %all-to-all-done.7 = f32[4,8,32,128]{3,2,1,0:T(8,128)S(1)} async-done(((f32[4,8,32,128]{3,2,1,0:T(8,128)}), f32[4,8,32,128]{3,2,1,0:T(8,128)S(1)}, u32[]{:S(2)}, u32[]{:S(2)}) %all-to-all-start.7) | async-done | bytes 524320 | tf_op jit(solution)/shard_map/all_to_all | solution.py:321
  (53 shorter events, 22.6 us)
Async XLA Ops:
  1.7 50.1 %copy-start.11 = (s32[1,256]{1,0:T(1,128)S(1)}, s32[1,256]{1,0:T(1,128)}, u32[]{:S(2)}) copy-start(s32[1,256]{1,0:T(1,128)} %param.12) | copy-start | bytes 3076
  1.7 55.4 %copy-start.8 = (f32[1,256]{1,0:T(1,128)S(1)}, f32[1,256]{1,0:T(1,128)}, u32[]{:S(2)}) copy-start(f32[1,256]{1,0:T(1,128)} %coef_ref.5) | copy-start | bytes 3076
  26.7 3.9 %collective-permute-start = (bf16[64,32,128]{2,1,0:T(8,128)(2,1)S(1)}, bf16[64,32,128]{2,1,0:T(8,128)(2,1)S(1)}, u32[]{:S(2)}, u32[]{:S(2)}) collective-permute-start(bf16[64,32,128]{2,1,0:T(8,128)(2,1)S(1)} %bitcast.31), channel_id=1, source_target_pairs={{0,1},{1,0},{2,3},{3,2},{4,5},{5,4},{6,7},{7,6},{8,9},{9,8},{10,11... | collective-permute-start | bytes 1572872 | tf_op jit(solution)/shard_map/ppermute | solution.py:271
  30.6 2.2 copy-start
  32.8 0.7 copy-start.9
  33.4 0.7 copy-start.10
  39.6 17.5 %all-to-all-start.1 = ((bf16[16,4,32,128]{3,2,1,0:T(8,128)(2,1)}), bf16[16,4,32,128]{3,2,1,0:T(8,128)(2,1)S(1)}, u32[]{:S(2)}, u32[]{:S(2)}) async-start(bf16[16,4,32,128]{3,2,1,0:T(8,128)(2,1)} %get-tuple-element.14), calls=%async_computation.1 | async-start | bytes 1048576 | tf_op jit(solution)/shard_map/all_to_all | solution.py:279
  51.9 59.1 %copy-start.7 = (s32[5,136]{1,0:T(8,128)S(1)}, s32[5,136]{1,0:T(8,128)}, u32[]{:S(2)}) copy-start(s32[5,136]{1,0:T(8,128)} %lists.1.lst) | copy-start | bytes 8164
  74.3 2.2 copy-start.1
  76.4 0.7 copy-start.6
  78.7 14.7 %all-to-all-start.2 = ((bf16[16,4,32,128]{3,2,1,0:T(8,128)(2,1)}), bf16[16,4,32,128]{3,2,1,0:T(8,128)(2,1)S(1)}, u32[]{:S(2)}, u32[]{:S(2)}) async-start(bf16[16,4,32,128]{3,2,1,0:T(8,128)(2,1)} %get-tuple-element.16), calls=%async_computation.2 | async-start | bytes 1048576 | tf_op jit(solution)/shard_map/all_to_all | solution.py:279
  111.0 2.2 copy-start.2
  114.7 14.8 %all-to-all-start.3 = ((bf16[16,4,32,128]{3,2,1,0:T(8,128)(2,1)}), bf16[16,4,32,128]{3,2,1,0:T(8,128)(2,1)S(1)}, u32[]{:S(2)}, u32[]{:S(2)}) async-start(bf16[16,4,32,128]{3,2,1,0:T(8,128)(2,1)} %get-tuple-element.18), calls=%async_computation.3 | async-start | bytes 1048576 | tf_op jit(solution)/shard_map/all_to_all | solution.py:279
  118.4 35.2 %collective-permute-start.1 = (f32[2,256]{1,0:T(2,128)S(1)}, f32[2,256]{1,0:T(2,128)S(1)}, u32[]{:S(2)}, u32[]{:S(2)}) collective-permute-start(f32[2,256]{1,0:T(2,128)S(1)} %pad_maximum_fusion), channel_id=1, source_target_pairs={{64,0},{128,64},{192,128},{65,1},{129,65},{193,129},{66,2},{130,66... | collective-permute-start | bytes 6152 | tf_op jit(solution)/shard_map/ppermute | solution.py:287
  146.5 2.2 copy-start.3
  150.1 12.0 %all-to-all-start.4 = ((bf16[16,2,32,128]{3,2,1,0:T(8,128)(2,1)}), bf16[16,2,32,128]{3,2,1,0:T(8,128)(2,1)S(1)}, u32[]{:S(2)}, u32[]{:S(2)}) async-start(bf16[16,2,32,128]{3,2,1,0:T(8,128)(2,1)} %get-tuple-element.20), calls=%async_computation.4 | async-start | bytes 524288 | tf_op jit(solution)/shard_map/all_to_all | solution.py:279
  180.0 2.2 copy-start.4
  182.2 30.1 %copy-start.5 = (bf16[1,128,128,128]{3,2,1,0:T(8,128)(2,1)S(1)}, bf16[1,128,128,128]{3,2,1,0:T(8,128)(2,1)}, u32[]{:S(2)}) copy-start(bf16[1,128,128,128]{3,2,1,0:T(8,128)(2,1)} %param.8) | copy-start | bytes 12582916
  245.2 12.9 %all-to-all-start.7 = ((f32[4,8,32,128]{3,2,1,0:T(8,128)}), f32[4,8,32,128]{3,2,1,0:T(8,128)S(1)}, u32[]{:S(2)}, u32[]{:S(2)}) async-start(f32[4,8,32,128]{3,2,1,0:T(8,128)} %get-tuple-element.22), calls=%async_computation.7 | async-start | bytes 1048576 | tf_op jit(solution)/shard_map/all_to_all | solution.py:321

commit v3 on v2

v3 whole, which is shorter than its diff:
```python
import functools

import jax
import jax.numpy as jnp
from jax import lax
from jax.experimental import pallas as pl
from jax.experimental.pallas import tpu as pltpu
from jax.sharding import PartitionSpec as P

B = 128
BLK = 8
NROW = 4
NCOL = 16
NSLAB = 4
W = 32
NT = 128
UNROLL = 8
TGT = 2
PRT = 4
LST = NT + UNROLL
BF = jnp.bfloat16
F32 = jnp.float32


def smem():
    return pl.BlockSpec(memory_space=pltpu.SMEM)


def vmem():
    return pl.BlockSpec(memory_space=pltpu.VMEM)


PARAMS = pltpu.CompilerParams(vmem_limit_bytes=24 * 2**20)
ACC = (NROW * BLK + 1, W, B)
LISTS = 4
TAB, TC, LA, LALL = range(LISTS)
HALF = NCOL // 2


def shr(x, n):
    return lax.shift_right_logical(x, jnp.int32(n))


def tile_codes(tile_rows, tile_cols, col_index):
    row = tile_rows - col_index * (NROW * BLK)
    part = tile_cols // (BLK * NROW)
    side = (part % 2 != col_index % 2).astype(jnp.int32)
    return row + 64 * (part // 2) + 512 * side + 1024 * (tile_cols % BLK)


def product(v, tile):
    return lax.dot_general(v, tile, (((1,), (1,)), ((), ())), preferred_element_type=F32)


def picked(side, own_ref, other_ref, at):
    return jnp.where(side == 0, own_ref[at], other_ref[at])


def apply_list(lst, which, pair, tiles_ref, acc):
    def group(g, _):
        rows, done = [], []
        for u in range(UNROLL):
            e = lst[which, g * UNROLL + u]
            v = picked(shr(e, 19), *pair, shr(e, 13) & 63)
            rows.append(shr(e, 7) & 63)
            done.append(product(v, tiles_ref[e & 127]))
        for r, d in zip(rows, done):
            acc[r] += d
        return 0

    lax.fori_loop(0, lst[LISTS, which], group, 0)


def write_down(acc, pos, hot_ref, msg_ref):
    for d in range(NROW):
        r = (pos[1] + d) & (NROW - 1)
        values = jnp.concatenate([acc[r * BLK + b].astype(BF) for b in range(PRT)], axis=1)
        part = jnp.dot(values, hot_ref[d], preferred_element_type=F32).astype(BF)
        for b in range(TGT):
            for s in range(NSLAB):
                msg_ref[s * NROW + r, b] = part[:, b * B : (b + 1) * B]


def write_up(acc, msg_ref):
    for r in range(NROW):
        for b in range(TGT):
            part = acc[r * BLK + b].astype(BF)
            for s in range(NSLAB):
                msg_ref[s * NROW + r, b] = part


MESSAGE = jax.ShapeDtypeStruct((NSLAB * NROW, TGT, W, B), BF)


def first_kernel(codes, pos, own_ref, other_ref, hot_ref, tiles_hbm, acc, tiles_ref, lst, msg_ref, sems):
    def load(g):
        at = pl.ds(pl.multiple_of(g * UNROLL, UNROLL), UNROLL)
        return pltpu.make_async_copy(tiles_hbm.at[at], tiles_ref.at[at], sems.at[g])

    def start(g, _):
        load(g).start()
        return 0

    lax.fori_loop(0, NT // UNROLL, start, 0)
    acc[...] = jnp.zeros(ACC, F32)

    def group(g, counts):
        rows, done = [], []
        load(g).wait()
        for u in range(UNROLL):
            t = g * UNROLL + u
            code = codes[0, t]
            row = code & 63
            half = shr(code, 6) & 7
            side = shr(code, 9) & 1
            blk = shr(code, 10)
            v = picked(side, own_ref, other_ref, half * BLK + blk)
            rows.append(row)
            done.append(product(v, tiles_ref[t]))
            out = row & (BLK - 1)
            head = t + row * NT + side * 2**19
            narrow = head + (half * TGT + blk) * 8192
            wide = head + (half * PRT + blk) * 8192
            target = blk < TGT
            low = blk < PRT
            member = (
                (narrow, target & (out < PRT)),
                (narrow, target & (out >= PRT)),
                (wide, low & (out < TGT)),
                (wide, low),
            )
            for k in range(LISTS):
                lst[k, counts[k]] = member[k][0]
            counts = tuple(
                counts[k] + jnp.where(member[k][1], jnp.int32(1), jnp.int32(0))
                for k in range(LISTS)
            )
        for r, d in zip(rows, done):
            acc[r] += d
        return counts

    counts = lax.fori_loop(0, NT // UNROLL, group, (jnp.int32(0),) * LISTS)
    for k in range(LISTS):
        for u in range(UNROLL):
            lst[k, counts[k] + u] = NROW * BLK * NT
        lst[LISTS, k] = shr(counts[k] + UNROLL - 1, 3)
    write_down(acc, pos, hot_ref, msg_ref)


def first_apply(codes, pos, pair, hots, tiles):
    return pl.pallas_call(
        first_kernel,
        out_shape=(
            jax.ShapeDtypeStruct(ACC, F32),
            jax.ShapeDtypeStruct(tiles.shape, BF),
            jax.ShapeDtypeStruct((LISTS + 1, LST), jnp.int32),
            MESSAGE,
        ),
        in_specs=[smem(), smem(), vmem(), vmem(), vmem(), pl.BlockSpec(memory_space=pltpu.HBM)],
        out_specs=(vmem(), vmem(), smem(), vmem()),
        scratch_shapes=[pltpu.SemaphoreType.DMA((NT // UNROLL,))],
        compiler_params=PARAMS,
        name="first",
    )(codes, pos, *pair, hots, pltpu.with_memory_space_constraint(tiles, pltpu.HBM))


def down_step_kernel(lst, pos, own_ref, other_ref, hot_ref, tiles_ref, acc_in, acc, msg_ref, *, section):
    @pl.when(pos[0] == section)
    def _():
        apply_list(lst, TAB, (own_ref, other_ref), tiles_ref, acc)

    if section < NSLAB - 1:
        write_down(acc, pos, hot_ref, msg_ref)
    else:
        write_up(acc, msg_ref)


def down_step(lst, pos, pair, hots, tiles, acc, section):
    return pl.pallas_call(
        functools.partial(down_step_kernel, section=section),
        out_shape=(jax.ShapeDtypeStruct(ACC, F32), MESSAGE),
        in_specs=[smem(), smem()] + [vmem()] * 5,
        out_specs=(vmem(), vmem()),
        input_output_aliases={6: 0},
        compiler_params=PARAMS,
        name="down_step",
    )(lst, pos, *pair, hots, tiles, acc)


def up_step_kernel(lst, pos, own_ref, other_ref, tiles_ref, acc_in, msg_ref, acc, *, section):
    for r in range(NROW):
        for b in range(TGT):
            acc[r * BLK + b] = acc_in[r * BLK + b]

    @pl.when(pos[0] == section)
    def _():
        apply_list(lst, LA, (own_ref, other_ref), tiles_ref, acc)

    write_up(acc, msg_ref)


def up_step(lst, pos, pair, tiles, acc, section):
    return pl.pallas_call(
        functools.partial(up_step_kernel, section=section),
        out_shape=MESSAGE,
        in_specs=[smem(), smem()] + [vmem()] * 4,
        out_specs=vmem(),
        scratch_shapes=[pltpu.VMEM(ACC, F32)],
        compiler_params=PARAMS,
        name="up_step",
    )(lst, pos, *pair, tiles, acc)


def last_kernel(lst, pos, tiles_ref, *refs):
    gathered, acc, msg_ref = refs[:12], refs[13], refs[14]
    for k, s in enumerate((1, 2, 3, 2, 1, 0)):
        @pl.when(pos[0] == s)
        def _(k=k):
            pair = gathered[2 * k], gathered[2 * k + 1]
            apply_list(lst, TC if k < NSLAB - 1 else LALL, pair, tiles_ref, acc)

    for r in range(NROW):
        for b in range(BLK):
            msg_ref[r, b] = acc[r * BLK + b]


def last_apply(lst, pos, tiles, pairs, acc):
    flat = [ref for pair in pairs for ref in pair]
    return pl.pallas_call(
        last_kernel,
        out_shape=(
            jax.ShapeDtypeStruct(ACC, F32),
            jax.ShapeDtypeStruct((NROW, BLK, W, B), F32),
        ),
        in_specs=[smem(), smem()] + [vmem()] * 14,
        out_specs=(vmem(), vmem()),
        input_output_aliases={15: 0},
        compiler_params=PARAMS,
        name="last",
    )(lst, pos, tiles, *flat, acc)[1]


def split(x):
    high = x.astype(BF)
    rest = x - high.astype(F32)
    return jnp.concatenate([high, rest.astype(BF)], axis=0)


def row_total(rcv_ref, section, b):
    part = rcv_ref[section * NROW, b].astype(F32)
    for r in range(1, NROW):
        part = part + rcv_ref[section * NROW + r, b].astype(F32)
    return part


def down_kernel(pos, rcv_ref, rhs_ref, coef_ref, out_ref):
    before = jnp.maximum(pos[0] - 1, 0)
    for b in range(TGT):
        pulled = row_total(rcv_ref, before, b) * coef_ref[:, b * B : (b + 1) * B]
        value = (rhs_ref[b] - pulled).astype(BF)
        for z in range(HALF):
            out_ref[z, b] = value


def up_kernel(pos, rcv_ref, coef_ref, hot_ref, out_ref):
    after = jnp.minimum(pos[0] + 1, NSLAB - 1)
    values = jnp.concatenate(
        [
            split(row_total(rcv_ref, after, b) * coef_ref[:, b * B : (b + 1) * B])
            for b in range(TGT)
        ],
        axis=1,
    )
    total = jnp.dot(values, hot_ref[...], preferred_element_type=F32)
    lifted = -(total[:W] + total[W:])
    for b in range(PRT):
        value = lifted[:, b * B : (b + 1) * B].astype(BF)
        for z in range(HALF):
            out_ref[z, b] = value


def combine(kernel, pos, received, others, blocks, name):
    return pl.pallas_call(
        kernel,
        out_shape=jax.ShapeDtypeStruct((HALF, blocks, W, B), BF),
        in_specs=[smem()] + [vmem()] * (1 + len(others)),
        out_specs=vmem(),
        compiler_params=PARAMS,
        name=name,
    )(pos, received, *others)


def finish_kernel(count, parts_ref, out_ref):
    for b in range(BLK):
        total = parts_ref[0, b]
        for r in range(1, NROW):
            total = total + parts_ref[r, b]
        out_ref[0, :, b * B : (b + 1) * B] = jnp.where(b < count[0], total, 0.0)


def finish(section_blocks, parts):
    return pl.pallas_call(
        finish_kernel,
        out_shape=jax.ShapeDtypeStruct((1, W, BLK * B), F32),
        in_specs=[smem(), vmem()],
        out_specs=vmem(),
        compiler_params=PARAMS,
        name="finish",
    )(section_blocks, parts)


Z_GROUPS = [[2 * z + k for z in range(HALF)] for k in range(2)]


def gather(copies):
    own = lax.all_to_all(copies, "col", 0, 0, tiled=True, axis_index_groups=Z_GROUPS)
    own = own.reshape(HALF * copies.shape[1], W, B)
    return own, lax.ppermute(own, "col", [(c, c ^ 1) for c in range(NCOL)])


def exchange(message):
    return lax.all_to_all(message, ("slab", "row"), 0, 0, tiled=True)


def from_next(value, turn):
    pairs = [
        ((s + 1) * NROW + (r + turn) % NROW, s * NROW + r)
        for s in range(NSLAB - 1)
        for r in range(NROW)
    ]
    return lax.ppermute(value, ("slab", "row"), pairs)


def body(right_sides, front_tiles, tile_rows, tile_cols, section_blocks, plane_map, interface_coef):
    slab = lax.axis_index("slab").astype(jnp.int32)
    row = lax.axis_index("row").astype(jnp.int32)
    col = lax.axis_index("col").astype(jnp.int32)
    pos = jnp.stack([slab, row])
    codes = tile_codes(tile_rows, tile_cols, col)
    map_own = plane_map.astype(F32)
    pack_next = from_next(jnp.concatenate([map_own, interface_coef], axis=0), 0)
    coef_next = pack_next[1:2]
    maps_next = jnp.concatenate(
        [pack_next[0:1]] + [from_next(map_own, d) for d in range(1, NROW)], axis=0
    ).astype(jnp.int32)

    source = right_sides[0].reshape(W, BLK, B).transpose(1, 0, 2)
    blk = jnp.arange(BLK, dtype=jnp.int32)
    keep = (blk < section_blocks[0]) & ((slab == 0) | (blk >= TGT))
    v0 = jnp.where(keep[:, None, None], source, 0.0).astype(BF)
    rhs_target = source[:TGT]
    partner = jnp.arange(PRT * B, dtype=jnp.int32)
    hots = (partner[None, :, None] == maps_next[:, None, :]).astype(BF)
    hot_next = (maps_next[0][:, None] == partner[None, :]).astype(BF)

    pair = gather(jnp.broadcast_to(v0[None], (HALF, *v0.shape)))
    pair, hots, hot_next, coef_next, rhs_target, codes, pos = lax.optimization_barrier(
        (pair, hots, hot_next, coef_next, rhs_target, codes, pos)
    )
    acc, tiles, lst, msg = first_apply(codes, pos, pair, hots, front_tiles[0])
    pairs = []
    for s in range(1, NSLAB):
        rcv = exchange(msg)
        pairs.append(gather(combine(down_kernel, pos, rcv, (rhs_target, interface_coef), TGT, "down")))
        acc, msg = down_step(lst, pos, pairs[-1], hots, tiles, acc, s)
    for s in range(NSLAB - 2, -1, -1):
        rcv = exchange(msg)
        pairs.append(gather(combine(up_kernel, pos, rcv, (coef_next, hot_next), PRT, "up")))
        if s > 0:
            msg = up_step(lst, pos, pairs[-1], tiles, acc, s)
    msg = last_apply(lst, pos, tiles, pairs, acc)
    parts = lax.all_to_all(msg, "row", 0, 0, tiled=True)
    return finish(section_blocks, parts)


def solution(mesh):
    placed = (
        P("slab", None, ("col", "row")),
        P("slab", ("col", "row"), None, None),
        P("slab", ("col", "row")),
        P("slab", ("col", "row")),
        P("slab"),
        P("slab", ("col", "row")),
        P("slab", ("col", "row")),
    )
    return jax.shard_map(
        body, mesh=mesh, in_specs=placed, out_specs=P("slab", None, ("col", "row")), check_vma=False
    )
```

time: 260 us -> 226 us (0.87)
  waiting for transfers between devices: 45.4 us -> 18.1 us
  local copies, waits for them, and re-layouts: 14.8 us -> 1.86 us
  starting transfers between devices: 24.6 us -> 30.3 us
  Pallas kernels: 21 us -> 18.3 us
    all_gather x6 -> x0, blocking collectives: 105 us -> none  [gather_step(): return lax.all_gather(value, 'col').reshape(NCOL * value.shape[0], W, B)]
    all_to_all x1 -> x7, blocking collectives: 24.9 us -> 81.9 us  [the longest x6 70.9 us: gather(): lax.all_to_all(copies, 'col', 0, 0, tiled=True, axis_index_groups=Z_GROUPS)]
    all_to_all x2 -> x6, blocking collectives: 22.5 us -> 71.9 us  [exchange(): return lax.all_to_all(message, ('slab', 'row'), 0, 0, tiled=True)]
    all_to_all x5 -> x1, waiting for transfers between devices: 43.8 us -> 4.66 us  [gather(): lax.all_to_all(copies, 'col', 0, 0, tiled=True, axis_index_groups=Z_GROUPS)]
    ppermute x2 -> x11, starting transfers between devices: 3.63 us -> 21.3 us  [the longest x7 16.2 us: gather(): return (own, lax.ppermute(own, 'col', [(c, c ^ 1) for c in range(NCOL)]))]
    unnamed x25 -> x3, local copies, waits for them, and re-layouts: 13.9 us -> 0.93 us
    all_to_all x5 -> x1, starting transfers between devices: 21 us -> 9 us  [gather(): lax.all_to_all(copies, 'col', 0, 0, tiled=True, axis_index_groups=Z_GROUPS)]
    ppermute x2 -> x11, waiting for transfers between devices: 1.54 us -> 13.4 us  [the longest x7 7.48 us: gather(): return (own, lax.ppermute(own, 'col', [(c, c ^ 1) for c in range(NCOL)]))]
  transfers between devices with their start and end apart: 7 -> 12, of which waited for: 6 -> 9; matrix products, arithmetic and copies ran while one was open for 0% -> 1% of each run, Pallas kernels for 3% -> 0%
where the time goes in v3:
time: 226 us
  blocking collectives  154 us (68%)
  starting transfers between devices  30.3 us (13%)
  Pallas kernels  18.3 us (8%)
  waiting for transfers between devices  18.1 us (8%)
  other arithmetic  2.69 us (1%)
    all_to_all x6, blocking collectives, exchange(): return lax.all_to_all(message, ('slab', 'row'), 0, 0, tiled=True)  71.9 us
    all_to_all x6, blocking collectives, gather(): lax.all_to_all(copies, 'col', 0, 0, tiled=True, axis_index_groups=Z_GROUPS)  70.9 us
    ppermute x7, starting transfers between devices, gather(): return (own, lax.ppermute(own, 'col', [(c, c ^ 1) for c in range(NCOL)]))  16.2 us
    all_to_all x1, blocking collectives, body(): parts = lax.all_to_all(msg, 'row', 0, 0, tiled=True)  11 us
    all_to_all x1, starting transfers between devices, gather(): lax.all_to_all(copies, 'col', 0, 0, tiled=True, axis_index_groups=Z_GROUPS)  9 us
    ppermute x7, waiting for transfers between devices, gather(): return (own, lax.ppermute(own, 'col', [(c, c ^ 1) for c in range(NCOL)]))  7.48 us
    pallas_call x1, Pallas kernels, first_apply(): pl.pallas_call(first_kernel, out_shape=(jax.ShapeDtypeStruct(ACC, F32), j...  6.97 us
    ppermute x4, waiting for transfers between devices, from_next(): return lax.ppermute(value, ('slab', 'row'), pairs)  5.92 us
  transfers between devices with their start and end apart: 12, of which 9 were waited for; matrix products, arithmetic and copies ran while one was open for 1% of the time, Pallas kernels for 0%

profile of v3, /device:TPU:1, one launch (start us, length us, event | category | flops | bytes accessed | tf_op | source)
XLA Modules:
  0.0 226.0 jit_solution(8744458705775266609)
XLA Ops:
  2.6 9.0 %all-to-all-start = ((bf16[8,8,32,128]{3,2,1,0:T(8,128)(2,1)}), bf16[8,8,32,128]{3,2,1,0:T(8,128)(2,1)S(1)}, u32[]{:S(2)}, u32[]{:S(2)}) async-start(bf16[8,8,32,128]{3,2,1,0:T(8,128)(2,1)} %broadcast_in_dim.24), calls=%async_computation | async-start | bytes 1048576 | tf_op jit(solution)/shard_map/all_to_all | solution.py:316
  19.0 5.9 %collective-permute-done.1 = f32[2,256]{1,0:T(2,128)S(1)} collective-permute-done((f32[2,256]{1,0:T(2,128)S(1)}, f32[2,256]{1,0:T(2,128)S(1)}, u32[]{:S(2)}, u32[]{:S(2)}) %collective-permute-start.1) | collective-permute-done | bytes 2080 | tf_op jit(solution)/shard_map/ppermute | solution.py:331
  24.9 4.7 %all-to-all-done = bf16[8,8,32,128]{3,2,1,0:T(8,128)(2,1)S(1)} async-done(((bf16[8,8,32,128]{3,2,1,0:T(8,128)(2,1)}), bf16[8,8,32,128]{3,2,1,0:T(8,128)(2,1)S(1)}, u32[]{:S(2)}, u32[]{:S(2)}) %all-to-all-start) | async-done | bytes 524320 | tf_op jit(solution)/shard_map/all_to_all | solution.py:316
  31.6 7.0 %first.1 = (f32[33,32,128]{2,1,0:T(8,128)S(1)}, bf16[128,128,128]{2,1,0:T(8,128)(2,1)S(1)}, s32[5,136]{1,0:T(8,128)S(1)}, bf16[16,2,32,128]{3,2,1,0:T(8,128)(2,1)S(1)}) custom-call(s32[1,128]{1,0:T(1,128)S(1)} %fusion.3.codes, s32[2]{0:T(128)S(1)} %pad_add_fusion.pos, bf16[64,32,128]{2,1,0:T(8,128)(2,1)S(1)} %bitcast.28, ...), custom_call_target="tpu_custom_call" | custom-call | tf_op jit(solution)/shard_map/first/pallas_call | solution.py:151
  38.5 14.7 %all_to_all.70.rcv_ref = bf16[16,2,32,128]{3,2,1,0:T(8,128)(2,1)S(1)} all-to-all(bf16[16,2,32,128]{3,2,1,0:T(8,128)(2,1)S(1)} %get-tuple-element.31), channel_id=1, replica_groups=mesh['slab'=4,'row'=4,'col'=16] {'slab','row'}, dimensions={0} | all-to-all | bytes 524288 | tf_op jit(solution)/shard_map/all_to_all | solution.py:322
  53.8 12.2 %all_to_all.71 = bf16[8,2,32,128]{3,2,1,0:T(8,128)(2,1)S(1)} all-to-all(bf16[8,2,32,128]{3,2,1,0:T(8,128)(2,1)S(1)} %down.3), channel_id=1, replica_groups={{0,2,4,6,8,10,12,14},{1,3,5,7,9,11,13,15},{16,18,20,22,24,26,28,30},{17..., dimensions={0} | all-to-all | bytes 262144 | tf_op jit(solution)/shard_map/all_to_all | solution.py:316
  66.0 2.9 %collective-permute-start.5 = (bf16[16,32,128]{2,1,0:T(8,128)(2,1)S(1)}, bf16[16,32,128]{2,1,0:T(8,128)(2,1)S(1)}, u32[]{:S(2)}, u32[]{:S(2)}) collective-permute-start(bf16[16,32,128]{2,1,0:T(8,128)(2,1)S(1)} %bitcast.29), channel_id=1, source_target_pairs={{0,1},{1,0},{2,3},{3,2},{4,5},{5,4},{6,7},{7,6},{8,9},{9,8},{10,11... | collective-permute-start | bytes 393224 | tf_op jit(solution)/shard_map/ppermute | solution.py:318
  70.9 10.8 %all_to_all.72.rcv_ref = bf16[16,2,32,128]{3,2,1,0:T(8,128)(2,1)S(1)} all-to-all(bf16[16,2,32,128]{3,2,1,0:T(8,128)(2,1)S(1)} %get-tuple-element.34), channel_id=1, replica_groups=mesh['slab'=4,'row'=4,'col'=16] {'slab','row'}, dimensions={0} | all-to-all | bytes 524288 | tf_op jit(solution)/shard_map/all_to_all | solution.py:322
  82.2 10.3 %all_to_all.73 = bf16[8,2,32,128]{3,2,1,0:T(8,128)(2,1)S(1)} all-to-all(bf16[8,2,32,128]{3,2,1,0:T(8,128)(2,1)S(1)} %down.4), channel_id=1, replica_groups={{0,2,4,6,8,10,12,14},{1,3,5,7,9,11,13,15},{16,18,20,22,24,26,28,30},{17..., dimensions={0} | all-to-all | bytes 262144 | tf_op jit(solution)/shard_map/all_to_all | solution.py:316
  92.5 2.6 %collective-permute-start.6 = (bf16[16,32,128]{2,1,0:T(8,128)(2,1)S(1)}, bf16[16,32,128]{2,1,0:T(8,128)(2,1)S(1)}, u32[]{:S(2)}, u32[]{:S(2)}) collective-permute-start(bf16[16,32,128]{2,1,0:T(8,128)(2,1)S(1)} %bitcast.32), channel_id=1, source_target_pairs={{0,1},{1,0},{2,3},{3,2},{4,5},{5,4},{6,7},{7,6},{8,9},{9,8},{10,11... | collective-permute-start | bytes 393224 | tf_op jit(solution)/shard_map/ppermute | solution.py:318
  97.1 11.7 %all_to_all.74.rcv_ref = bf16[16,2,32,128]{3,2,1,0:T(8,128)(2,1)S(1)} all-to-all(bf16[16,2,32,128]{3,2,1,0:T(8,128)(2,1)S(1)} %get-tuple-element.36), channel_id=1, replica_groups=mesh['slab'=4,'row'=4,'col'=16] {'slab','row'}, dimensions={0} | all-to-all | bytes 524288 | tf_op jit(solution)/shard_map/all_to_all | solution.py:322
  109.4 10.4 %all_to_all.75 = bf16[8,2,32,128]{3,2,1,0:T(8,128)(2,1)S(1)} all-to-all(bf16[8,2,32,128]{3,2,1,0:T(8,128)(2,1)S(1)} %down.5), channel_id=1, replica_groups={{0,2,4,6,8,10,12,14},{1,3,5,7,9,11,13,15},{16,18,20,22,24,26,28,30},{17..., dimensions={0} | all-to-all | bytes 262144 | tf_op jit(solution)/shard_map/all_to_all | solution.py:316
  119.8 2.4 %collective-permute-start.7 = (bf16[16,32,128]{2,1,0:T(8,128)(2,1)S(1)}, bf16[16,32,128]{2,1,0:T(8,128)(2,1)S(1)}, u32[]{:S(2)}, u32[]{:S(2)}) collective-permute-start(bf16[16,32,128]{2,1,0:T(8,128)(2,1)S(1)} %bitcast.35), channel_id=1, source_target_pairs={{0,1},{1,0},{2,3},{3,2},{4,5},{5,4},{6,7},{7,6},{8,9},{9,8},{10,11... | collective-permute-start | bytes 393224 | tf_op jit(solution)/shard_map/ppermute | solution.py:318
  123.9 12.0 %all_to_all.76.rcv_ref = bf16[16,2,32,128]{3,2,1,0:T(8,128)(2,1)S(1)} all-to-all(bf16[16,2,32,128]{3,2,1,0:T(8,128)(2,1)S(1)} %get-tuple-element.38), channel_id=1, replica_groups=mesh['slab'=4,'row'=4,'col'=16] {'slab','row'}, dimensions={0} | all-to-all | bytes 524288 | tf_op jit(solution)/shard_map/all_to_all | solution.py:322
  136.6 12.7 %all_to_all.77 = bf16[8,4,32,128]{3,2,1,0:T(8,128)(2,1)S(1)} all-to-all(bf16[8,4,32,128]{3,2,1,0:T(8,128)(2,1)S(1)} %up.3), channel_id=1, replica_groups={{0,2,4,6,8,10,12,14},{1,3,5,7,9,11,13,15},{16,18,20,22,24,26,28,30},{17..., dimensions={0} | all-to-all | bytes 524288 | tf_op jit(solution)/shard_map/all_to_all | solution.py:316
  149.3 2.5 %collective-permute-start.8 = (bf16[32,32,128]{2,1,0:T(8,128)(2,1)S(1)}, bf16[32,32,128]{2,1,0:T(8,128)(2,1)S(1)}, u32[]{:S(2)}, u32[]{:S(2)}) collective-permute-start(bf16[32,32,128]{2,1,0:T(8,128)(2,1)S(1)} %bitcast.21), channel_id=1, source_target_pairs={{0,1},{1,0},{2,3},{3,2},{4,5},{5,4},{6,7},{7,6},{8,9},{9,8},{10,11... | collective-permute-start | bytes 786440 | tf_op jit(solution)/shard_map/ppermute | solution.py:318
  153.7 12.0 %all_to_all.78.rcv_ref = bf16[16,2,32,128]{3,2,1,0:T(8,128)(2,1)S(1)} all-to-all(bf16[16,2,32,128]{3,2,1,0:T(8,128)(2,1)S(1)} %up_step.2), channel_id=1, replica_groups=mesh['slab'=4,'row'=4,'col'=16] {'slab','row'}, dimensions={0} | all-to-all | bytes 524288 | tf_op jit(solution)/shard_map/all_to_all | solution.py:322
  166.4 12.6 %all_to_all.79 = bf16[8,4,32,128]{3,2,1,0:T(8,128)(2,1)S(1)} all-to-all(bf16[8,4,32,128]{3,2,1,0:T(8,128)(2,1)S(1)} %up.4), channel_id=1, replica_groups={{0,2,4,6,8,10,12,14},{1,3,5,7,9,11,13,15},{16,18,20,22,24,26,28,30},{17..., dimensions={0} | all-to-all | bytes 524288 | tf_op jit(solution)/shard_map/all_to_all | solution.py:316
  179.1 2.6 %collective-permute-start.9 = (bf16[32,32,128]{2,1,0:T(8,128)(2,1)S(1)}, bf16[32,32,128]{2,1,0:T(8,128)(2,1)S(1)}, u32[]{:S(2)}, u32[]{:S(2)}) collective-permute-start(bf16[32,32,128]{2,1,0:T(8,128)(2,1)S(1)} %bitcast.24), channel_id=1, source_target_pairs={{0,1},{1,0},{2,3},{3,2},{4,5},{5,4},{6,7},{7,6},{8,9},{9,8},{10,11... | collective-permute-start | bytes 786440 | tf_op jit(solution)/shard_map/ppermute | solution.py:318
  183.5 10.8 %all_to_all.80.rcv_ref = bf16[16,2,32,128]{3,2,1,0:T(8,128)(2,1)S(1)} all-to-all(bf16[16,2,32,128]{3,2,1,0:T(8,128)(2,1)S(1)} %up_step.3), channel_id=1, replica_groups=mesh['slab'=4,'row'=4,'col'=16] {'slab','row'}, dimensions={0} | all-to-all | bytes 524288 | tf_op jit(solution)/shard_map/all_to_all | solution.py:322
  195.1 12.6 %all_to_all.81 = bf16[8,4,32,128]{3,2,1,0:T(8,128)(2,1)S(1)} all-to-all(bf16[8,4,32,128]{3,2,1,0:T(8,128)(2,1)S(1)} %up.5), channel_id=1, replica_groups={{0,2,4,6,8,10,12,14},{1,3,5,7,9,11,13,15},{16,18,20,22,24,26,28,30},{17..., dimensions={0} | all-to-all | bytes 524288 | tf_op jit(solution)/shard_map/all_to_all | solution.py:316
  207.7 2.6 %collective-permute-start.10 = (bf16[32,32,128]{2,1,0:T(8,128)(2,1)S(1)}, bf16[32,32,128]{2,1,0:T(8,128)(2,1)S(1)}, u32[]{:S(2)}, u32[]{:S(2)}) collective-permute-start(bf16[32,32,128]{2,1,0:T(8,128)(2,1)S(1)} %bitcast.38), channel_id=1, source_target_pairs={{0,1},{1,0},{2,3},{3,2},{4,5},{5,4},{6,7},{7,6},{8,9},{9,8},{10,11... | collective-permute-start | bytes 786440 | tf_op jit(solution)/shard_map/ppermute | solution.py:318
  211.5 2.8 %last.1 = (f32[33,32,128]{2,1,0:T(8,128)S(1)}, f32[4,8,32,128]{3,2,1,0:T(8,128)S(1)}) custom-call(s32[5,136]{1,0:T(8,128)S(1)} %get-tuple-element.29.lst, s32[2]{0:T(128)S(1)} %pad_add_fusion.pos, bf16[128,128,128]{2,1,0:T(8,128)(2,1)S(1)} %get-tuple-element.30.tiles_ref, bf16[16,32,128]{2,1,0:T(8,128)(2,1)S(1)} %bitcast.31, ...), custom_call_target="tpu_custom_call", output_to_operand_aliasing={{0}: (15, {})} | custom-call | tf_op jit(solution)/shard_map/last/pallas_call | solution.py:229
  214.3 11.0 %all_to_all.82.parts_ref = f32[4,8,32,128]{3,2,1,0:T(8,128)S(1)} all-to-all(f32[4,8,32,128]{3,2,1,0:T(8,128)S(1)} %get-tuple-element.42), channel_id=1, replica_groups=mesh['slab'=4,'row'=4,'col'=16] {'row'}, dimensions={0} | all-to-all | bytes 1048576 | tf_op jit(solution)/shard_map/all_to_all | solution.py:372
  (44 shorter events, 26.2 us)
Async XLA Ops:
  2.6 27.0 %all-to-all-start = ((bf16[8,8,32,128]{3,2,1,0:T(8,128)(2,1)}), bf16[8,8,32,128]{3,2,1,0:T(8,128)(2,1)S(1)}, u32[]{:S(2)}, u32[]{:S(2)}) async-start(bf16[8,8,32,128]{3,2,1,0:T(8,128)(2,1)} %broadcast_in_dim.24), calls=%async_computation | async-start | bytes 1048576 | tf_op jit(solution)/shard_map/all_to_all | solution.py:316
  12.3 17.8 %collective-permute-start.4 = (f32[1,256]{1,0:T(1,128)S(1)}, f32[1,256]{1,0:T(1,128)S(1)}, u32[]{:S(2)}, u32[]{:S(2)}) collective-permute-start(f32[1,256]{1,0:T(1,128)S(1)} %convert_element_type.21), channel_id=1, source_target_pairs={{112,0},{64,16},{80,32},{96,48},{176,64},{128,80},{144,96},{160,11... | collective-permute-start | bytes 3080 | tf_op jit(solution)/shard_map/ppermute | solution.py:331
  13.5 16.5 %collective-permute-start.3 = (f32[1,256]{1,0:T(1,128)S(1)}, f32[1,256]{1,0:T(1,128)S(1)}, u32[]{:S(2)}, u32[]{:S(2)}) collective-permute-start(f32[1,256]{1,0:T(1,128)S(1)} %convert_element_type.21), channel_id=1, source_target_pairs={{96,0},{112,16},{64,32},{80,48},{160,64},{176,80},{128,96},{144,11... | collective-permute-start | bytes 3080 | tf_op jit(solution)/shard_map/ppermute | solution.py:331
  14.8 15.2 %collective-permute-start.2 = (f32[1,256]{1,0:T(1,128)S(1)}, f32[1,256]{1,0:T(1,128)S(1)}, u32[]{:S(2)}, u32[]{:S(2)}) collective-permute-start(f32[1,256]{1,0:T(1,128)S(1)} %convert_element_type.21), channel_id=1, source_target_pairs={{80,0},{96,16},{112,32},{64,48},{144,64},{160,80},{176,96},{128,11... | collective-permute-start | bytes 3080 | tf_op jit(solution)/shard_map/ppermute | solution.py:331
  16.8 8.0 %collective-permute-start.1 = (f32[2,256]{1,0:T(2,128)S(1)}, f32[2,256]{1,0:T(2,128)S(1)}, u32[]{:S(2)}, u32[]{:S(2)}) collective-permute-start(f32[2,256]{1,0:T(2,128)S(1)} %pad_maximum_fusion), channel_id=1, source_target_pairs={{64,0},{80,16},{96,32},{112,48},{128,64},{144,80},{160,96},{176,11... | collective-permute-start | bytes 6152 | tf_op jit(solution)/shard_map/ppermute | solution.py:331
  18.9 34.3 %copy-start = (f32[1,256]{1,0:T(1,128)S(1)}, f32[1,256]{1,0:T(1,128)}, u32[]{:S(2)}) copy-start(f32[1,256]{1,0:T(1,128)} %coef_ref.5) | copy-start | bytes 3076
  29.5 2.0 collective-permute-start
  66.0 3.9 %collective-permute-start.5 = (bf16[16,32,128]{2,1,0:T(8,128)(2,1)S(1)}, bf16[16,32,128]{2,1,0:T(8,128)(2,1)S(1)}, u32[]{:S(2)}, u32[]{:S(2)}) collective-permute-start(bf16[16,32,128]{2,1,0:T(8,128)(2,1)S(1)} %bitcast.29), channel_id=1, source_target_pairs={{0,1},{1,0},{2,3},{3,2},{4,5},{5,4},{6,7},{7,6},{8,9},{9,8},{10,11... | collective-permute-start | bytes 393224 | tf_op jit(solution)/shard_map/ppermute | solution.py:318
  92.5 3.6 %collective-permute-start.6 = (bf16[16,32,128]{2,1,0:T(8,128)(2,1)S(1)}, bf16[16,32,128]{2,1,0:T(8,128)(2,1)S(1)}, u32[]{:S(2)}, u32[]{:S(2)}) collective-permute-start(bf16[16,32,128]{2,1,0:T(8,128)(2,1)S(1)} %bitcast.32), channel_id=1, source_target_pairs={{0,1},{1,0},{2,3},{3,2},{4,5},{5,4},{6,7},{7,6},{8,9},{9,8},{10,11... | collective-permute-start | bytes 393224 | tf_op jit(solution)/shard_map/ppermute | solution.py:318
  119.8 3.4 %collective-permute-start.7 = (bf16[16,32,128]{2,1,0:T(8,128)(2,1)S(1)}, bf16[16,32,128]{2,1,0:T(8,128)(2,1)S(1)}, u32[]{:S(2)}, u32[]{:S(2)}) collective-permute-start(bf16[16,32,128]{2,1,0:T(8,128)(2,1)S(1)} %bitcast.35), channel_id=1, source_target_pairs={{0,1},{1,0},{2,3},{3,2},{4,5},{5,4},{6,7},{7,6},{8,9},{9,8},{10,11... | collective-permute-start | bytes 393224 | tf_op jit(solution)/shard_map/ppermute | solution.py:318
  149.3 3.7 %collective-permute-start.8 = (bf16[32,32,128]{2,1,0:T(8,128)(2,1)S(1)}, bf16[32,32,128]{2,1,0:T(8,128)(2,1)S(1)}, u32[]{:S(2)}, u32[]{:S(2)}) collective-permute-start(bf16[32,32,128]{2,1,0:T(8,128)(2,1)S(1)} %bitcast.21), channel_id=1, source_target_pairs={{0,1},{1,0},{2,3},{3,2},{4,5},{5,4},{6,7},{7,6},{8,9},{9,8},{10,11... | collective-permute-start | bytes 786440 | tf_op jit(solution)/shard_map/ppermute | solution.py:318
  179.1 3.8 %collective-permute-start.9 = (bf16[32,32,128]{2,1,0:T(8,128)(2,1)S(1)}, bf16[32,32,128]{2,1,0:T(8,128)(2,1)S(1)}, u32[]{:S(2)}, u32[]{:S(2)}) collective-permute-start(bf16[32,32,128]{2,1,0:T(8,128)(2,1)S(1)} %bitcast.24), channel_id=1, source_target_pairs={{0,1},{1,0},{2,3},{3,2},{4,5},{5,4},{6,7},{7,6},{8,9},{9,8},{10,11... | collective-permute-start | bytes 786440 | tf_op jit(solution)/shard_map/ppermute | solution.py:318
  207.7 3.8 %collective-permute-start.10 = (bf16[32,32,128]{2,1,0:T(8,128)(2,1)S(1)}, bf16[32,32,128]{2,1,0:T(8,128)(2,1)S(1)}, u32[]{:S(2)}, u32[]{:S(2)}) collective-permute-start(bf16[32,32,128]{2,1,0:T(8,128)(2,1)S(1)} %bitcast.38), channel_id=1, source_target_pairs={{0,1},{1,0},{2,3},{3,2},{4,5},{5,4},{6,7},{7,6},{8,9},{9,8},{10,11... | collective-permute-start | bytes 786440 | tf_op jit(solution)/shard_map/ppermute | solution.py:318

commit v4 on v3

--- a/solution.py
+++ b/solution.py
@@ -71,13 +71,13 @@
     lax.fori_loop(0, lst[LISTS, which], group, 0)
 
 
-def write_down(acc, pos, hot_ref, msg_ref):
+def write_down(acc, row, hot_ref, msg_ref):
     for d in range(NROW):
-        r = (pos[1] + d) & (NROW - 1)
+        r = (row[0] + d) & (NROW - 1)
         values = jnp.concatenate([acc[r * BLK + b].astype(BF) for b in range(PRT)], axis=1)
         part = jnp.dot(values, hot_ref[d], preferred_element_type=F32).astype(BF)
         for b in range(TGT):
-            for s in range(NSLAB):
+            for s in range(2):
                 msg_ref[s * NROW + r, b] = part[:, b * B : (b + 1) * B]
 
 
@@ -85,14 +85,14 @@
     for r in range(NROW):
         for b in range(TGT):
             part = acc[r * BLK + b].astype(BF)
-            for s in range(NSLAB):
+            for s in range(2):
                 msg_ref[s * NROW + r, b] = part
 
 
-MESSAGE = jax.ShapeDtypeStruct((NSLAB * NROW, TGT, W, B), BF)
-
-
-def first_kernel(codes, pos, own_ref, other_ref, hot_ref, tiles_hbm, acc, tiles_ref, lst, msg_ref, sems):
+MESSAGE = jax.ShapeDtypeStruct((2 * NROW, TGT, W, B), BF)
+
+
+def first_kernel(codes, row_index, own_ref, other_ref, hot_ref, tiles_hbm, acc, tiles_ref, lst, msg_ref, sems):
     def load(g):
         at = pl.ds(pl.multiple_of(g * UNROLL, UNROLL), UNROLL)
         return pltpu.make_async_copy(tiles_hbm.at[at], tiles_ref.at[at], sems.at[g])
@@ -144,10 +144,10 @@
         for u in range(UNROLL):
             lst[k, counts[k] + u] = NROW * BLK * NT
         lst[LISTS, k] = shr(counts[k] + UNROLL - 1, 3)
-    write_down(acc, pos, hot_ref, msg_ref)
-
-
-def first_apply(codes, pos, pair, hots, tiles):
+    write_down(acc, row_index, hot_ref, msg_ref)
+
+
+def first_apply(codes, row_index, pair, hots, tiles):
     return pl.pallas_call(
         first_kernel,
         out_shape=(
@@ -161,45 +161,45 @@
         scratch_shapes=[pltpu.SemaphoreType.DMA((NT // UNROLL,))],
         compiler_params=PARAMS,
         name="first",
-    )(codes, pos, *pair, hots, pltpu.with_memory_space_constraint(tiles, pltpu.HBM))
-
-
-def down_step_kernel(lst, pos, own_ref, other_ref, hot_ref, tiles_ref, acc_in, acc, msg_ref, *, section):
-    @pl.when(pos[0] == section)
+    )(codes, row_index, *pair, hots, pltpu.with_memory_space_constraint(tiles, pltpu.HBM))
+
+
+def down_step_kernel(lst, slab, row, own_ref, other_ref, hot_ref, tiles_ref, acc_in, acc, msg_ref, *, section):
+    @pl.when(slab[0] == section)
     def _():
         apply_list(lst, TAB, (own_ref, other_ref), tiles_ref, acc)
 
     if section < NSLAB - 1:
-        write_down(acc, pos, hot_ref, msg_ref)
+        write_down(acc, row, hot_ref, msg_ref)
     else:
         write_up(acc, msg_ref)
 
 
-def down_step(lst, pos, pair, hots, tiles, acc, section):
+def down_step(lst, slab, row, pair, hots, tiles, acc, section):
     return pl.pallas_call(
         functools.partial(down_step_kernel, section=section),
         out_shape=(jax.ShapeDtypeStruct(ACC, F32), MESSAGE),
-        in_specs=[smem(), smem()] + [vmem()] * 5,
+        in_specs=[smem(), smem(), smem()] + [vmem()] * 5,
         out_specs=(vmem(), vmem()),
-        input_output_aliases={6: 0},
+        input_output_aliases={7: 0},
         compiler_params=PARAMS,
         name="down_step",
-    )(lst, pos, *pair, hots, tiles, acc)
-
-
-def up_step_kernel(lst, pos, own_ref, other_ref, tiles_ref, acc_in, msg_ref, acc, *, section):
+    )(lst, slab, row, *pair, hots, tiles, acc)
+
+
+def up_step_kernel(lst, slab, own_ref, other_ref, tiles_ref, acc_in, msg_ref, acc, *, section):
     for r in range(NROW):
         for b in range(TGT):
             acc[r * BLK + b] = acc_in[r * BLK + b]
 
-    @pl.when(pos[0] == section)
+    @pl.when(slab[0] == section)
     def _():
         apply_list(lst, LA, (own_ref, other_ref), tiles_ref, acc)
 
     write_up(acc, msg_ref)
 
 
-def up_step(lst, pos, pair, tiles, acc, section):
+def up_step(lst, slab, pair, tiles, acc, section):
     return pl.pallas_call(
         functools.partial(up_step_kernel, section=section),
         out_shape=MESSAGE,
@@ -208,36 +208,36 @@
         scratch_shapes=[pltpu.VMEM(ACC, F32)],
         compiler_params=PARAMS,
         name="up_step",
-    )(lst, pos, *pair, tiles, acc)
-
-
-def last_kernel(lst, pos, tiles_ref, *refs):
+    )(lst, slab, *pair, tiles, acc)
+
+
+def last_kernel(lst, slab, tiles_ref, *refs):
     gathered, acc, msg_ref = refs[:12], refs[13], refs[14]
     for k, s in enumerate((1, 2, 3, 2, 1, 0)):
-        @pl.when(pos[0] == s)
+        @pl.when(slab[0] == s)
         def _(k=k):
             pair = gathered[2 * k], gathered[2 * k + 1]
             apply_list(lst, TC if k < NSLAB - 1 else LALL, pair, tiles_ref, acc)
 
     for r in range(NROW):
         for b in range(BLK):
-            msg_ref[r, b] = acc[r * BLK + b]
-
-
-def last_apply(lst, pos, tiles, pairs, acc):
+            msg_ref[r, b] = acc[r * BLK + b].astype(BF)
+
+
+def last_apply(lst, slab, tiles, pairs, acc):
     flat = [ref for pair in pairs for ref in pair]
     return pl.pallas_call(
         last_kernel,
         out_shape=(
             jax.ShapeDtypeStruct(ACC, F32),
-            jax.ShapeDtypeStruct((NROW, BLK, W, B), F32),
+            jax.ShapeDtypeStruct((NROW, BLK, W, B), BF),
         ),
         in_specs=[smem(), smem()] + [vmem()] * 14,
         out_specs=(vmem(), vmem()),
         input_output_aliases={15: 0},
         compiler_params=PARAMS,
         name="last",
-    )(lst, pos, tiles, *flat, acc)[1]
+    )(lst, slab, tiles, *flat, acc)[1]
 
 
 def split(x):
@@ -246,27 +246,25 @@
     return jnp.concatenate([high, rest.astype(BF)], axis=0)
 
 
-def row_total(rcv_ref, section, b):
-    part = rcv_ref[section * NROW, b].astype(F32)
+def row_total(rcv_ref, place, b):
+    part = rcv_ref[place * NROW, b].astype(F32)
     for r in range(1, NROW):
-        part = part + rcv_ref[section * NROW + r, b].astype(F32)
+        part = part + rcv_ref[place * NROW + r, b].astype(F32)
     return part
 
 
-def down_kernel(pos, rcv_ref, rhs_ref, coef_ref, out_ref):
-    before = jnp.maximum(pos[0] - 1, 0)
+def down_kernel(rcv_ref, rhs_ref, coef_ref, out_ref):
     for b in range(TGT):
-        pulled = row_total(rcv_ref, before, b) * coef_ref[:, b * B : (b + 1) * B]
+        pulled = row_total(rcv_ref, 0, b) * coef_ref[:, b * B : (b + 1) * B]
         value = (rhs_ref[b] - pulled).astype(BF)
         for z in range(HALF):
             out_ref[z, b] = value
 
 
-def up_kernel(pos, rcv_ref, coef_ref, hot_ref, out_ref):
-    after = jnp.minimum(pos[0] + 1, NSLAB - 1)
+def up_kernel(rcv_ref, coef_ref, hot_ref, out_ref):
     values = jnp.concatenate(
         [
-            split(row_total(rcv_ref, after, b) * coef_ref[:, b * B : (b + 1) * B])
+            split(row_total(rcv_ref, 1, b) * coef_ref[:, b * B : (b + 1) * B])
             for b in range(TGT)
         ],
         axis=1,
@@ -279,22 +277,47 @@
             out_ref[z, b] = value
 
 
-def combine(kernel, pos, received, others, blocks, name):
+def combine(kernel, received, others, blocks, name):
     return pl.pallas_call(
         kernel,
         out_shape=jax.ShapeDtypeStruct((HALF, blocks, W, B), BF),
-        in_specs=[smem()] + [vmem()] * (1 + len(others)),
+        in_specs=[vmem()] * (1 + len(others)),
         out_specs=vmem(),
         compiler_params=PARAMS,
         name=name,
-    )(pos, received, *others)
+    )(received, *others)
+
+
+def prepare_kernel(count, slab, rhs_ref, out_ref, target_ref):
+    for b in range(BLK):
+        value = rhs_ref[0, :, b * B : (b + 1) * B]
+        if b < TGT:
+            target_ref[b] = value
+            value = jnp.where(slab[0] == 0, value, 0.0)
+        value = jnp.where(b < count[0], value, 0.0).astype(BF)
+        for z in range(HALF):
+            out_ref[z, b] = value
+
+
+def prepare(right_sides, section_blocks, slab):
+    return pl.pallas_call(
+        prepare_kernel,
+        out_shape=(
+            jax.ShapeDtypeStruct((HALF, BLK, W, B), BF),
+            jax.ShapeDtypeStruct((TGT, W, B), F32),
+        ),
+        in_specs=[smem(), smem(), vmem()],
+        out_specs=(vmem(), vmem()),
+        compiler_params=PARAMS,
+        name="prepare",
+    )(section_blocks, slab, right_sides)
 
 
 def finish_kernel(count, parts_ref, out_ref):
     for b in range(BLK):
-        total = parts_ref[0, b]
+        total = parts_ref[0, b].astype(F32)
         for r in range(1, NROW):
-            total = total + parts_ref[r, b]
+            total = total + parts_ref[r, b].astype(F32)
         out_ref[0, :, b * B : (b + 1) * B] = jnp.where(b < count[0], total, 0.0)
 
 
@@ -318,8 +341,12 @@
     return own, lax.ppermute(own, "col", [(c, c ^ 1) for c in range(NCOL)])
 
 
-def exchange(message):
-    return lax.all_to_all(message, ("slab", "row"), 0, 0, tiled=True)
+def exchange(message, low):
+    groups = [
+        [(s + k) % NSLAB * NROW + r for k in range(2) for r in range(NROW)]
+        for s in (low, low + 2)
+    ]
+    return lax.all_to_all(message, ("slab", "row"), 0, 0, tiled=True, axis_index_groups=groups)
 
 
 def from_next(value, turn):
@@ -335,7 +362,8 @@
     slab = lax.axis_index("slab").astype(jnp.int32)
     row = lax.axis_index("row").astype(jnp.int32)
     col = lax.axis_index("col").astype(jnp.int32)
-    pos = jnp.stack([slab, row])
+    slab = slab.reshape(1)
+    row = row.reshape(1)
     codes = tile_codes(tile_rows, tile_cols, col)
     map_own = plane_map.astype(F32)
     pack_next = from_next(jnp.concatenate([map_own, interface_coef], axis=0), 0)
@@ -344,33 +372,28 @@
         [pack_next[0:1]] + [from_next(map_own, d) for d in range(1, NROW)], axis=0
     ).astype(jnp.int32)
 
-    source = right_sides[0].reshape(W, BLK, B).transpose(1, 0, 2)
-    blk = jnp.arange(BLK, dtype=jnp.int32)
-    keep = (blk < section_blocks[0]) & ((slab == 0) | (blk >= TGT))
-    v0 = jnp.where(keep[:, None, None], source, 0.0).astype(BF)
-    rhs_target = source[:TGT]
+    copies, rhs_target = prepare(right_sides, section_blocks, slab)
     partner = jnp.arange(PRT * B, dtype=jnp.int32)
     hots = (partner[None, :, None] == maps_next[:, None, :]).astype(BF)
     hot_next = (maps_next[0][:, None] == partner[None, :]).astype(BF)
 
-    pair = gather(jnp.broadcast_to(v0[None], (HALF, *v0.shape)))
-    pair, hots, hot_next, coef_next, rhs_target, codes, pos = lax.optimization_barrier(
-        (pair, hots, hot_next, coef_next, rhs_target, codes, pos)
+    pair = gather(copies)
+    pair, hots, hot_next, coef_next, rhs_target, codes = lax.optimization_barrier(
+        (pair, hots, hot_next, coef_next, rhs_target, codes)
     )
-    acc, tiles, lst, msg = first_apply(codes, pos, pair, hots, front_tiles[0])
+    acc, tiles, lst, msg = first_apply(codes, row, pair, hots, front_tiles[0])
     pairs = []
     for s in range(1, NSLAB):
-        rcv = exchange(msg)
-        pairs.append(gather(combine(down_kernel, pos, rcv, (rhs_target, interface_coef), TGT, "down")))
-        acc, msg = down_step(lst, pos, pairs[-1], hots, tiles, acc, s)
+        rcv = exchange(msg, s - 1)
+        pairs.append(gather(combine(down_kernel, rcv, (rhs_target, interface_coef), TGT, "down")))
+        acc, msg = down_step(lst, slab, row, pairs[-1], hots, tiles, acc, s)
     for s in range(NSLAB - 2, -1, -1):
-        rcv = exchange(msg)
-        pairs.append(gather(combine(up_kernel, pos, rcv, (coef_next, hot_next), PRT, "up")))
+        rcv = exchange(msg, s)
+        pairs.append(gather(combine(up_kernel, rcv, (coef_next, hot_next), PRT, "up")))
         if s > 0:
-            msg = up_step(lst, pos, pairs[-1], tiles, acc, s)
-    msg = last_apply(lst, pos, tiles, pairs, acc)
-    parts = lax.all_to_all(msg, "row", 0, 0, tiled=True)
-    return finish(section_blocks, parts)
+            msg = up_step(lst, slab, pairs[-1], tiles, acc, s)
+    msg = last_apply(lst, slab, tiles, pairs, acc)
+    return finish(section_blocks, lax.all_to_all(msg, "row", 0, 0, tiled=True))
 
 
 def solution(mesh):

time: 226 us -> 204 us (0.903)
  blocking collectives: 154 us -> 131 us
  starting transfers between devices: 30.3 us -> 32.9 us
    all_to_all x7, blocking collectives: 83 us -> 62 us  [the longest x6 53.8 us: exchange(): lax.all_to_all(message, ('slab', 'row'), 0, 0, tiled=True, axis_index_gro...]
    pallas_call x6, Pallas kernels: 3.88 us -> 0.61 us  [combine(): pl.pallas_call(kernel, out_shape=jax.ShapeDtypeStruct((HALF, blocks, W, B...]
    ppermute x7, starting transfers between devices: 16.2 us -> 18.7 us  [gather(): return (own, lax.ppermute(own, 'col', [(c, c ^ 1) for c in range(NCOL)]))]
where the time goes in v4:
time: 204 us; the launch traced here: 202 us
  blocking collectives  131 us (64%)
  starting transfers between devices  32.9 us (16%)
  waiting for transfers between devices  18.2 us (9%)
  Pallas kernels  16.1 us (8%)
  other arithmetic  2.54 us (1%)
    all_to_all x6, blocking collectives, gather(): lax.all_to_all(copies, 'col', 0, 0, tiled=True, axis_index_groups=Z_GROUPS)  69 us
    all_to_all x6, blocking collectives, exchange(): lax.all_to_all(message, ('slab', 'row'), 0, 0, tiled=True, axis_index_gro...  53.8 us
    ppermute x7, starting transfers between devices, gather(): return (own, lax.ppermute(own, 'col', [(c, c ^ 1) for c in range(NCOL)]))  18.7 us
    all_to_all x1, starting transfers between devices, gather(): lax.all_to_all(copies, 'col', 0, 0, tiled=True, axis_index_groups=Z_GROUPS)  9 us
    all_to_all x1, blocking collectives, body(): return finish(section_blocks, lax.all_to_all(msg, 'row', 0, 0, tiled=True))  8.14 us
    ppermute x7, waiting for transfers between devices, gather(): return (own, lax.ppermute(own, 'col', [(c, c ^ 1) for c in range(NCOL)]))  7.48 us
    pallas_call x1, Pallas kernels, first_apply(): pl.pallas_call(first_kernel, out_shape=(jax.ShapeDtypeStruct(ACC, F32), j...  6.96 us
    ppermute x4, waiting for transfers between devices, from_next(): return lax.ppermute(value, ('slab', 'row'), pairs)  6.04 us
  transfers between devices with their start and end apart: 12, of which 9 were waited for; matrix products, arithmetic and copies ran while one was open for 1% of the time, Pallas kernels for 0%

profile of v4, /device:TPU:1, one launch (start us, length us, event | category | flops | bytes accessed | tf_op | source)
XLA Modules:
  0.0 202.3 jit_solution(5386452072414747762)
XLA Ops:
  2.4 9.0 %all-to-all-start = ((bf16[8,8,32,128]{3,2,1,0:T(8,128)(2,1)}), bf16[8,8,32,128]{3,2,1,0:T(8,128)(2,1)S(1)}, u32[]{:S(2)}, u32[]{:S(2)}) async-start(bf16[8,8,32,128]{3,2,1,0:T(8,128)(2,1)} %get-tuple-element.25), calls=%async_computation | async-start | bytes 1048576 | tf_op jit(solution)/shard_map/all_to_all | solution.py:339
  18.7 6.0 %collective-permute-done.1 = f32[2,256]{1,0:T(2,128)S(1)} collective-permute-done((f32[2,256]{1,0:T(2,128)S(1)}, f32[2,256]{1,0:T(2,128)S(1)}, u32[]{:S(2)}, u32[]{:S(2)}) %collective-permute-start.1) | collective-permute-done | bytes 2080 | tf_op jit(solution)/shard_map/ppermute | solution.py:358
  24.7 4.6 %all-to-all-done = bf16[8,8,32,128]{3,2,1,0:T(8,128)(2,1)S(1)} async-done(((bf16[8,8,32,128]{3,2,1,0:T(8,128)(2,1)}), bf16[8,8,32,128]{3,2,1,0:T(8,128)(2,1)S(1)}, u32[]{:S(2)}, u32[]{:S(2)}) %all-to-all-start) | async-done | bytes 524320 | tf_op jit(solution)/shard_map/all_to_all | solution.py:339
  31.4 7.0 %first.1 = (f32[33,32,128]{2,1,0:T(8,128)S(1)}, bf16[128,128,128]{2,1,0:T(8,128)(2,1)S(1)}, s32[5,136]{1,0:T(8,128)S(1)}, bf16[8,2,32,128]{3,2,1,0:T(8,128)(2,1)S(1)}) custom-call(s32[1,128]{1,0:T(1,128)S(1)} %fusion.3.codes, s32[1]{0:T(128)} %bitcast.3.row_index.row, bf16[64,32,128]{2,1,0:T(8,128)(2,1)S(1)} %bitcast.18, ...), custom_call_target="tpu_custom_call" | custom-call | tf_op jit(solution)/shard_map/first/pallas_call | solution.py:151
  38.4 10.3 %all_to_all.70.rcv_ref = bf16[8,2,32,128]{3,2,1,0:T(8,128)(2,1)S(1)} all-to-all(bf16[8,2,32,128]{3,2,1,0:T(8,128)(2,1)S(1)} %get-tuple-element.33), channel_id=1, replica_groups={{0,16,32,48,64,80,96,112},{128,144,160,176,192,208,224,240},{1,17,33,49..., dimensions={0} | all-to-all | bytes 262144 | tf_op jit(solution)/shard_map/all_to_all | solution.py:349
  48.7 11.8 %all_to_all.71 = bf16[8,2,32,128]{3,2,1,0:T(8,128)(2,1)S(1)} all-to-all(bf16[8,2,32,128]{3,2,1,0:T(8,128)(2,1)S(1)} %down.3), channel_id=1, replica_groups={{0,2,4,6,8,10,12,14},{1,3,5,7,9,11,13,15},{16,18,20,22,24,26,28,30},{17..., dimensions={0} | all-to-all | bytes 262144 | tf_op jit(solution)/shard_map/all_to_all | solution.py:339
  60.5 3.1 %collective-permute-start.5 = (bf16[16,32,128]{2,1,0:T(8,128)(2,1)S(1)}, bf16[16,32,128]{2,1,0:T(8,128)(2,1)S(1)}, u32[]{:S(2)}, u32[]{:S(2)}) collective-permute-start(bf16[16,32,128]{2,1,0:T(8,128)(2,1)S(1)} %bitcast.19), channel_id=1, source_target_pairs={{0,1},{1,0},{2,3},{3,2},{4,5},{5,4},{6,7},{7,6},{8,9},{9,8},{10,11... | collective-permute-start | bytes 393224 | tf_op jit(solution)/shard_map/ppermute | solution.py:341
  65.6 8.7 %all_to_all.72.rcv_ref = bf16[8,2,32,128]{3,2,1,0:T(8,128)(2,1)S(1)} all-to-all(bf16[8,2,32,128]{3,2,1,0:T(8,128)(2,1)S(1)} %get-tuple-element.36), channel_id=1, replica_groups={{64,80,96,112,128,144,160,176},{192,208,224,240,0,16,32,48},{65,81,97,1..., dimensions={0} | all-to-all | bytes 262144 | tf_op jit(solution)/shard_map/all_to_all | solution.py:349
  74.3 10.3 %all_to_all.73 = bf16[8,2,32,128]{3,2,1,0:T(8,128)(2,1)S(1)} all-to-all(bf16[8,2,32,128]{3,2,1,0:T(8,128)(2,1)S(1)} %down.4), channel_id=1, replica_groups={{0,2,4,6,8,10,12,14},{1,3,5,7,9,11,13,15},{16,18,20,22,24,26,28,30},{17..., dimensions={0} | all-to-all | bytes 262144 | tf_op jit(solution)/shard_map/all_to_all | solution.py:339
  84.6 2.9 %collective-permute-start.6 = (bf16[16,32,128]{2,1,0:T(8,128)(2,1)S(1)}, bf16[16,32,128]{2,1,0:T(8,128)(2,1)S(1)}, u32[]{:S(2)}, u32[]{:S(2)}) collective-permute-start(bf16[16,32,128]{2,1,0:T(8,128)(2,1)S(1)} %bitcast.22), channel_id=1, source_target_pairs={{0,1},{1,0},{2,3},{3,2},{4,5},{5,4},{6,7},{7,6},{8,9},{9,8},{10,11... | collective-permute-start | bytes 393224 | tf_op jit(solution)/shard_map/ppermute | solution.py:341
  89.5 7.9 %all_to_all.74.rcv_ref = bf16[8,2,32,128]{3,2,1,0:T(8,128)(2,1)S(1)} all-to-all(bf16[8,2,32,128]{3,2,1,0:T(8,128)(2,1)S(1)} %get-tuple-element.38), channel_id=1, replica_groups={{128,144,160,176,192,208,224,240},{0,16,32,48,64,80,96,112},{129,145,16..., dimensions={0} | all-to-all | bytes 262144 | tf_op jit(solution)/shard_map/all_to_all | solution.py:349
  97.4 10.3 %all_to_all.75 = bf16[8,2,32,128]{3,2,1,0:T(8,128)(2,1)S(1)} all-to-all(bf16[8,2,32,128]{3,2,1,0:T(8,128)(2,1)S(1)} %down.5), channel_id=1, replica_groups={{0,2,4,6,8,10,12,14},{1,3,5,7,9,11,13,15},{16,18,20,22,24,26,28,30},{17..., dimensions={0} | all-to-all | bytes 262144 | tf_op jit(solution)/shard_map/all_to_all | solution.py:339
  107.7 2.9 %collective-permute-start.7 = (bf16[16,32,128]{2,1,0:T(8,128)(2,1)S(1)}, bf16[16,32,128]{2,1,0:T(8,128)(2,1)S(1)}, u32[]{:S(2)}, u32[]{:S(2)}) collective-permute-start(bf16[16,32,128]{2,1,0:T(8,128)(2,1)S(1)} %bitcast.25), channel_id=1, source_target_pairs={{0,1},{1,0},{2,3},{3,2},{4,5},{5,4},{6,7},{7,6},{8,9},{9,8},{10,11... | collective-permute-start | bytes 393224 | tf_op jit(solution)/shard_map/ppermute | solution.py:341
  112.3 7.8 %all_to_all.76.rcv_ref = bf16[8,2,32,128]{3,2,1,0:T(8,128)(2,1)S(1)} all-to-all(bf16[8,2,32,128]{3,2,1,0:T(8,128)(2,1)S(1)} %get-tuple-element.40), channel_id=1, replica_groups={{128,144,160,176,192,208,224,240},{0,16,32,48,64,80,96,112},{129,145,16..., dimensions={0} | all-to-all | bytes 262144 | tf_op jit(solution)/shard_map/all_to_all | solution.py:349
  120.3 12.3 %all_to_all.77 = bf16[8,4,32,128]{3,2,1,0:T(8,128)(2,1)S(1)} all-to-all(bf16[8,4,32,128]{3,2,1,0:T(8,128)(2,1)S(1)} %up.3), channel_id=1, replica_groups={{0,2,4,6,8,10,12,14},{1,3,5,7,9,11,13,15},{16,18,20,22,24,26,28,30},{17..., dimensions={0} | all-to-all | bytes 524288 | tf_op jit(solution)/shard_map/all_to_all | solution.py:339
  132.6 3.0 %collective-permute-start.8 = (bf16[32,32,128]{2,1,0:T(8,128)(2,1)S(1)}, bf16[32,32,128]{2,1,0:T(8,128)(2,1)S(1)}, u32[]{:S(2)}, u32[]{:S(2)}) collective-permute-start(bf16[32,32,128]{2,1,0:T(8,128)(2,1)S(1)} %bitcast.11), channel_id=1, source_target_pairs={{0,1},{1,0},{2,3},{3,2},{4,5},{5,4},{6,7},{7,6},{8,9},{9,8},{10,11... | collective-permute-start | bytes 786440 | tf_op jit(solution)/shard_map/ppermute | solution.py:341
  137.4 9.1 %all_to_all.78.rcv_ref = bf16[8,2,32,128]{3,2,1,0:T(8,128)(2,1)S(1)} all-to-all(bf16[8,2,32,128]{3,2,1,0:T(8,128)(2,1)S(1)} %up_step.2), channel_id=1, replica_groups={{64,80,96,112,128,144,160,176},{192,208,224,240,0,16,32,48},{65,81,97,1..., dimensions={0} | all-to-all | bytes 262144 | tf_op jit(solution)/shard_map/all_to_all | solution.py:349
  146.7 12.2 %all_to_all.79 = bf16[8,4,32,128]{3,2,1,0:T(8,128)(2,1)S(1)} all-to-all(bf16[8,4,32,128]{3,2,1,0:T(8,128)(2,1)S(1)} %up.4), channel_id=1, replica_groups={{0,2,4,6,8,10,12,14},{1,3,5,7,9,11,13,15},{16,18,20,22,24,26,28,30},{17..., dimensions={0} | all-to-all | bytes 524288 | tf_op jit(solution)/shard_map/all_to_all | solution.py:339
  158.9 3.0 %collective-permute-start.9 = (bf16[32,32,128]{2,1,0:T(8,128)(2,1)S(1)}, bf16[32,32,128]{2,1,0:T(8,128)(2,1)S(1)}, u32[]{:S(2)}, u32[]{:S(2)}) collective-permute-start(bf16[32,32,128]{2,1,0:T(8,128)(2,1)S(1)} %bitcast.14), channel_id=1, source_target_pairs={{0,1},{1,0},{2,3},{3,2},{4,5},{5,4},{6,7},{7,6},{8,9},{9,8},{10,11... | collective-permute-start | bytes 786440 | tf_op jit(solution)/shard_map/ppermute | solution.py:341
  163.8 10.1 %all_to_all.80.rcv_ref = bf16[8,2,32,128]{3,2,1,0:T(8,128)(2,1)S(1)} all-to-all(bf16[8,2,32,128]{3,2,1,0:T(8,128)(2,1)S(1)} %up_step.3), channel_id=1, replica_groups={{0,16,32,48,64,80,96,112},{128,144,160,176,192,208,224,240},{1,17,33,49..., dimensions={0} | all-to-all | bytes 262144 | tf_op jit(solution)/shard_map/all_to_all | solution.py:349
  174.1 12.0 %all_to_all.81 = bf16[8,4,32,128]{3,2,1,0:T(8,128)(2,1)S(1)} all-to-all(bf16[8,4,32,128]{3,2,1,0:T(8,128)(2,1)S(1)} %up.5), channel_id=1, replica_groups={{0,2,4,6,8,10,12,14},{1,3,5,7,9,11,13,15},{16,18,20,22,24,26,28,30},{17..., dimensions={0} | all-to-all | bytes 524288 | tf_op jit(solution)/shard_map/all_to_all | solution.py:339
  186.1 3.2 %collective-permute-start.10 = (bf16[32,32,128]{2,1,0:T(8,128)(2,1)S(1)}, bf16[32,32,128]{2,1,0:T(8,128)(2,1)S(1)}, u32[]{:S(2)}, u32[]{:S(2)}) collective-permute-start(bf16[32,32,128]{2,1,0:T(8,128)(2,1)S(1)} %bitcast.28), channel_id=1, source_target_pairs={{0,1},{1,0},{2,3},{3,2},{4,5},{5,4},{6,7},{7,6},{8,9},{9,8},{10,11... | collective-permute-start | bytes 786440 | tf_op jit(solution)/shard_map/ppermute | solution.py:341
  190.5 3.0 %last.1 = (f32[33,32,128]{2,1,0:T(8,128)S(1)}, bf16[4,8,32,128]{3,2,1,0:T(8,128)(2,1)S(1)}) custom-call(s32[5,136]{1,0:T(8,128)S(1)} %get-tuple-element.31.lst, s32[1]{0:T(128)} %bitcast.slab, bf16[128,128,128]{2,1,0:T(8,128)(2,1)S(1)} %get-tuple-element.32.tiles_ref, bf16[16,32,128]{2,1,0:T(8,128)(2,1)S(1)} %bitcast.21, ...), custom_call_target="tpu_custom_call", output_to_operand_aliasing={{0}: (15, {})} | custom-call | tf_op jit(solution)/shard_map/last/pallas_call | solution.py:229
  193.5 8.1 %all_to_all.82.parts_ref = bf16[4,8,32,128]{3,2,1,0:T(8,128)(2,1)S(1)} all-to-all(bf16[4,8,32,128]{3,2,1,0:T(8,128)(2,1)S(1)} %get-tuple-element.44), channel_id=1, replica_groups=mesh['slab'=4,'row'=4,'col'=16] {'row'}, dimensions={0} | all-to-all | bytes 524288 | tf_op jit(solution)/shard_map/all_to_all | solution.py:396
  (40 shorter events, 22.7 us)
Async XLA Ops:
  0.7 0.9 copy-start
  2.4 27.0 %all-to-all-start = ((bf16[8,8,32,128]{3,2,1,0:T(8,128)(2,1)}), bf16[8,8,32,128]{3,2,1,0:T(8,128)(2,1)S(1)}, u32[]{:S(2)}, u32[]{:S(2)}) async-start(bf16[8,8,32,128]{3,2,1,0:T(8,128)(2,1)} %get-tuple-element.25), calls=%async_computation | async-start | bytes 1048576 | tf_op jit(solution)/shard_map/all_to_all | solution.py:339
  11.4 37.2 %copy-start.1 = (f32[1,256]{1,0:T(1,128)S(1)}, f32[1,256]{1,0:T(1,128)}, u32[]{:S(2)}) copy-start(f32[1,256]{1,0:T(1,128)} %coef_ref.5) | copy-start | bytes 3076
  12.1 17.8 %collective-permute-start.4 = (f32[1,256]{1,0:T(1,128)S(1)}, f32[1,256]{1,0:T(1,128)S(1)}, u32[]{:S(2)}, u32[]{:S(2)}) collective-permute-start(f32[1,256]{1,0:T(1,128)S(1)} %convert_element_type.17), channel_id=1, source_target_pairs={{112,0},{64,16},{80,32},{96,48},{176,64},{128,80},{144,96},{160,11... | collective-permute-start | bytes 3080 | tf_op jit(solution)/shard_map/ppermute | solution.py:358
  13.4 16.5 %collective-permute-start.3 = (f32[1,256]{1,0:T(1,128)S(1)}, f32[1,256]{1,0:T(1,128)S(1)}, u32[]{:S(2)}, u32[]{:S(2)}) collective-permute-start(f32[1,256]{1,0:T(1,128)S(1)} %convert_element_type.17), channel_id=1, source_target_pairs={{96,0},{112,16},{64,32},{80,48},{160,64},{176,80},{128,96},{144,11... | collective-permute-start | bytes 3080 | tf_op jit(solution)/shard_map/ppermute | solution.py:358
  14.7 15.2 %collective-permute-start.2 = (f32[1,256]{1,0:T(1,128)S(1)}, f32[1,256]{1,0:T(1,128)S(1)}, u32[]{:S(2)}, u32[]{:S(2)}) collective-permute-start(f32[1,256]{1,0:T(1,128)S(1)} %convert_element_type.17), channel_id=1, source_target_pairs={{80,0},{96,16},{112,32},{64,48},{144,64},{160,80},{176,96},{128,11... | collective-permute-start | bytes 3080 | tf_op jit(solution)/shard_map/ppermute | solution.py:358
  16.7 8.0 %collective-permute-start.1 = (f32[2,256]{1,0:T(2,128)S(1)}, f32[2,256]{1,0:T(2,128)S(1)}, u32[]{:S(2)}, u32[]{:S(2)}) collective-permute-start(f32[2,256]{1,0:T(2,128)S(1)} %pad_maximum_fusion), channel_id=1, source_target_pairs={{64,0},{80,16},{96,32},{112,48},{128,64},{144,80},{160,96},{176,11... | collective-permute-start | bytes 6152 | tf_op jit(solution)/shard_map/ppermute | solution.py:358
  29.4 2.0 %collective-permute-start = (bf16[64,32,128]{2,1,0:T(8,128)(2,1)S(1)}, bf16[64,32,128]{2,1,0:T(8,128)(2,1)S(1)}, u32[]{:S(2)}, u32[]{:S(2)}) collective-permute-start(bf16[64,32,128]{2,1,0:T(8,128)(2,1)S(1)} %bitcast.17), channel_id=1, source_target_pairs={{0,1},{1,0},{2,3},{3,2},{4,5},{5,4},{6,7},{7,6},{8,9},{9,8},{10,11... | collective-permute-start | bytes 1572872 | tf_op jit(solution)/shard_map/ppermute | solution.py:341
  60.5 4.1 %collective-permute-start.5 = (bf16[16,32,128]{2,1,0:T(8,128)(2,1)S(1)}, bf16[16,32,128]{2,1,0:T(8,128)(2,1)S(1)}, u32[]{:S(2)}, u32[]{:S(2)}) collective-permute-start(bf16[16,32,128]{2,1,0:T(8,128)(2,1)S(1)} %bitcast.19), channel_id=1, source_target_pairs={{0,1},{1,0},{2,3},{3,2},{4,5},{5,4},{6,7},{7,6},{8,9},{9,8},{10,11... | collective-permute-start | bytes 393224 | tf_op jit(solution)/shard_map/ppermute | solution.py:341
  84.6 3.9 %collective-permute-start.6 = (bf16[16,32,128]{2,1,0:T(8,128)(2,1)S(1)}, bf16[16,32,128]{2,1,0:T(8,128)(2,1)S(1)}, u32[]{:S(2)}, u32[]{:S(2)}) collective-permute-start(bf16[16,32,128]{2,1,0:T(8,128)(2,1)S(1)} %bitcast.22), channel_id=1, source_target_pairs={{0,1},{1,0},{2,3},{3,2},{4,5},{5,4},{6,7},{7,6},{8,9},{9,8},{10,11... | collective-permute-start | bytes 393224 | tf_op jit(solution)/shard_map/ppermute | solution.py:341
  107.7 3.9 %collective-permute-start.7 = (bf16[16,32,128]{2,1,0:T(8,128)(2,1)S(1)}, bf16[16,32,128]{2,1,0:T(8,128)(2,1)S(1)}, u32[]{:S(2)}, u32[]{:S(2)}) collective-permute-start(bf16[16,32,128]{2,1,0:T(8,128)(2,1)S(1)} %bitcast.25), channel_id=1, source_target_pairs={{0,1},{1,0},{2,3},{3,2},{4,5},{5,4},{6,7},{7,6},{8,9},{9,8},{10,11... | collective-permute-start | bytes 393224 | tf_op jit(solution)/shard_map/ppermute | solution.py:341
  132.6 4.1 %collective-permute-start.8 = (bf16[32,32,128]{2,1,0:T(8,128)(2,1)S(1)}, bf16[32,32,128]{2,1,0:T(8,128)(2,1)S(1)}, u32[]{:S(2)}, u32[]{:S(2)}) collective-permute-start(bf16[32,32,128]{2,1,0:T(8,128)(2,1)S(1)} %bitcast.11), channel_id=1, source_target_pairs={{0,1},{1,0},{2,3},{3,2},{4,5},{5,4},{6,7},{7,6},{8,9},{9,8},{10,11... | collective-permute-start | bytes 786440 | tf_op jit(solution)/shard_map/ppermute | solution.py:341
  158.9 4.2 %collective-permute-start.9 = (bf16[32,32,128]{2,1,0:T(8,128)(2,1)S(1)}, bf16[32,32,128]{2,1,0:T(8,128)(2,1)S(1)}, u32[]{:S(2)}, u32[]{:S(2)}) collective-permute-start(bf16[32,32,128]{2,1,0:T(8,128)(2,1)S(1)} %bitcast.14), channel_id=1, source_target_pairs={{0,1},{1,0},{2,3},{3,2},{4,5},{5,4},{6,7},{7,6},{8,9},{9,8},{10,11... | collective-permute-start | bytes 786440 | tf_op jit(solution)/shard_map/ppermute | solution.py:341
  186.1 4.4 %collective-permute-start.10 = (bf16[32,32,128]{2,1,0:T(8,128)(2,1)S(1)}, bf16[32,32,128]{2,1,0:T(8,128)(2,1)S(1)}, u32[]{:S(2)}, u32[]{:S(2)}) collective-permute-start(bf16[32,32,128]{2,1,0:T(8,128)(2,1)S(1)} %bitcast.28), channel_id=1, source_target_pairs={{0,1},{1,0},{2,3},{3,2},{4,5},{5,4},{6,7},{7,6},{8,9},{9,8},{10,11... | collective-permute-start | bytes 786440 | tf_op jit(solution)/shard_map/ppermute | solution.py:341

commit v5 on v4

--- a/solution.py
+++ b/solution.py
@@ -32,8 +32,10 @@
 
 PARAMS = pltpu.CompilerParams(vmem_limit_bytes=24 * 2**20)
 ACC = (NROW * BLK + 1, W, B)
-LISTS = 4
-TAB, TC, LA, LALL = range(LISTS)
+LISTS = 6
+V0AB, V0C, TAB, TC, LA, LBC = range(LISTS)
+CHUNK = 3
+ORDER = (1, 2, 3, 2, 1)
 HALF = NCOL // 2
 
 
@@ -56,19 +58,85 @@
     return jnp.where(side == 0, own_ref[at], other_ref[at])
 
 
-def apply_list(lst, which, pair, tiles_ref, acc):
+def lists_kernel(codes, lst):
+    def step(t, counts):
+        code = codes[0, t]
+        row = code & 63
+        half = shr(code, 6) & 7
+        side = shr(code, 9) & 1
+        blk = shr(code, 10)
+        out = row & (BLK - 1)
+        head = t + row * NT + side * 2**19
+        early = out < PRT
+        target = blk < TGT
+        low = blk < PRT
+        member = (
+            (BLK, early),
+            (BLK, out >= PRT),
+            (TGT, target & early),
+            (TGT, target & (out >= PRT)),
+            (PRT, low & (out < TGT)),
+            (PRT, low & (out >= TGT)),
+        )
+        entry = {n: head + (half * n + blk) * 8192 for n in (BLK, TGT, PRT)}
+        for k in range(LISTS):
+            lst[k, counts[k]] = entry[member[k][0]]
+        return tuple(
+            counts[k] + jnp.where(member[k][1], jnp.int32(1), jnp.int32(0)) for k in range(LISTS)
+        )
+
+    counts = lax.fori_loop(0, NT, step, (jnp.int32(0),) * LISTS)
+    for k in range(LISTS):
+        for u in range(UNROLL):
+            lst[k, counts[k] + u] = NROW * BLK * NT
+        lst[LISTS, k] = shr(counts[k] + UNROLL - 1, 3)
+
+
+def make_lists(codes):
+    return pl.pallas_call(
+        lists_kernel,
+        out_shape=jax.ShapeDtypeStruct((LISTS + 1, LST), jnp.int32),
+        in_specs=[smem()],
+        out_specs=smem(),
+        name="lists",
+    )(codes)
+
+
+def apply_group(lst, which, g, pair, tiles_ref, acc):
+    rows, done = [], []
+    for u in range(UNROLL):
+        e = lst[which, g * UNROLL + u]
+        v = picked(shr(e, 19), *pair, shr(e, 13) & 63)
+        rows.append(shr(e, 7) & 63)
+        done.append(product(v, tiles_ref[e & 127]))
+    for r, d in zip(rows, done):
+        acc[r] += d
+
+
+def apply_list(lst, which, pair, tiles_ref, acc, low=0, most=NT):
     def group(g, _):
-        rows, done = [], []
-        for u in range(UNROLL):
-            e = lst[which, g * UNROLL + u]
-            v = picked(shr(e, 19), *pair, shr(e, 13) & 63)
-            rows.append(shr(e, 7) & 63)
-            done.append(product(v, tiles_ref[e & 127]))
-        for r, d in zip(rows, done):
-            acc[r] += d
+        apply_group(lst, which, g, pair, tiles_ref, acc)
         return 0
 
-    lax.fori_loop(0, lst[LISTS, which], group, 0)
+    groups = lst[LISTS, which]
+    lax.fori_loop(low, jnp.minimum(groups, low + most), group, 0)
+
+
+def late_start(slab, step):
+    used = jnp.int32(step)
+    for active in ORDER[:step]:
+        used = used - jnp.where(slab[0] == active, jnp.int32(1), jnp.int32(0))
+    return used * CHUNK
+
+
+def step_work(lst, slab, which, pair, first_pair, tiles_ref, acc, step):
+    @pl.when(slab[0] == ORDER[step])
+    def _():
+        apply_list(lst, which, pair, tiles_ref, acc)
+
+    @pl.when(slab[0] != ORDER[step])
+    def _():
+        apply_list(lst, V0C, first_pair, tiles_ref, acc, late_start(slab, step), CHUNK)
 
 
 def write_down(acc, row, hot_ref, msg_ref):
@@ -92,7 +160,7 @@
 MESSAGE = jax.ShapeDtypeStruct((2 * NROW, TGT, W, B), BF)
 
 
-def first_kernel(codes, row_index, own_ref, other_ref, hot_ref, tiles_hbm, acc, tiles_ref, lst, msg_ref, sems):
+def first_kernel(lst, row, own_ref, other_ref, hot_ref, tiles_hbm, acc, tiles_ref, msg_ref, sems):
     def load(g):
         at = pl.ds(pl.multiple_of(g * UNROLL, UNROLL), UNROLL)
         return pltpu.make_async_copy(tiles_hbm.at[at], tiles_ref.at[at], sems.at[g])
@@ -101,130 +169,101 @@
         load(g).start()
         return 0
 
+    def wait(g, _):
+        load(g).wait()
+        return 0
+
     lax.fori_loop(0, NT // UNROLL, start, 0)
     acc[...] = jnp.zeros(ACC, F32)
 
-    def group(g, counts):
-        rows, done = [], []
-        load(g).wait()
+    def group(g, loaded):
+        need = loaded
         for u in range(UNROLL):
-            t = g * UNROLL + u
-            code = codes[0, t]
-            row = code & 63
-            half = shr(code, 6) & 7
-            side = shr(code, 9) & 1
-            blk = shr(code, 10)
-            v = picked(side, own_ref, other_ref, half * BLK + blk)
-            rows.append(row)
-            done.append(product(v, tiles_ref[t]))
-            out = row & (BLK - 1)
-            head = t + row * NT + side * 2**19
-            narrow = head + (half * TGT + blk) * 8192
-            wide = head + (half * PRT + blk) * 8192
-            target = blk < TGT
-            low = blk < PRT
-            member = (
-                (narrow, target & (out < PRT)),
-                (narrow, target & (out >= PRT)),
-                (wide, low & (out < TGT)),
-                (wide, low),
-            )
-            for k in range(LISTS):
-                lst[k, counts[k]] = member[k][0]
-            counts = tuple(
-                counts[k] + jnp.where(member[k][1], jnp.int32(1), jnp.int32(0))
-                for k in range(LISTS)
-            )
-        for r, d in zip(rows, done):
-            acc[r] += d
-        return counts
-
-    counts = lax.fori_loop(0, NT // UNROLL, group, (jnp.int32(0),) * LISTS)
-    for k in range(LISTS):
-        for u in range(UNROLL):
-            lst[k, counts[k] + u] = NROW * BLK * NT
-        lst[LISTS, k] = shr(counts[k] + UNROLL - 1, 3)
-    write_down(acc, row_index, hot_ref, msg_ref)
-
-
-def first_apply(codes, row_index, pair, hots, tiles):
+            need = jnp.maximum(need, shr(lst[V0AB, g * UNROLL + u] & 127, 3) + 1)
+        lax.fori_loop(loaded, need, wait, 0)
+        apply_group(lst, V0AB, g, (own_ref, other_ref), tiles_ref, acc)
+        return need
+
+    loaded = lax.fori_loop(0, lst[LISTS, V0AB], group, jnp.int32(0))
+    write_down(acc, row, hot_ref, msg_ref)
+    lax.fori_loop(loaded, NT // UNROLL, wait, 0)
+
+
+def first_apply(lst, row, pair, hots, tiles):
     return pl.pallas_call(
         first_kernel,
         out_shape=(
             jax.ShapeDtypeStruct(ACC, F32),
             jax.ShapeDtypeStruct(tiles.shape, BF),
-            jax.ShapeDtypeStruct((LISTS + 1, LST), jnp.int32),
             MESSAGE,
         ),
         in_specs=[smem(), smem(), vmem(), vmem(), vmem(), pl.BlockSpec(memory_space=pltpu.HBM)],
-        out_specs=(vmem(), vmem(), smem(), vmem()),
+        out_specs=(vmem(), vmem(), vmem()),
         scratch_shapes=[pltpu.SemaphoreType.DMA((NT // UNROLL,))],
         compiler_params=PARAMS,
         name="first",
-    )(codes, row_index, *pair, hots, pltpu.with_memory_space_constraint(tiles, pltpu.HBM))
-
-
-def down_step_kernel(lst, slab, row, own_ref, other_ref, hot_ref, tiles_ref, acc_in, acc, msg_ref, *, section):
-    @pl.when(slab[0] == section)
-    def _():
-        apply_list(lst, TAB, (own_ref, other_ref), tiles_ref, acc)
-
-    if section < NSLAB - 1:
+    )(lst, row, *pair, hots, pltpu.with_memory_space_constraint(tiles, pltpu.HBM))
+
+
+def down_step_kernel(
+    lst, slab, row, own_ref, other_ref, own0, other0, hot_ref, tiles_ref, acc_in, acc, msg_ref, *, step
+):
+    step_work(lst, slab, TAB, (own_ref, other_ref), (own0, other0), tiles_ref, acc, step)
+    if ORDER[step] < NSLAB - 1:
         write_down(acc, row, hot_ref, msg_ref)
     else:
         write_up(acc, msg_ref)
 
 
-def down_step(lst, slab, row, pair, hots, tiles, acc, section):
-    return pl.pallas_call(
-        functools.partial(down_step_kernel, section=section),
+def down_step(lst, slab, row, pair, first_pair, hots, tiles, acc, step):
+    return pl.pallas_call(
+        functools.partial(down_step_kernel, step=step),
         out_shape=(jax.ShapeDtypeStruct(ACC, F32), MESSAGE),
-        in_specs=[smem(), smem(), smem()] + [vmem()] * 5,
+        in_specs=[smem(), smem(), smem()] + [vmem()] * 7,
+        out_specs=(vmem(), vmem()),
+        input_output_aliases={9: 0},
+        compiler_params=PARAMS,
+        name="down_step",
+    )(lst, slab, row, *pair, *first_pair, hots, tiles, acc)
+
+
+def up_step_kernel(
+    lst, slab, own_ref, other_ref, own0, other0, tiles_ref, acc_in, acc, msg_ref, *, step
+):
+    step_work(lst, slab, LA, (own_ref, other_ref), (own0, other0), tiles_ref, acc, step)
+    write_up(acc, msg_ref)
+
+
+def up_step(lst, slab, pair, first_pair, tiles, acc, step):
+    return pl.pallas_call(
+        functools.partial(up_step_kernel, step=step),
+        out_shape=(jax.ShapeDtypeStruct(ACC, F32), MESSAGE),
+        in_specs=[smem(), smem()] + [vmem()] * 6,
         out_specs=(vmem(), vmem()),
         input_output_aliases={7: 0},
         compiler_params=PARAMS,
-        name="down_step",
-    )(lst, slab, row, *pair, hots, tiles, acc)
-
-
-def up_step_kernel(lst, slab, own_ref, other_ref, tiles_ref, acc_in, msg_ref, acc, *, section):
-    for r in range(NROW):
-        for b in range(TGT):
-            acc[r * BLK + b] = acc_in[r * BLK + b]
-
-    @pl.when(slab[0] == section)
-    def _():
-        apply_list(lst, LA, (own_ref, other_ref), tiles_ref, acc)
-
-    write_up(acc, msg_ref)
-
-
-def up_step(lst, slab, pair, tiles, acc, section):
-    return pl.pallas_call(
-        functools.partial(up_step_kernel, section=section),
-        out_shape=MESSAGE,
-        in_specs=[smem(), smem()] + [vmem()] * 4,
-        out_specs=vmem(),
-        scratch_shapes=[pltpu.VMEM(ACC, F32)],
-        compiler_params=PARAMS,
         name="up_step",
-    )(lst, slab, *pair, tiles, acc)
-
-
-def last_kernel(lst, slab, tiles_ref, *refs):
+    )(lst, slab, *pair, *first_pair, tiles, acc)
+
+
+def last_kernel(lst, slab, tiles_ref, own0, other0, *refs):
     gathered, acc, msg_ref = refs[:12], refs[13], refs[14]
     for k, s in enumerate((1, 2, 3, 2, 1, 0)):
+        pair = gathered[2 * k], gathered[2 * k + 1]
+
         @pl.when(slab[0] == s)
-        def _(k=k):
-            pair = gathered[2 * k], gathered[2 * k + 1]
-            apply_list(lst, TC if k < NSLAB - 1 else LALL, pair, tiles_ref, acc)
-
+        def _(k=k, s=s, pair=pair):
+            if s == 0:
+                apply_list(lst, LA, pair, tiles_ref, acc)
+            apply_list(lst, TC if k < NSLAB - 1 else LBC, pair, tiles_ref, acc)
+
+    apply_list(lst, V0C, (own0, other0), tiles_ref, acc, late_start(slab, len(ORDER)))
     for r in range(NROW):
         for b in range(BLK):
             msg_ref[r, b] = acc[r * BLK + b].astype(BF)
 
 
-def last_apply(lst, slab, tiles, pairs, acc):
+def last_apply(lst, slab, tiles, first_pair, pairs, acc):
     flat = [ref for pair in pairs for ref in pair]
     return pl.pallas_call(
         last_kernel,
@@ -232,12 +271,12 @@
             jax.ShapeDtypeStruct(ACC, F32),
             jax.ShapeDtypeStruct((NROW, BLK, W, B), BF),
         ),
-        in_specs=[smem(), smem()] + [vmem()] * 14,
+        in_specs=[smem(), smem()] + [vmem()] * 16,
         out_specs=(vmem(), vmem()),
-        input_output_aliases={15: 0},
+        input_output_aliases={17: 0},
         compiler_params=PARAMS,
         name="last",
-    )(lst, slab, tiles, *flat, acc)[1]
+    )(lst, slab, tiles, *first_pair, *flat, acc)[1]
 
 
 def split(x):
@@ -377,22 +416,22 @@
     hots = (partner[None, :, None] == maps_next[:, None, :]).astype(BF)
     hot_next = (maps_next[0][:, None] == partner[None, :]).astype(BF)
 
-    pair = gather(copies)
-    pair, hots, hot_next, coef_next, rhs_target, codes = lax.optimization_barrier(
-        (pair, hots, hot_next, coef_next, rhs_target, codes)
+    start = gather(copies)
+    start, hots, hot_next, coef_next, rhs_target, lst = lax.optimization_barrier(
+        (start, hots, hot_next, coef_next, rhs_target, make_lists(codes))
     )
-    acc, tiles, lst, msg = first_apply(codes, row, pair, hots, front_tiles[0])
+    acc, tiles, msg = first_apply(lst, row, start, hots, front_tiles[0])
     pairs = []
-    for s in range(1, NSLAB):
-        rcv = exchange(msg, s - 1)
+    for step, active in enumerate(ORDER[: NSLAB - 1]):
+        rcv = exchange(msg, active - 1)
         pairs.append(gather(combine(down_kernel, rcv, (rhs_target, interface_coef), TGT, "down")))
-        acc, msg = down_step(lst, slab, row, pairs[-1], hots, tiles, acc, s)
+        acc, msg = down_step(lst, slab, row, pairs[-1], start, hots, tiles, acc, step)
     for s in range(NSLAB - 2, -1, -1):
         rcv = exchange(msg, s)
         pairs.append(gather(combine(up_kernel, rcv, (coef_next, hot_next), PRT, "up")))
         if s > 0:
-            msg = up_step(lst, slab, pairs[-1], tiles, acc, s)
-    msg = last_apply(lst, slab, tiles, pairs, acc)
+            acc, msg = up_step(lst, slab, pairs[-1], start, tiles, acc, 2 * NSLAB - 3 - s)
+    msg = last_apply(lst, slab, tiles, start, pairs, acc)
     return finish(section_blocks, lax.all_to_all(msg, "row", 0, 0, tiled=True))
 
 

time: 204 us -> 208 us (1.020)
  waiting for transfers between devices: 18.2 us -> 12 us
  Pallas kernels: 16.1 us -> 21.7 us
  blocking collectives: 131 us -> 135 us
    pallas_call x5 -> x6, Pallas kernels: 3.95 us -> 11.9 us  [the longest x1 5.51 us: make_lists(): pl.pallas_call(lists_kernel, out_shape=jax.ShapeDtypeStruct((LISTS + 1, L...]
    ppermute x4, waiting for transfers between devices: 6.04 us -> 0.01 us  [from_next(): return lax.ppermute(value, ('slab', 'row'), pairs)]
    pallas_call x1, Pallas kernels: 6.96 us -> 4.37 us  [first_apply(): pl.pallas_call(first_kernel, out_shape=(jax.ShapeDtypeStruct(ACC, F32), j...]
  transfers between devices with their start and end apart: 12 -> 12, of which waited for: 9 -> 8; matrix products, arithmetic and copies ran while one was open for 1% -> 1% of each run, Pallas kernels for 0% -> 3%
where the time goes in v5:
time: 208 us
  blocking collectives  135 us (65%)
  starting transfers between devices  33.3 us (16%)
  Pallas kernels  21.7 us (10%)
  waiting for transfers between devices  12 us (6%)
  other arithmetic  3.11 us (1%)
    all_to_all x6, blocking collectives, gather(): lax.all_to_all(copies, 'col', 0, 0, tiled=True, axis_index_groups=Z_GROUPS)  70.6 us
    all_to_all x6, blocking collectives, exchange(): lax.all_to_all(message, ('slab', 'row'), 0, 0, tiled=True, axis_index_gro...  55.8 us
    ppermute x7, starting transfers between devices, gather(): return (own, lax.ppermute(own, 'col', [(c, c ^ 1) for c in range(NCOL)]))  19.1 us
    all_to_all x1, starting transfers between devices, gather(): lax.all_to_all(copies, 'col', 0, 0, tiled=True, axis_index_groups=Z_GROUPS)  9 us
    all_to_all x1, blocking collectives, body(): return finish(section_blocks, lax.all_to_all(msg, 'row', 0, 0, tiled=True))  8.87 us
    ppermute x7, waiting for transfers between devices, gather(): return (own, lax.ppermute(own, 'col', [(c, c ^ 1) for c in range(NCOL)]))  7.47 us
    pallas_call x1, Pallas kernels, make_lists(): pl.pallas_call(lists_kernel, out_shape=jax.ShapeDtypeStruct((LISTS + 1, L...  5.51 us
    ppermute x4, starting transfers between devices, from_next(): return lax.ppermute(value, ('slab', 'row'), pairs)  5.14 us
  transfers between devices with their start and end apart: 12, of which 8 were waited for; matrix products, arithmetic and copies ran while one was open for 1% of the time, Pallas kernels for 3%

profile of v5, /device:TPU:1, one launch (start us, length us, event | category | flops | bytes accessed | tf_op | source)
XLA Modules:
  0.0 208.0 jit_solution(17355048552881042296)
XLA Ops:
  2.4 9.0 %all-to-all-start = ((bf16[8,8,32,128]{3,2,1,0:T(8,128)(2,1)}), bf16[8,8,32,128]{3,2,1,0:T(8,128)(2,1)S(1)}, u32[]{:S(2)}, u32[]{:S(2)}) async-start(bf16[8,8,32,128]{3,2,1,0:T(8,128)(2,1)} %get-tuple-element.28), calls=%async_computation | async-start | bytes 1048576 | tf_op jit(solution)/shard_map/all_to_all | solution.py:378
  19.2 5.5 %lists.1.lst = s32[7,136]{1,0:T(8,128)} custom-call(s32[1,128]{1,0:T(1,128)} %fusion.3.codes), custom_call_target="tpu_custom_call" | custom-call | tf_op jit(solution)/shard_map/lists/pallas_call | solution.py:96
  24.8 4.6 %all-to-all-done = bf16[8,8,32,128]{3,2,1,0:T(8,128)(2,1)S(1)} async-done(((bf16[8,8,32,128]{3,2,1,0:T(8,128)(2,1)}), bf16[8,8,32,128]{3,2,1,0:T(8,128)(2,1)S(1)}, u32[]{:S(2)}, u32[]{:S(2)}) %all-to-all-start) | async-done | bytes 524320 | tf_op jit(solution)/shard_map/all_to_all | solution.py:378
  32.1 4.4 %first.1 = (f32[33,32,128]{2,1,0:T(8,128)S(1)}, bf16[128,128,128]{2,1,0:T(8,128)(2,1)S(1)}, bf16[8,2,32,128]{3,2,1,0:T(8,128)(2,1)S(1)}) custom-call(s32[7,136]{1,0:T(8,128)S(1)} %copy-done, s32[1]{0:T(128)} %bitcast.3.row, bf16[64,32,128]{2,1,0:T(8,128)(2,1)S(1)} %bitcast.12, bf16[64,32,128]{2,1,0:T(8,128)(2,1)S(1)} %collective-permute-done.other_ref.other0, ...), custom_call_target="tpu_custom_call" | custom-call | tf_op jit(solution)/shard_map/first/pallas_call | solution.py:193
  36.5 10.4 %all_to_all.70.rcv_ref = bf16[8,2,32,128]{3,2,1,0:T(8,128)(2,1)S(1)} all-to-all(bf16[8,2,32,128]{3,2,1,0:T(8,128)(2,1)S(1)} %get-tuple-element.35), channel_id=1, replica_groups={{0,16,32,48,64,80,96,112},{128,144,160,176,192,208,224,240},{1,17,33,49..., dimensions={0} | all-to-all | bytes 262144 | tf_op jit(solution)/shard_map/all_to_all | solution.py:388
  46.9 13.8 %all_to_all.71 = bf16[8,2,32,128]{3,2,1,0:T(8,128)(2,1)S(1)} all-to-all(bf16[8,2,32,128]{3,2,1,0:T(8,128)(2,1)S(1)} %down.3), channel_id=1, replica_groups={{0,2,4,6,8,10,12,14},{1,3,5,7,9,11,13,15},{16,18,20,22,24,26,28,30},{17..., dimensions={0} | all-to-all | bytes 262144 | tf_op jit(solution)/shard_map/all_to_all | solution.py:378
  60.7 3.4 %collective-permute-start.5 = (bf16[16,32,128]{2,1,0:T(8,128)(2,1)S(1)}, bf16[16,32,128]{2,1,0:T(8,128)(2,1)S(1)}, u32[]{:S(2)}, u32[]{:S(2)}) collective-permute-start(bf16[16,32,128]{2,1,0:T(8,128)(2,1)S(1)} %bitcast.25), channel_id=1, source_target_pairs={{0,1},{1,0},{2,3},{3,2},{4,5},{5,4},{6,7},{7,6},{8,9},{9,8},{10,11... | collective-permute-start | bytes 393224 | tf_op jit(solution)/shard_map/ppermute | solution.py:380
  66.9 10.9 %all_to_all.72.rcv_ref = bf16[8,2,32,128]{3,2,1,0:T(8,128)(2,1)S(1)} all-to-all(bf16[8,2,32,128]{3,2,1,0:T(8,128)(2,1)S(1)} %get-tuple-element.38), channel_id=1, replica_groups={{64,80,96,112,128,144,160,176},{192,208,224,240,0,16,32,48},{65,81,97,1..., dimensions={0} | all-to-all | bytes 262144 | tf_op jit(solution)/shard_map/all_to_all | solution.py:388
  77.8 10.3 %all_to_all.73 = bf16[8,2,32,128]{3,2,1,0:T(8,128)(2,1)S(1)} all-to-all(bf16[8,2,32,128]{3,2,1,0:T(8,128)(2,1)S(1)} %down.4), channel_id=1, replica_groups={{0,2,4,6,8,10,12,14},{1,3,5,7,9,11,13,15},{16,18,20,22,24,26,28,30},{17..., dimensions={0} | all-to-all | bytes 262144 | tf_op jit(solution)/shard_map/all_to_all | solution.py:378
  88.1 2.8 %collective-permute-start.6 = (bf16[16,32,128]{2,1,0:T(8,128)(2,1)S(1)}, bf16[16,32,128]{2,1,0:T(8,128)(2,1)S(1)}, u32[]{:S(2)}, u32[]{:S(2)}) collective-permute-start(bf16[16,32,128]{2,1,0:T(8,128)(2,1)S(1)} %bitcast.28), channel_id=1, source_target_pairs={{0,1},{1,0},{2,3},{3,2},{4,5},{5,4},{6,7},{7,6},{8,9},{9,8},{10,11... | collective-permute-start | bytes 393224 | tf_op jit(solution)/shard_map/ppermute | solution.py:380
  93.7 8.5 %all_to_all.74.rcv_ref = bf16[8,2,32,128]{3,2,1,0:T(8,128)(2,1)S(1)} all-to-all(bf16[8,2,32,128]{3,2,1,0:T(8,128)(2,1)S(1)} %get-tuple-element.40), channel_id=1, replica_groups={{128,144,160,176,192,208,224,240},{0,16,32,48,64,80,96,112},{129,145,16..., dimensions={0} | all-to-all | bytes 262144 | tf_op jit(solution)/shard_map/all_to_all | solution.py:388
  102.2 10.3 %all_to_all.75 = bf16[8,2,32,128]{3,2,1,0:T(8,128)(2,1)S(1)} all-to-all(bf16[8,2,32,128]{3,2,1,0:T(8,128)(2,1)S(1)} %down.5), channel_id=1, replica_groups={{0,2,4,6,8,10,12,14},{1,3,5,7,9,11,13,15},{16,18,20,22,24,26,28,30},{17..., dimensions={0} | all-to-all | bytes 262144 | tf_op jit(solution)/shard_map/all_to_all | solution.py:378
  112.5 2.9 %collective-permute-start.7 = (bf16[16,32,128]{2,1,0:T(8,128)(2,1)S(1)}, bf16[16,32,128]{2,1,0:T(8,128)(2,1)S(1)}, u32[]{:S(2)}, u32[]{:S(2)}) collective-permute-start(bf16[16,32,128]{2,1,0:T(8,128)(2,1)S(1)} %bitcast.31), channel_id=1, source_target_pairs={{0,1},{1,0},{2,3},{3,2},{4,5},{5,4},{6,7},{7,6},{8,9},{9,8},{10,11... | collective-permute-start | bytes 393224 | tf_op jit(solution)/shard_map/ppermute | solution.py:380
  118.0 7.8 %all_to_all.76.rcv_ref = bf16[8,2,32,128]{3,2,1,0:T(8,128)(2,1)S(1)} all-to-all(bf16[8,2,32,128]{3,2,1,0:T(8,128)(2,1)S(1)} %get-tuple-element.42), channel_id=1, replica_groups={{128,144,160,176,192,208,224,240},{0,16,32,48,64,80,96,112},{129,145,16..., dimensions={0} | all-to-all | bytes 262144 | tf_op jit(solution)/shard_map/all_to_all | solution.py:388
  126.0 12.3 %all_to_all.77 = bf16[8,4,32,128]{3,2,1,0:T(8,128)(2,1)S(1)} all-to-all(bf16[8,4,32,128]{3,2,1,0:T(8,128)(2,1)S(1)} %up.3), channel_id=1, replica_groups={{0,2,4,6,8,10,12,14},{1,3,5,7,9,11,13,15},{16,18,20,22,24,26,28,30},{17..., dimensions={0} | all-to-all | bytes 524288 | tf_op jit(solution)/shard_map/all_to_all | solution.py:378
  138.2 3.0 %collective-permute-start.8 = (bf16[32,32,128]{2,1,0:T(8,128)(2,1)S(1)}, bf16[32,32,128]{2,1,0:T(8,128)(2,1)S(1)}, u32[]{:S(2)}, u32[]{:S(2)}) collective-permute-start(bf16[32,32,128]{2,1,0:T(8,128)(2,1)S(1)} %bitcast.19), channel_id=1, source_target_pairs={{0,1},{1,0},{2,3},{3,2},{4,5},{5,4},{6,7},{7,6},{8,9},{9,8},{10,11... | collective-permute-start | bytes 786440 | tf_op jit(solution)/shard_map/ppermute | solution.py:380
  143.1 8.8 %all_to_all.78.rcv_ref = bf16[8,2,32,128]{3,2,1,0:T(8,128)(2,1)S(1)} all-to-all(bf16[8,2,32,128]{3,2,1,0:T(8,128)(2,1)S(1)} %get-tuple-element.46), channel_id=1, replica_groups={{64,80,96,112,128,144,160,176},{192,208,224,240,0,16,32,48},{65,81,97,1..., dimensions={0} | all-to-all | bytes 262144 | tf_op jit(solution)/shard_map/all_to_all | solution.py:388
  152.1 12.0 %all_to_all.79 = bf16[8,4,32,128]{3,2,1,0:T(8,128)(2,1)S(1)} all-to-all(bf16[8,4,32,128]{3,2,1,0:T(8,128)(2,1)S(1)} %up.4), channel_id=1, replica_groups={{0,2,4,6,8,10,12,14},{1,3,5,7,9,11,13,15},{16,18,20,22,24,26,28,30},{17..., dimensions={0} | all-to-all | bytes 524288 | tf_op jit(solution)/shard_map/all_to_all | solution.py:378
  164.1 3.2 %collective-permute-start.9 = (bf16[32,32,128]{2,1,0:T(8,128)(2,1)S(1)}, bf16[32,32,128]{2,1,0:T(8,128)(2,1)S(1)}, u32[]{:S(2)}, u32[]{:S(2)}) collective-permute-start(bf16[32,32,128]{2,1,0:T(8,128)(2,1)S(1)} %bitcast.22), channel_id=1, source_target_pairs={{0,1},{1,0},{2,3},{3,2},{4,5},{5,4},{6,7},{7,6},{8,9},{9,8},{10,11... | collective-permute-start | bytes 786440 | tf_op jit(solution)/shard_map/ppermute | solution.py:380
  169.2 9.3 %all_to_all.80.rcv_ref = bf16[8,2,32,128]{3,2,1,0:T(8,128)(2,1)S(1)} all-to-all(bf16[8,2,32,128]{3,2,1,0:T(8,128)(2,1)S(1)} %get-tuple-element.48), channel_id=1, replica_groups={{0,16,32,48,64,80,96,112},{128,144,160,176,192,208,224,240},{1,17,33,49..., dimensions={0} | all-to-all | bytes 262144 | tf_op jit(solution)/shard_map/all_to_all | solution.py:388
  178.7 11.9 %all_to_all.81 = bf16[8,4,32,128]{3,2,1,0:T(8,128)(2,1)S(1)} all-to-all(bf16[8,4,32,128]{3,2,1,0:T(8,128)(2,1)S(1)} %up.5), channel_id=1, replica_groups={{0,2,4,6,8,10,12,14},{1,3,5,7,9,11,13,15},{16,18,20,22,24,26,28,30},{17..., dimensions={0} | all-to-all | bytes 524288 | tf_op jit(solution)/shard_map/all_to_all | solution.py:378
  190.6 3.3 %collective-permute-start.10 = (bf16[32,32,128]{2,1,0:T(8,128)(2,1)S(1)}, bf16[32,32,128]{2,1,0:T(8,128)(2,1)S(1)}, u32[]{:S(2)}, u32[]{:S(2)}) collective-permute-start(bf16[32,32,128]{2,1,0:T(8,128)(2,1)S(1)} %bitcast.34), channel_id=1, source_target_pairs={{0,1},{1,0},{2,3},{3,2},{4,5},{5,4},{6,7},{7,6},{8,9},{9,8},{10,11... | collective-permute-start | bytes 786440 | tf_op jit(solution)/shard_map/ppermute | solution.py:380
  195.1 3.3 %last.1 = (f32[33,32,128]{2,1,0:T(8,128)S(1)}, bf16[4,8,32,128]{3,2,1,0:T(8,128)(2,1)S(1)}) custom-call(s32[7,136]{1,0:T(8,128)S(1)} %copy-done.1, s32[1]{0:T(128)} %bitcast.slab, bf16[128,128,128]{2,1,0:T(8,128)(2,1)S(1)} %get-tuple-element.34.tiles_ref, bf16[64,32,128]{2,1,0:T(8,128)(2,1)S(1)} %bitcast.18, ...), custom_call_target="tpu_custom_call", output_to_operand_aliasing={{0}: (17, {})} | custom-call | tf_op jit(solution)/shard_map/last/pallas_call | solution.py:268
  198.4 8.9 %all_to_all.82.parts_ref = bf16[4,8,32,128]{3,2,1,0:T(8,128)(2,1)S(1)} all-to-all(bf16[4,8,32,128]{3,2,1,0:T(8,128)(2,1)S(1)} %get-tuple-element.50), channel_id=1, replica_groups=mesh['slab'=4,'row'=4,'col'=16] {'row'}, dimensions={0} | all-to-all | bytes 524288 | tf_op jit(solution)/shard_map/all_to_all | solution.py:435
  (45 shorter events, 26.4 us)
Async XLA Ops:
  0.7 0.9 copy-start.2
  2.4 27.0 %all-to-all-start = ((bf16[8,8,32,128]{3,2,1,0:T(8,128)(2,1)}), bf16[8,8,32,128]{3,2,1,0:T(8,128)(2,1)S(1)}, u32[]{:S(2)}, u32[]{:S(2)}) async-start(bf16[8,8,32,128]{3,2,1,0:T(8,128)(2,1)} %get-tuple-element.28), calls=%async_computation | async-start | bytes 1048576 | tf_op jit(solution)/shard_map/all_to_all | solution.py:378
  11.4 35.5 %copy-start.3 = (f32[1,256]{1,0:T(1,128)S(1)}, f32[1,256]{1,0:T(1,128)}, u32[]{:S(2)}) copy-start(f32[1,256]{1,0:T(1,128)} %coef_ref.5) | copy-start | bytes 3076
  12.1 17.8 %collective-permute-start.4 = (f32[1,256]{1,0:T(1,128)S(1)}, f32[1,256]{1,0:T(1,128)S(1)}, u32[]{:S(2)}, u32[]{:S(2)}) collective-permute-start(f32[1,256]{1,0:T(1,128)S(1)} %convert_element_type.17), channel_id=1, source_target_pairs={{112,0},{64,16},{80,32},{96,48},{176,64},{128,80},{144,96},{160,11... | collective-permute-start | bytes 3080 | tf_op jit(solution)/shard_map/ppermute | solution.py:397
  13.4 16.5 %collective-permute-start.3 = (f32[1,256]{1,0:T(1,128)S(1)}, f32[1,256]{1,0:T(1,128)S(1)}, u32[]{:S(2)}, u32[]{:S(2)}) collective-permute-start(f32[1,256]{1,0:T(1,128)S(1)} %convert_element_type.17), channel_id=1, source_target_pairs={{96,0},{112,16},{64,32},{80,48},{160,64},{176,80},{128,96},{144,11... | collective-permute-start | bytes 3080 | tf_op jit(solution)/shard_map/ppermute | solution.py:397
  14.7 15.2 %collective-permute-start.2 = (f32[1,256]{1,0:T(1,128)S(1)}, f32[1,256]{1,0:T(1,128)S(1)}, u32[]{:S(2)}, u32[]{:S(2)}) collective-permute-start(f32[1,256]{1,0:T(1,128)S(1)} %convert_element_type.17), channel_id=1, source_target_pairs={{80,0},{96,16},{112,32},{64,48},{144,64},{160,80},{176,96},{128,11... | collective-permute-start | bytes 3080 | tf_op jit(solution)/shard_map/ppermute | solution.py:397
  16.7 8.1 %collective-permute-start.1 = (f32[2,256]{1,0:T(2,128)S(1)}, f32[2,256]{1,0:T(2,128)S(1)}, u32[]{:S(2)}, u32[]{:S(2)}) collective-permute-start(f32[2,256]{1,0:T(2,128)S(1)} %pad_maximum_fusion), channel_id=1, source_target_pairs={{64,0},{80,16},{96,32},{112,48},{128,64},{144,80},{160,96},{176,11... | collective-permute-start | bytes 6152 | tf_op jit(solution)/shard_map/ppermute | solution.py:397
  29.4 2.0 collective-permute-start
  29.9 35.2 %copy-start.1 = (s32[7,136]{1,0:T(8,128)S(1)}, s32[7,136]{1,0:T(8,128)}, u32[]{:S(2)}) copy-start(s32[7,136]{1,0:T(8,128)} %lists.1.lst) | copy-start | bytes 11428
  31.4 0.7 copy-start
  60.7 4.4 %collective-permute-start.5 = (bf16[16,32,128]{2,1,0:T(8,128)(2,1)S(1)}, bf16[16,32,128]{2,1,0:T(8,128)(2,1)S(1)}, u32[]{:S(2)}, u32[]{:S(2)}) collective-permute-start(bf16[16,32,128]{2,1,0:T(8,128)(2,1)S(1)} %bitcast.25), channel_id=1, source_target_pairs={{0,1},{1,0},{2,3},{3,2},{4,5},{5,4},{6,7},{7,6},{8,9},{9,8},{10,11... | collective-permute-start | bytes 393224 | tf_op jit(solution)/shard_map/ppermute | solution.py:380
  88.1 3.8 %collective-permute-start.6 = (bf16[16,32,128]{2,1,0:T(8,128)(2,1)S(1)}, bf16[16,32,128]{2,1,0:T(8,128)(2,1)S(1)}, u32[]{:S(2)}, u32[]{:S(2)}) collective-permute-start(bf16[16,32,128]{2,1,0:T(8,128)(2,1)S(1)} %bitcast.28), channel_id=1, source_target_pairs={{0,1},{1,0},{2,3},{3,2},{4,5},{5,4},{6,7},{7,6},{8,9},{9,8},{10,11... | collective-permute-start | bytes 393224 | tf_op jit(solution)/shard_map/ppermute | solution.py:380
  112.5 3.9 %collective-permute-start.7 = (bf16[16,32,128]{2,1,0:T(8,128)(2,1)S(1)}, bf16[16,32,128]{2,1,0:T(8,128)(2,1)S(1)}, u32[]{:S(2)}, u32[]{:S(2)}) collective-permute-start(bf16[16,32,128]{2,1,0:T(8,128)(2,1)S(1)} %bitcast.31), channel_id=1, source_target_pairs={{0,1},{1,0},{2,3},{3,2},{4,5},{5,4},{6,7},{7,6},{8,9},{9,8},{10,11... | collective-permute-start | bytes 393224 | tf_op jit(solution)/shard_map/ppermute | solution.py:380
  138.2 4.1 %collective-permute-start.8 = (bf16[32,32,128]{2,1,0:T(8,128)(2,1)S(1)}, bf16[32,32,128]{2,1,0:T(8,128)(2,1)S(1)}, u32[]{:S(2)}, u32[]{:S(2)}) collective-permute-start(bf16[32,32,128]{2,1,0:T(8,128)(2,1)S(1)} %bitcast.19), channel_id=1, source_target_pairs={{0,1},{1,0},{2,3},{3,2},{4,5},{5,4},{6,7},{7,6},{8,9},{9,8},{10,11... | collective-permute-start | bytes 786440 | tf_op jit(solution)/shard_map/ppermute | solution.py:380
  164.1 4.4 %collective-permute-start.9 = (bf16[32,32,128]{2,1,0:T(8,128)(2,1)S(1)}, bf16[32,32,128]{2,1,0:T(8,128)(2,1)S(1)}, u32[]{:S(2)}, u32[]{:S(2)}) collective-permute-start(bf16[32,32,128]{2,1,0:T(8,128)(2,1)S(1)} %bitcast.22), channel_id=1, source_target_pairs={{0,1},{1,0},{2,3},{3,2},{4,5},{5,4},{6,7},{7,6},{8,9},{9,8},{10,11... | collective-permute-start | bytes 786440 | tf_op jit(solution)/shard_map/ppermute | solution.py:380
  190.6 4.5 %collective-permute-start.10 = (bf16[32,32,128]{2,1,0:T(8,128)(2,1)S(1)}, bf16[32,32,128]{2,1,0:T(8,128)(2,1)S(1)}, u32[]{:S(2)}, u32[]{:S(2)}) collective-permute-start(bf16[32,32,128]{2,1,0:T(8,128)(2,1)S(1)} %bitcast.34), channel_id=1, source_target_pairs={{0,1},{1,0},{2,3},{3,2},{4,5},{5,4},{6,7},{7,6},{8,9},{9,8},{10,11... | collective-permute-start | bytes 786440 | tf_op jit(solution)/shard_map/ppermute | solution.py:380

commit v6 on v5

--- a/solution.py
+++ b/solution.py
@@ -43,13 +43,6 @@
     return lax.shift_right_logical(x, jnp.int32(n))
 
 
-def tile_codes(tile_rows, tile_cols, col_index):
-    row = tile_rows - col_index * (NROW * BLK)
-    part = tile_cols // (BLK * NROW)
-    side = (part % 2 != col_index % 2).astype(jnp.int32)
-    return row + 64 * (part // 2) + 512 * side + 1024 * (tile_cols % BLK)
-
-
 def product(v, tile):
     return lax.dot_general(v, tile, (((1,), (1,)), ((), ())), preferred_element_type=F32)
 
@@ -58,15 +51,18 @@
     return jnp.where(side == 0, own_ref[at], other_ref[at])
 
 
-def lists_kernel(codes, lst):
-    def step(t, counts):
-        code = codes[0, t]
-        row = code & 63
-        half = shr(code, 6) & 7
-        side = shr(code, 9) & 1
-        blk = shr(code, 10)
+def lists_kernel(rows, cols, col_index, lst):
+    base = col_index[0] * (NROW * BLK)
+    core = col_index[0] & 1
+
+    def step(t, ends):
+        row = rows[0, t] - base
+        col = cols[0, t]
+        part = shr(col, 5)
+        half = shr(part, 1)
+        blk = col & (BLK - 1)
         out = row & (BLK - 1)
-        head = t + row * NT + side * 2**19
+        head = t + row * NT + ((part & 1) ^ core) * 2**19
         early = out < PRT
         target = blk < TGT
         low = blk < PRT
@@ -80,32 +76,32 @@
         )
         entry = {n: head + (half * n + blk) * 8192 for n in (BLK, TGT, PRT)}
         for k in range(LISTS):
-            lst[k, counts[k]] = entry[member[k][0]]
+            lst[ends[k]] = entry[member[k][0]]
         return tuple(
-            counts[k] + jnp.where(member[k][1], jnp.int32(1), jnp.int32(0)) for k in range(LISTS)
+            ends[k] + jnp.where(member[k][1], jnp.int32(1), jnp.int32(0)) for k in range(LISTS)
         )
 
-    counts = lax.fori_loop(0, NT, step, (jnp.int32(0),) * LISTS)
+    ends = lax.fori_loop(0, NT, step, tuple(jnp.int32(k * LST) for k in range(LISTS)))
     for k in range(LISTS):
         for u in range(UNROLL):
-            lst[k, counts[k] + u] = NROW * BLK * NT
-        lst[LISTS, k] = shr(counts[k] + UNROLL - 1, 3)
-
-
-def make_lists(codes):
+            lst[ends[k] + u] = NROW * BLK * NT
+        lst[LISTS * LST + k] = shr(ends[k] - k * LST + UNROLL - 1, 3)
+
+
+def make_lists(tile_rows, tile_cols, col_index):
     return pl.pallas_call(
         lists_kernel,
-        out_shape=jax.ShapeDtypeStruct((LISTS + 1, LST), jnp.int32),
-        in_specs=[smem()],
+        out_shape=jax.ShapeDtypeStruct((LISTS * LST + UNROLL,), jnp.int32),
+        in_specs=[smem(), smem(), smem()],
         out_specs=smem(),
         name="lists",
-    )(codes)
+    )(tile_rows, tile_cols, col_index)
 
 
 def apply_group(lst, which, g, pair, tiles_ref, acc):
     rows, done = [], []
     for u in range(UNROLL):
-        e = lst[which, g * UNROLL + u]
+        e = lst[which * LST + g * UNROLL + u]
         v = picked(shr(e, 19), *pair, shr(e, 13) & 63)
         rows.append(shr(e, 7) & 63)
         done.append(product(v, tiles_ref[e & 127]))
@@ -118,7 +114,7 @@
         apply_group(lst, which, g, pair, tiles_ref, acc)
         return 0
 
-    groups = lst[LISTS, which]
+    groups = lst[LISTS * LST + which]
     lax.fori_loop(low, jnp.minimum(groups, low + most), group, 0)
 
 
@@ -139,28 +135,19 @@
         apply_list(lst, V0C, first_pair, tiles_ref, acc, late_start(slab, step), CHUNK)
 
 
-def write_down(acc, row, hot_ref, msg_ref):
-    for d in range(NROW):
-        r = (row[0] + d) & (NROW - 1)
-        values = jnp.concatenate([acc[r * BLK + b].astype(BF) for b in range(PRT)], axis=1)
-        part = jnp.dot(values, hot_ref[d], preferred_element_type=F32).astype(BF)
-        for b in range(TGT):
-            for s in range(2):
-                msg_ref[s * NROW + r, b] = part[:, b * B : (b + 1) * B]
-
-
-def write_up(acc, msg_ref):
+def write_message(acc, msg_ref):
     for r in range(NROW):
-        for b in range(TGT):
+        for b in range(msg_ref.shape[1]):
             part = acc[r * BLK + b].astype(BF)
             for s in range(2):
                 msg_ref[s * NROW + r, b] = part
 
 
-MESSAGE = jax.ShapeDtypeStruct((2 * NROW, TGT, W, B), BF)
-
-
-def first_kernel(lst, row, own_ref, other_ref, hot_ref, tiles_hbm, acc, tiles_ref, msg_ref, sems):
+def message(blocks):
+    return jax.ShapeDtypeStruct((2 * NROW, blocks, W, B), BF)
+
+
+def first_kernel(lst, own_ref, other_ref, tiles_hbm, acc, tiles_ref, msg_ref, sems):
     def load(g):
         at = pl.ds(pl.multiple_of(g * UNROLL, UNROLL), UNROLL)
         return pltpu.make_async_copy(tiles_hbm.at[at], tiles_ref.at[at], sems.at[g])
@@ -179,70 +166,49 @@
     def group(g, loaded):
         need = loaded
         for u in range(UNROLL):
-            need = jnp.maximum(need, shr(lst[V0AB, g * UNROLL + u] & 127, 3) + 1)
+            need = jnp.maximum(need, shr(lst[V0AB * LST + g * UNROLL + u] & 127, 3) + 1)
         lax.fori_loop(loaded, need, wait, 0)
         apply_group(lst, V0AB, g, (own_ref, other_ref), tiles_ref, acc)
         return need
 
-    loaded = lax.fori_loop(0, lst[LISTS, V0AB], group, jnp.int32(0))
-    write_down(acc, row, hot_ref, msg_ref)
+    loaded = lax.fori_loop(0, lst[LISTS * LST + V0AB], group, jnp.int32(0))
+    write_message(acc, msg_ref)
     lax.fori_loop(loaded, NT // UNROLL, wait, 0)
 
 
-def first_apply(lst, row, pair, hots, tiles):
+def first_apply(lst, pair, tiles):
     return pl.pallas_call(
         first_kernel,
         out_shape=(
             jax.ShapeDtypeStruct(ACC, F32),
             jax.ShapeDtypeStruct(tiles.shape, BF),
-            MESSAGE,
+            message(PRT),
         ),
-        in_specs=[smem(), smem(), vmem(), vmem(), vmem(), pl.BlockSpec(memory_space=pltpu.HBM)],
+        in_specs=[smem(), vmem(), vmem(), pl.BlockSpec(memory_space=pltpu.HBM)],
         out_specs=(vmem(), vmem(), vmem()),
         scratch_shapes=[pltpu.SemaphoreType.DMA((NT // UNROLL,))],
         compiler_params=PARAMS,
         name="first",
-    )(lst, row, *pair, hots, pltpu.with_memory_space_constraint(tiles, pltpu.HBM))
-
-
-def down_step_kernel(
-    lst, slab, row, own_ref, other_ref, own0, other0, hot_ref, tiles_ref, acc_in, acc, msg_ref, *, step
+    )(lst, *pair, pltpu.with_memory_space_constraint(tiles, pltpu.HBM))
+
+
+def step_kernel(
+    lst, slab, own_ref, other_ref, own0, other0, tiles_ref, acc_in, acc, msg_ref, *, which, step
 ):
-    step_work(lst, slab, TAB, (own_ref, other_ref), (own0, other0), tiles_ref, acc, step)
-    if ORDER[step] < NSLAB - 1:
-        write_down(acc, row, hot_ref, msg_ref)
-    else:
-        write_up(acc, msg_ref)
-
-
-def down_step(lst, slab, row, pair, first_pair, hots, tiles, acc, step):
-    return pl.pallas_call(
-        functools.partial(down_step_kernel, step=step),
-        out_shape=(jax.ShapeDtypeStruct(ACC, F32), MESSAGE),
-        in_specs=[smem(), smem(), smem()] + [vmem()] * 7,
-        out_specs=(vmem(), vmem()),
-        input_output_aliases={9: 0},
-        compiler_params=PARAMS,
-        name="down_step",
-    )(lst, slab, row, *pair, *first_pair, hots, tiles, acc)
-
-
-def up_step_kernel(
-    lst, slab, own_ref, other_ref, own0, other0, tiles_ref, acc_in, acc, msg_ref, *, step
-):
-    step_work(lst, slab, LA, (own_ref, other_ref), (own0, other0), tiles_ref, acc, step)
-    write_up(acc, msg_ref)
-
-
-def up_step(lst, slab, pair, first_pair, tiles, acc, step):
-    return pl.pallas_call(
-        functools.partial(up_step_kernel, step=step),
-        out_shape=(jax.ShapeDtypeStruct(ACC, F32), MESSAGE),
+    step_work(lst, slab, which, (own_ref, other_ref), (own0, other0), tiles_ref, acc, step)
+    write_message(acc, msg_ref)
+
+
+def step_apply(lst, slab, which, pair, first_pair, tiles, acc, step):
+    blocks = PRT if ORDER[step + 1 :] and ORDER[step] < ORDER[step + 1] else TGT
+    return pl.pallas_call(
+        functools.partial(step_kernel, which=which, step=step),
+        out_shape=(jax.ShapeDtypeStruct(ACC, F32), message(blocks)),
         in_specs=[smem(), smem()] + [vmem()] * 6,
         out_specs=(vmem(), vmem()),
         input_output_aliases={7: 0},
         compiler_params=PARAMS,
-        name="up_step",
+        name="step",
     )(lst, slab, *pair, *first_pair, tiles, acc)
 
 
@@ -292,10 +258,12 @@
     return part
 
 
-def down_kernel(rcv_ref, rhs_ref, coef_ref, out_ref):
+def down_kernel(rcv_ref, rhs_ref, coef_ref, hot_ref, out_ref):
+    values = jnp.concatenate([split(row_total(rcv_ref, 0, b)) for b in range(PRT)], axis=1)
+    total = jnp.dot(values, hot_ref[...], preferred_element_type=F32)
+    chosen = (total[:W] + total[W:]) * coef_ref[...]
     for b in range(TGT):
-        pulled = row_total(rcv_ref, 0, b) * coef_ref[:, b * B : (b + 1) * B]
-        value = (rhs_ref[b] - pulled).astype(BF)
+        value = (rhs_ref[b] - chosen[:, b * B : (b + 1) * B]).astype(BF)
         for z in range(HALF):
             out_ref[z, b] = value
 
@@ -388,49 +356,35 @@
     return lax.all_to_all(message, ("slab", "row"), 0, 0, tiled=True, axis_index_groups=groups)
 
 
-def from_next(value, turn):
-    pairs = [
-        ((s + 1) * NROW + (r + turn) % NROW, s * NROW + r)
-        for s in range(NSLAB - 1)
-        for r in range(NROW)
-    ]
-    return lax.ppermute(value, ("slab", "row"), pairs)
-
-
 def body(right_sides, front_tiles, tile_rows, tile_cols, section_blocks, plane_map, interface_coef):
-    slab = lax.axis_index("slab").astype(jnp.int32)
-    row = lax.axis_index("row").astype(jnp.int32)
-    col = lax.axis_index("col").astype(jnp.int32)
-    slab = slab.reshape(1)
-    row = row.reshape(1)
-    codes = tile_codes(tile_rows, tile_cols, col)
-    map_own = plane_map.astype(F32)
-    pack_next = from_next(jnp.concatenate([map_own, interface_coef], axis=0), 0)
+    slab = lax.axis_index("slab").astype(jnp.int32).reshape(1)
+    col = lax.axis_index("col").astype(jnp.int32).reshape(1)
+    pack = jnp.concatenate([plane_map.astype(F32), interface_coef], axis=0)
+    pack_next = lax.ppermute(pack, "slab", [(s + 1, s) for s in range(NSLAB - 1)])
+    map_next = pack_next[0].astype(jnp.int32)
     coef_next = pack_next[1:2]
-    maps_next = jnp.concatenate(
-        [pack_next[0:1]] + [from_next(map_own, d) for d in range(1, NROW)], axis=0
-    ).astype(jnp.int32)
+    partner = jnp.arange(PRT * B, dtype=jnp.int32)
+    hot_own = (partner[:, None] == plane_map[0][None, :]).astype(BF)
+    hot_next = (map_next[:, None] == partner[None, :]).astype(BF)
 
     copies, rhs_target = prepare(right_sides, section_blocks, slab)
-    partner = jnp.arange(PRT * B, dtype=jnp.int32)
-    hots = (partner[None, :, None] == maps_next[:, None, :]).astype(BF)
-    hot_next = (maps_next[0][:, None] == partner[None, :]).astype(BF)
-
     start = gather(copies)
-    start, hots, hot_next, coef_next, rhs_target, lst = lax.optimization_barrier(
-        (start, hots, hot_next, coef_next, rhs_target, make_lists(codes))
+    lst = make_lists(tile_rows, tile_cols, col)
+    start, hot_own, hot_next, coef_next, rhs_target, lst = lax.optimization_barrier(
+        (start, hot_own, hot_next, coef_next, rhs_target, lst)
     )
-    acc, tiles, msg = first_apply(lst, row, start, hots, front_tiles[0])
+    acc, tiles, msg = first_apply(lst, start, front_tiles[0])
     pairs = []
-    for step, active in enumerate(ORDER[: NSLAB - 1]):
-        rcv = exchange(msg, active - 1)
-        pairs.append(gather(combine(down_kernel, rcv, (rhs_target, interface_coef), TGT, "down")))
-        acc, msg = down_step(lst, slab, row, pairs[-1], start, hots, tiles, acc, step)
-    for s in range(NSLAB - 2, -1, -1):
-        rcv = exchange(msg, s)
+    for step in range(NSLAB - 1):
+        rcv = exchange(msg, step)
+        value = combine(down_kernel, rcv, (rhs_target, interface_coef, hot_own), TGT, "down")
+        pairs.append(gather(value))
+        acc, msg = step_apply(lst, slab, TAB, pairs[-1], start, tiles, acc, step)
+    for step in range(NSLAB - 1, 2 * NSLAB - 2):
+        rcv = exchange(msg, 2 * NSLAB - 3 - step)
         pairs.append(gather(combine(up_kernel, rcv, (coef_next, hot_next), PRT, "up")))
-        if s > 0:
-            acc, msg = up_step(lst, slab, pairs[-1], start, tiles, acc, 2 * NSLAB - 3 - s)
+        if step < len(ORDER):
+            acc, msg = step_apply(lst, slab, LA, pairs[-1], start, tiles, acc, step)
     msg = last_apply(lst, slab, tiles, start, pairs, acc)
     return finish(section_blocks, lax.all_to_all(msg, "row", 0, 0, tiled=True))
 

time: 208 us -> 208 us (level)
  waiting for transfers between devices: 12 us -> 21.8 us
  starting transfers between devices: 33.3 us -> 26.5 us
    all_to_all x1, waiting for transfers between devices: 4.57 us -> 15.3 us  [gather(): lax.all_to_all(copies, 'col', 0, 0, tiled=True, axis_index_groups=Z_GROUPS)]
    ppermute x4 -> x1, starting transfers between devices: 5.14 us -> 1.28 us  [body(): lax.ppermute(pack, 'slab', [(s + 1, s) for s in range(NSLAB - 1)])]
    all_to_all x6, blocking collectives: 70.6 us -> 67.2 us  [gather(): lax.all_to_all(copies, 'col', 0, 0, tiled=True, axis_index_groups=Z_GROUPS)]
    all_to_all x6, blocking collectives: 55.8 us -> 58.9 us  [exchange(): lax.all_to_all(message, ('slab', 'row'), 0, 0, tiled=True, axis_index_gro...]
    ppermute x7, starting transfers between devices: 19.1 us -> 16.2 us  [gather(): return (own, lax.ppermute(own, 'col', [(c, c ^ 1) for c in range(NCOL)]))]
  transfers between devices with their start and end apart: 12 -> 9, of which waited for: 8 -> 7; matrix products, arithmetic and copies ran while one was open for 1% -> 1% of each run, Pallas kernels for 3% -> 2%
where the time goes in v6:
time: 208 us; the launch traced here: 207 us
  blocking collectives  135 us (65%)
  starting transfers between devices  26.5 us (13%)
  waiting for transfers between devices  21.8 us (10%)
  Pallas kernels  19.7 us (9%)
  other arithmetic  2.23 us (1%)
    all_to_all x6, blocking collectives, gather(): lax.all_to_all(copies, 'col', 0, 0, tiled=True, axis_index_groups=Z_GROUPS)  67.2 us
    all_to_all x6, blocking collectives, exchange(): lax.all_to_all(message, ('slab', 'row'), 0, 0, tiled=True, axis_index_gro...  58.9 us
    ppermute x7, starting transfers between devices, gather(): return (own, lax.ppermute(own, 'col', [(c, c ^ 1) for c in range(NCOL)]))  16.2 us
    all_to_all x1, waiting for transfers between devices, gather(): lax.all_to_all(copies, 'col', 0, 0, tiled=True, axis_index_groups=Z_GROUPS)  15.3 us
    all_to_all x1, starting transfers between devices, gather(): lax.all_to_all(copies, 'col', 0, 0, tiled=True, axis_index_groups=Z_GROUPS)  9 us
    all_to_all x1, blocking collectives, body(): return finish(section_blocks, lax.all_to_all(msg, 'row', 0, 0, tiled=True))  8.69 us
    ppermute x7, waiting for transfers between devices, gather(): return (own, lax.ppermute(own, 'col', [(c, c ^ 1) for c in range(NCOL)]))  6.45 us
    pallas_call x5, Pallas kernels, step_apply(): pl.pallas_call(functools.partial(step_kernel, which=which, step=step), ou...  5.46 us
  transfers between devices with their start and end apart: 9, of which 7 were waited for; matrix products, arithmetic and copies ran while one was open for 1% of the time, Pallas kernels for 2%

profile of v6, /device:TPU:1, one launch (start us, length us, event | category | flops | bytes accessed | tf_op | source)
XLA Modules:
  0.0 207.3 jit_solution(242344184634106040)
XLA Ops:
  2.4 9.0 %all-to-all-start = ((bf16[8,8,32,128]{3,2,1,0:T(8,128)(2,1)}), bf16[8,8,32,128]{3,2,1,0:T(8,128)(2,1)S(1)}, u32[]{:S(2)}, u32[]{:S(2)}) async-start(bf16[8,8,32,128]{3,2,1,0:T(8,128)(2,1)} %get-tuple-element.28), calls=%async_computation | async-start | bytes 1048576 | tf_op jit(solution)/shard_map/all_to_all | solution.py:346
  14.1 15.3 %all-to-all-done = bf16[8,8,32,128]{3,2,1,0:T(8,128)(2,1)S(1)} async-done(((bf16[8,8,32,128]{3,2,1,0:T(8,128)(2,1)}), bf16[8,8,32,128]{3,2,1,0:T(8,128)(2,1)S(1)}, u32[]{:S(2)}, u32[]{:S(2)}) %all-to-all-start) | async-done | bytes 524320 | tf_op jit(solution)/shard_map/all_to_all | solution.py:346
  30.6 4.7 %lists.1.lst = s32[824]{0:T(1024)} custom-call(s32[1,128]{1,0:T(1,128)} %rows.1, s32[1,128]{1,0:T(1,128)} %cols.1, s32[1]{0:T(128)} %bitcast.4.col_index), custom_call_target="tpu_custom_call" | custom-call | tf_op jit(solution)/shard_map/lists/pallas_call | solution.py:92
  36.2 3.9 %first.1 = (f32[33,32,128]{2,1,0:T(8,128)S(1)}, bf16[128,128,128]{2,1,0:T(8,128)(2,1)S(1)}, bf16[8,4,32,128]{3,2,1,0:T(8,128)(2,1)S(1)}) custom-call(s32[824]{0:T(1024)S(1)} %copy-done, bf16[64,32,128]{2,1,0:T(8,128)(2,1)S(1)} %bitcast.13, bf16[64,32,128]{2,1,0:T(8,128)(2,1)S(1)} %collective-permute-done.other_ref.other0, bf16[128,128,128]{2,1,0:T(8,128)(2,1)} %bitcast.37), custom_call_target="tpu_custom_call" | custom-call | tf_op jit(solution)/shard_map/first/pallas_call | solution.py:180
  40.1 12.2 %all_to_all.70.rcv_ref = bf16[8,4,32,128]{3,2,1,0:T(8,128)(2,1)S(1)} all-to-all(bf16[8,4,32,128]{3,2,1,0:T(8,128)(2,1)S(1)} %get-tuple-element.34), channel_id=1, replica_groups={{0,16,32,48,64,80,96,112},{128,144,160,176,192,208,224,240},{1,17,33,49..., dimensions={0} | all-to-all | bytes 524288 | tf_op jit(solution)/shard_map/all_to_all | solution.py:356
  52.5 10.1 %all_to_all.71 = bf16[8,2,32,128]{3,2,1,0:T(8,128)(2,1)S(1)} all-to-all(bf16[8,2,32,128]{3,2,1,0:T(8,128)(2,1)S(1)} %down.3), channel_id=1, replica_groups={{0,2,4,6,8,10,12,14},{1,3,5,7,9,11,13,15},{16,18,20,22,24,26,28,30},{17..., dimensions={0} | all-to-all | bytes 262144 | tf_op jit(solution)/shard_map/all_to_all | solution.py:346
  62.6 2.3 %collective-permute-start.2 = (bf16[16,32,128]{2,1,0:T(8,128)(2,1)S(1)}, bf16[16,32,128]{2,1,0:T(8,128)(2,1)S(1)}, u32[]{:S(2)}, u32[]{:S(2)}) collective-permute-start(bf16[16,32,128]{2,1,0:T(8,128)(2,1)S(1)} %bitcast.26), channel_id=1, source_target_pairs={{0,1},{1,0},{2,3},{3,2},{4,5},{5,4},{6,7},{7,6},{8,9},{9,8},{10,11... | collective-permute-start | bytes 393224 | tf_op jit(solution)/shard_map/ppermute | solution.py:348
  67.3 10.4 %all_to_all.72.rcv_ref = bf16[8,4,32,128]{3,2,1,0:T(8,128)(2,1)S(1)} all-to-all(bf16[8,4,32,128]{3,2,1,0:T(8,128)(2,1)S(1)} %get-tuple-element.38), channel_id=1, replica_groups={{64,80,96,112,128,144,160,176},{192,208,224,240,0,16,32,48},{65,81,97,1..., dimensions={0} | all-to-all | bytes 524288 | tf_op jit(solution)/shard_map/all_to_all | solution.py:356
  77.9 10.1 %all_to_all.73 = bf16[8,2,32,128]{3,2,1,0:T(8,128)(2,1)S(1)} all-to-all(bf16[8,2,32,128]{3,2,1,0:T(8,128)(2,1)S(1)} %down.4), channel_id=1, replica_groups={{0,2,4,6,8,10,12,14},{1,3,5,7,9,11,13,15},{16,18,20,22,24,26,28,30},{17..., dimensions={0} | all-to-all | bytes 262144 | tf_op jit(solution)/shard_map/all_to_all | solution.py:346
  88.1 2.3 %collective-permute-start.3 = (bf16[16,32,128]{2,1,0:T(8,128)(2,1)S(1)}, bf16[16,32,128]{2,1,0:T(8,128)(2,1)S(1)}, u32[]{:S(2)}, u32[]{:S(2)}) collective-permute-start(bf16[16,32,128]{2,1,0:T(8,128)(2,1)S(1)} %bitcast.29), channel_id=1, source_target_pairs={{0,1},{1,0},{2,3},{3,2},{4,5},{5,4},{6,7},{7,6},{8,9},{9,8},{10,11... | collective-permute-start | bytes 393224 | tf_op jit(solution)/shard_map/ppermute | solution.py:348
  92.7 9.8 %all_to_all.74.rcv_ref = bf16[8,4,32,128]{3,2,1,0:T(8,128)(2,1)S(1)} all-to-all(bf16[8,4,32,128]{3,2,1,0:T(8,128)(2,1)S(1)} %get-tuple-element.40), channel_id=1, replica_groups={{128,144,160,176,192,208,224,240},{0,16,32,48,64,80,96,112},{129,145,16..., dimensions={0} | all-to-all | bytes 524288 | tf_op jit(solution)/shard_map/all_to_all | solution.py:356
  102.8 10.1 %all_to_all.75 = bf16[8,2,32,128]{3,2,1,0:T(8,128)(2,1)S(1)} all-to-all(bf16[8,2,32,128]{3,2,1,0:T(8,128)(2,1)S(1)} %down.5), channel_id=1, replica_groups={{0,2,4,6,8,10,12,14},{1,3,5,7,9,11,13,15},{16,18,20,22,24,26,28,30},{17..., dimensions={0} | all-to-all | bytes 262144 | tf_op jit(solution)/shard_map/all_to_all | solution.py:346
  112.9 2.3 %collective-permute-start.4 = (bf16[16,32,128]{2,1,0:T(8,128)(2,1)S(1)}, bf16[16,32,128]{2,1,0:T(8,128)(2,1)S(1)}, u32[]{:S(2)}, u32[]{:S(2)}) collective-permute-start(bf16[16,32,128]{2,1,0:T(8,128)(2,1)S(1)} %bitcast.32), channel_id=1, source_target_pairs={{0,1},{1,0},{2,3},{3,2},{4,5},{5,4},{6,7},{7,6},{8,9},{9,8},{10,11... | collective-permute-start | bytes 393224 | tf_op jit(solution)/shard_map/ppermute | solution.py:348
  117.6 7.8 %all_to_all.76.rcv_ref = bf16[8,2,32,128]{3,2,1,0:T(8,128)(2,1)S(1)} all-to-all(bf16[8,2,32,128]{3,2,1,0:T(8,128)(2,1)S(1)} %get-tuple-element.42), channel_id=1, replica_groups={{128,144,160,176,192,208,224,240},{0,16,32,48,64,80,96,112},{129,145,16..., dimensions={0} | all-to-all | bytes 262144 | tf_op jit(solution)/shard_map/all_to_all | solution.py:356
  125.6 12.6 %all_to_all.77 = bf16[8,4,32,128]{3,2,1,0:T(8,128)(2,1)S(1)} all-to-all(bf16[8,4,32,128]{3,2,1,0:T(8,128)(2,1)S(1)} %up.3), channel_id=1, replica_groups={{0,2,4,6,8,10,12,14},{1,3,5,7,9,11,13,15},{16,18,20,22,24,26,28,30},{17..., dimensions={0} | all-to-all | bytes 524288 | tf_op jit(solution)/shard_map/all_to_all | solution.py:346
  138.2 2.6 %collective-permute-start.5 = (bf16[32,32,128]{2,1,0:T(8,128)(2,1)S(1)}, bf16[32,32,128]{2,1,0:T(8,128)(2,1)S(1)}, u32[]{:S(2)}, u32[]{:S(2)}) collective-permute-start(bf16[32,32,128]{2,1,0:T(8,128)(2,1)S(1)} %bitcast.20), channel_id=1, source_target_pairs={{0,1},{1,0},{2,3},{3,2},{4,5},{5,4},{6,7},{7,6},{8,9},{9,8},{10,11... | collective-permute-start | bytes 786440 | tf_op jit(solution)/shard_map/ppermute | solution.py:348
  142.6 9.0 %all_to_all.78.rcv_ref = bf16[8,2,32,128]{3,2,1,0:T(8,128)(2,1)S(1)} all-to-all(bf16[8,2,32,128]{3,2,1,0:T(8,128)(2,1)S(1)} %get-tuple-element.46), channel_id=1, replica_groups={{64,80,96,112,128,144,160,176},{192,208,224,240,0,16,32,48},{65,81,97,1..., dimensions={0} | all-to-all | bytes 262144 | tf_op jit(solution)/shard_map/all_to_all | solution.py:356
  151.8 12.2 %all_to_all.79 = bf16[8,4,32,128]{3,2,1,0:T(8,128)(2,1)S(1)} all-to-all(bf16[8,4,32,128]{3,2,1,0:T(8,128)(2,1)S(1)} %up.4), channel_id=1, replica_groups={{0,2,4,6,8,10,12,14},{1,3,5,7,9,11,13,15},{16,18,20,22,24,26,28,30},{17..., dimensions={0} | all-to-all | bytes 524288 | tf_op jit(solution)/shard_map/all_to_all | solution.py:346
  164.0 3.0 %collective-permute-start.6 = (bf16[32,32,128]{2,1,0:T(8,128)(2,1)S(1)}, bf16[32,32,128]{2,1,0:T(8,128)(2,1)S(1)}, u32[]{:S(2)}, u32[]{:S(2)}) collective-permute-start(bf16[32,32,128]{2,1,0:T(8,128)(2,1)S(1)} %bitcast.23), channel_id=1, source_target_pairs={{0,1},{1,0},{2,3},{3,2},{4,5},{5,4},{6,7},{7,6},{8,9},{9,8},{10,11... | collective-permute-start | bytes 786440 | tf_op jit(solution)/shard_map/ppermute | solution.py:348
  168.8 9.6 %all_to_all.80.rcv_ref = bf16[8,2,32,128]{3,2,1,0:T(8,128)(2,1)S(1)} all-to-all(bf16[8,2,32,128]{3,2,1,0:T(8,128)(2,1)S(1)} %get-tuple-element.48), channel_id=1, replica_groups={{0,16,32,48,64,80,96,112},{128,144,160,176,192,208,224,240},{1,17,33,49..., dimensions={0} | all-to-all | bytes 262144 | tf_op jit(solution)/shard_map/all_to_all | solution.py:356
  178.6 12.0 %all_to_all.81 = bf16[8,4,32,128]{3,2,1,0:T(8,128)(2,1)S(1)} all-to-all(bf16[8,4,32,128]{3,2,1,0:T(8,128)(2,1)S(1)} %up.5), channel_id=1, replica_groups={{0,2,4,6,8,10,12,14},{1,3,5,7,9,11,13,15},{16,18,20,22,24,26,28,30},{17..., dimensions={0} | all-to-all | bytes 524288 | tf_op jit(solution)/shard_map/all_to_all | solution.py:346
  190.5 3.3 %collective-permute-start.7 = (bf16[32,32,128]{2,1,0:T(8,128)(2,1)S(1)}, bf16[32,32,128]{2,1,0:T(8,128)(2,1)S(1)}, u32[]{:S(2)}, u32[]{:S(2)}) collective-permute-start(bf16[32,32,128]{2,1,0:T(8,128)(2,1)S(1)} %bitcast.35), channel_id=1, source_target_pairs={{0,1},{1,0},{2,3},{3,2},{4,5},{5,4},{6,7},{7,6},{8,9},{9,8},{10,11... | collective-permute-start | bytes 786440 | tf_op jit(solution)/shard_map/ppermute | solution.py:348
  195.0 3.0 %last.1 = (f32[33,32,128]{2,1,0:T(8,128)S(1)}, bf16[4,8,32,128]{3,2,1,0:T(8,128)(2,1)S(1)}) custom-call(s32[824]{0:T(1024)S(1)} %copy-done.1, s32[1]{0:T(128)} %bitcast.slab, bf16[128,128,128]{2,1,0:T(8,128)(2,1)S(1)} %get-tuple-element.33.tiles_ref, bf16[64,32,128]{2,1,0:T(8,128)(2,1)S(1)} %bitcast.19, ...), custom_call_target="tpu_custom_call", output_to_operand_aliasing={{0}: (17, {})} | custom-call | tf_op jit(solution)/shard_map/last/pallas_call | solution.py:234
  198.0 8.7 %all_to_all.82.parts_ref = bf16[4,8,32,128]{3,2,1,0:T(8,128)(2,1)S(1)} all-to-all(bf16[4,8,32,128]{3,2,1,0:T(8,128)(2,1)S(1)} %get-tuple-element.50), channel_id=1, replica_groups=mesh['slab'=4,'row'=4,'col'=16] {'row'}, dimensions={0} | all-to-all | bytes 524288 | tf_op jit(solution)/shard_map/all_to_all | solution.py:389
  (36 shorter events, 20.1 us)
Async XLA Ops:
  0.0 52.3 %copy-start.3 = (f32[1,256]{1,0:T(1,128)S(1)}, f32[1,256]{1,0:T(1,128)}, u32[]{:S(2)}) copy-start(f32[1,256]{1,0:T(1,128)} %coef_ref.5) | copy-start | bytes 3076
  0.7 0.9 copy-start.2
  2.4 27.0 %all-to-all-start = ((bf16[8,8,32,128]{3,2,1,0:T(8,128)(2,1)}), bf16[8,8,32,128]{3,2,1,0:T(8,128)(2,1)S(1)}, u32[]{:S(2)}, u32[]{:S(2)}) async-start(bf16[8,8,32,128]{3,2,1,0:T(8,128)(2,1)} %get-tuple-element.28), calls=%async_computation | async-start | bytes 1048576 | tf_op jit(solution)/shard_map/all_to_all | solution.py:346
  12.8 22.6 %collective-permute-start.1 = (f32[2,256]{1,0:T(2,128)S(1)}, f32[2,256]{1,0:T(2,128)S(1)}, u32[]{:S(2)}, u32[]{:S(2)}) collective-permute-start(f32[2,256]{1,0:T(2,128)S(1)} %pad_maximum_fusion), channel_id=1, source_target_pairs={{64,0},{128,64},{192,128},{65,1},{129,65},{193,129},{66,2},{130,66... | collective-permute-start | bytes 6152 | tf_op jit(solution)/shard_map/ppermute | solution.py:363
  29.4 6.1 %collective-permute-start = (bf16[64,32,128]{2,1,0:T(8,128)(2,1)S(1)}, bf16[64,32,128]{2,1,0:T(8,128)(2,1)S(1)}, u32[]{:S(2)}, u32[]{:S(2)}) collective-permute-start(bf16[64,32,128]{2,1,0:T(8,128)(2,1)S(1)} %bitcast.12), channel_id=1, source_target_pairs={{0,1},{1,0},{2,3},{3,2},{4,5},{5,4},{6,7},{7,6},{8,9},{9,8},{10,11... | collective-permute-start | bytes 1572872 | tf_op jit(solution)/shard_map/ppermute | solution.py:348
  35.5 0.7 copy-start
  52.3 39.0 %copy-start.1 = (s32[824]{0:T(1024)S(1)}, s32[824]{0:T(1024)}, u32[]{:S(2)}) copy-start(s32[824]{0:T(1024)} %lists.1.lst) | copy-start | bytes 9892
  62.6 3.3 %collective-permute-start.2 = (bf16[16,32,128]{2,1,0:T(8,128)(2,1)S(1)}, bf16[16,32,128]{2,1,0:T(8,128)(2,1)S(1)}, u32[]{:S(2)}, u32[]{:S(2)}) collective-permute-start(bf16[16,32,128]{2,1,0:T(8,128)(2,1)S(1)} %bitcast.26), channel_id=1, source_target_pairs={{0,1},{1,0},{2,3},{3,2},{4,5},{5,4},{6,7},{7,6},{8,9},{9,8},{10,11... | collective-permute-start | bytes 393224 | tf_op jit(solution)/shard_map/ppermute | solution.py:348
  88.1 3.3 %collective-permute-start.3 = (bf16[16,32,128]{2,1,0:T(8,128)(2,1)S(1)}, bf16[16,32,128]{2,1,0:T(8,128)(2,1)S(1)}, u32[]{:S(2)}, u32[]{:S(2)}) collective-permute-start(bf16[16,32,128]{2,1,0:T(8,128)(2,1)S(1)} %bitcast.29), channel_id=1, source_target_pairs={{0,1},{1,0},{2,3},{3,2},{4,5},{5,4},{6,7},{7,6},{8,9},{9,8},{10,11... | collective-permute-start | bytes 393224 | tf_op jit(solution)/shard_map/ppermute | solution.py:348
  112.9 3.3 %collective-permute-start.4 = (bf16[16,32,128]{2,1,0:T(8,128)(2,1)S(1)}, bf16[16,32,128]{2,1,0:T(8,128)(2,1)S(1)}, u32[]{:S(2)}, u32[]{:S(2)}) collective-permute-start(bf16[16,32,128]{2,1,0:T(8,128)(2,1)S(1)} %bitcast.32), channel_id=1, source_target_pairs={{0,1},{1,0},{2,3},{3,2},{4,5},{5,4},{6,7},{7,6},{8,9},{9,8},{10,11... | collective-permute-start | bytes 393224 | tf_op jit(solution)/shard_map/ppermute | solution.py:348
  138.2 3.8 %collective-permute-start.5 = (bf16[32,32,128]{2,1,0:T(8,128)(2,1)S(1)}, bf16[32,32,128]{2,1,0:T(8,128)(2,1)S(1)}, u32[]{:S(2)}, u32[]{:S(2)}) collective-permute-start(bf16[32,32,128]{2,1,0:T(8,128)(2,1)S(1)} %bitcast.20), channel_id=1, source_target_pairs={{0,1},{1,0},{2,3},{3,2},{4,5},{5,4},{6,7},{7,6},{8,9},{9,8},{10,11... | collective-permute-start | bytes 786440 | tf_op jit(solution)/shard_map/ppermute | solution.py:348
  164.0 4.2 %collective-permute-start.6 = (bf16[32,32,128]{2,1,0:T(8,128)(2,1)S(1)}, bf16[32,32,128]{2,1,0:T(8,128)(2,1)S(1)}, u32[]{:S(2)}, u32[]{:S(2)}) collective-permute-start(bf16[32,32,128]{2,1,0:T(8,128)(2,1)S(1)} %bitcast.23), channel_id=1, source_target_pairs={{0,1},{1,0},{2,3},{3,2},{4,5},{5,4},{6,7},{7,6},{8,9},{9,8},{10,11... | collective-permute-start | bytes 786440 | tf_op jit(solution)/shard_map/ppermute | solution.py:348
  190.5 4.4 %collective-permute-start.7 = (bf16[32,32,128]{2,1,0:T(8,128)(2,1)S(1)}, bf16[32,32,128]{2,1,0:T(8,128)(2,1)S(1)}, u32[]{:S(2)}, u32[]{:S(2)}) collective-permute-start(bf16[32,32,128]{2,1,0:T(8,128)(2,1)S(1)} %bitcast.35), channel_id=1, source_target_pairs={{0,1},{1,0},{2,3},{3,2},{4,5},{5,4},{6,7},{7,6},{8,9},{9,8},{10,11... | collective-permute-start | bytes 786440 | tf_op jit(solution)/shard_map/ppermute | solution.py:348

commit v7 on v5

--- a/solution.py
+++ b/solution.py
@@ -17,7 +17,6 @@
 UNROLL = 8
 TGT = 2
 PRT = 4
-LST = NT + UNROLL
 BF = jnp.bfloat16
 F32 = jnp.float32
 
@@ -43,13 +42,6 @@
     return lax.shift_right_logical(x, jnp.int32(n))
 
 
-def tile_codes(tile_rows, tile_cols, col_index):
-    row = tile_rows - col_index * (NROW * BLK)
-    part = tile_cols // (BLK * NROW)
-    side = (part % 2 != col_index % 2).astype(jnp.int32)
-    return row + 64 * (part // 2) + 512 * side + 1024 * (tile_cols % BLK)
-
-
 def product(v, tile):
     return lax.dot_general(v, tile, (((1,), (1,)), ((), ())), preferred_element_type=F32)
 
@@ -58,48 +50,79 @@
     return jnp.where(side == 0, own_ref[at], other_ref[at])
 
 
-def lists_kernel(codes, lst):
-    def step(t, counts):
-        code = codes[0, t]
-        row = code & 63
-        half = shr(code, 6) & 7
-        side = shr(code, 9) & 1
-        blk = shr(code, 10)
-        out = row & (BLK - 1)
-        head = t + row * NT + side * 2**19
-        early = out < PRT
-        target = blk < TGT
-        low = blk < PRT
-        member = (
-            (BLK, early),
-            (BLK, out >= PRT),
-            (TGT, target & early),
-            (TGT, target & (out >= PRT)),
-            (PRT, low & (out < TGT)),
-            (PRT, low & (out >= TGT)),
-        )
-        entry = {n: head + (half * n + blk) * 8192 for n in (BLK, TGT, PRT)}
-        for k in range(LISTS):
-            lst[k, counts[k]] = entry[member[k][0]]
-        return tuple(
-            counts[k] + jnp.where(member[k][1], jnp.int32(1), jnp.int32(0)) for k in range(LISTS)
-        )
-
-    counts = lax.fori_loop(0, NT, step, (jnp.int32(0),) * LISTS)
-    for k in range(LISTS):
-        for u in range(UNROLL):
-            lst[k, counts[k] + u] = NROW * BLK * NT
-        lst[LISTS, k] = shr(counts[k] + UNROLL - 1, 3)
-
-
-def make_lists(codes):
+def lists_kernel(col_index, rows_ref, cols_ref, out_ref):
+    lane = lax.broadcasted_iota(jnp.int32, (1, NT), 1)
+    down = lax.broadcasted_iota(jnp.int32, (NT, NT), 0)
+    across = lax.broadcasted_iota(jnp.int32, (NT, NT), 1)
+    before = jnp.where(down < across, 1.0, 0.0).astype(BF)
+    row = rows_ref[...] - col_index[0] * (NROW * BLK)
+    col = cols_ref[...]
+    part = shr(col, 5)
+    half = shr(part, 1)
+    side = (part & 1) ^ (col_index[0] & 1)
+    blk = col & (BLK - 1)
+    out = row & (BLK - 1)
+    early = out < PRT
+    target = blk < TGT
+    low = blk < PRT
+    member = (
+        (BLK, early),
+        (BLK, out >= PRT),
+        (TGT, target & early),
+        (TGT, target & (out >= PRT)),
+        (PRT, low & (out < TGT)),
+        (PRT, low & (out >= TGT)),
+    )
+    sizes = jnp.zeros((1, NT), jnp.int32)
+    for k, (width, belongs) in enumerate(member):
+        one = jnp.where(belongs, 1.0, 0.0)
+        count = jnp.sum(one, axis=1, keepdims=True).astype(jnp.int32)
+        rank = jnp.dot(
+            jnp.broadcast_to(one, (8, NT)).astype(BF), before, preferred_element_type=F32
+        )[0:1].astype(jnp.int32)
+        rank = jnp.where(belongs, rank, -1)
+        place = jnp.where(jnp.broadcast_to(rank, (NT, NT)) == down, 1.0, 0.0).astype(BF)
+        upper = half * width + blk + side * 64
+        digits = jnp.concatenate(
+            [x.astype(F32) for x in (lane, row, upper, upper, upper, upper, upper, upper)], axis=0
+        ).astype(BF)
+        moved = lax.dot_general(
+            digits, place, (((1,), (1,)), ((), ())), preferred_element_type=F32
+        ).astype(jnp.int32)
+        entry = moved[0:1] + moved[1:2] * NT + moved[2:3] * 8192
+        out_ref[k : k + 1, :] = jnp.where(lane < count, entry, NROW * BLK * NT)
+        sizes = jnp.where(lane == k, shr(count + UNROLL - 1, 3), sizes)
+    out_ref[LISTS : LISTS + 1, :] = sizes
+    out_ref[LISTS + 1 : LISTS + 2, :] = sizes
+
+
+def make_lists(tile_rows, tile_cols, col_index):
     return pl.pallas_call(
         lists_kernel,
-        out_shape=jax.ShapeDtypeStruct((LISTS + 1, LST), jnp.int32),
-        in_specs=[smem()],
-        out_specs=smem(),
+        out_shape=jax.ShapeDtypeStruct((LISTS + 2, NT), jnp.int32),
+        in_specs=[smem(), vmem(), vmem()],
+        out_specs=vmem(),
+        compiler_params=PARAMS,
         name="lists",
-    )(codes)
+    )(col_index, tile_rows, tile_cols)
+
+
+def load_kernel(tiles_hbm, own_ref, tiles_ref, sem):
+    copy = pltpu.make_async_copy(tiles_hbm, tiles_ref, sem)
+    copy.start()
+    copy.wait()
+
+
+def load_tiles(tiles, own):
+    return pl.pallas_call(
+        load_kernel,
+        out_shape=jax.ShapeDtypeStruct(tiles.shape, BF),
+        in_specs=[pl.BlockSpec(memory_space=pltpu.HBM), vmem()],
+        out_specs=vmem(),
+        scratch_shapes=[pltpu.SemaphoreType.DMA],
+        compiler_params=PARAMS,
+        name="load",
+    )(pltpu.with_memory_space_constraint(tiles, pltpu.HBM), own)
 
 
 def apply_group(lst, which, g, pair, tiles_ref, acc):
@@ -160,49 +183,21 @@
 MESSAGE = jax.ShapeDtypeStruct((2 * NROW, TGT, W, B), BF)
 
 
-def first_kernel(lst, row, own_ref, other_ref, hot_ref, tiles_hbm, acc, tiles_ref, msg_ref, sems):
-    def load(g):
-        at = pl.ds(pl.multiple_of(g * UNROLL, UNROLL), UNROLL)
-        return pltpu.make_async_copy(tiles_hbm.at[at], tiles_ref.at[at], sems.at[g])
-
-    def start(g, _):
-        load(g).start()
-        return 0
-
-    def wait(g, _):
-        load(g).wait()
-        return 0
-
-    lax.fori_loop(0, NT // UNROLL, start, 0)
+def first_kernel(lst, row, own_ref, other_ref, hot_ref, tiles_ref, acc, msg_ref):
     acc[...] = jnp.zeros(ACC, F32)
-
-    def group(g, loaded):
-        need = loaded
-        for u in range(UNROLL):
-            need = jnp.maximum(need, shr(lst[V0AB, g * UNROLL + u] & 127, 3) + 1)
-        lax.fori_loop(loaded, need, wait, 0)
-        apply_group(lst, V0AB, g, (own_ref, other_ref), tiles_ref, acc)
-        return need
-
-    loaded = lax.fori_loop(0, lst[LISTS, V0AB], group, jnp.int32(0))
+    apply_list(lst, V0AB, (own_ref, other_ref), tiles_ref, acc)
     write_down(acc, row, hot_ref, msg_ref)
-    lax.fori_loop(loaded, NT // UNROLL, wait, 0)
 
 
 def first_apply(lst, row, pair, hots, tiles):
     return pl.pallas_call(
         first_kernel,
-        out_shape=(
-            jax.ShapeDtypeStruct(ACC, F32),
-            jax.ShapeDtypeStruct(tiles.shape, BF),
-            MESSAGE,
-        ),
-        in_specs=[smem(), smem(), vmem(), vmem(), vmem(), pl.BlockSpec(memory_space=pltpu.HBM)],
-        out_specs=(vmem(), vmem(), vmem()),
-        scratch_shapes=[pltpu.SemaphoreType.DMA((NT // UNROLL,))],
+        out_shape=(jax.ShapeDtypeStruct(ACC, F32), MESSAGE),
+        in_specs=[smem(), smem()] + [vmem()] * 4,
+        out_specs=(vmem(), vmem()),
         compiler_params=PARAMS,
         name="first",
-    )(lst, row, *pair, hots, pltpu.with_memory_space_constraint(tiles, pltpu.HBM))
+    )(lst, row, *pair, hots, tiles)
 
 
 def down_step_kernel(
@@ -403,7 +398,7 @@
     col = lax.axis_index("col").astype(jnp.int32)
     slab = slab.reshape(1)
     row = row.reshape(1)
-    codes = tile_codes(tile_rows, tile_cols, col)
+    col = col.reshape(1)
     map_own = plane_map.astype(F32)
     pack_next = from_next(jnp.concatenate([map_own, interface_coef], axis=0), 0)
     coef_next = pack_next[1:2]
@@ -417,10 +412,12 @@
     hot_next = (maps_next[0][:, None] == partner[None, :]).astype(BF)
 
     start = gather(copies)
-    start, hots, hot_next, coef_next, rhs_target, lst = lax.optimization_barrier(
-        (start, hots, hot_next, coef_next, rhs_target, make_lists(codes))
+    lst = make_lists(tile_rows, tile_cols, col)
+    tiles = load_tiles(front_tiles[0], start[0])
+    start, hots, hot_next, coef_next, rhs_target, lst, tiles = lax.optimization_barrier(
+        (start, hots, hot_next, coef_next, rhs_target, lst, tiles)
     )
-    acc, tiles, msg = first_apply(lst, row, start, hots, front_tiles[0])
+    acc, msg = first_apply(lst, row, start, hots, tiles)
     pairs = []
     for step, active in enumerate(ORDER[: NSLAB - 1]):
         rcv = exchange(msg, active - 1)

time: 208 us -> 203 us (0.976)
  Pallas kernels: 21.7 us -> 16.7 us
  blocking collectives: 135 us -> 131 us
  waiting for transfers between devices: 12 us -> 15.9 us
    all_to_all x1, waiting for transfers between devices: 4.57 us -> 9.43 us  [gather(): lax.all_to_all(copies, 'col', 0, 0, tiled=True, axis_index_groups=Z_GROUPS)]
    pallas_call x2 -> x3, Pallas kernels: 9.88 us -> 6.32 us  [the longest x1 3.5 us: first_apply(): pl.pallas_call(first_kernel, out_shape=(jax.ShapeDtypeStruct(ACC, F32), M...]
    all_to_all x6, blocking collectives: 70.6 us -> 67.8 us  [gather(): lax.all_to_all(copies, 'col', 0, 0, tiled=True, axis_index_groups=Z_GROUPS)]
  transfers between devices with their start and end apart: 12 -> 12, of which waited for: 8 -> 7; matrix products, arithmetic and copies ran while one was open for 1% -> 1% of each run, Pallas kernels for 3% -> 1%
where the time goes in v7:
time: 203 us; the launch traced here: 202 us
  blocking collectives  131 us (65%)
  starting transfers between devices  33.8 us (17%)
  Pallas kernels  16.7 us (8%)
  waiting for transfers between devices  15.9 us (8%)
  local copies, waits for them, and re-layouts  2.22 us (1%)
    all_to_all x6, blocking collectives, gather(): lax.all_to_all(copies, 'col', 0, 0, tiled=True, axis_index_groups=Z_GROUPS)  67.8 us
    all_to_all x6, blocking collectives, exchange(): lax.all_to_all(message, ('slab', 'row'), 0, 0, tiled=True, axis_index_gro...  54 us
    ppermute x7, starting transfers between devices, gather(): return (own, lax.ppermute(own, 'col', [(c, c ^ 1) for c in range(NCOL)]))  19.6 us
    all_to_all x1, waiting for transfers between devices, gather(): lax.all_to_all(copies, 'col', 0, 0, tiled=True, axis_index_groups=Z_GROUPS)  9.43 us
    all_to_all x1, blocking collectives, body(): return finish(section_blocks, lax.all_to_all(msg, 'row', 0, 0, tiled=True))  9.06 us
    all_to_all x1, starting transfers between devices, gather(): lax.all_to_all(copies, 'col', 0, 0, tiled=True, axis_index_groups=Z_GROUPS)  9 us
    ppermute x7, waiting for transfers between devices, gather(): return (own, lax.ppermute(own, 'col', [(c, c ^ 1) for c in range(NCOL)]))  6.45 us
    ppermute x4, starting transfers between devices, from_next(): return lax.ppermute(value, ('slab', 'row'), pairs)  5.16 us
  transfers between devices with their start and end apart: 12, of which 7 were waited for; matrix products, arithmetic and copies ran while one was open for 1% of the time, Pallas kernels for 1%

profile of v7, /device:TPU:1, one launch (start us, length us, event | category | flops | bytes accessed | tf_op | source)
XLA Modules:
  0.0 202.3 jit_solution(5968431209325576475)
XLA Ops:
  2.4 9.0 %all-to-all-start = ((bf16[8,8,32,128]{3,2,1,0:T(8,128)(2,1)}), bf16[8,8,32,128]{3,2,1,0:T(8,128)(2,1)S(1)}, u32[]{:S(2)}, u32[]{:S(2)}) async-start(bf16[8,8,32,128]{3,2,1,0:T(8,128)(2,1)} %get-tuple-element.28), calls=%async_computation | async-start | bytes 1048576 | tf_op jit(solution)/shard_map/all_to_all | solution.py:373
  19.9 9.4 %all-to-all-done = bf16[8,8,32,128]{3,2,1,0:T(8,128)(2,1)S(1)} async-done(((bf16[8,8,32,128]{3,2,1,0:T(8,128)(2,1)}), bf16[8,8,32,128]{3,2,1,0:T(8,128)(2,1)S(1)}, u32[]{:S(2)}, u32[]{:S(2)}) %all-to-all-start) | async-done | bytes 524320 | tf_op jit(solution)/shard_map/all_to_all | solution.py:373
  30.4 2.2 %load.1.tiles_ref = bf16[128,128,128]{2,1,0:T(8,128)(2,1)S(1)} custom-call(bf16[128,128,128]{2,1,0:T(8,128)(2,1)} %bitcast.38, bf16[64,32,128]{2,1,0:T(8,128)(2,1)S(1)} %bitcast.13), custom_call_target="tpu_custom_call" | custom-call | tf_op jit(solution)/shard_map/load/pallas_call | solution.py:117
  32.6 3.5 %first.1 = (f32[33,32,128]{2,1,0:T(8,128)S(1)}, bf16[8,2,32,128]{3,2,1,0:T(8,128)(2,1)S(1)}) custom-call(s32[8,128]{1,0:T(8,128)S(1)} %lists.1.lst, s32[1]{0:T(128)} %bitcast.5.row, bf16[64,32,128]{2,1,0:T(8,128)(2,1)S(1)} %bitcast.14, bf16[64,32,128]{2,1,0:T(8,128)(2,1)S(1)} %collective-permute-done.other_ref.other0, bf16[4,512,256]{2,1,0:T(8,128)(2,1)S(1)} %fusion.hot_ref, ...), custom_call_target="tpu_custom_call" | custom-call | tf_op jit(solution)/shard_map/first/pallas_call | solution.py:193
  36.1 10.0 %all_to_all.70.rcv_ref = bf16[8,2,32,128]{3,2,1,0:T(8,128)(2,1)S(1)} all-to-all(bf16[8,2,32,128]{3,2,1,0:T(8,128)(2,1)S(1)} %get-tuple-element.35), channel_id=1, replica_groups={{0,16,32,48,64,80,96,112},{128,144,160,176,192,208,224,240},{1,17,33,49..., dimensions={0} | all-to-all | bytes 262144 | tf_op jit(solution)/shard_map/all_to_all | solution.py:383
  46.1 10.4 %all_to_all.71 = bf16[8,2,32,128]{3,2,1,0:T(8,128)(2,1)S(1)} all-to-all(bf16[8,2,32,128]{3,2,1,0:T(8,128)(2,1)S(1)} %down.3), channel_id=1, replica_groups={{0,2,4,6,8,10,12,14},{1,3,5,7,9,11,13,15},{16,18,20,22,24,26,28,30},{17..., dimensions={0} | all-to-all | bytes 262144 | tf_op jit(solution)/shard_map/all_to_all | solution.py:373
  56.5 4.5 %collective-permute-start.5 = (bf16[16,32,128]{2,1,0:T(8,128)(2,1)S(1)}, bf16[16,32,128]{2,1,0:T(8,128)(2,1)S(1)}, u32[]{:S(2)}, u32[]{:S(2)}) collective-permute-start(bf16[16,32,128]{2,1,0:T(8,128)(2,1)S(1)} %bitcast.27), channel_id=1, source_target_pairs={{0,1},{1,0},{2,3},{3,2},{4,5},{5,4},{6,7},{7,6},{8,9},{9,8},{10,11... | collective-permute-start | bytes 393224 | tf_op jit(solution)/shard_map/ppermute | solution.py:375
  63.7 8.9 %all_to_all.72.rcv_ref = bf16[8,2,32,128]{3,2,1,0:T(8,128)(2,1)S(1)} all-to-all(bf16[8,2,32,128]{3,2,1,0:T(8,128)(2,1)S(1)} %get-tuple-element.38), channel_id=1, replica_groups={{64,80,96,112,128,144,160,176},{192,208,224,240,0,16,32,48},{65,81,97,1..., dimensions={0} | all-to-all | bytes 262144 | tf_op jit(solution)/shard_map/all_to_all | solution.py:383
  72.7 10.3 %all_to_all.73 = bf16[8,2,32,128]{3,2,1,0:T(8,128)(2,1)S(1)} all-to-all(bf16[8,2,32,128]{3,2,1,0:T(8,128)(2,1)S(1)} %down.4), channel_id=1, replica_groups={{0,2,4,6,8,10,12,14},{1,3,5,7,9,11,13,15},{16,18,20,22,24,26,28,30},{17..., dimensions={0} | all-to-all | bytes 262144 | tf_op jit(solution)/shard_map/all_to_all | solution.py:373
  83.0 2.8 %collective-permute-start.6 = (bf16[16,32,128]{2,1,0:T(8,128)(2,1)S(1)}, bf16[16,32,128]{2,1,0:T(8,128)(2,1)S(1)}, u32[]{:S(2)}, u32[]{:S(2)}) collective-permute-start(bf16[16,32,128]{2,1,0:T(8,128)(2,1)S(1)} %bitcast.30), channel_id=1, source_target_pairs={{0,1},{1,0},{2,3},{3,2},{4,5},{5,4},{6,7},{7,6},{8,9},{9,8},{10,11... | collective-permute-start | bytes 393224 | tf_op jit(solution)/shard_map/ppermute | solution.py:375
  88.5 8.5 %all_to_all.74.rcv_ref = bf16[8,2,32,128]{3,2,1,0:T(8,128)(2,1)S(1)} all-to-all(bf16[8,2,32,128]{3,2,1,0:T(8,128)(2,1)S(1)} %get-tuple-element.40), channel_id=1, replica_groups={{128,144,160,176,192,208,224,240},{0,16,32,48,64,80,96,112},{129,145,16..., dimensions={0} | all-to-all | bytes 262144 | tf_op jit(solution)/shard_map/all_to_all | solution.py:383
  97.0 10.3 %all_to_all.75 = bf16[8,2,32,128]{3,2,1,0:T(8,128)(2,1)S(1)} all-to-all(bf16[8,2,32,128]{3,2,1,0:T(8,128)(2,1)S(1)} %down.5), channel_id=1, replica_groups={{0,2,4,6,8,10,12,14},{1,3,5,7,9,11,13,15},{16,18,20,22,24,26,28,30},{17..., dimensions={0} | all-to-all | bytes 262144 | tf_op jit(solution)/shard_map/all_to_all | solution.py:373
  107.3 2.9 %collective-permute-start.7 = (bf16[16,32,128]{2,1,0:T(8,128)(2,1)S(1)}, bf16[16,32,128]{2,1,0:T(8,128)(2,1)S(1)}, u32[]{:S(2)}, u32[]{:S(2)}) collective-permute-start(bf16[16,32,128]{2,1,0:T(8,128)(2,1)S(1)} %bitcast.33), channel_id=1, source_target_pairs={{0,1},{1,0},{2,3},{3,2},{4,5},{5,4},{6,7},{7,6},{8,9},{9,8},{10,11... | collective-permute-start | bytes 393224 | tf_op jit(solution)/shard_map/ppermute | solution.py:375
  112.2 8.2 %all_to_all.76.rcv_ref = bf16[8,2,32,128]{3,2,1,0:T(8,128)(2,1)S(1)} all-to-all(bf16[8,2,32,128]{3,2,1,0:T(8,128)(2,1)S(1)} %get-tuple-element.42), channel_id=1, replica_groups={{128,144,160,176,192,208,224,240},{0,16,32,48,64,80,96,112},{129,145,16..., dimensions={0} | all-to-all | bytes 262144 | tf_op jit(solution)/shard_map/all_to_all | solution.py:383
  120.6 12.1 %all_to_all.77 = bf16[8,4,32,128]{3,2,1,0:T(8,128)(2,1)S(1)} all-to-all(bf16[8,4,32,128]{3,2,1,0:T(8,128)(2,1)S(1)} %up.3), channel_id=1, replica_groups={{0,2,4,6,8,10,12,14},{1,3,5,7,9,11,13,15},{16,18,20,22,24,26,28,30},{17..., dimensions={0} | all-to-all | bytes 524288 | tf_op jit(solution)/shard_map/all_to_all | solution.py:373
  132.7 3.1 %collective-permute-start.8 = (bf16[32,32,128]{2,1,0:T(8,128)(2,1)S(1)}, bf16[32,32,128]{2,1,0:T(8,128)(2,1)S(1)}, u32[]{:S(2)}, u32[]{:S(2)}) collective-permute-start(bf16[32,32,128]{2,1,0:T(8,128)(2,1)S(1)} %bitcast.21), channel_id=1, source_target_pairs={{0,1},{1,0},{2,3},{3,2},{4,5},{5,4},{6,7},{7,6},{8,9},{9,8},{10,11... | collective-permute-start | bytes 786440 | tf_op jit(solution)/shard_map/ppermute | solution.py:375
  137.6 9.2 %all_to_all.78.rcv_ref = bf16[8,2,32,128]{3,2,1,0:T(8,128)(2,1)S(1)} all-to-all(bf16[8,2,32,128]{3,2,1,0:T(8,128)(2,1)S(1)} %get-tuple-element.46), channel_id=1, replica_groups={{64,80,96,112,128,144,160,176},{192,208,224,240,0,16,32,48},{65,81,97,1..., dimensions={0} | all-to-all | bytes 262144 | tf_op jit(solution)/shard_map/all_to_all | solution.py:383
  147.0 12.6 %all_to_all.79 = bf16[8,4,32,128]{3,2,1,0:T(8,128)(2,1)S(1)} all-to-all(bf16[8,4,32,128]{3,2,1,0:T(8,128)(2,1)S(1)} %up.4), channel_id=1, replica_groups={{0,2,4,6,8,10,12,14},{1,3,5,7,9,11,13,15},{16,18,20,22,24,26,28,30},{17..., dimensions={0} | all-to-all | bytes 524288 | tf_op jit(solution)/shard_map/all_to_all | solution.py:373
  159.6 2.6 %collective-permute-start.9 = (bf16[32,32,128]{2,1,0:T(8,128)(2,1)S(1)}, bf16[32,32,128]{2,1,0:T(8,128)(2,1)S(1)}, u32[]{:S(2)}, u32[]{:S(2)}) collective-permute-start(bf16[32,32,128]{2,1,0:T(8,128)(2,1)S(1)} %bitcast.24), channel_id=1, source_target_pairs={{0,1},{1,0},{2,3},{3,2},{4,5},{5,4},{6,7},{7,6},{8,9},{9,8},{10,11... | collective-permute-start | bytes 786440 | tf_op jit(solution)/shard_map/ppermute | solution.py:375
  164.0 9.2 %all_to_all.80.rcv_ref = bf16[8,2,32,128]{3,2,1,0:T(8,128)(2,1)S(1)} all-to-all(bf16[8,2,32,128]{3,2,1,0:T(8,128)(2,1)S(1)} %get-tuple-element.48), channel_id=1, replica_groups={{0,16,32,48,64,80,96,112},{128,144,160,176,192,208,224,240},{1,17,33,49..., dimensions={0} | all-to-all | bytes 262144 | tf_op jit(solution)/shard_map/all_to_all | solution.py:383
  173.4 12.1 %all_to_all.81 = bf16[8,4,32,128]{3,2,1,0:T(8,128)(2,1)S(1)} all-to-all(bf16[8,4,32,128]{3,2,1,0:T(8,128)(2,1)S(1)} %up.5), channel_id=1, replica_groups={{0,2,4,6,8,10,12,14},{1,3,5,7,9,11,13,15},{16,18,20,22,24,26,28,30},{17..., dimensions={0} | all-to-all | bytes 524288 | tf_op jit(solution)/shard_map/all_to_all | solution.py:373
  185.5 3.1 %collective-permute-start.10 = (bf16[32,32,128]{2,1,0:T(8,128)(2,1)S(1)}, bf16[32,32,128]{2,1,0:T(8,128)(2,1)S(1)}, u32[]{:S(2)}, u32[]{:S(2)}) collective-permute-start(bf16[32,32,128]{2,1,0:T(8,128)(2,1)S(1)} %bitcast.36), channel_id=1, source_target_pairs={{0,1},{1,0},{2,3},{3,2},{4,5},{5,4},{6,7},{7,6},{8,9},{9,8},{10,11... | collective-permute-start | bytes 786440 | tf_op jit(solution)/shard_map/ppermute | solution.py:375
  189.8 2.7 %last.1 = (f32[33,32,128]{2,1,0:T(8,128)S(1)}, bf16[4,8,32,128]{3,2,1,0:T(8,128)(2,1)S(1)}) custom-call(s32[8,128]{1,0:T(8,128)S(1)} %lists.1.lst, s32[1]{0:T(128)} %bitcast.slab, bf16[128,128,128]{2,1,0:T(8,128)(2,1)S(1)} %load.1.tiles_ref, bf16[64,32,128]{2,1,0:T(8,128)(2,1)S(1)} %bitcast.20, ...), custom_call_target="tpu_custom_call", output_to_operand_aliasing={{0}: (17, {})} | custom-call | tf_op jit(solution)/shard_map/last/pallas_call | solution.py:263
  192.5 9.1 %all_to_all.82.parts_ref = bf16[4,8,32,128]{3,2,1,0:T(8,128)(2,1)S(1)} all-to-all(bf16[4,8,32,128]{3,2,1,0:T(8,128)(2,1)S(1)} %get-tuple-element.50), channel_id=1, replica_groups=mesh['slab'=4,'row'=4,'col'=16] {'row'}, dimensions={0} | all-to-all | bytes 524288 | tf_op jit(solution)/shard_map/all_to_all | solution.py:432
  (45 shorter events, 24.5 us)
Async XLA Ops:
  0.7 0.9 copy-start
  2.4 27.0 %all-to-all-start = ((bf16[8,8,32,128]{3,2,1,0:T(8,128)(2,1)}), bf16[8,8,32,128]{3,2,1,0:T(8,128)(2,1)S(1)}, u32[]{:S(2)}, u32[]{:S(2)}) async-start(bf16[8,8,32,128]{3,2,1,0:T(8,128)(2,1)} %get-tuple-element.28), calls=%async_computation | async-start | bytes 1048576 | tf_op jit(solution)/shard_map/all_to_all | solution.py:373
  12.8 7.1 %collective-permute-start.1 = (f32[2,256]{1,0:T(2,128)S(1)}, f32[2,256]{1,0:T(2,128)S(1)}, u32[]{:S(2)}, u32[]{:S(2)}) collective-permute-start(f32[2,256]{1,0:T(2,128)S(1)} %pad_maximum_fusion), channel_id=1, source_target_pairs={{64,0},{80,16},{96,32},{112,48},{128,64},{144,80},{160,96},{176,11... | collective-permute-start | bytes 6152 | tf_op jit(solution)/shard_map/ppermute | solution.py:392
  14.1 15.8 %collective-permute-start.4 = (f32[1,256]{1,0:T(1,128)S(1)}, f32[1,256]{1,0:T(1,128)S(1)}, u32[]{:S(2)}, u32[]{:S(2)}) collective-permute-start(f32[1,256]{1,0:T(1,128)S(1)} %convert_element_type.16), channel_id=1, source_target_pairs={{112,0},{64,16},{80,32},{96,48},{176,64},{128,80},{144,96},{160,11... | collective-permute-start | bytes 3080 | tf_op jit(solution)/shard_map/ppermute | solution.py:392
  15.4 14.5 %collective-permute-start.3 = (f32[1,256]{1,0:T(1,128)S(1)}, f32[1,256]{1,0:T(1,128)S(1)}, u32[]{:S(2)}, u32[]{:S(2)}) collective-permute-start(f32[1,256]{1,0:T(1,128)S(1)} %convert_element_type.16), channel_id=1, source_target_pairs={{96,0},{112,16},{64,32},{80,48},{160,64},{176,80},{128,96},{144,11... | collective-permute-start | bytes 3080 | tf_op jit(solution)/shard_map/ppermute | solution.py:392
  16.7 13.2 %collective-permute-start.2 = (f32[1,256]{1,0:T(1,128)S(1)}, f32[1,256]{1,0:T(1,128)S(1)}, u32[]{:S(2)}, u32[]{:S(2)}) collective-permute-start(f32[1,256]{1,0:T(1,128)S(1)} %convert_element_type.16), channel_id=1, source_target_pairs={{80,0},{96,16},{112,32},{64,48},{144,64},{160,80},{176,96},{128,11... | collective-permute-start | bytes 3080 | tf_op jit(solution)/shard_map/ppermute | solution.py:392
  18.0 0.7 copy-start.2
  18.6 0.7 copy-start.3
  29.4 3.2 %collective-permute-start = (bf16[64,32,128]{2,1,0:T(8,128)(2,1)S(1)}, bf16[64,32,128]{2,1,0:T(8,128)(2,1)S(1)}, u32[]{:S(2)}, u32[]{:S(2)}) collective-permute-start(bf16[64,32,128]{2,1,0:T(8,128)(2,1)S(1)} %bitcast.12), channel_id=1, source_target_pairs={{0,1},{1,0},{2,3},{3,2},{4,5},{5,4},{6,7},{7,6},{8,9},{9,8},{10,11... | collective-permute-start | bytes 1572872 | tf_op jit(solution)/shard_map/ppermute | solution.py:375
  32.6 13.5 %copy-start.1 = (f32[1,256]{1,0:T(1,128)S(1)}, f32[1,256]{1,0:T(1,128)}, u32[]{:S(2)}) copy-start(f32[1,256]{1,0:T(1,128)} %coef_ref.5) | copy-start | bytes 3076
  56.5 5.5 %collective-permute-start.5 = (bf16[16,32,128]{2,1,0:T(8,128)(2,1)S(1)}, bf16[16,32,128]{2,1,0:T(8,128)(2,1)S(1)}, u32[]{:S(2)}, u32[]{:S(2)}) collective-permute-start(bf16[16,32,128]{2,1,0:T(8,128)(2,1)S(1)} %bitcast.27), channel_id=1, source_target_pairs={{0,1},{1,0},{2,3},{3,2},{4,5},{5,4},{6,7},{7,6},{8,9},{9,8},{10,11... | collective-permute-start | bytes 393224 | tf_op jit(solution)/shard_map/ppermute | solution.py:375
  83.0 3.8 %collective-permute-start.6 = (bf16[16,32,128]{2,1,0:T(8,128)(2,1)S(1)}, bf16[16,32,128]{2,1,0:T(8,128)(2,1)S(1)}, u32[]{:S(2)}, u32[]{:S(2)}) collective-permute-start(bf16[16,32,128]{2,1,0:T(8,128)(2,1)S(1)} %bitcast.30), channel_id=1, source_target_pairs={{0,1},{1,0},{2,3},{3,2},{4,5},{5,4},{6,7},{7,6},{8,9},{9,8},{10,11... | collective-permute-start | bytes 393224 | tf_op jit(solution)/shard_map/ppermute | solution.py:375
  107.3 3.9 %collective-permute-start.7 = (bf16[16,32,128]{2,1,0:T(8,128)(2,1)S(1)}, bf16[16,32,128]{2,1,0:T(8,128)(2,1)S(1)}, u32[]{:S(2)}, u32[]{:S(2)}) collective-permute-start(bf16[16,32,128]{2,1,0:T(8,128)(2,1)S(1)} %bitcast.33), channel_id=1, source_target_pairs={{0,1},{1,0},{2,3},{3,2},{4,5},{5,4},{6,7},{7,6},{8,9},{9,8},{10,11... | collective-permute-start | bytes 393224 | tf_op jit(solution)/shard_map/ppermute | solution.py:375
  132.7 4.3 %collective-permute-start.8 = (bf16[32,32,128]{2,1,0:T(8,128)(2,1)S(1)}, bf16[32,32,128]{2,1,0:T(8,128)(2,1)S(1)}, u32[]{:S(2)}, u32[]{:S(2)}) collective-permute-start(bf16[32,32,128]{2,1,0:T(8,128)(2,1)S(1)} %bitcast.21), channel_id=1, source_target_pairs={{0,1},{1,0},{2,3},{3,2},{4,5},{5,4},{6,7},{7,6},{8,9},{9,8},{10,11... | collective-permute-start | bytes 786440 | tf_op jit(solution)/shard_map/ppermute | solution.py:375
  159.6 3.8 %collective-permute-start.9 = (bf16[32,32,128]{2,1,0:T(8,128)(2,1)S(1)}, bf16[32,32,128]{2,1,0:T(8,128)(2,1)S(1)}, u32[]{:S(2)}, u32[]{:S(2)}) collective-permute-start(bf16[32,32,128]{2,1,0:T(8,128)(2,1)S(1)} %bitcast.24), channel_id=1, source_target_pairs={{0,1},{1,0},{2,3},{3,2},{4,5},{5,4},{6,7},{7,6},{8,9},{9,8},{10,11... | collective-permute-start | bytes 786440 | tf_op jit(solution)/shard_map/ppermute | solution.py:375
  185.5 4.3 %collective-permute-start.10 = (bf16[32,32,128]{2,1,0:T(8,128)(2,1)S(1)}, bf16[32,32,128]{2,1,0:T(8,128)(2,1)S(1)}, u32[]{:S(2)}, u32[]{:S(2)}) collective-permute-start(bf16[32,32,128]{2,1,0:T(8,128)(2,1)S(1)} %bitcast.36), channel_id=1, source_target_pairs={{0,1},{1,0},{2,3},{3,2},{4,5},{5,4},{6,7},{7,6},{8,9},{9,8},{10,11... | collective-permute-start | bytes 786440 | tf_op jit(solution)/shard_map/ppermute | solution.py:375

commit v8 on v7

--- a/solution.py
+++ b/solution.py
@@ -31,8 +31,8 @@
 
 PARAMS = pltpu.CompilerParams(vmem_limit_bytes=24 * 2**20)
 ACC = (NROW * BLK + 1, W, B)
-LISTS = 6
-V0AB, V0C, TAB, TC, LA, LBC = range(LISTS)
+LISTS = 9
+V0AB, V0C, TC, TAB, LA, LBC = 0, 1, 2, 3, 5, 7
 CHUNK = 3
 ORDER = (1, 2, 3, 2, 1)
 HALF = NCOL // 2
@@ -50,7 +50,21 @@
     return jnp.where(side == 0, own_ref[at], other_ref[at])
 
 
-def lists_kernel(col_index, rows_ref, cols_ref, out_ref):
+def helper_kernel(
+    col_index, rows_hbm, cols_hbm, map_hbm, coef_hbm, out_ref, pack_ref,
+    rows_ref, cols_ref, map_ref, coef_ref, sems,
+):
+    ins = (rows_hbm, cols_hbm, map_hbm, coef_hbm)
+    copies = [
+        pltpu.make_async_copy(src, dst, sems.at[k])
+        for k, (src, dst) in enumerate(zip(ins, (rows_ref, cols_ref, map_ref, coef_ref)))
+    ]
+    for copy in copies:
+        copy.start()
+    for copy in copies:
+        copy.wait()
+    pack_ref[0:1, :] = map_ref[...].astype(F32)
+    pack_ref[1:2, :] = coef_ref[...]
     lane = lax.broadcasted_iota(jnp.int32, (1, NT), 1)
     down = lax.broadcasted_iota(jnp.int32, (NT, NT), 0)
     across = lax.broadcasted_iota(jnp.int32, (NT, NT), 1)
@@ -65,13 +79,18 @@
     early = out < PRT
     target = blk < TGT
     low = blk < PRT
+    own = side == 0
+    other = side == 1
     member = (
         (BLK, early),
         (BLK, out >= PRT),
-        (TGT, target & early),
         (TGT, target & (out >= PRT)),
-        (PRT, low & (out < TGT)),
-        (PRT, low & (out >= TGT)),
+        (TGT, target & early & own),
+        (TGT, target & early & other),
+        (PRT, low & (out < TGT) & own),
+        (PRT, low & (out < TGT) & other),
+        (PRT, low & (out >= TGT) & own),
+        (PRT, low & (out >= TGT) & other),
     )
     sizes = jnp.zeros((1, NT), jnp.int32)
     for k, (width, belongs) in enumerate(member):
@@ -92,19 +111,24 @@
         entry = moved[0:1] + moved[1:2] * NT + moved[2:3] * 8192
         out_ref[k : k + 1, :] = jnp.where(lane < count, entry, NROW * BLK * NT)
         sizes = jnp.where(lane == k, shr(count + UNROLL - 1, 3), sizes)
-    out_ref[LISTS : LISTS + 1, :] = sizes
-    out_ref[LISTS + 1 : LISTS + 2, :] = sizes
-
-
-def make_lists(tile_rows, tile_cols, col_index):
-    return pl.pallas_call(
-        lists_kernel,
-        out_shape=jax.ShapeDtypeStruct((LISTS + 2, NT), jnp.int32),
-        in_specs=[smem(), vmem(), vmem()],
-        out_specs=vmem(),
-        compiler_params=PARAMS,
-        name="lists",
-    )(col_index, tile_rows, tile_cols)
+    for k in range(LISTS, 16):
+        out_ref[k : k + 1, :] = sizes
+
+
+def helper(col_index, tile_rows, tile_cols, plane_map, interface_coef):
+    ins = (tile_rows, tile_cols, plane_map, interface_coef)
+    return pl.pallas_call(
+        helper_kernel,
+        out_shape=(
+            jax.ShapeDtypeStruct((16, NT), jnp.int32),
+            jax.ShapeDtypeStruct((2, TGT * B), F32),
+        ),
+        in_specs=[smem()] + [pl.BlockSpec(memory_space=pltpu.HBM)] * 4,
+        out_specs=(vmem(), vmem()),
+        scratch_shapes=[pltpu.VMEM(x.shape, x.dtype) for x in ins] + [pltpu.SemaphoreType.DMA((4,))],
+        compiler_params=PARAMS,
+        name="helper",
+    )(col_index, *[pltpu.with_memory_space_constraint(x, pltpu.HBM) for x in ins])
 
 
 def load_kernel(tiles_hbm, own_ref, tiles_ref, sem):
@@ -125,20 +149,17 @@
     )(pltpu.with_memory_space_constraint(tiles, pltpu.HBM), own)
 
 
-def apply_group(lst, which, g, pair, tiles_ref, acc):
-    rows, done = [], []
-    for u in range(UNROLL):
-        e = lst[which, g * UNROLL + u]
-        v = picked(shr(e, 19), *pair, shr(e, 13) & 63)
-        rows.append(shr(e, 7) & 63)
-        done.append(product(v, tiles_ref[e & 127]))
-    for r, d in zip(rows, done):
-        acc[r] += d
-
-
-def apply_list(lst, which, pair, tiles_ref, acc, low=0, most=NT):
+def apply_list(lst, which, sources, tiles_ref, acc, low=0, most=NT):
     def group(g, _):
-        apply_group(lst, which, g, pair, tiles_ref, acc)
+        rows, done = [], []
+        for u in range(UNROLL):
+            e = lst[which, g * UNROLL + u]
+            at = shr(e, 13) & 63
+            v = sources[0][at] if len(sources) == 1 else picked(shr(e, 19), *sources, at)
+            rows.append(shr(e, 7) & 63)
+            done.append(product(v, tiles_ref[e & 127]))
+        for r, d in zip(rows, done):
+            acc[r] += d
         return 0
 
     groups = lst[LISTS, which]
@@ -150,16 +171,6 @@
     for active in ORDER[:step]:
         used = used - jnp.where(slab[0] == active, jnp.int32(1), jnp.int32(0))
     return used * CHUNK
-
-
-def step_work(lst, slab, which, pair, first_pair, tiles_ref, acc, step):
-    @pl.when(slab[0] == ORDER[step])
-    def _():
-        apply_list(lst, which, pair, tiles_ref, acc)
-
-    @pl.when(slab[0] != ORDER[step])
-    def _():
-        apply_list(lst, V0C, first_pair, tiles_ref, acc, late_start(slab, step), CHUNK)
 
 
 def write_down(acc, row, hot_ref, msg_ref):
@@ -200,59 +211,79 @@
     )(lst, row, *pair, hots, tiles)
 
 
-def down_step_kernel(
-    lst, slab, row, own_ref, other_ref, own0, other0, hot_ref, tiles_ref, acc_in, acc, msg_ref, *, step
-):
-    step_work(lst, slab, TAB, (own_ref, other_ref), (own0, other0), tiles_ref, acc, step)
-    if ORDER[step] < NSLAB - 1:
+def own_kernel(lst, slab, own_ref, own0, other0, tiles_ref, acc_in, acc, *, which, step):
+    @pl.when(slab[0] == ORDER[step])
+    def _():
+        apply_list(lst, which, (own_ref,), tiles_ref, acc)
+
+    @pl.when(slab[0] != ORDER[step])
+    def _():
+        apply_list(lst, V0C, (own0, other0), tiles_ref, acc, late_start(slab, step), CHUNK)
+
+
+def own_apply(lst, slab, which, own, first_pair, tiles, acc, step):
+    return pl.pallas_call(
+        functools.partial(own_kernel, which=which, step=step),
+        out_shape=jax.ShapeDtypeStruct(ACC, F32),
+        in_specs=[smem(), smem()] + [vmem()] * 5,
+        out_specs=vmem(),
+        input_output_aliases={6: 0},
+        compiler_params=PARAMS,
+        name="own",
+    )(lst, slab, own, *first_pair, tiles, acc)
+
+
+def other_kernel(lst, slab, row, other_ref, hot_ref, tiles_ref, acc_in, acc, msg_ref, *, which, step):
+    @pl.when(slab[0] == ORDER[step])
+    def _():
+        apply_list(lst, which + 1, (other_ref,), tiles_ref, acc)
+
+    if step + 1 < len(ORDER) and ORDER[step] < ORDER[step + 1]:
         write_down(acc, row, hot_ref, msg_ref)
     else:
         write_up(acc, msg_ref)
 
 
-def down_step(lst, slab, row, pair, first_pair, hots, tiles, acc, step):
-    return pl.pallas_call(
-        functools.partial(down_step_kernel, step=step),
+def other_apply(lst, slab, row, which, other, hots, tiles, acc, step):
+    return pl.pallas_call(
+        functools.partial(other_kernel, which=which, step=step),
         out_shape=(jax.ShapeDtypeStruct(ACC, F32), MESSAGE),
-        in_specs=[smem(), smem(), smem()] + [vmem()] * 7,
+        in_specs=[smem(), smem(), smem()] + [vmem()] * 4,
         out_specs=(vmem(), vmem()),
-        input_output_aliases={9: 0},
-        compiler_params=PARAMS,
-        name="down_step",
-    )(lst, slab, row, *pair, *first_pair, hots, tiles, acc)
-
-
-def up_step_kernel(
-    lst, slab, own_ref, other_ref, own0, other0, tiles_ref, acc_in, acc, msg_ref, *, step
-):
-    step_work(lst, slab, LA, (own_ref, other_ref), (own0, other0), tiles_ref, acc, step)
-    write_up(acc, msg_ref)
-
-
-def up_step(lst, slab, pair, first_pair, tiles, acc, step):
-    return pl.pallas_call(
-        functools.partial(up_step_kernel, step=step),
-        out_shape=(jax.ShapeDtypeStruct(ACC, F32), MESSAGE),
-        in_specs=[smem(), smem()] + [vmem()] * 6,
-        out_specs=(vmem(), vmem()),
-        input_output_aliases={7: 0},
-        compiler_params=PARAMS,
-        name="up_step",
-    )(lst, slab, *pair, *first_pair, tiles, acc)
-
-
-def last_kernel(lst, slab, tiles_ref, own0, other0, *refs):
-    gathered, acc, msg_ref = refs[:12], refs[13], refs[14]
+        input_output_aliases={6: 0},
+        compiler_params=PARAMS,
+        name="other",
+    )(lst, slab, row, other, hots, tiles, acc)
+
+
+def step_apply(lst, slab, row, which, pair, first_pair, hots, tiles, acc, step):
+    acc = own_apply(lst, slab, which, pair[0], first_pair, tiles, acc, step)
+    return other_apply(lst, slab, row, which, pair[1], hots, tiles, acc, step)
+
+
+def last_own_kernel(lst, slab, tiles_ref, own0, other0, *refs):
+    gathered, acc = refs[:11], refs[12]
     for k, s in enumerate((1, 2, 3, 2, 1, 0)):
-        pair = gathered[2 * k], gathered[2 * k + 1]
-
         @pl.when(slab[0] == s)
-        def _(k=k, s=s, pair=pair):
+        def _(k=k, s=s):
             if s == 0:
-                apply_list(lst, LA, pair, tiles_ref, acc)
-            apply_list(lst, TC if k < NSLAB - 1 else LBC, pair, tiles_ref, acc)
+                apply_list(lst, LA, gathered[2 * k : 2 * k + 1], tiles_ref, acc)
+            if k < NSLAB - 1:
+                apply_list(lst, TC, gathered[2 * k : 2 * k + 2], tiles_ref, acc)
+            else:
+                apply_list(lst, LBC, gathered[2 * k : 2 * k + 1], tiles_ref, acc)
+                if s > 0:
+                    apply_list(lst, LBC + 1, gathered[2 * k + 1 : 2 * k + 2], tiles_ref, acc)
 
     apply_list(lst, V0C, (own0, other0), tiles_ref, acc, late_start(slab, len(ORDER)))
+
+
+def last_other_kernel(lst, slab, tiles_ref, other_ref, acc_in, acc, msg_ref):
+    @pl.when(slab[0] == 0)
+    def _():
+        apply_list(lst, LA + 1, (other_ref,), tiles_ref, acc)
+        apply_list(lst, LBC + 1, (other_ref,), tiles_ref, acc)
+
     for r in range(NROW):
         for b in range(BLK):
             msg_ref[r, b] = acc[r * BLK + b].astype(BF)
@@ -260,18 +291,25 @@
 
 def last_apply(lst, slab, tiles, first_pair, pairs, acc):
     flat = [ref for pair in pairs for ref in pair]
-    return pl.pallas_call(
-        last_kernel,
-        out_shape=(
-            jax.ShapeDtypeStruct(ACC, F32),
-            jax.ShapeDtypeStruct((NROW, BLK, W, B), BF),
-        ),
-        in_specs=[smem(), smem()] + [vmem()] * 16,
+    whole = jax.ShapeDtypeStruct(ACC, F32)
+    acc = pl.pallas_call(
+        last_own_kernel,
+        out_shape=whole,
+        in_specs=[smem(), smem()] + [vmem()] * 15,
+        out_specs=vmem(),
+        input_output_aliases={16: 0},
+        compiler_params=PARAMS,
+        name="last_own",
+    )(lst, slab, tiles, *first_pair, *flat[:-1], acc)
+    return pl.pallas_call(
+        last_other_kernel,
+        out_shape=(whole, jax.ShapeDtypeStruct((NROW, BLK, W, B), BF)),
+        in_specs=[smem(), smem()] + [vmem()] * 3,
         out_specs=(vmem(), vmem()),
-        input_output_aliases={17: 0},
-        compiler_params=PARAMS,
-        name="last",
-    )(lst, slab, tiles, *first_pair, *flat, acc)[1]
+        input_output_aliases={4: 0},
+        compiler_params=PARAMS,
+        name="last_other",
+    )(lst, slab, tiles, flat[-1], acc)[1]
 
 
 def split(x):
@@ -322,9 +360,20 @@
     )(received, *others)
 
 
-def prepare_kernel(count, slab, rhs_ref, out_ref, target_ref):
+def prepare_kernel(count, slab, rhs_hbm, out_ref, target_ref, rhs_ref, sems):
+    wide = 2 * B
+    copies = [
+        pltpu.make_async_copy(
+            rhs_hbm.at[0, :, pl.ds(k * wide, wide)], rhs_ref.at[k], sems.at[k]
+        )
+        for k in range(BLK // 2)
+    ]
+    for copy in copies:
+        copy.start()
     for b in range(BLK):
-        value = rhs_ref[0, :, b * B : (b + 1) * B]
+        if b % 2 == 0:
+            copies[b // 2].wait()
+        value = rhs_ref[b // 2, :, b % 2 * B : (b % 2 + 1) * B]
         if b < TGT:
             target_ref[b] = value
             value = jnp.where(slab[0] == 0, value, 0.0)
@@ -340,11 +389,15 @@
             jax.ShapeDtypeStruct((HALF, BLK, W, B), BF),
             jax.ShapeDtypeStruct((TGT, W, B), F32),
         ),
-        in_specs=[smem(), smem(), vmem()],
+        in_specs=[smem(), smem(), pl.BlockSpec(memory_space=pltpu.HBM)],
         out_specs=(vmem(), vmem()),
+        scratch_shapes=[
+            pltpu.VMEM((BLK // 2, W, 2 * B), F32),
+            pltpu.SemaphoreType.DMA((BLK // 2,)),
+        ],
         compiler_params=PARAMS,
         name="prepare",
-    )(section_blocks, slab, right_sides)
+    )(section_blocks, slab, pltpu.with_memory_space_constraint(right_sides, pltpu.HBM))
 
 
 def finish_kernel(count, parts_ref, out_ref):
@@ -399,12 +452,10 @@
     slab = slab.reshape(1)
     row = row.reshape(1)
     col = col.reshape(1)
-    map_own = plane_map.astype(F32)
-    pack_next = from_next(jnp.concatenate([map_own, interface_coef], axis=0), 0)
-    coef_next = pack_next[1:2]
-    maps_next = jnp.concatenate(
-        [pack_next[0:1]] + [from_next(map_own, d) for d in range(1, NROW)], axis=0
-    ).astype(jnp.int32)
+    lst, pack = helper(col, tile_rows, tile_cols, plane_map, interface_coef)
+    packs = [from_next(pack, d) for d in range(NROW)]
+    coef_next = packs[0][1:2]
+    maps_next = jnp.concatenate([p[0:1] for p in packs], axis=0).astype(jnp.int32)
 
     copies, rhs_target = prepare(right_sides, section_blocks, slab)
     partner = jnp.arange(PRT * B, dtype=jnp.int32)
@@ -412,22 +463,23 @@
     hot_next = (maps_next[0][:, None] == partner[None, :]).astype(BF)
 
     start = gather(copies)
-    lst = make_lists(tile_rows, tile_cols, col)
     tiles = load_tiles(front_tiles[0], start[0])
     start, hots, hot_next, coef_next, rhs_target, lst, tiles = lax.optimization_barrier(
         (start, hots, hot_next, coef_next, rhs_target, lst, tiles)
     )
     acc, msg = first_apply(lst, row, start, hots, tiles)
     pairs = []
-    for step, active in enumerate(ORDER[: NSLAB - 1]):
-        rcv = exchange(msg, active - 1)
-        pairs.append(gather(combine(down_kernel, rcv, (rhs_target, interface_coef), TGT, "down")))
-        acc, msg = down_step(lst, slab, row, pairs[-1], start, hots, tiles, acc, step)
-    for s in range(NSLAB - 2, -1, -1):
-        rcv = exchange(msg, s)
-        pairs.append(gather(combine(up_kernel, rcv, (coef_next, hot_next), PRT, "up")))
-        if s > 0:
-            acc, msg = up_step(lst, slab, pairs[-1], start, tiles, acc, 2 * NSLAB - 3 - s)
+    for step in range(2 * NSLAB - 2):
+        if step < NSLAB - 1:
+            rcv = exchange(msg, step)
+            value = combine(down_kernel, rcv, (rhs_target, interface_coef), TGT, "down")
+        else:
+            rcv = exchange(msg, 2 * NSLAB - 3 - step)
+            value = combine(up_kernel, rcv, (coef_next, hot_next), PRT, "up")
+        pairs.append(gather(value))
+        if step < len(ORDER):
+            which = TAB if step < NSLAB - 1 else LA
+            acc, msg = step_apply(lst, slab, row, which, pairs[-1], start, hots, tiles, acc, step)
     msg = last_apply(lst, slab, tiles, start, pairs, acc)
     return finish(section_blocks, lax.all_to_all(msg, "row", 0, 0, tiled=True))
 

time: 203 us -> 201 us (level)
  Pallas kernels: 16.7 us -> 23.3 us
  waiting for transfers between devices: 15.9 us -> 12 us
  starting transfers between devices: 33.8 us -> 31.3 us
  local copies, waits for them, and re-layouts: 2.22 us -> 0.02 us
    ppermute x4, waiting for transfers between devices: 0.02 us -> 6.73 us  [from_next(): return lax.ppermute(value, ('slab', 'row'), pairs)]
    pallas_call x7 -> x13, Pallas kernels: 8.87 us -> 14.9 us  [the longest x5 5.47 us: own_apply(): pl.pallas_call(functools.partial(own_kernel, which=which, step=step), out...]
    ppermute x7, waiting for transfers between devices: 6.45 us -> 0.96 us  [gather(): return (own, lax.ppermute(own, 'col', [(c, c ^ 1) for c in range(NCOL)]))]
    all_to_all x1, waiting for transfers between devices: 9.43 us -> 4.27 us  [gather(): lax.all_to_all(copies, 'col', 0, 0, tiled=True, axis_index_groups=Z_GROUPS)]
    ppermute x7, starting transfers between devices: 19.6 us -> 17.1 us  [gather(): return (own, lax.ppermute(own, 'col', [(c, c ^ 1) for c in range(NCOL)]))]
    all_to_all x6, blocking collectives: 67.8 us -> 70.1 us  [gather(): lax.all_to_all(copies, 'col', 0, 0, tiled=True, axis_index_groups=Z_GROUPS)]
    unnamed x8 -> x2, local copies, waits for them, and re-layouts: 2.21 us -> 0.01 us
  transfers between devices with their start and end apart: 12 -> 12, of which waited for: 7 -> 7; matrix products, arithmetic and copies ran while one was open for 1% -> 0% of each run, Pallas kernels for 1% -> 6%
where the time goes in v8:
time: 201 us; the launch traced here: 200 us
  blocking collectives  132 us (66%)
  starting transfers between devices  31.3 us (16%)
  Pallas kernels  23.3 us (12%)
  waiting for transfers between devices  12 us (6%)
    all_to_all x6, blocking collectives, gather(): lax.all_to_all(copies, 'col', 0, 0, tiled=True, axis_index_groups=Z_GROUPS)  70.1 us
    all_to_all x6, blocking collectives, exchange(): lax.all_to_all(message, ('slab', 'row'), 0, 0, tiled=True, axis_index_gro...  52.8 us
    ppermute x7, starting transfers between devices, gather(): return (own, lax.ppermute(own, 'col', [(c, c ^ 1) for c in range(NCOL)]))  17.1 us
    all_to_all x1, starting transfers between devices, gather(): lax.all_to_all(copies, 'col', 0, 0, tiled=True, axis_index_groups=Z_GROUPS)  9.02 us
    all_to_all x1, blocking collectives, body(): return finish(section_blocks, lax.all_to_all(msg, 'row', 0, 0, tiled=True))  8.81 us
    ppermute x4, waiting for transfers between devices, from_next(): return lax.ppermute(value, ('slab', 'row'), pairs)  6.73 us
    pallas_call x5, Pallas kernels, own_apply(): pl.pallas_call(functools.partial(own_kernel, which=which, step=step), out...  5.47 us
    ppermute x4, starting transfers between devices, from_next(): return lax.ppermute(value, ('slab', 'row'), pairs)  5.17 us
  transfers between devices with their start and end apart: 12, of which 7 were waited for; matrix products, arithmetic and copies ran while one was open for 0% of the time, Pallas kernels for 6%

profile of v8, /device:TPU:1, one launch (start us, length us, event | category | flops | bytes accessed | tf_op | source)
XLA Modules:
  0.0 199.7 jit_solution(4631737291448920483)
XLA Ops:
  2.3 9.0 %all-to-all-start = ((bf16[8,8,32,128]{3,2,1,0:T(8,128)(2,1)}), bf16[8,8,32,128]{3,2,1,0:T(8,128)(2,1)S(1)}, u32[]{:S(2)}, u32[]{:S(2)}) async-start(bf16[8,8,32,128]{3,2,1,0:T(8,128)(2,1)} %get-tuple-element.30), calls=%async_computation | async-start | bytes 1048576 | tf_op jit(solution)/shard_map/all_to_all | solution.py:426
  19.8 2.8 %collective-permute-done.3 = f32[2,256]{1,0:T(2,128)S(1)} collective-permute-done((f32[2,256]{1,0:T(2,128)S(1)}, f32[2,256]{1,0:T(2,128)S(1)}, u32[]{:S(2)}, u32[]{:S(2)}) %collective-permute-start.3) | collective-permute-done | bytes 2080 | tf_op jit(solution)/shard_map/ppermute | solution.py:445
  25.0 4.3 %all-to-all-done = bf16[8,8,32,128]{3,2,1,0:T(8,128)(2,1)S(1)} async-done(((bf16[8,8,32,128]{3,2,1,0:T(8,128)(2,1)}), bf16[8,8,32,128]{3,2,1,0:T(8,128)(2,1)S(1)}, u32[]{:S(2)}, u32[]{:S(2)}) %all-to-all-start) | async-done | bytes 524320 | tf_op jit(solution)/shard_map/all_to_all | solution.py:426
  32.5 3.3 %first.1 = (f32[33,32,128]{2,1,0:T(8,128)S(1)}, bf16[8,2,32,128]{3,2,1,0:T(8,128)(2,1)S(1)}) custom-call(s32[16,128]{1,0:T(8,128)S(1)} %get-tuple-element.34.lst, s32[1]{0:T(128)} %bitcast.5.row, bf16[64,32,128]{2,1,0:T(8,128)(2,1)S(1)} %bitcast.14, bf16[64,32,128]{2,1,0:T(8,128)(2,1)S(1)} %collective-permute-done.other_ref.other0, ...), custom_call_target="tpu_custom_call" | custom-call | tf_op jit(solution)/shard_map/first/pallas_call | solution.py:204
  35.8 10.0 %all_to_all.70.rcv_ref = bf16[8,2,32,128]{3,2,1,0:T(8,128)(2,1)S(1)} all-to-all(bf16[8,2,32,128]{3,2,1,0:T(8,128)(2,1)S(1)} %get-tuple-element.39), channel_id=1, replica_groups={{0,16,32,48,64,80,96,112},{128,144,160,176,192,208,224,240},{1,17,33,49..., dimensions={0} | all-to-all | bytes 262144 | tf_op jit(solution)/shard_map/all_to_all | solution.py:436
  45.8 12.4 %all_to_all.71 = bf16[8,2,32,128]{3,2,1,0:T(8,128)(2,1)S(1)} all-to-all(bf16[8,2,32,128]{3,2,1,0:T(8,128)(2,1)S(1)} %down.3), channel_id=1, replica_groups={{0,2,4,6,8,10,12,14},{1,3,5,7,9,11,13,15},{16,18,20,22,24,26,28,30},{17..., dimensions={0} | all-to-all | bytes 262144 | tf_op jit(solution)/shard_map/all_to_all | solution.py:426
  58.2 2.9 %collective-permute-start.5 = (bf16[16,32,128]{2,1,0:T(8,128)(2,1)S(1)}, bf16[16,32,128]{2,1,0:T(8,128)(2,1)S(1)}, u32[]{:S(2)}, u32[]{:S(2)}) collective-permute-start(bf16[16,32,128]{2,1,0:T(8,128)(2,1)S(1)} %bitcast.27), channel_id=1, source_target_pairs={{0,1},{1,0},{2,3},{3,2},{4,5},{5,4},{6,7},{7,6},{8,9},{9,8},{10,11... | collective-permute-start | bytes 393224 | tf_op jit(solution)/shard_map/ppermute | solution.py:428
  63.5 8.8 %all_to_all.72.rcv_ref = bf16[8,2,32,128]{3,2,1,0:T(8,128)(2,1)S(1)} all-to-all(bf16[8,2,32,128]{3,2,1,0:T(8,128)(2,1)S(1)} %get-tuple-element.42), channel_id=1, replica_groups={{64,80,96,112,128,144,160,176},{192,208,224,240,0,16,32,48},{65,81,97,1..., dimensions={0} | all-to-all | bytes 262144 | tf_op jit(solution)/shard_map/all_to_all | solution.py:436
  72.3 10.4 %all_to_all.73 = bf16[8,2,32,128]{3,2,1,0:T(8,128)(2,1)S(1)} all-to-all(bf16[8,2,32,128]{3,2,1,0:T(8,128)(2,1)S(1)} %down.4), channel_id=1, replica_groups={{0,2,4,6,8,10,12,14},{1,3,5,7,9,11,13,15},{16,18,20,22,24,26,28,30},{17..., dimensions={0} | all-to-all | bytes 262144 | tf_op jit(solution)/shard_map/all_to_all | solution.py:426
  82.7 2.4 %collective-permute-start.6 = (bf16[16,32,128]{2,1,0:T(8,128)(2,1)S(1)}, bf16[16,32,128]{2,1,0:T(8,128)(2,1)S(1)}, u32[]{:S(2)}, u32[]{:S(2)}) collective-permute-start(bf16[16,32,128]{2,1,0:T(8,128)(2,1)S(1)} %bitcast.30), channel_id=1, source_target_pairs={{0,1},{1,0},{2,3},{3,2},{4,5},{5,4},{6,7},{7,6},{8,9},{9,8},{10,11... | collective-permute-start | bytes 393224 | tf_op jit(solution)/shard_map/ppermute | solution.py:428
  87.6 8.1 %all_to_all.74.rcv_ref = bf16[8,2,32,128]{3,2,1,0:T(8,128)(2,1)S(1)} all-to-all(bf16[8,2,32,128]{3,2,1,0:T(8,128)(2,1)S(1)} %get-tuple-element.44), channel_id=1, replica_groups={{128,144,160,176,192,208,224,240},{0,16,32,48,64,80,96,112},{129,145,16..., dimensions={0} | all-to-all | bytes 262144 | tf_op jit(solution)/shard_map/all_to_all | solution.py:436
  95.7 10.4 %all_to_all.75 = bf16[8,2,32,128]{3,2,1,0:T(8,128)(2,1)S(1)} all-to-all(bf16[8,2,32,128]{3,2,1,0:T(8,128)(2,1)S(1)} %down.5), channel_id=1, replica_groups={{0,2,4,6,8,10,12,14},{1,3,5,7,9,11,13,15},{16,18,20,22,24,26,28,30},{17..., dimensions={0} | all-to-all | bytes 262144 | tf_op jit(solution)/shard_map/all_to_all | solution.py:426
  106.1 2.5 %collective-permute-start.7 = (bf16[16,32,128]{2,1,0:T(8,128)(2,1)S(1)}, bf16[16,32,128]{2,1,0:T(8,128)(2,1)S(1)}, u32[]{:S(2)}, u32[]{:S(2)}) collective-permute-start(bf16[16,32,128]{2,1,0:T(8,128)(2,1)S(1)} %bitcast.33), channel_id=1, source_target_pairs={{0,1},{1,0},{2,3},{3,2},{4,5},{5,4},{6,7},{7,6},{8,9},{9,8},{10,11... | collective-permute-start | bytes 393224 | tf_op jit(solution)/shard_map/ppermute | solution.py:428
  110.5 7.9 %all_to_all.76.rcv_ref = bf16[8,2,32,128]{3,2,1,0:T(8,128)(2,1)S(1)} all-to-all(bf16[8,2,32,128]{3,2,1,0:T(8,128)(2,1)S(1)} %get-tuple-element.46), channel_id=1, replica_groups={{128,144,160,176,192,208,224,240},{0,16,32,48,64,80,96,112},{129,145,16..., dimensions={0} | all-to-all | bytes 262144 | tf_op jit(solution)/shard_map/all_to_all | solution.py:436
  118.7 12.6 %all_to_all.77 = bf16[8,4,32,128]{3,2,1,0:T(8,128)(2,1)S(1)} all-to-all(bf16[8,4,32,128]{3,2,1,0:T(8,128)(2,1)S(1)} %up.3), channel_id=1, replica_groups={{0,2,4,6,8,10,12,14},{1,3,5,7,9,11,13,15},{16,18,20,22,24,26,28,30},{17..., dimensions={0} | all-to-all | bytes 524288 | tf_op jit(solution)/shard_map/all_to_all | solution.py:426
  131.3 2.6 %collective-permute-start.8 = (bf16[32,32,128]{2,1,0:T(8,128)(2,1)S(1)}, bf16[32,32,128]{2,1,0:T(8,128)(2,1)S(1)}, u32[]{:S(2)}, u32[]{:S(2)}) collective-permute-start(bf16[32,32,128]{2,1,0:T(8,128)(2,1)S(1)} %bitcast.21), channel_id=1, source_target_pairs={{0,1},{1,0},{2,3},{3,2},{4,5},{5,4},{6,7},{7,6},{8,9},{9,8},{10,11... | collective-permute-start | bytes 786440 | tf_op jit(solution)/shard_map/ppermute | solution.py:428
  135.7 8.8 %all_to_all.78.rcv_ref = bf16[8,2,32,128]{3,2,1,0:T(8,128)(2,1)S(1)} all-to-all(bf16[8,2,32,128]{3,2,1,0:T(8,128)(2,1)S(1)} %get-tuple-element.50), channel_id=1, replica_groups={{64,80,96,112,128,144,160,176},{192,208,224,240,0,16,32,48},{65,81,97,1..., dimensions={0} | all-to-all | bytes 262144 | tf_op jit(solution)/shard_map/all_to_all | solution.py:436
  144.8 12.1 %all_to_all.79 = bf16[8,4,32,128]{3,2,1,0:T(8,128)(2,1)S(1)} all-to-all(bf16[8,4,32,128]{3,2,1,0:T(8,128)(2,1)S(1)} %up.4), channel_id=1, replica_groups={{0,2,4,6,8,10,12,14},{1,3,5,7,9,11,13,15},{16,18,20,22,24,26,28,30},{17..., dimensions={0} | all-to-all | bytes 524288 | tf_op jit(solution)/shard_map/all_to_all | solution.py:426
  156.9 3.1 %collective-permute-start.9 = (bf16[32,32,128]{2,1,0:T(8,128)(2,1)S(1)}, bf16[32,32,128]{2,1,0:T(8,128)(2,1)S(1)}, u32[]{:S(2)}, u32[]{:S(2)}) collective-permute-start(bf16[32,32,128]{2,1,0:T(8,128)(2,1)S(1)} %bitcast.24), channel_id=1, source_target_pairs={{0,1},{1,0},{2,3},{3,2},{4,5},{5,4},{6,7},{7,6},{8,9},{9,8},{10,11... | collective-permute-start | bytes 786440 | tf_op jit(solution)/shard_map/ppermute | solution.py:428
  161.9 9.1 %all_to_all.80.rcv_ref = bf16[8,2,32,128]{3,2,1,0:T(8,128)(2,1)S(1)} all-to-all(bf16[8,2,32,128]{3,2,1,0:T(8,128)(2,1)S(1)} %get-tuple-element.52), channel_id=1, replica_groups={{0,16,32,48,64,80,96,112},{128,144,160,176,192,208,224,240},{1,17,33,49..., dimensions={0} | all-to-all | bytes 262144 | tf_op jit(solution)/shard_map/all_to_all | solution.py:436
  171.2 12.2 %all_to_all.81 = bf16[8,4,32,128]{3,2,1,0:T(8,128)(2,1)S(1)} all-to-all(bf16[8,4,32,128]{3,2,1,0:T(8,128)(2,1)S(1)} %up.5), channel_id=1, replica_groups={{0,2,4,6,8,10,12,14},{1,3,5,7,9,11,13,15},{16,18,20,22,24,26,28,30},{17..., dimensions={0} | all-to-all | bytes 524288 | tf_op jit(solution)/shard_map/all_to_all | solution.py:426
  183.3 3.1 %collective-permute-start.10 = (bf16[32,32,128]{2,1,0:T(8,128)(2,1)S(1)}, bf16[32,32,128]{2,1,0:T(8,128)(2,1)S(1)}, u32[]{:S(2)}, u32[]{:S(2)}) collective-permute-start(bf16[32,32,128]{2,1,0:T(8,128)(2,1)S(1)} %bitcast.36), channel_id=1, source_target_pairs={{0,1},{1,0},{2,3},{3,2},{4,5},{5,4},{6,7},{7,6},{8,9},{9,8},{10,11... | collective-permute-start | bytes 786440 | tf_op jit(solution)/shard_map/ppermute | solution.py:428
  186.4 2.2 %last_own.1.acc_in = f32[33,32,128]{2,1,0:T(8,128)S(1)} custom-call(s32[16,128]{1,0:T(8,128)S(1)} %get-tuple-element.34.lst, s32[1]{0:T(128)} %bitcast.slab, bf16[128,128,128]{2,1,0:T(8,128)(2,1)S(1)} %load.1.tiles_ref, bf16[64,32,128]{2,1,0:T(8,128)(2,1)S(1)} %bitcast.20, ...), custom_call_target="tpu_custom_call", output_to_operand_aliasing={{}: (16, {})} | custom-call | tf_op jit(solution)/shard_map/last_own/pallas_call | solution.py:295
  190.2 8.8 %all_to_all.82.parts_ref = bf16[4,8,32,128]{3,2,1,0:T(8,128)(2,1)S(1)} all-to-all(bf16[4,8,32,128]{3,2,1,0:T(8,128)(2,1)S(1)} %get-tuple-element.54), channel_id=1, replica_groups=mesh['slab'=4,'row'=4,'col'=16] {'row'}, dimensions={0} | all-to-all | bytes 524288 | tf_op jit(solution)/shard_map/all_to_all | solution.py:484
  (46 shorter events, 28.9 us)
Async XLA Ops:
  2.3 27.0 %all-to-all-start = ((bf16[8,8,32,128]{3,2,1,0:T(8,128)(2,1)}), bf16[8,8,32,128]{3,2,1,0:T(8,128)(2,1)S(1)}, u32[]{:S(2)}, u32[]{:S(2)}) async-start(bf16[8,8,32,128]{3,2,1,0:T(8,128)(2,1)} %get-tuple-element.30), calls=%async_computation | async-start | bytes 1048576 | tf_op jit(solution)/shard_map/all_to_all | solution.py:426
  13.1 6.7 %collective-permute-start.4 = (f32[2,256]{1,0:T(2,128)S(1)}, f32[2,256]{1,0:T(2,128)S(1)}, u32[]{:S(2)}, u32[]{:S(2)}) collective-permute-start(f32[2,256]{1,0:T(2,128)S(1)} %get-tuple-element.31), channel_id=1, source_target_pairs={{112,0},{64,16},{80,32},{96,48},{176,64},{128,80},{144,96},{160,11... | collective-permute-start | bytes 6152 | tf_op jit(solution)/shard_map/ppermute | solution.py:445
  14.4 8.2 %collective-permute-start.3 = (f32[2,256]{1,0:T(2,128)S(1)}, f32[2,256]{1,0:T(2,128)S(1)}, u32[]{:S(2)}, u32[]{:S(2)}) collective-permute-start(f32[2,256]{1,0:T(2,128)S(1)} %get-tuple-element.31), channel_id=1, source_target_pairs={{96,0},{112,16},{64,32},{80,48},{160,64},{176,80},{128,96},{144,11... | collective-permute-start | bytes 6152 | tf_op jit(solution)/shard_map/ppermute | solution.py:445
  15.7 7.7 %collective-permute-start.2 = (f32[2,256]{1,0:T(2,128)S(1)}, f32[2,256]{1,0:T(2,128)S(1)}, u32[]{:S(2)}, u32[]{:S(2)}) collective-permute-start(f32[2,256]{1,0:T(2,128)S(1)} %get-tuple-element.31), channel_id=1, source_target_pairs={{80,0},{96,16},{112,32},{64,48},{144,64},{160,80},{176,96},{128,11... | collective-permute-start | bytes 6152 | tf_op jit(solution)/shard_map/ppermute | solution.py:445
  17.0 8.0 %collective-permute-start.1 = (f32[2,256]{1,0:T(2,128)S(1)}, f32[2,256]{1,0:T(2,128)S(1)}, u32[]{:S(2)}, u32[]{:S(2)}) collective-permute-start(f32[2,256]{1,0:T(2,128)S(1)} %get-tuple-element.31), channel_id=1, source_target_pairs={{64,0},{80,16},{96,32},{112,48},{128,64},{144,80},{160,96},{176,11... | collective-permute-start | bytes 6152 | tf_op jit(solution)/shard_map/ppermute | solution.py:445
  29.3 3.2 %collective-permute-start = (bf16[64,32,128]{2,1,0:T(8,128)(2,1)S(1)}, bf16[64,32,128]{2,1,0:T(8,128)(2,1)S(1)}, u32[]{:S(2)}, u32[]{:S(2)}) collective-permute-start(bf16[64,32,128]{2,1,0:T(8,128)(2,1)S(1)} %bitcast.12), channel_id=1, source_target_pairs={{0,1},{1,0},{2,3},{3,2},{4,5},{5,4},{6,7},{7,6},{8,9},{9,8},{10,11... | collective-permute-start | bytes 1572872 | tf_op jit(solution)/shard_map/ppermute | solution.py:428
  32.5 13.3 %copy-start = (f32[1,256]{1,0:T(1,128)S(1)}, f32[1,256]{1,0:T(1,128)}, u32[]{:S(2)}) copy-start(f32[1,256]{1,0:T(1,128)} %coef_ref.5) | copy-start | bytes 3076
  58.2 4.3 %collective-permute-start.5 = (bf16[16,32,128]{2,1,0:T(8,128)(2,1)S(1)}, bf16[16,32,128]{2,1,0:T(8,128)(2,1)S(1)}, u32[]{:S(2)}, u32[]{:S(2)}) collective-permute-start(bf16[16,32,128]{2,1,0:T(8,128)(2,1)S(1)} %bitcast.27), channel_id=1, source_target_pairs={{0,1},{1,0},{2,3},{3,2},{4,5},{5,4},{6,7},{7,6},{8,9},{9,8},{10,11... | collective-permute-start | bytes 393224 | tf_op jit(solution)/shard_map/ppermute | solution.py:428
  82.7 3.9 %collective-permute-start.6 = (bf16[16,32,128]{2,1,0:T(8,128)(2,1)S(1)}, bf16[16,32,128]{2,1,0:T(8,128)(2,1)S(1)}, u32[]{:S(2)}, u32[]{:S(2)}) collective-permute-start(bf16[16,32,128]{2,1,0:T(8,128)(2,1)S(1)} %bitcast.30), channel_id=1, source_target_pairs={{0,1},{1,0},{2,3},{3,2},{4,5},{5,4},{6,7},{7,6},{8,9},{9,8},{10,11... | collective-permute-start | bytes 393224 | tf_op jit(solution)/shard_map/ppermute | solution.py:428
  106.1 3.7 %collective-permute-start.7 = (bf16[16,32,128]{2,1,0:T(8,128)(2,1)S(1)}, bf16[16,32,128]{2,1,0:T(8,128)(2,1)S(1)}, u32[]{:S(2)}, u32[]{:S(2)}) collective-permute-start(bf16[16,32,128]{2,1,0:T(8,128)(2,1)S(1)} %bitcast.33), channel_id=1, source_target_pairs={{0,1},{1,0},{2,3},{3,2},{4,5},{5,4},{6,7},{7,6},{8,9},{9,8},{10,11... | collective-permute-start | bytes 393224 | tf_op jit(solution)/shard_map/ppermute | solution.py:428
  131.3 3.8 %collective-permute-start.8 = (bf16[32,32,128]{2,1,0:T(8,128)(2,1)S(1)}, bf16[32,32,128]{2,1,0:T(8,128)(2,1)S(1)}, u32[]{:S(2)}, u32[]{:S(2)}) collective-permute-start(bf16[32,32,128]{2,1,0:T(8,128)(2,1)S(1)} %bitcast.21), channel_id=1, source_target_pairs={{0,1},{1,0},{2,3},{3,2},{4,5},{5,4},{6,7},{7,6},{8,9},{9,8},{10,11... | collective-permute-start | bytes 786440 | tf_op jit(solution)/shard_map/ppermute | solution.py:428
  156.9 4.3 %collective-permute-start.9 = (bf16[32,32,128]{2,1,0:T(8,128)(2,1)S(1)}, bf16[32,32,128]{2,1,0:T(8,128)(2,1)S(1)}, u32[]{:S(2)}, u32[]{:S(2)}) collective-permute-start(bf16[32,32,128]{2,1,0:T(8,128)(2,1)S(1)} %bitcast.24), channel_id=1, source_target_pairs={{0,1},{1,0},{2,3},{3,2},{4,5},{5,4},{6,7},{7,6},{8,9},{9,8},{10,11... | collective-permute-start | bytes 786440 | tf_op jit(solution)/shard_map/ppermute | solution.py:428
  183.3 5.3 %collective-permute-start.10 = (bf16[32,32,128]{2,1,0:T(8,128)(2,1)S(1)}, bf16[32,32,128]{2,1,0:T(8,128)(2,1)S(1)}, u32[]{:S(2)}, u32[]{:S(2)}) collective-permute-start(bf16[32,32,128]{2,1,0:T(8,128)(2,1)S(1)} %bitcast.36), channel_id=1, source_target_pairs={{0,1},{1,0},{2,3},{3,2},{4,5},{5,4},{6,7},{7,6},{8,9},{9,8},{10,11... | collective-permute-start | bytes 786440 | tf_op jit(solution)/shard_map/ppermute | solution.py:428

commit v9 on v8

--- a/solution.py
+++ b/solution.py
@@ -33,7 +33,7 @@
 ACC = (NROW * BLK + 1, W, B)
 LISTS = 9
 V0AB, V0C, TC, TAB, LA, LBC = 0, 1, 2, 3, 5, 7
-CHUNK = 3
+CHUNK = 4
 ORDER = (1, 2, 3, 2, 1)
 HALF = NCOL // 2
 
@@ -131,8 +131,16 @@
     )(col_index, *[pltpu.with_memory_space_constraint(x, pltpu.HBM) for x in ins])
 
 
+SPLIT = NT // 2
+
+
+def half_load(tiles_hbm, tiles_ref, sem, k):
+    at = pl.ds(k * SPLIT, SPLIT)
+    return pltpu.make_async_copy(tiles_hbm.at[at], tiles_ref.at[at], sem)
+
+
 def load_kernel(tiles_hbm, own_ref, tiles_ref, sem):
-    copy = pltpu.make_async_copy(tiles_hbm, tiles_ref, sem)
+    copy = half_load(tiles_hbm, tiles_ref, sem, 0)
     copy.start()
     copy.wait()
 
@@ -149,17 +157,21 @@
     )(pltpu.with_memory_space_constraint(tiles, pltpu.HBM), own)
 
 
+def apply_group(lst, which, g, sources, tiles_ref, acc):
+    rows, done = [], []
+    for u in range(UNROLL):
+        e = lst[which, g * UNROLL + u]
+        at = shr(e, 13) & 63
+        v = sources[0][at] if len(sources) == 1 else picked(shr(e, 19), *sources, at)
+        rows.append(shr(e, 7) & 63)
+        done.append(product(v, tiles_ref[e & 127]))
+    for r, d in zip(rows, done):
+        acc[r] += d
+
+
 def apply_list(lst, which, sources, tiles_ref, acc, low=0, most=NT):
     def group(g, _):
-        rows, done = [], []
-        for u in range(UNROLL):
-            e = lst[which, g * UNROLL + u]
-            at = shr(e, 13) & 63
-            v = sources[0][at] if len(sources) == 1 else picked(shr(e, 19), *sources, at)
-            rows.append(shr(e, 7) & 63)
-            done.append(product(v, tiles_ref[e & 127]))
-        for r, d in zip(rows, done):
-            acc[r] += d
+        apply_group(lst, which, g, sources, tiles_ref, acc)
         return 0
 
     groups = lst[LISTS, which]
@@ -168,8 +180,11 @@
 
 def late_start(slab, step):
     used = jnp.int32(step)
-    for active in ORDER[:step]:
-        used = used - jnp.where(slab[0] == active, jnp.int32(1), jnp.int32(0))
+    for j in range(step):
+        busy = slab[0] == ORDER[j]
+        if 0 < j < NSLAB:
+            busy = busy | (slab[0] == ORDER[j - 1])
+        used = used - jnp.where(busy, jnp.int32(1), jnp.int32(0))
     return used * CHUNK
 
 
@@ -194,43 +209,79 @@
 MESSAGE = jax.ShapeDtypeStruct((2 * NROW, TGT, W, B), BF)
 
 
-def first_kernel(lst, row, own_ref, other_ref, hot_ref, tiles_ref, acc, msg_ref):
+def first_kernel(lst, row, own_ref, other_ref, hot_ref, tiles_hbm, tiles_in, acc, tiles_ref, msg_ref, sem):
+    rest = half_load(tiles_hbm, tiles_ref, sem, 1)
+    rest.start()
     acc[...] = jnp.zeros(ACC, F32)
-    apply_list(lst, V0AB, (own_ref, other_ref), tiles_ref, acc)
+
+    def group(g, loaded):
+        late = lst[V0AB, g * UNROLL] & SPLIT
+        for u in range(1, UNROLL):
+            late = late | (lst[V0AB, g * UNROLL + u] & SPLIT)
+
+        @pl.when((late > 0) & (loaded == 0))
+        def _():
+            rest.wait()
+
+        apply_group(lst, V0AB, g, (own_ref, other_ref), tiles_ref, acc)
+        return loaded | late
+
+    loaded = lax.fori_loop(0, lst[LISTS, V0AB], group, jnp.int32(0))
+
+    @pl.when(loaded == 0)
+    def _():
+        rest.wait()
+
     write_down(acc, row, hot_ref, msg_ref)
 
 
-def first_apply(lst, row, pair, hots, tiles):
+def first_apply(lst, row, pair, hots, front, tiles):
     return pl.pallas_call(
         first_kernel,
-        out_shape=(jax.ShapeDtypeStruct(ACC, F32), MESSAGE),
-        in_specs=[smem(), smem()] + [vmem()] * 4,
-        out_specs=(vmem(), vmem()),
+        out_shape=(
+            jax.ShapeDtypeStruct(ACC, F32),
+            jax.ShapeDtypeStruct(tiles.shape, BF),
+            MESSAGE,
+        ),
+        in_specs=[smem(), smem()] + [vmem()] * 3 + [pl.BlockSpec(memory_space=pltpu.HBM), vmem()],
+        out_specs=(vmem(), vmem(), vmem()),
+        scratch_shapes=[pltpu.SemaphoreType.DMA],
+        input_output_aliases={6: 1},
         compiler_params=PARAMS,
         name="first",
-    )(lst, row, *pair, hots, tiles)
-
-
-def own_kernel(lst, slab, own_ref, own0, other0, tiles_ref, acc_in, acc, *, which, step):
-    @pl.when(slab[0] == ORDER[step])
+    )(lst, row, *pair, hots, pltpu.with_memory_space_constraint(front, pltpu.HBM), tiles)
+
+
+def own_kernel(lst, slab, own_ref, own0, other0, tiles_ref, *refs, which, step):
+    before, acc = refs[:-2], refs[-1]
+    active = slab[0] == ORDER[step]
+    after = slab[0] == ORDER[step - 1] if before else slab[0] < 0
+
+    @pl.when(active)
     def _():
         apply_list(lst, which, (own_ref,), tiles_ref, acc)
 
-    @pl.when(slab[0] != ORDER[step])
+    if before:
+        @pl.when(after)
+        def _():
+            apply_list(lst, TC, before, tiles_ref, acc)
+
+    @pl.when(jnp.logical_not(active | after))
     def _():
         apply_list(lst, V0C, (own0, other0), tiles_ref, acc, late_start(slab, step), CHUNK)
 
 
-def own_apply(lst, slab, which, own, first_pair, tiles, acc, step):
+def own_apply(lst, slab, which, own, before, first_pair, tiles, acc, step):
+    ins = (own, *first_pair, tiles, *before, acc)
     return pl.pallas_call(
         functools.partial(own_kernel, which=which, step=step),
         out_shape=jax.ShapeDtypeStruct(ACC, F32),
-        in_specs=[smem(), smem()] + [vmem()] * 5,
+        in_specs=[smem(), smem()] + [vmem()] * len(ins),
         out_specs=vmem(),
-        input_output_aliases={6: 0},
+        input_output_aliases={1 + len(ins): 0},
         compiler_params=PARAMS,
         name="own",
-    )(lst, slab, own, *first_pair, tiles, acc)
+    )(lst, slab, *ins)
 
 
 def other_kernel(lst, slab, row, other_ref, hot_ref, tiles_ref, acc_in, acc, msg_ref, *, which, step):
@@ -256,24 +307,25 @@
     )(lst, slab, row, other, hots, tiles, acc)
 
 
-def step_apply(lst, slab, row, which, pair, first_pair, hots, tiles, acc, step):
-    acc = own_apply(lst, slab, which, pair[0], first_pair, tiles, acc, step)
-    return other_apply(lst, slab, row, which, pair[1], hots, tiles, acc, step)
+def step_apply(lst, slab, row, which, pairs, first_pair, hots, tiles, acc, step):
+    own, other = pairs[-1]
+    before = pairs[-2] if 0 < step < NSLAB else ()
+    acc = own_apply(lst, slab, which, own, before, first_pair, tiles, acc, step)
+    return other_apply(lst, slab, row, which, other, hots, tiles, acc, step)
 
 
 def last_own_kernel(lst, slab, tiles_ref, own0, other0, *refs):
-    gathered, acc = refs[:11], refs[12]
-    for k, s in enumerate((1, 2, 3, 2, 1, 0)):
+    gathered, acc = refs[:5], refs[6]
+    for s in range(NSLAB - 1):
+        at = 2 * (NSLAB - 2 - s)
+
         @pl.when(slab[0] == s)
-        def _(k=k, s=s):
+        def _(s=s, at=at):
             if s == 0:
-                apply_list(lst, LA, gathered[2 * k : 2 * k + 1], tiles_ref, acc)
-            if k < NSLAB - 1:
-                apply_list(lst, TC, gathered[2 * k : 2 * k + 2], tiles_ref, acc)
-            else:
-                apply_list(lst, LBC, gathered[2 * k : 2 * k + 1], tiles_ref, acc)
-                if s > 0:
-                    apply_list(lst, LBC + 1, gathered[2 * k + 1 : 2 * k + 2], tiles_ref, acc)
+                apply_list(lst, LA, gathered[at : at + 1], tiles_ref, acc)
+            apply_list(lst, LBC, gathered[at : at + 1], tiles_ref, acc)
+            if s > 0:
+                apply_list(lst, LBC + 1, gathered[at + 1 : at + 2], tiles_ref, acc)
 
     apply_list(lst, V0C, (own0, other0), tiles_ref, acc, late_start(slab, len(ORDER)))
 
@@ -290,14 +342,14 @@
 
 
 def last_apply(lst, slab, tiles, first_pair, pairs, acc):
-    flat = [ref for pair in pairs for ref in pair]
+    flat = [ref for pair in pairs[NSLAB - 1 :] for ref in pair]
     whole = jax.ShapeDtypeStruct(ACC, F32)
     acc = pl.pallas_call(
         last_own_kernel,
         out_shape=whole,
-        in_specs=[smem(), smem()] + [vmem()] * 15,
+        in_specs=[smem(), smem()] + [vmem()] * 9,
         out_specs=vmem(),
-        input_output_aliases={16: 0},
+        input_output_aliases={10: 0},
         compiler_params=PARAMS,
         name="last_own",
     )(lst, slab, tiles, *first_pair, *flat[:-1], acc)
@@ -467,7 +519,7 @@
     start, hots, hot_next, coef_next, rhs_target, lst, tiles = lax.optimization_barrier(
         (start, hots, hot_next, coef_next, rhs_target, lst, tiles)
     )
-    acc, msg = first_apply(lst, row, start, hots, tiles)
+    acc, tiles, msg = first_apply(lst, row, start, hots, front_tiles[0], tiles)
     pairs = []
     for step in range(2 * NSLAB - 2):
         if step < NSLAB - 1:
@@ -479,7 +531,7 @@
         pairs.append(gather(value))
         if step < len(ORDER):
             which = TAB if step < NSLAB - 1 else LA
-            acc, msg = step_apply(lst, slab, row, which, pairs[-1], start, hots, tiles, acc, step)
+            acc, msg = step_apply(lst, slab, row, which, pairs, start, hots, tiles, acc, step)
     msg = last_apply(lst, slab, tiles, start, pairs, acc)
     return finish(section_blocks, lax.all_to_all(msg, "row", 0, 0, tiled=True))
 

time: 201 us -> 201 us (level)
  transfers between devices with their start and end apart: 12 -> 12, of which waited for: 7 -> 8; matrix products, arithmetic and copies ran while one was open for 0% -> 0% of each run, Pallas kernels for 6% -> 5%
where the time goes in v9:
time: 201 us; the launch traced here: 200 us
  blocking collectives  132 us (66%)
  starting transfers between devices  31.1 us (15%)
  Pallas kernels  23.3 us (12%)
  waiting for transfers between devices  12.2 us (6%)
    all_to_all x6, blocking collectives, gather(): lax.all_to_all(copies, 'col', 0, 0, tiled=True, axis_index_groups=Z_GROUPS)  70.1 us
    all_to_all x6, blocking collectives, exchange(): lax.all_to_all(message, ('slab', 'row'), 0, 0, tiled=True, axis_index_gro...  52.9 us
    ppermute x7, starting transfers between devices, gather(): return (own, lax.ppermute(own, 'col', [(c, c ^ 1) for c in range(NCOL)]))  16.9 us
    all_to_all x1, starting transfers between devices, gather(): lax.all_to_all(copies, 'col', 0, 0, tiled=True, axis_index_groups=Z_GROUPS)  9.02 us
    all_to_all x1, blocking collectives, body(): return finish(section_blocks, lax.all_to_all(msg, 'row', 0, 0, tiled=True))  8.63 us
    ppermute x4, waiting for transfers between devices, from_next(): return lax.ppermute(value, ('slab', 'row'), pairs)  6.73 us
    pallas_call x5, Pallas kernels, own_apply(): pl.pallas_call(functools.partial(own_kernel, which=which, step=step), out...  5.49 us
    ppermute x4, starting transfers between devices, from_next(): return lax.ppermute(value, ('slab', 'row'), pairs)  5.17 us
  transfers between devices with their start and end apart: 12, of which 8 were waited for; matrix products, arithmetic and copies ran while one was open for 0% of the time, Pallas kernels for 5%

profile of v9, /device:TPU:1, one launch (start us, length us, event | category | flops | bytes accessed | tf_op | source)
XLA Modules:
  0.0 199.6 jit_solution(15301067419188650497)
XLA Ops:
  2.3 9.0 %all-to-all-start = ((bf16[8,8,32,128]{3,2,1,0:T(8,128)(2,1)}), bf16[8,8,32,128]{3,2,1,0:T(8,128)(2,1)S(1)}, u32[]{:S(2)}, u32[]{:S(2)}) async-start(bf16[8,8,32,128]{3,2,1,0:T(8,128)(2,1)} %get-tuple-element.31), calls=%async_computation | async-start | bytes 1048576 | tf_op jit(solution)/shard_map/all_to_all | solution.py:478
  19.8 2.8 %collective-permute-done.3 = f32[2,256]{1,0:T(2,128)S(1)} collective-permute-done((f32[2,256]{1,0:T(2,128)S(1)}, f32[2,256]{1,0:T(2,128)S(1)}, u32[]{:S(2)}, u32[]{:S(2)}) %collective-permute-start.3) | collective-permute-done | bytes 2080 | tf_op jit(solution)/shard_map/ppermute | solution.py:497
  25.0 4.3 %all-to-all-done = bf16[8,8,32,128]{3,2,1,0:T(8,128)(2,1)S(1)} async-done(((bf16[8,8,32,128]{3,2,1,0:T(8,128)(2,1)}), bf16[8,8,32,128]{3,2,1,0:T(8,128)(2,1)S(1)}, u32[]{:S(2)}, u32[]{:S(2)}) %all-to-all-start) | async-done | bytes 524320 | tf_op jit(solution)/shard_map/all_to_all | solution.py:478
  31.9 3.8 %first.1 = (f32[33,32,128]{2,1,0:T(8,128)S(1)}, bf16[128,128,128]{2,1,0:T(8,128)(2,1)S(1)}, bf16[8,2,32,128]{3,2,1,0:T(8,128)(2,1)S(1)}) custom-call(s32[16,128]{1,0:T(8,128)S(1)} %get-tuple-element.35.lst, s32[1]{0:T(128)} %bitcast.5.row, bf16[64,32,128]{2,1,0:T(8,128)(2,1)S(1)} %bitcast.14, ...), custom_call_target="tpu_custom_call", output_to_operand_aliasing={{1}: (6, {})} | custom-call | tf_op jit(solution)/shard_map/first/pallas_call | solution.py:239
  35.7 10.3 %all_to_all.70.rcv_ref = bf16[8,2,32,128]{3,2,1,0:T(8,128)(2,1)S(1)} all-to-all(bf16[8,2,32,128]{3,2,1,0:T(8,128)(2,1)S(1)} %get-tuple-element.41), channel_id=1, replica_groups={{0,16,32,48,64,80,96,112},{128,144,160,176,192,208,224,240},{1,17,33,49..., dimensions={0} | all-to-all | bytes 262144 | tf_op jit(solution)/shard_map/all_to_all | solution.py:488
  46.0 12.1 %all_to_all.71 = bf16[8,2,32,128]{3,2,1,0:T(8,128)(2,1)S(1)} all-to-all(bf16[8,2,32,128]{3,2,1,0:T(8,128)(2,1)S(1)} %down.3), channel_id=1, replica_groups={{0,2,4,6,8,10,12,14},{1,3,5,7,9,11,13,15},{16,18,20,22,24,26,28,30},{17..., dimensions={0} | all-to-all | bytes 262144 | tf_op jit(solution)/shard_map/all_to_all | solution.py:478
  58.2 2.9 %collective-permute-start.5 = (bf16[16,32,128]{2,1,0:T(8,128)(2,1)S(1)}, bf16[16,32,128]{2,1,0:T(8,128)(2,1)S(1)}, u32[]{:S(2)}, u32[]{:S(2)}) collective-permute-start(bf16[16,32,128]{2,1,0:T(8,128)(2,1)S(1)} %bitcast.33), channel_id=1, source_target_pairs={{0,1},{1,0},{2,3},{3,2},{4,5},{5,4},{6,7},{7,6},{8,9},{9,8},{10,11... | collective-permute-start | bytes 393224 | tf_op jit(solution)/shard_map/ppermute | solution.py:480
  63.7 8.8 %all_to_all.72.rcv_ref = bf16[8,2,32,128]{3,2,1,0:T(8,128)(2,1)S(1)} all-to-all(bf16[8,2,32,128]{3,2,1,0:T(8,128)(2,1)S(1)} %get-tuple-element.44), channel_id=1, replica_groups={{64,80,96,112,128,144,160,176},{192,208,224,240,0,16,32,48},{65,81,97,1..., dimensions={0} | all-to-all | bytes 262144 | tf_op jit(solution)/shard_map/all_to_all | solution.py:488
  72.5 10.4 %all_to_all.73 = bf16[8,2,32,128]{3,2,1,0:T(8,128)(2,1)S(1)} all-to-all(bf16[8,2,32,128]{3,2,1,0:T(8,128)(2,1)S(1)} %down.4), channel_id=1, replica_groups={{0,2,4,6,8,10,12,14},{1,3,5,7,9,11,13,15},{16,18,20,22,24,26,28,30},{17..., dimensions={0} | all-to-all | bytes 262144 | tf_op jit(solution)/shard_map/all_to_all | solution.py:478
  82.9 2.4 %collective-permute-start.6 = (bf16[16,32,128]{2,1,0:T(8,128)(2,1)S(1)}, bf16[16,32,128]{2,1,0:T(8,128)(2,1)S(1)}, u32[]{:S(2)}, u32[]{:S(2)}) collective-permute-start(bf16[16,32,128]{2,1,0:T(8,128)(2,1)S(1)} %bitcast.27), channel_id=1, source_target_pairs={{0,1},{1,0},{2,3},{3,2},{4,5},{5,4},{6,7},{7,6},{8,9},{9,8},{10,11... | collective-permute-start | bytes 393224 | tf_op jit(solution)/shard_map/ppermute | solution.py:480
  88.0 7.8 %all_to_all.74.rcv_ref = bf16[8,2,32,128]{3,2,1,0:T(8,128)(2,1)S(1)} all-to-all(bf16[8,2,32,128]{3,2,1,0:T(8,128)(2,1)S(1)} %get-tuple-element.46), channel_id=1, replica_groups={{128,144,160,176,192,208,224,240},{0,16,32,48,64,80,96,112},{129,145,16..., dimensions={0} | all-to-all | bytes 262144 | tf_op jit(solution)/shard_map/all_to_all | solution.py:488
  95.9 10.3 %all_to_all.75 = bf16[8,2,32,128]{3,2,1,0:T(8,128)(2,1)S(1)} all-to-all(bf16[8,2,32,128]{3,2,1,0:T(8,128)(2,1)S(1)} %down.5), channel_id=1, replica_groups={{0,2,4,6,8,10,12,14},{1,3,5,7,9,11,13,15},{16,18,20,22,24,26,28,30},{17..., dimensions={0} | all-to-all | bytes 262144 | tf_op jit(solution)/shard_map/all_to_all | solution.py:478
  106.2 2.6 %collective-permute-start.7 = (bf16[16,32,128]{2,1,0:T(8,128)(2,1)S(1)}, bf16[16,32,128]{2,1,0:T(8,128)(2,1)S(1)}, u32[]{:S(2)}, u32[]{:S(2)}) collective-permute-start(bf16[16,32,128]{2,1,0:T(8,128)(2,1)S(1)} %bitcast.30), channel_id=1, source_target_pairs={{0,1},{1,0},{2,3},{3,2},{4,5},{5,4},{6,7},{7,6},{8,9},{9,8},{10,11... | collective-permute-start | bytes 393224 | tf_op jit(solution)/shard_map/ppermute | solution.py:480
  110.5 8.4 %all_to_all.76.rcv_ref = bf16[8,2,32,128]{3,2,1,0:T(8,128)(2,1)S(1)} all-to-all(bf16[8,2,32,128]{3,2,1,0:T(8,128)(2,1)S(1)} %get-tuple-element.48), channel_id=1, replica_groups={{128,144,160,176,192,208,224,240},{0,16,32,48,64,80,96,112},{129,145,16..., dimensions={0} | all-to-all | bytes 262144 | tf_op jit(solution)/shard_map/all_to_all | solution.py:488
  119.2 12.6 %all_to_all.77 = bf16[8,4,32,128]{3,2,1,0:T(8,128)(2,1)S(1)} all-to-all(bf16[8,4,32,128]{3,2,1,0:T(8,128)(2,1)S(1)} %up.3), channel_id=1, replica_groups={{0,2,4,6,8,10,12,14},{1,3,5,7,9,11,13,15},{16,18,20,22,24,26,28,30},{17..., dimensions={0} | all-to-all | bytes 524288 | tf_op jit(solution)/shard_map/all_to_all | solution.py:478
  131.8 2.6 %collective-permute-start.8 = (bf16[32,32,128]{2,1,0:T(8,128)(2,1)S(1)}, bf16[32,32,128]{2,1,0:T(8,128)(2,1)S(1)}, u32[]{:S(2)}, u32[]{:S(2)}) collective-permute-start(bf16[32,32,128]{2,1,0:T(8,128)(2,1)S(1)} %bitcast.21), channel_id=1, source_target_pairs={{0,1},{1,0},{2,3},{3,2},{4,5},{5,4},{6,7},{7,6},{8,9},{9,8},{10,11... | collective-permute-start | bytes 786440 | tf_op jit(solution)/shard_map/ppermute | solution.py:480
  136.2 8.8 %all_to_all.78.rcv_ref = bf16[8,2,32,128]{3,2,1,0:T(8,128)(2,1)S(1)} all-to-all(bf16[8,2,32,128]{3,2,1,0:T(8,128)(2,1)S(1)} %get-tuple-element.52), channel_id=1, replica_groups={{64,80,96,112,128,144,160,176},{192,208,224,240,0,16,32,48},{65,81,97,1..., dimensions={0} | all-to-all | bytes 262144 | tf_op jit(solution)/shard_map/all_to_all | solution.py:488
  145.2 12.0 %all_to_all.79 = bf16[8,4,32,128]{3,2,1,0:T(8,128)(2,1)S(1)} all-to-all(bf16[8,4,32,128]{3,2,1,0:T(8,128)(2,1)S(1)} %up.4), channel_id=1, replica_groups={{0,2,4,6,8,10,12,14},{1,3,5,7,9,11,13,15},{16,18,20,22,24,26,28,30},{17..., dimensions={0} | all-to-all | bytes 524288 | tf_op jit(solution)/shard_map/all_to_all | solution.py:478
  157.3 3.2 %collective-permute-start.9 = (bf16[32,32,128]{2,1,0:T(8,128)(2,1)S(1)}, bf16[32,32,128]{2,1,0:T(8,128)(2,1)S(1)}, u32[]{:S(2)}, u32[]{:S(2)}) collective-permute-start(bf16[32,32,128]{2,1,0:T(8,128)(2,1)S(1)} %bitcast.24), channel_id=1, source_target_pairs={{0,1},{1,0},{2,3},{3,2},{4,5},{5,4},{6,7},{7,6},{8,9},{9,8},{10,11... | collective-permute-start | bytes 786440 | tf_op jit(solution)/shard_map/ppermute | solution.py:480
  162.3 8.8 %all_to_all.80.rcv_ref = bf16[8,2,32,128]{3,2,1,0:T(8,128)(2,1)S(1)} all-to-all(bf16[8,2,32,128]{3,2,1,0:T(8,128)(2,1)S(1)} %get-tuple-element.54), channel_id=1, replica_groups={{0,16,32,48,64,80,96,112},{128,144,160,176,192,208,224,240},{1,17,33,49..., dimensions={0} | all-to-all | bytes 262144 | tf_op jit(solution)/shard_map/all_to_all | solution.py:488
  171.4 12.6 %all_to_all.81 = bf16[8,4,32,128]{3,2,1,0:T(8,128)(2,1)S(1)} all-to-all(bf16[8,4,32,128]{3,2,1,0:T(8,128)(2,1)S(1)} %up.5), channel_id=1, replica_groups={{0,2,4,6,8,10,12,14},{1,3,5,7,9,11,13,15},{16,18,20,22,24,26,28,30},{17..., dimensions={0} | all-to-all | bytes 524288 | tf_op jit(solution)/shard_map/all_to_all | solution.py:478
  183.9 2.6 %collective-permute-start.10 = (bf16[32,32,128]{2,1,0:T(8,128)(2,1)S(1)}, bf16[32,32,128]{2,1,0:T(8,128)(2,1)S(1)}, u32[]{:S(2)}, u32[]{:S(2)}) collective-permute-start(bf16[32,32,128]{2,1,0:T(8,128)(2,1)S(1)} %bitcast.36), channel_id=1, source_target_pairs={{0,1},{1,0},{2,3},{3,2},{4,5},{5,4},{6,7},{7,6},{8,9},{9,8},{10,11... | collective-permute-start | bytes 786440 | tf_op jit(solution)/shard_map/ppermute | solution.py:480
  186.6 2.0 last_own.1.acc_in
  190.3 8.6 %all_to_all.82.parts_ref = bf16[4,8,32,128]{3,2,1,0:T(8,128)(2,1)S(1)} all-to-all(bf16[4,8,32,128]{3,2,1,0:T(8,128)(2,1)S(1)} %get-tuple-element.56), channel_id=1, replica_groups=mesh['slab'=4,'row'=4,'col'=16] {'row'}, dimensions={0} | all-to-all | bytes 524288 | tf_op jit(solution)/shard_map/all_to_all | solution.py:536
  (46 shorter events, 28.8 us)
Async XLA Ops:
  2.3 27.0 %all-to-all-start = ((bf16[8,8,32,128]{3,2,1,0:T(8,128)(2,1)}), bf16[8,8,32,128]{3,2,1,0:T(8,128)(2,1)S(1)}, u32[]{:S(2)}, u32[]{:S(2)}) async-start(bf16[8,8,32,128]{3,2,1,0:T(8,128)(2,1)} %get-tuple-element.31), calls=%async_computation | async-start | bytes 1048576 | tf_op jit(solution)/shard_map/all_to_all | solution.py:478
  13.1 6.7 %collective-permute-start.4 = (f32[2,256]{1,0:T(2,128)S(1)}, f32[2,256]{1,0:T(2,128)S(1)}, u32[]{:S(2)}, u32[]{:S(2)}) collective-permute-start(f32[2,256]{1,0:T(2,128)S(1)} %get-tuple-element.32), channel_id=1, source_target_pairs={{112,0},{64,16},{80,32},{96,48},{176,64},{128,80},{144,96},{160,11... | collective-permute-start | bytes 6152 | tf_op jit(solution)/shard_map/ppermute | solution.py:497
  14.4 8.2 %collective-permute-start.3 = (f32[2,256]{1,0:T(2,128)S(1)}, f32[2,256]{1,0:T(2,128)S(1)}, u32[]{:S(2)}, u32[]{:S(2)}) collective-permute-start(f32[2,256]{1,0:T(2,128)S(1)} %get-tuple-element.32), channel_id=1, source_target_pairs={{96,0},{112,16},{64,32},{80,48},{160,64},{176,80},{128,96},{144,11... | collective-permute-start | bytes 6152 | tf_op jit(solution)/shard_map/ppermute | solution.py:497
  15.7 7.7 %collective-permute-start.2 = (f32[2,256]{1,0:T(2,128)S(1)}, f32[2,256]{1,0:T(2,128)S(1)}, u32[]{:S(2)}, u32[]{:S(2)}) collective-permute-start(f32[2,256]{1,0:T(2,128)S(1)} %get-tuple-element.32), channel_id=1, source_target_pairs={{80,0},{96,16},{112,32},{64,48},{144,64},{160,80},{176,96},{128,11... | collective-permute-start | bytes 6152 | tf_op jit(solution)/shard_map/ppermute | solution.py:497
  17.0 8.0 %collective-permute-start.1 = (f32[2,256]{1,0:T(2,128)S(1)}, f32[2,256]{1,0:T(2,128)S(1)}, u32[]{:S(2)}, u32[]{:S(2)}) collective-permute-start(f32[2,256]{1,0:T(2,128)S(1)} %get-tuple-element.32), channel_id=1, source_target_pairs={{64,0},{80,16},{96,32},{112,48},{128,64},{144,80},{160,96},{176,11... | collective-permute-start | bytes 6152 | tf_op jit(solution)/shard_map/ppermute | solution.py:497
  29.3 2.6 %collective-permute-start = (bf16[64,32,128]{2,1,0:T(8,128)(2,1)S(1)}, bf16[64,32,128]{2,1,0:T(8,128)(2,1)S(1)}, u32[]{:S(2)}, u32[]{:S(2)}) collective-permute-start(bf16[64,32,128]{2,1,0:T(8,128)(2,1)S(1)} %bitcast.12), channel_id=1, source_target_pairs={{0,1},{1,0},{2,3},{3,2},{4,5},{5,4},{6,7},{7,6},{8,9},{9,8},{10,11... | collective-permute-start | bytes 1572872 | tf_op jit(solution)/shard_map/ppermute | solution.py:480
  31.9 14.1 %copy-start = (f32[1,256]{1,0:T(1,128)S(1)}, f32[1,256]{1,0:T(1,128)}, u32[]{:S(2)}) copy-start(f32[1,256]{1,0:T(1,128)} %coef_ref.5) | copy-start | bytes 3076
  58.2 4.6 %collective-permute-start.5 = (bf16[16,32,128]{2,1,0:T(8,128)(2,1)S(1)}, bf16[16,32,128]{2,1,0:T(8,128)(2,1)S(1)}, u32[]{:S(2)}, u32[]{:S(2)}) collective-permute-start(bf16[16,32,128]{2,1,0:T(8,128)(2,1)S(1)} %bitcast.33), channel_id=1, source_target_pairs={{0,1},{1,0},{2,3},{3,2},{4,5},{5,4},{6,7},{7,6},{8,9},{9,8},{10,11... | collective-permute-start | bytes 393224 | tf_op jit(solution)/shard_map/ppermute | solution.py:480
  82.9 4.1 %collective-permute-start.6 = (bf16[16,32,128]{2,1,0:T(8,128)(2,1)S(1)}, bf16[16,32,128]{2,1,0:T(8,128)(2,1)S(1)}, u32[]{:S(2)}, u32[]{:S(2)}) collective-permute-start(bf16[16,32,128]{2,1,0:T(8,128)(2,1)S(1)} %bitcast.27), channel_id=1, source_target_pairs={{0,1},{1,0},{2,3},{3,2},{4,5},{5,4},{6,7},{7,6},{8,9},{9,8},{10,11... | collective-permute-start | bytes 393224 | tf_op jit(solution)/shard_map/ppermute | solution.py:480
  106.2 3.6 %collective-permute-start.7 = (bf16[16,32,128]{2,1,0:T(8,128)(2,1)S(1)}, bf16[16,32,128]{2,1,0:T(8,128)(2,1)S(1)}, u32[]{:S(2)}, u32[]{:S(2)}) collective-permute-start(bf16[16,32,128]{2,1,0:T(8,128)(2,1)S(1)} %bitcast.30), channel_id=1, source_target_pairs={{0,1},{1,0},{2,3},{3,2},{4,5},{5,4},{6,7},{7,6},{8,9},{9,8},{10,11... | collective-permute-start | bytes 393224 | tf_op jit(solution)/shard_map/ppermute | solution.py:480
  131.8 3.8 %collective-permute-start.8 = (bf16[32,32,128]{2,1,0:T(8,128)(2,1)S(1)}, bf16[32,32,128]{2,1,0:T(8,128)(2,1)S(1)}, u32[]{:S(2)}, u32[]{:S(2)}) collective-permute-start(bf16[32,32,128]{2,1,0:T(8,128)(2,1)S(1)} %bitcast.21), channel_id=1, source_target_pairs={{0,1},{1,0},{2,3},{3,2},{4,5},{5,4},{6,7},{7,6},{8,9},{9,8},{10,11... | collective-permute-start | bytes 786440 | tf_op jit(solution)/shard_map/ppermute | solution.py:480
  157.3 4.4 %collective-permute-start.9 = (bf16[32,32,128]{2,1,0:T(8,128)(2,1)S(1)}, bf16[32,32,128]{2,1,0:T(8,128)(2,1)S(1)}, u32[]{:S(2)}, u32[]{:S(2)}) collective-permute-start(bf16[32,32,128]{2,1,0:T(8,128)(2,1)S(1)} %bitcast.24), channel_id=1, source_target_pairs={{0,1},{1,0},{2,3},{3,2},{4,5},{5,4},{6,7},{7,6},{8,9},{9,8},{10,11... | collective-permute-start | bytes 786440 | tf_op jit(solution)/shard_map/ppermute | solution.py:480
  183.9 4.6 %collective-permute-start.10 = (bf16[32,32,128]{2,1,0:T(8,128)(2,1)S(1)}, bf16[32,32,128]{2,1,0:T(8,128)(2,1)S(1)}, u32[]{:S(2)}, u32[]{:S(2)}) collective-permute-start(bf16[32,32,128]{2,1,0:T(8,128)(2,1)S(1)} %bitcast.36), channel_id=1, source_target_pairs={{0,1},{1,0},{2,3},{3,2},{4,5},{5,4},{6,7},{7,6},{8,9},{9,8},{10,11... | collective-permute-start | bytes 786440 | tf_op jit(solution)/shard_map/ppermute | solution.py:480

commit v10 on v9

--- a/solution.py
+++ b/solution.py
@@ -6,6 +6,7 @@
 from jax.experimental import pallas as pl
 from jax.experimental.pallas import tpu as pltpu
 from jax.sharding import PartitionSpec as P
+
 
 B = 128
 BLK = 8
@@ -33,7 +34,7 @@
 ACC = (NROW * BLK + 1, W, B)
 LISTS = 9
 V0AB, V0C, TC, TAB, LA, LBC = 0, 1, 2, 3, 5, 7
-CHUNK = 4
+CHUNK = 3
 ORDER = (1, 2, 3, 2, 1)
 HALF = NCOL // 2
 
@@ -131,16 +132,8 @@
     )(col_index, *[pltpu.with_memory_space_constraint(x, pltpu.HBM) for x in ins])
 
 
-SPLIT = NT // 2
-
-
-def half_load(tiles_hbm, tiles_ref, sem, k):
-    at = pl.ds(k * SPLIT, SPLIT)
-    return pltpu.make_async_copy(tiles_hbm.at[at], tiles_ref.at[at], sem)
-
-
 def load_kernel(tiles_hbm, own_ref, tiles_ref, sem):
-    copy = half_load(tiles_hbm, tiles_ref, sem, 0)
+    copy = pltpu.make_async_copy(tiles_hbm, tiles_ref, sem)
     copy.start()
     copy.wait()
 
@@ -209,47 +202,21 @@
 MESSAGE = jax.ShapeDtypeStruct((2 * NROW, TGT, W, B), BF)
 
 
-def first_kernel(lst, row, own_ref, other_ref, hot_ref, tiles_hbm, tiles_in, acc, tiles_ref, msg_ref, sem):
-    rest = half_load(tiles_hbm, tiles_ref, sem, 1)
-    rest.start()
+def first_kernel(lst, row, own_ref, other_ref, hot_ref, tiles_ref, acc, msg_ref):
     acc[...] = jnp.zeros(ACC, F32)
-
-    def group(g, loaded):
-        late = lst[V0AB, g * UNROLL] & SPLIT
-        for u in range(1, UNROLL):
-            late = late | (lst[V0AB, g * UNROLL + u] & SPLIT)
-
-        @pl.when((late > 0) & (loaded == 0))
-        def _():
-            rest.wait()
-
-        apply_group(lst, V0AB, g, (own_ref, other_ref), tiles_ref, acc)
-        return loaded | late
-
-    loaded = lax.fori_loop(0, lst[LISTS, V0AB], group, jnp.int32(0))
-
-    @pl.when(loaded == 0)
-    def _():
-        rest.wait()
-
+    apply_list(lst, V0AB, (own_ref, other_ref), tiles_ref, acc)
     write_down(acc, row, hot_ref, msg_ref)
 
 
-def first_apply(lst, row, pair, hots, front, tiles):
+def first_apply(lst, row, pair, hots, tiles):
     return pl.pallas_call(
         first_kernel,
-        out_shape=(
-            jax.ShapeDtypeStruct(ACC, F32),
-            jax.ShapeDtypeStruct(tiles.shape, BF),
-            MESSAGE,
-        ),
-        in_specs=[smem(), smem()] + [vmem()] * 3 + [pl.BlockSpec(memory_space=pltpu.HBM), vmem()],
-        out_specs=(vmem(), vmem(), vmem()),
-        scratch_shapes=[pltpu.SemaphoreType.DMA],
-        input_output_aliases={6: 1},
+        out_shape=(jax.ShapeDtypeStruct(ACC, F32), MESSAGE),
+        in_specs=[smem(), smem()] + [vmem()] * 4,
+        out_specs=(vmem(), vmem()),
         compiler_params=PARAMS,
         name="first",
-    )(lst, row, *pair, hots, pltpu.with_memory_space_constraint(front, pltpu.HBM), tiles)
+    )(lst, row, *pair, hots, tiles)
 
 
 def own_kernel(lst, slab, own_ref, own0, other0, tiles_ref, *refs, which, step):
@@ -401,14 +368,13 @@
             out_ref[z, b] = value
 
 
-def combine(kernel, received, others, blocks, name):
+def combine(kernel, received, others, blocks):
     return pl.pallas_call(
         kernel,
         out_shape=jax.ShapeDtypeStruct((HALF, blocks, W, B), BF),
         in_specs=[vmem()] * (1 + len(others)),
         out_specs=vmem(),
         compiler_params=PARAMS,
-        name=name,
     )(received, *others)
 
 
@@ -504,10 +470,11 @@
     slab = slab.reshape(1)
     row = row.reshape(1)
     col = col.reshape(1)
+    others = [from_next(plane_map, d) for d in range(1, NROW)]
     lst, pack = helper(col, tile_rows, tile_cols, plane_map, interface_coef)
-    packs = [from_next(pack, d) for d in range(NROW)]
-    coef_next = packs[0][1:2]
-    maps_next = jnp.concatenate([p[0:1] for p in packs], axis=0).astype(jnp.int32)
+    pack_next = from_next(pack, 0)
+    coef_next = pack_next[1:2]
+    maps_next = jnp.concatenate([pack_next[0:1].astype(jnp.int32)] + others, axis=0)
 
     copies, rhs_target = prepare(right_sides, section_blocks, slab)
     partner = jnp.arange(PRT * B, dtype=jnp.int32)
@@ -519,15 +486,15 @@
     start, hots, hot_next, coef_next, rhs_target, lst, tiles = lax.optimization_barrier(
         (start, hots, hot_next, coef_next, rhs_target, lst, tiles)
     )
-    acc, tiles, msg = first_apply(lst, row, start, hots, front_tiles[0], tiles)
+    acc, msg = first_apply(lst, row, start, hots, tiles)
     pairs = []
     for step in range(2 * NSLAB - 2):
         if step < NSLAB - 1:
             rcv = exchange(msg, step)
-            value = combine(down_kernel, rcv, (rhs_target, interface_coef), TGT, "down")
+            value = combine(down_kernel, rcv, (rhs_target, interface_coef), TGT)
         else:
             rcv = exchange(msg, 2 * NSLAB - 3 - step)
-            value = combine(up_kernel, rcv, (coef_next, hot_next), PRT, "up")
+            value = combine(up_kernel, rcv, (coef_next, hot_next), PRT)
         pairs.append(gather(value))
         if step < len(ORDER):
             which = TAB if step < NSLAB - 1 else LA

time: 201 us -> 202 us (level)
  starting transfers between devices: 31.1 us -> 34 us
    ppermute x4, waiting for transfers between devices: 6.73 us -> 0.01 us  [from_next(): return lax.ppermute(value, ('slab', 'row'), pairs)]
    all_to_all x1, waiting for transfers between devices: 4.27 us -> 11 us  [gather(): lax.all_to_all(copies, 'col', 0, 0, tiled=True, axis_index_groups=Z_GROUPS)]
    ppermute x7, starting transfers between devices: 16.9 us -> 19.8 us  [gather(): return (own, lax.ppermute(own, 'col', [(c, c ^ 1) for c in range(NCOL)]))]
    all_to_all x6, blocking collectives: 70.1 us -> 67.8 us  [gather(): lax.all_to_all(copies, 'col', 0, 0, tiled=True, axis_index_groups=Z_GROUPS)]
  transfers between devices with their start and end apart: 12 -> 12, of which waited for: 8 -> 3; matrix products, arithmetic and copies ran while one was open for 0% -> 0% of each run, Pallas kernels for 5% -> 6%
where the time goes in v10:
time: 202 us
  blocking collectives  131 us (65%)
  starting transfers between devices  34 us (17%)
  Pallas kernels  23.1 us (11%)
  waiting for transfers between devices  12 us (6%)
    all_to_all x6, blocking collectives, gather(): lax.all_to_all(copies, 'col', 0, 0, tiled=True, axis_index_groups=Z_GROUPS)  67.8 us
    all_to_all x6, blocking collectives, exchange(): lax.all_to_all(message, ('slab', 'row'), 0, 0, tiled=True, axis_index_gro...  54.3 us
    ppermute x7, starting transfers between devices, gather(): return (own, lax.ppermute(own, 'col', [(c, c ^ 1) for c in range(NCOL)]))  19.8 us
    all_to_all x1, waiting for transfers between devices, gather(): lax.all_to_all(copies, 'col', 0, 0, tiled=True, axis_index_groups=Z_GROUPS)  11 us
    all_to_all x1, blocking collectives, body(): return finish(section_blocks, lax.all_to_all(msg, 'row', 0, 0, tiled=True))  9.18 us
    all_to_all x1, starting transfers between devices, gather(): lax.all_to_all(copies, 'col', 0, 0, tiled=True, axis_index_groups=Z_GROUPS)  9.02 us
    pallas_call x5, Pallas kernels, own_apply(): pl.pallas_call(functools.partial(own_kernel, which=which, step=step), out...  5.74 us
    ppermute x4, starting transfers between devices, from_next(): return lax.ppermute(value, ('slab', 'row'), pairs)  5.17 us
  transfers between devices with their start and end apart: 12, of which 3 were waited for; matrix products, arithmetic and copies ran while one was open for 0% of the time, Pallas kernels for 6%

profile of v10, /device:TPU:1, one launch (start us, length us, event | category | flops | bytes accessed | tf_op | source)
XLA Modules:
  0.0 201.6 jit_solution(6642657912295579269)
XLA Ops:
  2.3 9.0 %all-to-all-start = ((bf16[8,8,32,128]{3,2,1,0:T(8,128)(2,1)}), bf16[8,8,32,128]{3,2,1,0:T(8,128)(2,1)S(1)}, u32[]{:S(2)}, u32[]{:S(2)}) async-start(bf16[8,8,32,128]{3,2,1,0:T(8,128)(2,1)} %get-tuple-element.30), calls=%async_computation | async-start | bytes 1048576 | tf_op jit(solution)/shard_map/all_to_all | solution.py:444
  18.3 11.0 %all-to-all-done = bf16[8,8,32,128]{3,2,1,0:T(8,128)(2,1)S(1)} async-done(((bf16[8,8,32,128]{3,2,1,0:T(8,128)(2,1)}), bf16[8,8,32,128]{3,2,1,0:T(8,128)(2,1)S(1)}, u32[]{:S(2)}, u32[]{:S(2)}) %all-to-all-start) | async-done | bytes 524320 | tf_op jit(solution)/shard_map/all_to_all | solution.py:444
  30.3 2.2 %load.1.tiles_ref = bf16[128,128,128]{2,1,0:T(8,128)(2,1)S(1)} custom-call(bf16[128,128,128]{2,1,0:T(8,128)(2,1)} %bitcast.38, bf16[64,32,128]{2,1,0:T(8,128)(2,1)S(1)} %bitcast.13), custom_call_target="tpu_custom_call" | custom-call | tf_op jit(solution)/shard_map/load/pallas_call | solution.py:142
  32.5 3.0 %first.1 = (f32[33,32,128]{2,1,0:T(8,128)S(1)}, bf16[8,2,32,128]{3,2,1,0:T(8,128)(2,1)S(1)}) custom-call(s32[16,128]{1,0:T(8,128)S(1)} %get-tuple-element.34.lst, s32[1]{0:T(128)} %bitcast.5.row, bf16[64,32,128]{2,1,0:T(8,128)(2,1)S(1)} %bitcast.14, bf16[64,32,128]{2,1,0:T(8,128)(2,1)S(1)} %collective-permute-done.other_ref.other0, ...), custom_call_target="tpu_custom_call" | custom-call | tf_op jit(solution)/shard_map/first/pallas_call | solution.py:212
  35.5 10.8 %all_to_all.70.rcv_ref = bf16[8,2,32,128]{3,2,1,0:T(8,128)(2,1)S(1)} all-to-all(bf16[8,2,32,128]{3,2,1,0:T(8,128)(2,1)S(1)} %get-tuple-element.39), channel_id=1, replica_groups={{0,16,32,48,64,80,96,112},{128,144,160,176,192,208,224,240},{1,17,33,49..., dimensions={0} | all-to-all | bytes 262144 | tf_op jit(solution)/shard_map/all_to_all | solution.py:454
  46.4 10.3 %all_to_all.71 = bf16[8,2,32,128]{3,2,1,0:T(8,128)(2,1)S(1)} all-to-all(bf16[8,2,32,128]{3,2,1,0:T(8,128)(2,1)S(1)} %shard_map.73), channel_id=1, replica_groups={{0,2,4,6,8,10,12,14},{1,3,5,7,9,11,13,15},{16,18,20,22,24,26,28,30},{17..., dimensions={0} | all-to-all | bytes 262144 | tf_op jit(solution)/shard_map/all_to_all | solution.py:444
  56.7 5.2 %collective-permute-start.5 = (bf16[16,32,128]{2,1,0:T(8,128)(2,1)S(1)}, bf16[16,32,128]{2,1,0:T(8,128)(2,1)S(1)}, u32[]{:S(2)}, u32[]{:S(2)}) collective-permute-start(bf16[16,32,128]{2,1,0:T(8,128)(2,1)S(1)} %bitcast.33), channel_id=1, source_target_pairs={{0,1},{1,0},{2,3},{3,2},{4,5},{5,4},{6,7},{7,6},{8,9},{9,8},{10,11... | collective-permute-start | bytes 393224 | tf_op jit(solution)/shard_map/ppermute | solution.py:446
  64.3 9.6 %all_to_all.72.rcv_ref = bf16[8,2,32,128]{3,2,1,0:T(8,128)(2,1)S(1)} all-to-all(bf16[8,2,32,128]{3,2,1,0:T(8,128)(2,1)S(1)} %get-tuple-element.42), channel_id=1, replica_groups={{64,80,96,112,128,144,160,176},{192,208,224,240,0,16,32,48},{65,81,97,1..., dimensions={0} | all-to-all | bytes 262144 | tf_op jit(solution)/shard_map/all_to_all | solution.py:454
  73.9 10.4 %all_to_all.73 = bf16[8,2,32,128]{3,2,1,0:T(8,128)(2,1)S(1)} all-to-all(bf16[8,2,32,128]{3,2,1,0:T(8,128)(2,1)S(1)} %shard_map.74), channel_id=1, replica_groups={{0,2,4,6,8,10,12,14},{1,3,5,7,9,11,13,15},{16,18,20,22,24,26,28,30},{17..., dimensions={0} | all-to-all | bytes 262144 | tf_op jit(solution)/shard_map/all_to_all | solution.py:444
  84.3 2.4 %collective-permute-start.6 = (bf16[16,32,128]{2,1,0:T(8,128)(2,1)S(1)}, bf16[16,32,128]{2,1,0:T(8,128)(2,1)S(1)}, u32[]{:S(2)}, u32[]{:S(2)}) collective-permute-start(bf16[16,32,128]{2,1,0:T(8,128)(2,1)S(1)} %bitcast.27), channel_id=1, source_target_pairs={{0,1},{1,0},{2,3},{3,2},{4,5},{5,4},{6,7},{7,6},{8,9},{9,8},{10,11... | collective-permute-start | bytes 393224 | tf_op jit(solution)/shard_map/ppermute | solution.py:446
  89.2 8.2 %all_to_all.74.rcv_ref = bf16[8,2,32,128]{3,2,1,0:T(8,128)(2,1)S(1)} all-to-all(bf16[8,2,32,128]{3,2,1,0:T(8,128)(2,1)S(1)} %get-tuple-element.44), channel_id=1, replica_groups={{128,144,160,176,192,208,224,240},{0,16,32,48,64,80,96,112},{129,145,16..., dimensions={0} | all-to-all | bytes 262144 | tf_op jit(solution)/shard_map/all_to_all | solution.py:454
  97.4 10.3 %all_to_all.75 = bf16[8,2,32,128]{3,2,1,0:T(8,128)(2,1)S(1)} all-to-all(bf16[8,2,32,128]{3,2,1,0:T(8,128)(2,1)S(1)} %shard_map.75), channel_id=1, replica_groups={{0,2,4,6,8,10,12,14},{1,3,5,7,9,11,13,15},{16,18,20,22,24,26,28,30},{17..., dimensions={0} | all-to-all | bytes 262144 | tf_op jit(solution)/shard_map/all_to_all | solution.py:444
  107.7 2.7 %collective-permute-start.7 = (bf16[16,32,128]{2,1,0:T(8,128)(2,1)S(1)}, bf16[16,32,128]{2,1,0:T(8,128)(2,1)S(1)}, u32[]{:S(2)}, u32[]{:S(2)}) collective-permute-start(bf16[16,32,128]{2,1,0:T(8,128)(2,1)S(1)} %bitcast.30), channel_id=1, source_target_pairs={{0,1},{1,0},{2,3},{3,2},{4,5},{5,4},{6,7},{7,6},{8,9},{9,8},{10,11... | collective-permute-start | bytes 393224 | tf_op jit(solution)/shard_map/ppermute | solution.py:446
  112.6 7.8 %all_to_all.76.rcv_ref = bf16[8,2,32,128]{3,2,1,0:T(8,128)(2,1)S(1)} all-to-all(bf16[8,2,32,128]{3,2,1,0:T(8,128)(2,1)S(1)} %get-tuple-element.46), channel_id=1, replica_groups={{128,144,160,176,192,208,224,240},{0,16,32,48,64,80,96,112},{129,145,16..., dimensions={0} | all-to-all | bytes 262144 | tf_op jit(solution)/shard_map/all_to_all | solution.py:454
  120.6 12.6 %all_to_all.77 = bf16[8,4,32,128]{3,2,1,0:T(8,128)(2,1)S(1)} all-to-all(bf16[8,4,32,128]{3,2,1,0:T(8,128)(2,1)S(1)} %shard_map.76), channel_id=1, replica_groups={{0,2,4,6,8,10,12,14},{1,3,5,7,9,11,13,15},{16,18,20,22,24,26,28,30},{17..., dimensions={0} | all-to-all | bytes 524288 | tf_op jit(solution)/shard_map/all_to_all | solution.py:444
  133.2 2.7 %collective-permute-start.8 = (bf16[32,32,128]{2,1,0:T(8,128)(2,1)S(1)}, bf16[32,32,128]{2,1,0:T(8,128)(2,1)S(1)}, u32[]{:S(2)}, u32[]{:S(2)}) collective-permute-start(bf16[32,32,128]{2,1,0:T(8,128)(2,1)S(1)} %bitcast.21), channel_id=1, source_target_pairs={{0,1},{1,0},{2,3},{3,2},{4,5},{5,4},{6,7},{7,6},{8,9},{9,8},{10,11... | collective-permute-start | bytes 786440 | tf_op jit(solution)/shard_map/ppermute | solution.py:446
  137.7 8.8 %all_to_all.78.rcv_ref = bf16[8,2,32,128]{3,2,1,0:T(8,128)(2,1)S(1)} all-to-all(bf16[8,2,32,128]{3,2,1,0:T(8,128)(2,1)S(1)} %get-tuple-element.50), channel_id=1, replica_groups={{64,80,96,112,128,144,160,176},{192,208,224,240,0,16,32,48},{65,81,97,1..., dimensions={0} | all-to-all | bytes 262144 | tf_op jit(solution)/shard_map/all_to_all | solution.py:454
  146.7 12.0 %all_to_all.79 = bf16[8,4,32,128]{3,2,1,0:T(8,128)(2,1)S(1)} all-to-all(bf16[8,4,32,128]{3,2,1,0:T(8,128)(2,1)S(1)} %shard_map.77), channel_id=1, replica_groups={{0,2,4,6,8,10,12,14},{1,3,5,7,9,11,13,15},{16,18,20,22,24,26,28,30},{17..., dimensions={0} | all-to-all | bytes 524288 | tf_op jit(solution)/shard_map/all_to_all | solution.py:444
  158.7 3.2 %collective-permute-start.9 = (bf16[32,32,128]{2,1,0:T(8,128)(2,1)S(1)}, bf16[32,32,128]{2,1,0:T(8,128)(2,1)S(1)}, u32[]{:S(2)}, u32[]{:S(2)}) collective-permute-start(bf16[32,32,128]{2,1,0:T(8,128)(2,1)S(1)} %bitcast.24), channel_id=1, source_target_pairs={{0,1},{1,0},{2,3},{3,2},{4,5},{5,4},{6,7},{7,6},{8,9},{9,8},{10,11... | collective-permute-start | bytes 786440 | tf_op jit(solution)/shard_map/ppermute | solution.py:446
  163.8 9.0 %all_to_all.80.rcv_ref = bf16[8,2,32,128]{3,2,1,0:T(8,128)(2,1)S(1)} all-to-all(bf16[8,2,32,128]{3,2,1,0:T(8,128)(2,1)S(1)} %get-tuple-element.52), channel_id=1, replica_groups={{0,16,32,48,64,80,96,112},{128,144,160,176,192,208,224,240},{1,17,33,49..., dimensions={0} | all-to-all | bytes 262144 | tf_op jit(solution)/shard_map/all_to_all | solution.py:454
  173.0 12.1 %all_to_all.81 = bf16[8,4,32,128]{3,2,1,0:T(8,128)(2,1)S(1)} all-to-all(bf16[8,4,32,128]{3,2,1,0:T(8,128)(2,1)S(1)} %shard_map.78), channel_id=1, replica_groups={{0,2,4,6,8,10,12,14},{1,3,5,7,9,11,13,15},{16,18,20,22,24,26,28,30},{17..., dimensions={0} | all-to-all | bytes 524288 | tf_op jit(solution)/shard_map/all_to_all | solution.py:444
  185.1 3.1 %collective-permute-start.10 = (bf16[32,32,128]{2,1,0:T(8,128)(2,1)S(1)}, bf16[32,32,128]{2,1,0:T(8,128)(2,1)S(1)}, u32[]{:S(2)}, u32[]{:S(2)}) collective-permute-start(bf16[32,32,128]{2,1,0:T(8,128)(2,1)S(1)} %bitcast.36), channel_id=1, source_target_pairs={{0,1},{1,0},{2,3},{3,2},{4,5},{5,4},{6,7},{7,6},{8,9},{9,8},{10,11... | collective-permute-start | bytes 786440 | tf_op jit(solution)/shard_map/ppermute | solution.py:446
  188.2 2.0 last_own.1.acc_in
  191.7 9.2 %all_to_all.82.parts_ref = bf16[4,8,32,128]{3,2,1,0:T(8,128)(2,1)S(1)} all-to-all(bf16[4,8,32,128]{3,2,1,0:T(8,128)(2,1)S(1)} %get-tuple-element.54), channel_id=1, replica_groups=mesh['slab'=4,'row'=4,'col'=16] {'row'}, dimensions={0} | all-to-all | bytes 524288 | tf_op jit(solution)/shard_map/all_to_all | solution.py:503
  (42 shorter events, 23.0 us)
Async XLA Ops:
  2.3 27.0 %all-to-all-start = ((bf16[8,8,32,128]{3,2,1,0:T(8,128)(2,1)}), bf16[8,8,32,128]{3,2,1,0:T(8,128)(2,1)S(1)}, u32[]{:S(2)}, u32[]{:S(2)}) async-start(bf16[8,8,32,128]{3,2,1,0:T(8,128)(2,1)} %get-tuple-element.30), calls=%async_computation | async-start | bytes 1048576 | tf_op jit(solution)/shard_map/all_to_all | solution.py:444
  13.1 5.2 %collective-permute-start.1 = (f32[2,256]{1,0:T(2,128)S(1)}, f32[2,256]{1,0:T(2,128)S(1)}, u32[]{:S(2)}, u32[]{:S(2)}) collective-permute-start(f32[2,256]{1,0:T(2,128)S(1)} %get-tuple-element.31), channel_id=1, source_target_pairs={{64,0},{80,16},{96,32},{112,48},{128,64},{144,80},{160,96},{176,11... | collective-permute-start | bytes 6152 | tf_op jit(solution)/shard_map/ppermute | solution.py:463
  14.4 15.4 %collective-permute-start.2 = (s32[1,256]{1,0:T(1,128)}, s32[1,256]{1,0:T(1,128)S(1)}, u32[]{:S(2)}, u32[]{:S(2)}) collective-permute-start(s32[1,256]{1,0:T(1,128)} %map_hbm.1), channel_id=1, source_target_pairs={{80,0},{96,16},{112,32},{64,48},{144,64},{160,80},{176,96},{128,11... | collective-permute-start | bytes 3080 | tf_op jit(solution)/shard_map/ppermute | solution.py:463
  15.7 14.1 %collective-permute-start.4 = (s32[1,256]{1,0:T(1,128)}, s32[1,256]{1,0:T(1,128)S(1)}, u32[]{:S(2)}, u32[]{:S(2)}) collective-permute-start(s32[1,256]{1,0:T(1,128)} %map_hbm.1), channel_id=1, source_target_pairs={{112,0},{64,16},{80,32},{96,48},{176,64},{128,80},{144,96},{160,11... | collective-permute-start | bytes 3080 | tf_op jit(solution)/shard_map/ppermute | solution.py:463
  17.0 12.8 %collective-permute-start.3 = (s32[1,256]{1,0:T(1,128)}, s32[1,256]{1,0:T(1,128)S(1)}, u32[]{:S(2)}, u32[]{:S(2)}) collective-permute-start(s32[1,256]{1,0:T(1,128)} %map_hbm.1), channel_id=1, source_target_pairs={{96,0},{112,16},{64,32},{80,48},{160,64},{176,80},{128,96},{144,11... | collective-permute-start | bytes 3080 | tf_op jit(solution)/shard_map/ppermute | solution.py:463
  29.3 3.2 %collective-permute-start = (bf16[64,32,128]{2,1,0:T(8,128)(2,1)S(1)}, bf16[64,32,128]{2,1,0:T(8,128)(2,1)S(1)}, u32[]{:S(2)}, u32[]{:S(2)}) collective-permute-start(bf16[64,32,128]{2,1,0:T(8,128)(2,1)S(1)} %bitcast.12), channel_id=1, source_target_pairs={{0,1},{1,0},{2,3},{3,2},{4,5},{5,4},{6,7},{7,6},{8,9},{9,8},{10,11... | collective-permute-start | bytes 1572872 | tf_op jit(solution)/shard_map/ppermute | solution.py:446
  32.5 13.9 %copy-start = (f32[1,256]{1,0:T(1,128)S(1)}, f32[1,256]{1,0:T(1,128)}, u32[]{:S(2)}) copy-start(f32[1,256]{1,0:T(1,128)} %coef_ref.5) | copy-start | bytes 3076
  56.7 6.7 %collective-permute-start.5 = (bf16[16,32,128]{2,1,0:T(8,128)(2,1)S(1)}, bf16[16,32,128]{2,1,0:T(8,128)(2,1)S(1)}, u32[]{:S(2)}, u32[]{:S(2)}) collective-permute-start(bf16[16,32,128]{2,1,0:T(8,128)(2,1)S(1)} %bitcast.33), channel_id=1, source_target_pairs={{0,1},{1,0},{2,3},{3,2},{4,5},{5,4},{6,7},{7,6},{8,9},{9,8},{10,11... | collective-permute-start | bytes 393224 | tf_op jit(solution)/shard_map/ppermute | solution.py:446
  84.3 3.8 %collective-permute-start.6 = (bf16[16,32,128]{2,1,0:T(8,128)(2,1)S(1)}, bf16[16,32,128]{2,1,0:T(8,128)(2,1)S(1)}, u32[]{:S(2)}, u32[]{:S(2)}) collective-permute-start(bf16[16,32,128]{2,1,0:T(8,128)(2,1)S(1)} %bitcast.27), channel_id=1, source_target_pairs={{0,1},{1,0},{2,3},{3,2},{4,5},{5,4},{6,7},{7,6},{8,9},{9,8},{10,11... | collective-permute-start | bytes 393224 | tf_op jit(solution)/shard_map/ppermute | solution.py:446
  107.7 4.2 %collective-permute-start.7 = (bf16[16,32,128]{2,1,0:T(8,128)(2,1)S(1)}, bf16[16,32,128]{2,1,0:T(8,128)(2,1)S(1)}, u32[]{:S(2)}, u32[]{:S(2)}) collective-permute-start(bf16[16,32,128]{2,1,0:T(8,128)(2,1)S(1)} %bitcast.30), channel_id=1, source_target_pairs={{0,1},{1,0},{2,3},{3,2},{4,5},{5,4},{6,7},{7,6},{8,9},{9,8},{10,11... | collective-permute-start | bytes 393224 | tf_op jit(solution)/shard_map/ppermute | solution.py:446
  133.2 3.8 %collective-permute-start.8 = (bf16[32,32,128]{2,1,0:T(8,128)(2,1)S(1)}, bf16[32,32,128]{2,1,0:T(8,128)(2,1)S(1)}, u32[]{:S(2)}, u32[]{:S(2)}) collective-permute-start(bf16[32,32,128]{2,1,0:T(8,128)(2,1)S(1)} %bitcast.21), channel_id=1, source_target_pairs={{0,1},{1,0},{2,3},{3,2},{4,5},{5,4},{6,7},{7,6},{8,9},{9,8},{10,11... | collective-permute-start | bytes 786440 | tf_op jit(solution)/shard_map/ppermute | solution.py:446
  158.7 4.4 %collective-permute-start.9 = (bf16[32,32,128]{2,1,0:T(8,128)(2,1)S(1)}, bf16[32,32,128]{2,1,0:T(8,128)(2,1)S(1)}, u32[]{:S(2)}, u32[]{:S(2)}) collective-permute-start(bf16[32,32,128]{2,1,0:T(8,128)(2,1)S(1)} %bitcast.24), channel_id=1, source_target_pairs={{0,1},{1,0},{2,3},{3,2},{4,5},{5,4},{6,7},{7,6},{8,9},{9,8},{10,11... | collective-permute-start | bytes 786440 | tf_op jit(solution)/shard_map/ppermute | solution.py:446
  185.1 5.1 %collective-permute-start.10 = (bf16[32,32,128]{2,1,0:T(8,128)(2,1)S(1)}, bf16[32,32,128]{2,1,0:T(8,128)(2,1)S(1)}, u32[]{:S(2)}, u32[]{:S(2)}) collective-permute-start(bf16[32,32,128]{2,1,0:T(8,128)(2,1)S(1)} %bitcast.36), channel_id=1, source_target_pairs={{0,1},{1,0},{2,3},{3,2},{4,5},{5,4},{6,7},{7,6},{8,9},{9,8},{10,11... | collective-permute-start | bytes 786440 | tf_op jit(solution)/shard_map/ppermute | solution.py:446

commit v11 on v10

--- a/solution.py
+++ b/solution.py
@@ -35,6 +35,7 @@
 LISTS = 9
 V0AB, V0C, TC, TAB, LA, LBC = 0, 1, 2, 3, 5, 7
 CHUNK = 3
+EXTRA = 2
 ORDER = (1, 2, 3, 2, 1)
 HALF = NCOL // 2
 
@@ -51,21 +52,15 @@
     return jnp.where(side == 0, own_ref[at], other_ref[at])
 
 
-def helper_kernel(
-    col_index, rows_hbm, cols_hbm, map_hbm, coef_hbm, out_ref, pack_ref,
-    rows_ref, cols_ref, map_ref, coef_ref, sems,
-):
-    ins = (rows_hbm, cols_hbm, map_hbm, coef_hbm)
+def helper_kernel(col_index, rows_hbm, cols_hbm, out_ref, rows_ref, cols_ref, sems):
     copies = [
-        pltpu.make_async_copy(src, dst, sems.at[k])
-        for k, (src, dst) in enumerate(zip(ins, (rows_ref, cols_ref, map_ref, coef_ref)))
+        pltpu.make_async_copy(rows_hbm, rows_ref, sems.at[0]),
+        pltpu.make_async_copy(cols_hbm, cols_ref, sems.at[1]),
     ]
     for copy in copies:
         copy.start()
     for copy in copies:
         copy.wait()
-    pack_ref[0:1, :] = map_ref[...].astype(F32)
-    pack_ref[1:2, :] = coef_ref[...]
     lane = lax.broadcasted_iota(jnp.int32, (1, NT), 1)
     down = lax.broadcasted_iota(jnp.int32, (NT, NT), 0)
     across = lax.broadcasted_iota(jnp.int32, (NT, NT), 1)
@@ -116,17 +111,14 @@
         out_ref[k : k + 1, :] = sizes
 
 
-def helper(col_index, tile_rows, tile_cols, plane_map, interface_coef):
-    ins = (tile_rows, tile_cols, plane_map, interface_coef)
+def helper(col_index, tile_rows, tile_cols):
+    ins = (tile_rows, tile_cols)
     return pl.pallas_call(
         helper_kernel,
-        out_shape=(
-            jax.ShapeDtypeStruct((16, NT), jnp.int32),
-            jax.ShapeDtypeStruct((2, TGT * B), F32),
-        ),
-        in_specs=[smem()] + [pl.BlockSpec(memory_space=pltpu.HBM)] * 4,
-        out_specs=(vmem(), vmem()),
-        scratch_shapes=[pltpu.VMEM(x.shape, x.dtype) for x in ins] + [pltpu.SemaphoreType.DMA((4,))],
+        out_shape=jax.ShapeDtypeStruct((16, NT), jnp.int32),
+        in_specs=[smem()] + [pl.BlockSpec(memory_space=pltpu.HBM)] * 2,
+        out_specs=vmem(),
+        scratch_shapes=[pltpu.VMEM(x.shape, x.dtype) for x in ins] + [pltpu.SemaphoreType.DMA((2,))],
         compiler_params=PARAMS,
         name="helper",
     )(col_index, *[pltpu.with_memory_space_constraint(x, pltpu.HBM) for x in ins])
@@ -178,7 +170,7 @@
         if 0 < j < NSLAB:
             busy = busy | (slab[0] == ORDER[j - 1])
         used = used - jnp.where(busy, jnp.int32(1), jnp.int32(0))
-    return used * CHUNK
+    return used * (CHUNK + EXTRA)
 
 
 def write_down(acc, row, hot_ref, msg_ref):
@@ -251,10 +243,19 @@
     )(lst, slab, *ins)
 
 
-def other_kernel(lst, slab, row, other_ref, hot_ref, tiles_ref, acc_in, acc, msg_ref, *, which, step):
-    @pl.when(slab[0] == ORDER[step])
+def other_kernel(
+    lst, slab, row, other_ref, own0, other0, hot_ref, tiles_ref, acc_in, acc, msg_ref, *, which, step
+):
+    active = slab[0] == ORDER[step]
+    after = slab[0] == ORDER[step - 1] if 0 < step < NSLAB else slab[0] < 0
+
+    @pl.when(active)
     def _():
         apply_list(lst, which + 1, (other_ref,), tiles_ref, acc)
+
+    @pl.when(jnp.logical_not(active | after))
+    def _():
+        apply_list(lst, V0C, (own0, other0), tiles_ref, acc, late_start(slab, step) + CHUNK, EXTRA)
 
     if step + 1 < len(ORDER) and ORDER[step] < ORDER[step + 1]:
         write_down(acc, row, hot_ref, msg_ref)
@@ -262,23 +263,23 @@
         write_up(acc, msg_ref)
 
 
-def other_apply(lst, slab, row, which, other, hots, tiles, acc, step):
+def other_apply(lst, slab, row, which, other, first_pair, hots, tiles, acc, step):
     return pl.pallas_call(
         functools.partial(other_kernel, which=which, step=step),
         out_shape=(jax.ShapeDtypeStruct(ACC, F32), MESSAGE),
-        in_specs=[smem(), smem(), smem()] + [vmem()] * 4,
+        in_specs=[smem(), smem(), smem()] + [vmem()] * 6,
         out_specs=(vmem(), vmem()),
-        input_output_aliases={6: 0},
+        input_output_aliases={8: 0},
         compiler_params=PARAMS,
         name="other",
-    )(lst, slab, row, other, hots, tiles, acc)
+    )(lst, slab, row, other, *first_pair, hots, tiles, acc)
 
 
 def step_apply(lst, slab, row, which, pairs, first_pair, hots, tiles, acc, step):
     own, other = pairs[-1]
     before = pairs[-2] if 0 < step < NSLAB else ()
     acc = own_apply(lst, slab, which, own, before, first_pair, tiles, acc, step)
-    return other_apply(lst, slab, row, which, other, hots, tiles, acc, step)
+    return other_apply(lst, slab, row, which, other, first_pair, hots, tiles, acc, step)
 
 
 def last_own_kernel(lst, slab, tiles_ref, own0, other0, *refs):
@@ -470,11 +471,10 @@
     slab = slab.reshape(1)
     row = row.reshape(1)
     col = col.reshape(1)
-    others = [from_next(plane_map, d) for d in range(1, NROW)]
-    lst, pack = helper(col, tile_rows, tile_cols, plane_map, interface_coef)
-    pack_next = from_next(pack, 0)
-    coef_next = pack_next[1:2]
-    maps_next = jnp.concatenate([pack_next[0:1].astype(jnp.int32)] + others, axis=0)
+    maps = [from_next(plane_map, d) for d in range(NROW)]
+    coef_next = from_next(interface_coef, 0)
+    lst = helper(col, tile_rows, tile_cols)
+    maps_next = jnp.concatenate(maps, axis=0)
 
     copies, rhs_target = prepare(right_sides, section_blocks, slab)
     partner = jnp.arange(PRT * B, dtype=jnp.int32)

time: 202 us -> 202 us (level)
    ppermute x4 -> x5, starting transfers between devices: 5.17 us -> 6.45 us  [from_next(): return lax.ppermute(value, ('slab', 'row'), pairs)]
  transfers between devices with their start and end apart: 12 -> 13, of which waited for: 3 -> 4; matrix products, arithmetic and copies ran while one was open for 0% -> 0% of each run, Pallas kernels for 6% -> 5%
where the time goes in v11:
time: 202 us; the launch traced here: 201 us
  blocking collectives  132 us (65%)
  starting transfers between devices  33.7 us (17%)
  Pallas kernels  23.1 us (11%)
  waiting for transfers between devices  11 us (5%)
    all_to_all x6, blocking collectives, gather(): lax.all_to_all(copies, 'col', 0, 0, tiled=True, axis_index_groups=Z_GROUPS)  67.8 us
    all_to_all x6, blocking collectives, exchange(): lax.all_to_all(message, ('slab', 'row'), 0, 0, tiled=True, axis_index_gro...  54.7 us
    ppermute x7, starting transfers between devices, gather(): return (own, lax.ppermute(own, 'col', [(c, c ^ 1) for c in range(NCOL)]))  18.2 us
    all_to_all x1, waiting for transfers between devices, gather(): lax.all_to_all(copies, 'col', 0, 0, tiled=True, axis_index_groups=Z_GROUPS)  9.79 us
    all_to_all x1, blocking collectives, body(): return finish(section_blocks, lax.all_to_all(msg, 'row', 0, 0, tiled=True))  9.19 us
    all_to_all x1, starting transfers between devices, gather(): lax.all_to_all(copies, 'col', 0, 0, tiled=True, axis_index_groups=Z_GROUPS)  9.02 us
    ppermute x5, starting transfers between devices, from_next(): return lax.ppermute(value, ('slab', 'row'), pairs)  6.45 us
    pallas_call x5, Pallas kernels, own_apply(): pl.pallas_call(functools.partial(own_kernel, which=which, step=step), out...  4.98 us
  transfers between devices with their start and end apart: 13, of which 4 were waited for; matrix products, arithmetic and copies ran while one was open for 0% of the time, Pallas kernels for 5%

profile of v11, /device:TPU:1, one launch (start us, length us, event | category | flops | bytes accessed | tf_op | source)
XLA Modules:
  0.0 200.9 jit_solution(4401568064847704942)
XLA Ops:
  2.3 9.0 %all-to-all-start = ((bf16[8,8,32,128]{3,2,1,0:T(8,128)(2,1)}), bf16[8,8,32,128]{3,2,1,0:T(8,128)(2,1)S(1)}, u32[]{:S(2)}, u32[]{:S(2)}) async-start(bf16[8,8,32,128]{3,2,1,0:T(8,128)(2,1)} %get-tuple-element.28), calls=%async_computation | async-start | bytes 1048576 | tf_op jit(solution)/shard_map/all_to_all | solution.py:445
  19.5 9.8 %all-to-all-done = bf16[8,8,32,128]{3,2,1,0:T(8,128)(2,1)S(1)} async-done(((bf16[8,8,32,128]{3,2,1,0:T(8,128)(2,1)}), bf16[8,8,32,128]{3,2,1,0:T(8,128)(2,1)S(1)}, u32[]{:S(2)}, u32[]{:S(2)}) %all-to-all-start) | async-done | bytes 524320 | tf_op jit(solution)/shard_map/all_to_all | solution.py:445
  30.3 2.2 %load.1.tiles_ref = bf16[128,128,128]{2,1,0:T(8,128)(2,1)S(1)} custom-call(bf16[128,128,128]{2,1,0:T(8,128)(2,1)} %bitcast.43, bf16[64,32,128]{2,1,0:T(8,128)(2,1)S(1)} %bitcast.13), custom_call_target="tpu_custom_call" | custom-call | tf_op jit(solution)/shard_map/load/pallas_call | solution.py:134
  32.5 3.1 %first.1 = (f32[33,32,128]{2,1,0:T(8,128)S(1)}, bf16[8,2,32,128]{3,2,1,0:T(8,128)(2,1)S(1)}) custom-call(s32[16,128]{1,0:T(8,128)S(1)} %helper.1.lst, s32[1]{0:T(128)} %bitcast.5.row, bf16[64,32,128]{2,1,0:T(8,128)(2,1)S(1)} %bitcast.14, bf16[64,32,128]{2,1,0:T(8,128)(2,1)S(1)} %collective-permute-done.other_ref.other0, ...), custom_call_target="tpu_custom_call" | custom-call | tf_op jit(solution)/shard_map/first/pallas_call | solution.py:204
  35.6 10.8 %all_to_all.70.rcv_ref = bf16[8,2,32,128]{3,2,1,0:T(8,128)(2,1)S(1)} all-to-all(bf16[8,2,32,128]{3,2,1,0:T(8,128)(2,1)S(1)} %get-tuple-element.35), channel_id=1, replica_groups={{0,16,32,48,64,80,96,112},{128,144,160,176,192,208,224,240},{1,17,33,49..., dimensions={0} | all-to-all | bytes 262144 | tf_op jit(solution)/shard_map/all_to_all | solution.py:455
  46.4 10.3 %all_to_all.71 = bf16[8,2,32,128]{3,2,1,0:T(8,128)(2,1)S(1)} all-to-all(bf16[8,2,32,128]{3,2,1,0:T(8,128)(2,1)S(1)} %shard_map.73), channel_id=1, replica_groups={{0,2,4,6,8,10,12,14},{1,3,5,7,9,11,13,15},{16,18,20,22,24,26,28,30},{17..., dimensions={0} | all-to-all | bytes 262144 | tf_op jit(solution)/shard_map/all_to_all | solution.py:445
  56.7 3.7 %collective-permute-start.6 = (bf16[16,32,128]{2,1,0:T(8,128)(2,1)S(1)}, bf16[16,32,128]{2,1,0:T(8,128)(2,1)S(1)}, u32[]{:S(2)}, u32[]{:S(2)}) collective-permute-start(bf16[16,32,128]{2,1,0:T(8,128)(2,1)S(1)} %bitcast.38), channel_id=1, source_target_pairs={{0,1},{1,0},{2,3},{3,2},{4,5},{5,4},{6,7},{7,6},{8,9},{9,8},{10,11... | collective-permute-start | bytes 393224 | tf_op jit(solution)/shard_map/ppermute | solution.py:447
  63.4 10.0 %all_to_all.72.rcv_ref = bf16[8,2,32,128]{3,2,1,0:T(8,128)(2,1)S(1)} all-to-all(bf16[8,2,32,128]{3,2,1,0:T(8,128)(2,1)S(1)} %get-tuple-element.38), channel_id=1, replica_groups={{64,80,96,112,128,144,160,176},{192,208,224,240,0,16,32,48},{65,81,97,1..., dimensions={0} | all-to-all | bytes 262144 | tf_op jit(solution)/shard_map/all_to_all | solution.py:455
  73.4 10.4 %all_to_all.73 = bf16[8,2,32,128]{3,2,1,0:T(8,128)(2,1)S(1)} all-to-all(bf16[8,2,32,128]{3,2,1,0:T(8,128)(2,1)S(1)} %shard_map.74), channel_id=1, replica_groups={{0,2,4,6,8,10,12,14},{1,3,5,7,9,11,13,15},{16,18,20,22,24,26,28,30},{17..., dimensions={0} | all-to-all | bytes 262144 | tf_op jit(solution)/shard_map/all_to_all | solution.py:445
  83.8 2.4 %collective-permute-start.7 = (bf16[16,32,128]{2,1,0:T(8,128)(2,1)S(1)}, bf16[16,32,128]{2,1,0:T(8,128)(2,1)S(1)}, u32[]{:S(2)}, u32[]{:S(2)}) collective-permute-start(bf16[16,32,128]{2,1,0:T(8,128)(2,1)S(1)} %bitcast.32), channel_id=1, source_target_pairs={{0,1},{1,0},{2,3},{3,2},{4,5},{5,4},{6,7},{7,6},{8,9},{9,8},{10,11... | collective-permute-start | bytes 393224 | tf_op jit(solution)/shard_map/ppermute | solution.py:447
  88.9 7.9 %all_to_all.74.rcv_ref = bf16[8,2,32,128]{3,2,1,0:T(8,128)(2,1)S(1)} all-to-all(bf16[8,2,32,128]{3,2,1,0:T(8,128)(2,1)S(1)} %get-tuple-element.40), channel_id=1, replica_groups={{128,144,160,176,192,208,224,240},{0,16,32,48,64,80,96,112},{129,145,16..., dimensions={0} | all-to-all | bytes 262144 | tf_op jit(solution)/shard_map/all_to_all | solution.py:455
  96.8 10.3 %all_to_all.75 = bf16[8,2,32,128]{3,2,1,0:T(8,128)(2,1)S(1)} all-to-all(bf16[8,2,32,128]{3,2,1,0:T(8,128)(2,1)S(1)} %shard_map.75), channel_id=1, replica_groups={{0,2,4,6,8,10,12,14},{1,3,5,7,9,11,13,15},{16,18,20,22,24,26,28,30},{17..., dimensions={0} | all-to-all | bytes 262144 | tf_op jit(solution)/shard_map/all_to_all | solution.py:445
  107.2 2.7 %collective-permute-start.8 = (bf16[16,32,128]{2,1,0:T(8,128)(2,1)S(1)}, bf16[16,32,128]{2,1,0:T(8,128)(2,1)S(1)}, u32[]{:S(2)}, u32[]{:S(2)}) collective-permute-start(bf16[16,32,128]{2,1,0:T(8,128)(2,1)S(1)} %bitcast.35), channel_id=1, source_target_pairs={{0,1},{1,0},{2,3},{3,2},{4,5},{5,4},{6,7},{7,6},{8,9},{9,8},{10,11... | collective-permute-start | bytes 393224 | tf_op jit(solution)/shard_map/ppermute | solution.py:447
  111.5 8.7 %all_to_all.76.rcv_ref = bf16[8,2,32,128]{3,2,1,0:T(8,128)(2,1)S(1)} all-to-all(bf16[8,2,32,128]{3,2,1,0:T(8,128)(2,1)S(1)} %get-tuple-element.42), channel_id=1, replica_groups={{128,144,160,176,192,208,224,240},{0,16,32,48,64,80,96,112},{129,145,16..., dimensions={0} | all-to-all | bytes 262144 | tf_op jit(solution)/shard_map/all_to_all | solution.py:455
  120.4 12.6 %all_to_all.77 = bf16[8,4,32,128]{3,2,1,0:T(8,128)(2,1)S(1)} all-to-all(bf16[8,4,32,128]{3,2,1,0:T(8,128)(2,1)S(1)} %shard_map.76), channel_id=1, replica_groups={{0,2,4,6,8,10,12,14},{1,3,5,7,9,11,13,15},{16,18,20,22,24,26,28,30},{17..., dimensions={0} | all-to-all | bytes 524288 | tf_op jit(solution)/shard_map/all_to_all | solution.py:445
  133.0 2.6 %collective-permute-start.9 = (bf16[32,32,128]{2,1,0:T(8,128)(2,1)S(1)}, bf16[32,32,128]{2,1,0:T(8,128)(2,1)S(1)}, u32[]{:S(2)}, u32[]{:S(2)}) collective-permute-start(bf16[32,32,128]{2,1,0:T(8,128)(2,1)S(1)} %bitcast.26), channel_id=1, source_target_pairs={{0,1},{1,0},{2,3},{3,2},{4,5},{5,4},{6,7},{7,6},{8,9},{9,8},{10,11... | collective-permute-start | bytes 786440 | tf_op jit(solution)/shard_map/ppermute | solution.py:447
  137.5 8.8 %all_to_all.78.rcv_ref = bf16[8,2,32,128]{3,2,1,0:T(8,128)(2,1)S(1)} all-to-all(bf16[8,2,32,128]{3,2,1,0:T(8,128)(2,1)S(1)} %get-tuple-element.46), channel_id=1, replica_groups={{64,80,96,112,128,144,160,176},{192,208,224,240,0,16,32,48},{65,81,97,1..., dimensions={0} | all-to-all | bytes 262144 | tf_op jit(solution)/shard_map/all_to_all | solution.py:455
  146.5 12.0 %all_to_all.79 = bf16[8,4,32,128]{3,2,1,0:T(8,128)(2,1)S(1)} all-to-all(bf16[8,4,32,128]{3,2,1,0:T(8,128)(2,1)S(1)} %shard_map.77), channel_id=1, replica_groups={{0,2,4,6,8,10,12,14},{1,3,5,7,9,11,13,15},{16,18,20,22,24,26,28,30},{17..., dimensions={0} | all-to-all | bytes 524288 | tf_op jit(solution)/shard_map/all_to_all | solution.py:445
  158.5 3.2 %collective-permute-start.10 = (bf16[32,32,128]{2,1,0:T(8,128)(2,1)S(1)}, bf16[32,32,128]{2,1,0:T(8,128)(2,1)S(1)}, u32[]{:S(2)}, u32[]{:S(2)}) collective-permute-start(bf16[32,32,128]{2,1,0:T(8,128)(2,1)S(1)} %bitcast.29), channel_id=1, source_target_pairs={{0,1},{1,0},{2,3},{3,2},{4,5},{5,4},{6,7},{7,6},{8,9},{9,8},{10,11... | collective-permute-start | bytes 786440 | tf_op jit(solution)/shard_map/ppermute | solution.py:447
  163.6 8.5 %all_to_all.80.rcv_ref = bf16[8,2,32,128]{3,2,1,0:T(8,128)(2,1)S(1)} all-to-all(bf16[8,2,32,128]{3,2,1,0:T(8,128)(2,1)S(1)} %get-tuple-element.48), channel_id=1, replica_groups={{0,16,32,48,64,80,96,112},{128,144,160,176,192,208,224,240},{1,17,33,49..., dimensions={0} | all-to-all | bytes 262144 | tf_op jit(solution)/shard_map/all_to_all | solution.py:455
  172.3 12.1 %all_to_all.81 = bf16[8,4,32,128]{3,2,1,0:T(8,128)(2,1)S(1)} all-to-all(bf16[8,4,32,128]{3,2,1,0:T(8,128)(2,1)S(1)} %shard_map.78), channel_id=1, replica_groups={{0,2,4,6,8,10,12,14},{1,3,5,7,9,11,13,15},{16,18,20,22,24,26,28,30},{17..., dimensions={0} | all-to-all | bytes 524288 | tf_op jit(solution)/shard_map/all_to_all | solution.py:445
  184.4 3.1 %collective-permute-start.11 = (bf16[32,32,128]{2,1,0:T(8,128)(2,1)S(1)}, bf16[32,32,128]{2,1,0:T(8,128)(2,1)S(1)}, u32[]{:S(2)}, u32[]{:S(2)}) collective-permute-start(bf16[32,32,128]{2,1,0:T(8,128)(2,1)S(1)} %bitcast.41), channel_id=1, source_target_pairs={{0,1},{1,0},{2,3},{3,2},{4,5},{5,4},{6,7},{7,6},{8,9},{9,8},{10,11... | collective-permute-start | bytes 786440 | tf_op jit(solution)/shard_map/ppermute | solution.py:447
  187.6 2.0 last_own.1.acc_in
  191.0 9.2 %all_to_all.82.parts_ref = bf16[4,8,32,128]{3,2,1,0:T(8,128)(2,1)S(1)} all-to-all(bf16[4,8,32,128]{3,2,1,0:T(8,128)(2,1)S(1)} %get-tuple-element.50), channel_id=1, replica_groups=mesh['slab'=4,'row'=4,'col'=16] {'row'}, dimensions={0} | all-to-all | bytes 524288 | tf_op jit(solution)/shard_map/all_to_all | solution.py:503
  (43 shorter events, 24.5 us)
Async XLA Ops:
  2.3 27.0 %all-to-all-start = ((bf16[8,8,32,128]{3,2,1,0:T(8,128)(2,1)}), bf16[8,8,32,128]{3,2,1,0:T(8,128)(2,1)S(1)}, u32[]{:S(2)}, u32[]{:S(2)}) async-start(bf16[8,8,32,128]{3,2,1,0:T(8,128)(2,1)} %get-tuple-element.28), calls=%async_computation | async-start | bytes 1048576 | tf_op jit(solution)/shard_map/all_to_all | solution.py:445
  11.3 8.2 %collective-permute-start.2 = (s32[1,256]{1,0:T(1,128)}, s32[1,256]{1,0:T(1,128)S(1)}, u32[]{:S(2)}, u32[]{:S(2)}) collective-permute-start(s32[1,256]{1,0:T(1,128)} %param.12), channel_id=1, source_target_pairs={{80,0},{96,16},{112,32},{64,48},{144,64},{160,80},{176,96},{128,11... | collective-permute-start | bytes 3080 | tf_op jit(solution)/shard_map/ppermute | solution.py:464
  12.6 17.2 %collective-permute-start.1 = (s32[1,256]{1,0:T(1,128)}, s32[1,256]{1,0:T(1,128)S(1)}, u32[]{:S(2)}, u32[]{:S(2)}) collective-permute-start(s32[1,256]{1,0:T(1,128)} %param.12), channel_id=1, source_target_pairs={{64,0},{80,16},{96,32},{112,48},{128,64},{144,80},{160,96},{176,11... | collective-permute-start | bytes 3080 | tf_op jit(solution)/shard_map/ppermute | solution.py:464
  13.9 15.9 %collective-permute-start.4 = (s32[1,256]{1,0:T(1,128)}, s32[1,256]{1,0:T(1,128)S(1)}, u32[]{:S(2)}, u32[]{:S(2)}) collective-permute-start(s32[1,256]{1,0:T(1,128)} %param.12), channel_id=1, source_target_pairs={{112,0},{64,16},{80,32},{96,48},{176,64},{128,80},{144,96},{160,11... | collective-permute-start | bytes 3080 | tf_op jit(solution)/shard_map/ppermute | solution.py:464
  15.2 14.6 %collective-permute-start.3 = (s32[1,256]{1,0:T(1,128)}, s32[1,256]{1,0:T(1,128)S(1)}, u32[]{:S(2)}, u32[]{:S(2)}) collective-permute-start(s32[1,256]{1,0:T(1,128)} %param.12), channel_id=1, source_target_pairs={{96,0},{112,16},{64,32},{80,48},{160,64},{176,80},{128,96},{144,11... | collective-permute-start | bytes 3080 | tf_op jit(solution)/shard_map/ppermute | solution.py:464
  16.5 16.0 %collective-permute-start.5 = (f32[1,256]{1,0:T(1,128)}, f32[1,256]{1,0:T(1,128)S(1)}, u32[]{:S(2)}, u32[]{:S(2)}) collective-permute-start(f32[1,256]{1,0:T(1,128)} %coef_ref.5), channel_id=1, source_target_pairs={{64,0},{80,16},{96,32},{112,48},{128,64},{144,80},{160,96},{176,11... | collective-permute-start | bytes 3080 | tf_op jit(solution)/shard_map/ppermute | solution.py:464
  29.3 3.2 %collective-permute-start = (bf16[64,32,128]{2,1,0:T(8,128)(2,1)S(1)}, bf16[64,32,128]{2,1,0:T(8,128)(2,1)S(1)}, u32[]{:S(2)}, u32[]{:S(2)}) collective-permute-start(bf16[64,32,128]{2,1,0:T(8,128)(2,1)S(1)} %bitcast.12), channel_id=1, source_target_pairs={{0,1},{1,0},{2,3},{3,2},{4,5},{5,4},{6,7},{7,6},{8,9},{9,8},{10,11... | collective-permute-start | bytes 1572872 | tf_op jit(solution)/shard_map/ppermute | solution.py:447
  32.5 13.9 %copy-start = (f32[1,256]{1,0:T(1,128)S(1)}, f32[1,256]{1,0:T(1,128)}, u32[]{:S(2)}) copy-start(f32[1,256]{1,0:T(1,128)} %coef_ref.5) | copy-start | bytes 3076
  56.7 5.2 %collective-permute-start.6 = (bf16[16,32,128]{2,1,0:T(8,128)(2,1)S(1)}, bf16[16,32,128]{2,1,0:T(8,128)(2,1)S(1)}, u32[]{:S(2)}, u32[]{:S(2)}) collective-permute-start(bf16[16,32,128]{2,1,0:T(8,128)(2,1)S(1)} %bitcast.38), channel_id=1, source_target_pairs={{0,1},{1,0},{2,3},{3,2},{4,5},{5,4},{6,7},{7,6},{8,9},{9,8},{10,11... | collective-permute-start | bytes 393224 | tf_op jit(solution)/shard_map/ppermute | solution.py:447
  83.8 3.8 %collective-permute-start.7 = (bf16[16,32,128]{2,1,0:T(8,128)(2,1)S(1)}, bf16[16,32,128]{2,1,0:T(8,128)(2,1)S(1)}, u32[]{:S(2)}, u32[]{:S(2)}) collective-permute-start(bf16[16,32,128]{2,1,0:T(8,128)(2,1)S(1)} %bitcast.32), channel_id=1, source_target_pairs={{0,1},{1,0},{2,3},{3,2},{4,5},{5,4},{6,7},{7,6},{8,9},{9,8},{10,11... | collective-permute-start | bytes 393224 | tf_op jit(solution)/shard_map/ppermute | solution.py:447
  107.2 3.7 %collective-permute-start.8 = (bf16[16,32,128]{2,1,0:T(8,128)(2,1)S(1)}, bf16[16,32,128]{2,1,0:T(8,128)(2,1)S(1)}, u32[]{:S(2)}, u32[]{:S(2)}) collective-permute-start(bf16[16,32,128]{2,1,0:T(8,128)(2,1)S(1)} %bitcast.35), channel_id=1, source_target_pairs={{0,1},{1,0},{2,3},{3,2},{4,5},{5,4},{6,7},{7,6},{8,9},{9,8},{10,11... | collective-permute-start | bytes 393224 | tf_op jit(solution)/shard_map/ppermute | solution.py:447
  133.0 3.8 %collective-permute-start.9 = (bf16[32,32,128]{2,1,0:T(8,128)(2,1)S(1)}, bf16[32,32,128]{2,1,0:T(8,128)(2,1)S(1)}, u32[]{:S(2)}, u32[]{:S(2)}) collective-permute-start(bf16[32,32,128]{2,1,0:T(8,128)(2,1)S(1)} %bitcast.26), channel_id=1, source_target_pairs={{0,1},{1,0},{2,3},{3,2},{4,5},{5,4},{6,7},{7,6},{8,9},{9,8},{10,11... | collective-permute-start | bytes 786440 | tf_op jit(solution)/shard_map/ppermute | solution.py:447
  158.5 4.4 %collective-permute-start.10 = (bf16[32,32,128]{2,1,0:T(8,128)(2,1)S(1)}, bf16[32,32,128]{2,1,0:T(8,128)(2,1)S(1)}, u32[]{:S(2)}, u32[]{:S(2)}) collective-permute-start(bf16[32,32,128]{2,1,0:T(8,128)(2,1)S(1)} %bitcast.29), channel_id=1, source_target_pairs={{0,1},{1,0},{2,3},{3,2},{4,5},{5,4},{6,7},{7,6},{8,9},{9,8},{10,11... | collective-permute-start | bytes 786440 | tf_op jit(solution)/shard_map/ppermute | solution.py:447
  184.4 5.1 %collective-permute-start.11 = (bf16[32,32,128]{2,1,0:T(8,128)(2,1)S(1)}, bf16[32,32,128]{2,1,0:T(8,128)(2,1)S(1)}, u32[]{:S(2)}, u32[]{:S(2)}) collective-permute-start(bf16[32,32,128]{2,1,0:T(8,128)(2,1)S(1)} %bitcast.41), channel_id=1, source_target_pairs={{0,1},{1,0},{2,3},{3,2},{4,5},{5,4},{6,7},{7,6},{8,9},{9,8},{10,11... | collective-permute-start | bytes 786440 | tf_op jit(solution)/shard_map/ppermute | solution.py:447

commit v12 on v8

--- a/solution.py
+++ b/solution.py
@@ -6,6 +6,7 @@
 from jax.experimental import pallas as pl
 from jax.experimental.pallas import tpu as pltpu
 from jax.sharding import PartitionSpec as P
+
 
 B = 128
 BLK = 8
@@ -50,21 +51,7 @@
     return jnp.where(side == 0, own_ref[at], other_ref[at])
 
 
-def helper_kernel(
-    col_index, rows_hbm, cols_hbm, map_hbm, coef_hbm, out_ref, pack_ref,
-    rows_ref, cols_ref, map_ref, coef_ref, sems,
-):
-    ins = (rows_hbm, cols_hbm, map_hbm, coef_hbm)
-    copies = [
-        pltpu.make_async_copy(src, dst, sems.at[k])
-        for k, (src, dst) in enumerate(zip(ins, (rows_ref, cols_ref, map_ref, coef_ref)))
-    ]
-    for copy in copies:
-        copy.start()
-    for copy in copies:
-        copy.wait()
-    pack_ref[0:1, :] = map_ref[...].astype(F32)
-    pack_ref[1:2, :] = coef_ref[...]
+def helper_kernel(col_index, rows_ref, cols_ref, out_ref):
     lane = lax.broadcasted_iota(jnp.int32, (1, NT), 1)
     down = lax.broadcasted_iota(jnp.int32, (NT, NT), 0)
     across = lax.broadcasted_iota(jnp.int32, (NT, NT), 1)
@@ -115,20 +102,15 @@
         out_ref[k : k + 1, :] = sizes
 
 
-def helper(col_index, tile_rows, tile_cols, plane_map, interface_coef):
-    ins = (tile_rows, tile_cols, plane_map, interface_coef)
+def helper(col_index, tile_rows, tile_cols):
     return pl.pallas_call(
         helper_kernel,
-        out_shape=(
-            jax.ShapeDtypeStruct((16, NT), jnp.int32),
-            jax.ShapeDtypeStruct((2, TGT * B), F32),
-        ),
-        in_specs=[smem()] + [pl.BlockSpec(memory_space=pltpu.HBM)] * 4,
-        out_specs=(vmem(), vmem()),
-        scratch_shapes=[pltpu.VMEM(x.shape, x.dtype) for x in ins] + [pltpu.SemaphoreType.DMA((4,))],
+        out_shape=jax.ShapeDtypeStruct((16, NT), jnp.int32),
+        in_specs=[smem(), vmem(), vmem()],
+        out_specs=vmem(),
         compiler_params=PARAMS,
         name="helper",
-    )(col_index, *[pltpu.with_memory_space_constraint(x, pltpu.HBM) for x in ins])
+    )(col_index, tile_rows, tile_cols)
 
 
 def load_kernel(tiles_hbm, own_ref, tiles_ref, sem):
@@ -147,6 +129,14 @@
         compiler_params=PARAMS,
         name="load",
     )(pltpu.with_memory_space_constraint(tiles, pltpu.HBM), own)
+
+
+def products(pairs):
+    out = []
+    for (va, ta), (vb, tb) in zip(pairs[::2], pairs[1::2]):
+        both = product(jnp.concatenate([va, vb], axis=0), jnp.concatenate([ta, tb], axis=0))
+        out += [both[:W, :B], both[W:, B:]]
+    return out
 
 
 def apply_list(lst, which, sources, tiles_ref, acc, low=0, most=NT):
@@ -157,8 +147,8 @@
             at = shr(e, 13) & 63
             v = sources[0][at] if len(sources) == 1 else picked(shr(e, 19), *sources, at)
             rows.append(shr(e, 7) & 63)
-            done.append(product(v, tiles_ref[e & 127]))
-        for r, d in zip(rows, done):
+            done.append((v, tiles_ref[e & 127]))
+        for r, d in zip(rows, products(done)):
             acc[r] += d
         return 0
 
@@ -349,18 +339,21 @@
             out_ref[z, b] = value
 
 
-def combine(kernel, received, others, blocks, name):
+def combine(kernel, received, others, blocks):
     return pl.pallas_call(
         kernel,
         out_shape=jax.ShapeDtypeStruct((HALF, blocks, W, B), BF),
         in_specs=[vmem()] * (1 + len(others)),
         out_specs=vmem(),
         compiler_params=PARAMS,
-        name=name,
     )(received, *others)
 
 
-def prepare_kernel(count, slab, rhs_hbm, out_ref, target_ref, rhs_ref, sems):
+def prepare_kernel(
+    count, slab, rhs_hbm, rows_hbm, cols_hbm, map_hbm, coef_hbm,
+    out_ref, target_ref, rows_ref, cols_ref, pack_ref,
+    rhs_ref, map_ref, coef_ref, sems,
+):
     wide = 2 * B
     copies = [
         pltpu.make_async_copy(
@@ -368,7 +361,13 @@
         )
         for k in range(BLK // 2)
     ]
-    for copy in copies:
+    small = [
+        pltpu.make_async_copy(src, dst, sems.at[BLK // 2 + k])
+        for k, (src, dst) in enumerate(
+            ((rows_hbm, rows_ref), (cols_hbm, cols_ref), (map_hbm, map_ref), (coef_hbm, coef_ref))
+        )
+    ]
+    for copy in copies + small:
         copy.start()
     for b in range(BLK):
         if b % 2 == 0:
@@ -380,24 +379,34 @@
         value = jnp.where(b < count[0], value, 0.0).astype(BF)
         for z in range(HALF):
             out_ref[z, b] = value
-
-
-def prepare(right_sides, section_blocks, slab):
+    for copy in small:
+        copy.wait()
+    pack_ref[0:1, :] = map_ref[...].astype(F32)
+    pack_ref[1:2, :] = coef_ref[...]
+
+
+def prepare(right_sides, section_blocks, slab, tile_rows, tile_cols, plane_map, interface_coef):
+    ins = (right_sides, tile_rows, tile_cols, plane_map, interface_coef)
     return pl.pallas_call(
         prepare_kernel,
         out_shape=(
             jax.ShapeDtypeStruct((HALF, BLK, W, B), BF),
             jax.ShapeDtypeStruct((TGT, W, B), F32),
+            jax.ShapeDtypeStruct(tile_rows.shape, jnp.int32),
+            jax.ShapeDtypeStruct(tile_cols.shape, jnp.int32),
+            jax.ShapeDtypeStruct((2, TGT * B), F32),
         ),
-        in_specs=[smem(), smem(), pl.BlockSpec(memory_space=pltpu.HBM)],
-        out_specs=(vmem(), vmem()),
+        in_specs=[smem(), smem()] + [pl.BlockSpec(memory_space=pltpu.HBM)] * 5,
+        out_specs=(vmem(),) * 5,
         scratch_shapes=[
             pltpu.VMEM((BLK // 2, W, 2 * B), F32),
-            pltpu.SemaphoreType.DMA((BLK // 2,)),
+            pltpu.VMEM((1, TGT * B), jnp.int32),
+            pltpu.VMEM((1, TGT * B), F32),
+            pltpu.SemaphoreType.DMA((BLK // 2 + 4,)),
         ],
         compiler_params=PARAMS,
         name="prepare",
-    )(section_blocks, slab, pltpu.with_memory_space_constraint(right_sides, pltpu.HBM))
+    )(section_blocks, slab, *[pltpu.with_memory_space_constraint(x, pltpu.HBM) for x in ins])
 
 
 def finish_kernel(count, parts_ref, out_ref):
@@ -452,12 +461,14 @@
     slab = slab.reshape(1)
     row = row.reshape(1)
     col = col.reshape(1)
-    lst, pack = helper(col, tile_rows, tile_cols, plane_map, interface_coef)
+    copies, rhs_target, rows, cols, pack = prepare(
+        right_sides, section_blocks, slab, tile_rows, tile_cols, plane_map, interface_coef
+    )
     packs = [from_next(pack, d) for d in range(NROW)]
+    lst = helper(col, rows, cols)
     coef_next = packs[0][1:2]
     maps_next = jnp.concatenate([p[0:1] for p in packs], axis=0).astype(jnp.int32)
 
-    copies, rhs_target = prepare(right_sides, section_blocks, slab)
     partner = jnp.arange(PRT * B, dtype=jnp.int32)
     hots = (partner[None, :, None] == maps_next[:, None, :]).astype(BF)
     hot_next = (maps_next[0][:, None] == partner[None, :]).astype(BF)
@@ -472,10 +483,10 @@
     for step in range(2 * NSLAB - 2):
         if step < NSLAB - 1:
             rcv = exchange(msg, step)
-            value = combine(down_kernel, rcv, (rhs_target, interface_coef), TGT, "down")
+            value = combine(down_kernel, rcv, (rhs_target, interface_coef), TGT)
         else:
             rcv = exchange(msg, 2 * NSLAB - 3 - step)
-            value = combine(up_kernel, rcv, (coef_next, hot_next), PRT, "up")
+            value = combine(up_kernel, rcv, (coef_next, hot_next), PRT)
         pairs.append(gather(value))
         if step < len(ORDER):
             which = TAB if step < NSLAB - 1 else LA

time: 201 us -> 198 us (0.985)
    all_to_all x6, blocking collectives: 70.1 us -> 67.8 us  [gather(): lax.all_to_all(copies, 'col', 0, 0, tiled=True, axis_index_groups=Z_GROUPS)]
  transfers between devices with their start and end apart: 12 -> 12, of which waited for: 7 -> 7; matrix products, arithmetic and copies ran while one was open for 0% -> 0% of each run, Pallas kernels for 6% -> 5%
where the time goes in v12:
time: 198 us; the launch traced here: 197 us
  blocking collectives  130 us (66%)
  starting transfers between devices  31.4 us (16%)
  Pallas kernels  21.5 us (11%)
  waiting for transfers between devices  12.7 us (6%)
    all_to_all x6, blocking collectives, gather(): lax.all_to_all(copies, 'col', 0, 0, tiled=True, axis_index_groups=Z_GROUPS)  67.8 us
    all_to_all x6, blocking collectives, exchange(): lax.all_to_all(message, ('slab', 'row'), 0, 0, tiled=True, axis_index_gro...  53.4 us
    ppermute x7, starting transfers between devices, gather(): return (own, lax.ppermute(own, 'col', [(c, c ^ 1) for c in range(NCOL)]))  17.2 us
    all_to_all x1, blocking collectives, body(): return finish(section_blocks, lax.all_to_all(msg, 'row', 0, 0, tiled=True))  9.1 us
    all_to_all x1, starting transfers between devices, gather(): lax.all_to_all(copies, 'col', 0, 0, tiled=True, axis_index_groups=Z_GROUPS)  9.02 us
    ppermute x4, waiting for transfers between devices, from_next(): return lax.ppermute(value, ('slab', 'row'), pairs)  6.08 us
    all_to_all x1, waiting for transfers between devices, gather(): lax.all_to_all(copies, 'col', 0, 0, tiled=True, axis_index_groups=Z_GROUPS)  5.72 us
    pallas_call x5, Pallas kernels, own_apply(): pl.pallas_call(functools.partial(own_kernel, which=which, step=step), out...  5.44 us
  transfers between devices with their start and end apart: 12, of which 7 were waited for; matrix products, arithmetic and copies ran while one was open for 0% of the time, Pallas kernels for 5%

profile of v12, /device:TPU:1, one launch (start us, length us, event | category | flops | bytes accessed | tf_op | source)
XLA Modules:
  0.0 197.3 jit_solution(6196882698988943743)
XLA Ops:
  2.4 9.0 %all-to-all-start = ((bf16[8,8,32,128]{3,2,1,0:T(8,128)(2,1)}), bf16[8,8,32,128]{3,2,1,0:T(8,128)(2,1)S(1)}, u32[]{:S(2)}, u32[]{:S(2)}) async-start(bf16[8,8,32,128]{3,2,1,0:T(8,128)(2,1)} %get-tuple-element.31), calls=%async_computation | async-start | bytes 1048576 | tf_op jit(solution)/shard_map/all_to_all | solution.py:435
  17.8 3.2 %collective-permute-done.3 = f32[2,256]{1,0:T(2,128)S(1)} collective-permute-done((f32[2,256]{1,0:T(2,128)S(1)}, f32[2,256]{1,0:T(2,128)S(1)}, u32[]{:S(2)}, u32[]{:S(2)}) %collective-permute-start.3) | collective-permute-done | bytes 2080 | tf_op jit(solution)/shard_map/ppermute | solution.py:454
  23.6 5.7 %all-to-all-done = bf16[8,8,32,128]{3,2,1,0:T(8,128)(2,1)S(1)} async-done(((bf16[8,8,32,128]{3,2,1,0:T(8,128)(2,1)}), bf16[8,8,32,128]{3,2,1,0:T(8,128)(2,1)S(1)}, u32[]{:S(2)}, u32[]{:S(2)}) %all-to-all-start) | async-done | bytes 524320 | tf_op jit(solution)/shard_map/all_to_all | solution.py:435
  30.3 2.2 %load.1.tiles_ref = bf16[128,128,128]{2,1,0:T(8,128)(2,1)S(1)} custom-call(bf16[128,128,128]{2,1,0:T(8,128)(2,1)} %bitcast.38, bf16[64,32,128]{2,1,0:T(8,128)(2,1)S(1)} %bitcast.13), custom_call_target="tpu_custom_call" | custom-call | tf_op jit(solution)/shard_map/load/pallas_call | solution.py:123
  32.5 2.7 %first.1 = (f32[33,32,128]{2,1,0:T(8,128)S(1)}, bf16[8,2,32,128]{3,2,1,0:T(8,128)(2,1)S(1)}) custom-call(s32[16,128]{1,0:T(8,128)S(1)} %helper.1.lst, s32[1]{0:T(128)} %bitcast.5.row, bf16[64,32,128]{2,1,0:T(8,128)(2,1)S(1)} %bitcast.14, bf16[64,32,128]{2,1,0:T(8,128)(2,1)S(1)} %collective-permute-done.other_ref.other0, ...), custom_call_target="tpu_custom_call" | custom-call | tf_op jit(solution)/shard_map/first/pallas_call | solution.py:194
  35.3 10.7 %all_to_all.70.rcv_ref = bf16[8,2,32,128]{3,2,1,0:T(8,128)(2,1)S(1)} all-to-all(bf16[8,2,32,128]{3,2,1,0:T(8,128)(2,1)S(1)} %get-tuple-element.41), channel_id=1, replica_groups={{0,16,32,48,64,80,96,112},{128,144,160,176,192,208,224,240},{1,17,33,49..., dimensions={0} | all-to-all | bytes 262144 | tf_op jit(solution)/shard_map/all_to_all | solution.py:445
  46.0 10.3 %all_to_all.71 = bf16[8,2,32,128]{3,2,1,0:T(8,128)(2,1)S(1)} all-to-all(bf16[8,2,32,128]{3,2,1,0:T(8,128)(2,1)S(1)} %shard_map.73), channel_id=1, replica_groups={{0,2,4,6,8,10,12,14},{1,3,5,7,9,11,13,15},{16,18,20,22,24,26,28,30},{17..., dimensions={0} | all-to-all | bytes 262144 | tf_op jit(solution)/shard_map/all_to_all | solution.py:435
  56.4 2.7 %collective-permute-start.5 = (bf16[16,32,128]{2,1,0:T(8,128)(2,1)S(1)}, bf16[16,32,128]{2,1,0:T(8,128)(2,1)S(1)}, u32[]{:S(2)}, u32[]{:S(2)}) collective-permute-start(bf16[16,32,128]{2,1,0:T(8,128)(2,1)S(1)} %bitcast.27), channel_id=1, source_target_pairs={{0,1},{1,0},{2,3},{3,2},{4,5},{5,4},{6,7},{7,6},{8,9},{9,8},{10,11... | collective-permute-start | bytes 393224 | tf_op jit(solution)/shard_map/ppermute | solution.py:437
  61.4 8.8 %all_to_all.72.rcv_ref = bf16[8,2,32,128]{3,2,1,0:T(8,128)(2,1)S(1)} all-to-all(bf16[8,2,32,128]{3,2,1,0:T(8,128)(2,1)S(1)} %get-tuple-element.44), channel_id=1, replica_groups={{64,80,96,112,128,144,160,176},{192,208,224,240,0,16,32,48},{65,81,97,1..., dimensions={0} | all-to-all | bytes 262144 | tf_op jit(solution)/shard_map/all_to_all | solution.py:445
  70.2 10.4 %all_to_all.73 = bf16[8,2,32,128]{3,2,1,0:T(8,128)(2,1)S(1)} all-to-all(bf16[8,2,32,128]{3,2,1,0:T(8,128)(2,1)S(1)} %shard_map.74), channel_id=1, replica_groups={{0,2,4,6,8,10,12,14},{1,3,5,7,9,11,13,15},{16,18,20,22,24,26,28,30},{17..., dimensions={0} | all-to-all | bytes 262144 | tf_op jit(solution)/shard_map/all_to_all | solution.py:435
  80.6 2.4 %collective-permute-start.6 = (bf16[16,32,128]{2,1,0:T(8,128)(2,1)S(1)}, bf16[16,32,128]{2,1,0:T(8,128)(2,1)S(1)}, u32[]{:S(2)}, u32[]{:S(2)}) collective-permute-start(bf16[16,32,128]{2,1,0:T(8,128)(2,1)S(1)} %bitcast.30), channel_id=1, source_target_pairs={{0,1},{1,0},{2,3},{3,2},{4,5},{5,4},{6,7},{7,6},{8,9},{9,8},{10,11... | collective-permute-start | bytes 393224 | tf_op jit(solution)/shard_map/ppermute | solution.py:437
  85.3 8.1 %all_to_all.74.rcv_ref = bf16[8,2,32,128]{3,2,1,0:T(8,128)(2,1)S(1)} all-to-all(bf16[8,2,32,128]{3,2,1,0:T(8,128)(2,1)S(1)} %get-tuple-element.46), channel_id=1, replica_groups={{128,144,160,176,192,208,224,240},{0,16,32,48,64,80,96,112},{129,145,16..., dimensions={0} | all-to-all | bytes 262144 | tf_op jit(solution)/shard_map/all_to_all | solution.py:445
  93.5 10.4 %all_to_all.75 = bf16[8,2,32,128]{3,2,1,0:T(8,128)(2,1)S(1)} all-to-all(bf16[8,2,32,128]{3,2,1,0:T(8,128)(2,1)S(1)} %shard_map.75), channel_id=1, replica_groups={{0,2,4,6,8,10,12,14},{1,3,5,7,9,11,13,15},{16,18,20,22,24,26,28,30},{17..., dimensions={0} | all-to-all | bytes 262144 | tf_op jit(solution)/shard_map/all_to_all | solution.py:435
  103.9 2.5 %collective-permute-start.7 = (bf16[16,32,128]{2,1,0:T(8,128)(2,1)S(1)}, bf16[16,32,128]{2,1,0:T(8,128)(2,1)S(1)}, u32[]{:S(2)}, u32[]{:S(2)}) collective-permute-start(bf16[16,32,128]{2,1,0:T(8,128)(2,1)S(1)} %bitcast.33), channel_id=1, source_target_pairs={{0,1},{1,0},{2,3},{3,2},{4,5},{5,4},{6,7},{7,6},{8,9},{9,8},{10,11... | collective-permute-start | bytes 393224 | tf_op jit(solution)/shard_map/ppermute | solution.py:437
  108.4 7.8 %all_to_all.76.rcv_ref = bf16[8,2,32,128]{3,2,1,0:T(8,128)(2,1)S(1)} all-to-all(bf16[8,2,32,128]{3,2,1,0:T(8,128)(2,1)S(1)} %get-tuple-element.48), channel_id=1, replica_groups={{128,144,160,176,192,208,224,240},{0,16,32,48,64,80,96,112},{129,145,16..., dimensions={0} | all-to-all | bytes 262144 | tf_op jit(solution)/shard_map/all_to_all | solution.py:445
  116.4 12.6 %all_to_all.77 = bf16[8,4,32,128]{3,2,1,0:T(8,128)(2,1)S(1)} all-to-all(bf16[8,4,32,128]{3,2,1,0:T(8,128)(2,1)S(1)} %shard_map.76), channel_id=1, replica_groups={{0,2,4,6,8,10,12,14},{1,3,5,7,9,11,13,15},{16,18,20,22,24,26,28,30},{17..., dimensions={0} | all-to-all | bytes 524288 | tf_op jit(solution)/shard_map/all_to_all | solution.py:435
  129.0 2.7 %collective-permute-start.8 = (bf16[32,32,128]{2,1,0:T(8,128)(2,1)S(1)}, bf16[32,32,128]{2,1,0:T(8,128)(2,1)S(1)}, u32[]{:S(2)}, u32[]{:S(2)}) collective-permute-start(bf16[32,32,128]{2,1,0:T(8,128)(2,1)S(1)} %bitcast.21), channel_id=1, source_target_pairs={{0,1},{1,0},{2,3},{3,2},{4,5},{5,4},{6,7},{7,6},{8,9},{9,8},{10,11... | collective-permute-start | bytes 786440 | tf_op jit(solution)/shard_map/ppermute | solution.py:437
  133.5 8.8 %all_to_all.78.rcv_ref = bf16[8,2,32,128]{3,2,1,0:T(8,128)(2,1)S(1)} all-to-all(bf16[8,2,32,128]{3,2,1,0:T(8,128)(2,1)S(1)} %get-tuple-element.52), channel_id=1, replica_groups={{64,80,96,112,128,144,160,176},{192,208,224,240,0,16,32,48},{65,81,97,1..., dimensions={0} | all-to-all | bytes 262144 | tf_op jit(solution)/shard_map/all_to_all | solution.py:445
  142.6 12.0 %all_to_all.79 = bf16[8,4,32,128]{3,2,1,0:T(8,128)(2,1)S(1)} all-to-all(bf16[8,4,32,128]{3,2,1,0:T(8,128)(2,1)S(1)} %shard_map.77), channel_id=1, replica_groups={{0,2,4,6,8,10,12,14},{1,3,5,7,9,11,13,15},{16,18,20,22,24,26,28,30},{17..., dimensions={0} | all-to-all | bytes 524288 | tf_op jit(solution)/shard_map/all_to_all | solution.py:435
  154.6 3.2 %collective-permute-start.9 = (bf16[32,32,128]{2,1,0:T(8,128)(2,1)S(1)}, bf16[32,32,128]{2,1,0:T(8,128)(2,1)S(1)}, u32[]{:S(2)}, u32[]{:S(2)}) collective-permute-start(bf16[32,32,128]{2,1,0:T(8,128)(2,1)S(1)} %bitcast.24), channel_id=1, source_target_pairs={{0,1},{1,0},{2,3},{3,2},{4,5},{5,4},{6,7},{7,6},{8,9},{9,8},{10,11... | collective-permute-start | bytes 786440 | tf_op jit(solution)/shard_map/ppermute | solution.py:437
  159.6 9.1 %all_to_all.80.rcv_ref = bf16[8,2,32,128]{3,2,1,0:T(8,128)(2,1)S(1)} all-to-all(bf16[8,2,32,128]{3,2,1,0:T(8,128)(2,1)S(1)} %get-tuple-element.54), channel_id=1, replica_groups={{0,16,32,48,64,80,96,112},{128,144,160,176,192,208,224,240},{1,17,33,49..., dimensions={0} | all-to-all | bytes 262144 | tf_op jit(solution)/shard_map/all_to_all | solution.py:445
  169.0 12.0 %all_to_all.81 = bf16[8,4,32,128]{3,2,1,0:T(8,128)(2,1)S(1)} all-to-all(bf16[8,4,32,128]{3,2,1,0:T(8,128)(2,1)S(1)} %shard_map.78), channel_id=1, replica_groups={{0,2,4,6,8,10,12,14},{1,3,5,7,9,11,13,15},{16,18,20,22,24,26,28,30},{17..., dimensions={0} | all-to-all | bytes 524288 | tf_op jit(solution)/shard_map/all_to_all | solution.py:435
  181.0 3.2 %collective-permute-start.10 = (bf16[32,32,128]{2,1,0:T(8,128)(2,1)S(1)}, bf16[32,32,128]{2,1,0:T(8,128)(2,1)S(1)}, u32[]{:S(2)}, u32[]{:S(2)}) collective-permute-start(bf16[32,32,128]{2,1,0:T(8,128)(2,1)S(1)} %bitcast.36), channel_id=1, source_target_pairs={{0,1},{1,0},{2,3},{3,2},{4,5},{5,4},{6,7},{7,6},{8,9},{9,8},{10,11... | collective-permute-start | bytes 786440 | tf_op jit(solution)/shard_map/ppermute | solution.py:437
  187.5 9.1 %all_to_all.82.parts_ref = bf16[4,8,32,128]{3,2,1,0:T(8,128)(2,1)S(1)} all-to-all(bf16[4,8,32,128]{3,2,1,0:T(8,128)(2,1)S(1)} %get-tuple-element.56), channel_id=1, replica_groups=mesh['slab'=4,'row'=4,'col'=16] {'row'}, dimensions={0} | all-to-all | bytes 524288 | tf_op jit(solution)/shard_map/all_to_all | solution.py:495
  (46 shorter events, 26.5 us)
Async XLA Ops:
  2.4 27.0 %all-to-all-start = ((bf16[8,8,32,128]{3,2,1,0:T(8,128)(2,1)}), bf16[8,8,32,128]{3,2,1,0:T(8,128)(2,1)S(1)}, u32[]{:S(2)}, u32[]{:S(2)}) async-start(bf16[8,8,32,128]{3,2,1,0:T(8,128)(2,1)} %get-tuple-element.31), calls=%async_computation | async-start | bytes 1048576 | tf_op jit(solution)/shard_map/all_to_all | solution.py:435
  11.4 6.4 %collective-permute-start.4 = (f32[2,256]{1,0:T(2,128)S(1)}, f32[2,256]{1,0:T(2,128)S(1)}, u32[]{:S(2)}, u32[]{:S(2)}) collective-permute-start(f32[2,256]{1,0:T(2,128)S(1)} %get-tuple-element.32), channel_id=1, source_target_pairs={{112,0},{64,16},{80,32},{96,48},{176,64},{128,80},{144,96},{160,11... | collective-permute-start | bytes 6152 | tf_op jit(solution)/shard_map/ppermute | solution.py:454
  12.7 8.3 %collective-permute-start.3 = (f32[2,256]{1,0:T(2,128)S(1)}, f32[2,256]{1,0:T(2,128)S(1)}, u32[]{:S(2)}, u32[]{:S(2)}) collective-permute-start(f32[2,256]{1,0:T(2,128)S(1)} %get-tuple-element.32), channel_id=1, source_target_pairs={{96,0},{112,16},{64,32},{80,48},{160,64},{176,80},{128,96},{144,11... | collective-permute-start | bytes 6152 | tf_op jit(solution)/shard_map/ppermute | solution.py:454
  14.0 7.7 %collective-permute-start.2 = (f32[2,256]{1,0:T(2,128)S(1)}, f32[2,256]{1,0:T(2,128)S(1)}, u32[]{:S(2)}, u32[]{:S(2)}) collective-permute-start(f32[2,256]{1,0:T(2,128)S(1)} %get-tuple-element.32), channel_id=1, source_target_pairs={{80,0},{96,16},{112,32},{64,48},{144,64},{160,80},{176,96},{128,11... | collective-permute-start | bytes 6152 | tf_op jit(solution)/shard_map/ppermute | solution.py:454
  15.3 8.3 %collective-permute-start.1 = (f32[2,256]{1,0:T(2,128)S(1)}, f32[2,256]{1,0:T(2,128)S(1)}, u32[]{:S(2)}, u32[]{:S(2)}) collective-permute-start(f32[2,256]{1,0:T(2,128)S(1)} %get-tuple-element.32), channel_id=1, source_target_pairs={{64,0},{80,16},{96,32},{112,48},{128,64},{144,80},{160,96},{176,11... | collective-permute-start | bytes 6152 | tf_op jit(solution)/shard_map/ppermute | solution.py:454
  29.3 3.2 %collective-permute-start = (bf16[64,32,128]{2,1,0:T(8,128)(2,1)S(1)}, bf16[64,32,128]{2,1,0:T(8,128)(2,1)S(1)}, u32[]{:S(2)}, u32[]{:S(2)}) collective-permute-start(bf16[64,32,128]{2,1,0:T(8,128)(2,1)S(1)} %bitcast.12), channel_id=1, source_target_pairs={{0,1},{1,0},{2,3},{3,2},{4,5},{5,4},{6,7},{7,6},{8,9},{9,8},{10,11... | collective-permute-start | bytes 1572872 | tf_op jit(solution)/shard_map/ppermute | solution.py:437
  32.5 13.5 %copy-start = (f32[1,256]{1,0:T(1,128)S(1)}, f32[1,256]{1,0:T(1,128)}, u32[]{:S(2)}) copy-start(f32[1,256]{1,0:T(1,128)} %coef_ref.5) | copy-start | bytes 3076
  56.4 4.0 %collective-permute-start.5 = (bf16[16,32,128]{2,1,0:T(8,128)(2,1)S(1)}, bf16[16,32,128]{2,1,0:T(8,128)(2,1)S(1)}, u32[]{:S(2)}, u32[]{:S(2)}) collective-permute-start(bf16[16,32,128]{2,1,0:T(8,128)(2,1)S(1)} %bitcast.27), channel_id=1, source_target_pairs={{0,1},{1,0},{2,3},{3,2},{4,5},{5,4},{6,7},{7,6},{8,9},{9,8},{10,11... | collective-permute-start | bytes 393224 | tf_op jit(solution)/shard_map/ppermute | solution.py:437
  80.6 3.8 %collective-permute-start.6 = (bf16[16,32,128]{2,1,0:T(8,128)(2,1)S(1)}, bf16[16,32,128]{2,1,0:T(8,128)(2,1)S(1)}, u32[]{:S(2)}, u32[]{:S(2)}) collective-permute-start(bf16[16,32,128]{2,1,0:T(8,128)(2,1)S(1)} %bitcast.30), channel_id=1, source_target_pairs={{0,1},{1,0},{2,3},{3,2},{4,5},{5,4},{6,7},{7,6},{8,9},{9,8},{10,11... | collective-permute-start | bytes 393224 | tf_op jit(solution)/shard_map/ppermute | solution.py:437
  103.9 3.8 %collective-permute-start.7 = (bf16[16,32,128]{2,1,0:T(8,128)(2,1)S(1)}, bf16[16,32,128]{2,1,0:T(8,128)(2,1)S(1)}, u32[]{:S(2)}, u32[]{:S(2)}) collective-permute-start(bf16[16,32,128]{2,1,0:T(8,128)(2,1)S(1)} %bitcast.33), channel_id=1, source_target_pairs={{0,1},{1,0},{2,3},{3,2},{4,5},{5,4},{6,7},{7,6},{8,9},{9,8},{10,11... | collective-permute-start | bytes 393224 | tf_op jit(solution)/shard_map/ppermute | solution.py:437
  129.0 3.8 %collective-permute-start.8 = (bf16[32,32,128]{2,1,0:T(8,128)(2,1)S(1)}, bf16[32,32,128]{2,1,0:T(8,128)(2,1)S(1)}, u32[]{:S(2)}, u32[]{:S(2)}) collective-permute-start(bf16[32,32,128]{2,1,0:T(8,128)(2,1)S(1)} %bitcast.21), channel_id=1, source_target_pairs={{0,1},{1,0},{2,3},{3,2},{4,5},{5,4},{6,7},{7,6},{8,9},{9,8},{10,11... | collective-permute-start | bytes 786440 | tf_op jit(solution)/shard_map/ppermute | solution.py:437
  154.6 4.4 %collective-permute-start.9 = (bf16[32,32,128]{2,1,0:T(8,128)(2,1)S(1)}, bf16[32,32,128]{2,1,0:T(8,128)(2,1)S(1)}, u32[]{:S(2)}, u32[]{:S(2)}) collective-permute-start(bf16[32,32,128]{2,1,0:T(8,128)(2,1)S(1)} %bitcast.24), channel_id=1, source_target_pairs={{0,1},{1,0},{2,3},{3,2},{4,5},{5,4},{6,7},{7,6},{8,9},{9,8},{10,11... | collective-permute-start | bytes 786440 | tf_op jit(solution)/shard_map/ppermute | solution.py:437
  181.0 5.1 %collective-permute-start.10 = (bf16[32,32,128]{2,1,0:T(8,128)(2,1)S(1)}, bf16[32,32,128]{2,1,0:T(8,128)(2,1)S(1)}, u32[]{:S(2)}, u32[]{:S(2)}) collective-permute-start(bf16[32,32,128]{2,1,0:T(8,128)(2,1)S(1)} %bitcast.36), channel_id=1, source_target_pairs={{0,1},{1,0},{2,3},{3,2},{4,5},{5,4},{6,7},{7,6},{8,9},{9,8},{10,11... | collective-permute-start | bytes 786440 | tf_op jit(solution)/shard_map/ppermute | solution.py:437

commit v13 on v12

--- a/solution.py
+++ b/solution.py
@@ -158,8 +158,11 @@
 
 def late_start(slab, step):
     used = jnp.int32(step)
-    for active in ORDER[:step]:
-        used = used - jnp.where(slab[0] == active, jnp.int32(1), jnp.int32(0))
+    for j in range(step):
+        busy = slab[0] == ORDER[j]
+        if 0 < j < NSLAB:
+            busy = busy | (slab[0] == ORDER[j - 1])
+        used = used - jnp.where(busy, jnp.int32(1), jnp.int32(0))
     return used * CHUNK
 
 
@@ -201,26 +204,36 @@
     )(lst, row, *pair, hots, tiles)
 
 
-def own_kernel(lst, slab, own_ref, own0, other0, tiles_ref, acc_in, acc, *, which, step):
-    @pl.when(slab[0] == ORDER[step])
+def own_kernel(lst, slab, own_ref, own0, other0, tiles_ref, *refs, which, step):
+    before, acc = refs[:-2], refs[-1]
+    active = slab[0] == ORDER[step]
+    after = slab[0] == ORDER[step - 1] if before else slab[0] < 0
+
+    @pl.when(active)
     def _():
         apply_list(lst, which, (own_ref,), tiles_ref, acc)
 
-    @pl.when(slab[0] != ORDER[step])
+    if before:
+        @pl.when(after)
+        def _():
+            apply_list(lst, TC, before, tiles_ref, acc)
+
+    @pl.when(jnp.logical_not(active | after))
     def _():
         apply_list(lst, V0C, (own0, other0), tiles_ref, acc, late_start(slab, step), CHUNK)
 
 
-def own_apply(lst, slab, which, own, first_pair, tiles, acc, step):
+def own_apply(lst, slab, which, own, before, first_pair, tiles, acc, step):
+    ins = (own, *first_pair, tiles, *before, acc)
     return pl.pallas_call(
         functools.partial(own_kernel, which=which, step=step),
         out_shape=jax.ShapeDtypeStruct(ACC, F32),
-        in_specs=[smem(), smem()] + [vmem()] * 5,
+        in_specs=[smem(), smem()] + [vmem()] * len(ins),
         out_specs=vmem(),
-        input_output_aliases={6: 0},
+        input_output_aliases={1 + len(ins): 0},
         compiler_params=PARAMS,
         name="own",
-    )(lst, slab, own, *first_pair, tiles, acc)
+    )(lst, slab, *ins)
 
 
 def other_kernel(lst, slab, row, other_ref, hot_ref, tiles_ref, acc_in, acc, msg_ref, *, which, step):
@@ -246,24 +259,25 @@
     )(lst, slab, row, other, hots, tiles, acc)
 
 
-def step_apply(lst, slab, row, which, pair, first_pair, hots, tiles, acc, step):
-    acc = own_apply(lst, slab, which, pair[0], first_pair, tiles, acc, step)
-    return other_apply(lst, slab, row, which, pair[1], hots, tiles, acc, step)
+def step_apply(lst, slab, row, which, pairs, first_pair, hots, tiles, acc, step):
+    own, other = pairs[-1]
+    before = pairs[-2] if 0 < step < NSLAB else ()
+    acc = own_apply(lst, slab, which, own, before, first_pair, tiles, acc, step)
+    return other_apply(lst, slab, row, which, other, hots, tiles, acc, step)
 
 
 def last_own_kernel(lst, slab, tiles_ref, own0, other0, *refs):
-    gathered, acc = refs[:11], refs[12]
-    for k, s in enumerate((1, 2, 3, 2, 1, 0)):
+    gathered, acc = refs[:5], refs[6]
+    for s in range(NSLAB - 1):
+        at = 2 * (NSLAB - 2 - s)
+
         @pl.when(slab[0] == s)
-        def _(k=k, s=s):
+        def _(s=s, at=at):
             if s == 0:
-                apply_list(lst, LA, gathered[2 * k : 2 * k + 1], tiles_ref, acc)
-            if k < NSLAB - 1:
-                apply_list(lst, TC, gathered[2 * k : 2 * k + 2], tiles_ref, acc)
-            else:
-                apply_list(lst, LBC, gathered[2 * k : 2 * k + 1], tiles_ref, acc)
-                if s > 0:
-                    apply_list(lst, LBC + 1, gathered[2 * k + 1 : 2 * k + 2], tiles_ref, acc)
+                apply_list(lst, LA, gathered[at : at + 1], tiles_ref, acc)
+            apply_list(lst, LBC, gathered[at : at + 1], tiles_ref, acc)
+            if s > 0:
+                apply_list(lst, LBC + 1, gathered[at + 1 : at + 2], tiles_ref, acc)
 
     apply_list(lst, V0C, (own0, other0), tiles_ref, acc, late_start(slab, len(ORDER)))
 
@@ -280,14 +294,14 @@
 
 
 def last_apply(lst, slab, tiles, first_pair, pairs, acc):
-    flat = [ref for pair in pairs for ref in pair]
+    flat = [ref for pair in pairs[NSLAB - 1 :] for ref in pair]
     whole = jax.ShapeDtypeStruct(ACC, F32)
     acc = pl.pallas_call(
         last_own_kernel,
         out_shape=whole,
-        in_specs=[smem(), smem()] + [vmem()] * 15,
+        in_specs=[smem(), smem()] + [vmem()] * 9,
         out_specs=vmem(),
-        input_output_aliases={16: 0},
+        input_output_aliases={10: 0},
         compiler_params=PARAMS,
         name="last_own",
     )(lst, slab, tiles, *first_pair, *flat[:-1], acc)
@@ -490,7 +504,7 @@
         pairs.append(gather(value))
         if step < len(ORDER):
             which = TAB if step < NSLAB - 1 else LA
-            acc, msg = step_apply(lst, slab, row, which, pairs[-1], start, hots, tiles, acc, step)
+            acc, msg = step_apply(lst, slab, row, which, pairs, start, hots, tiles, acc, step)
     msg = last_apply(lst, slab, tiles, start, pairs, acc)
     return finish(section_blocks, lax.all_to_all(msg, "row", 0, 0, tiled=True))
 

time: 198 us -> 198 us (level)
  no operation moved by 1% of the time
where the time goes in v13:
time: 198 us; the launch traced here: 197 us
  blocking collectives  130 us (66%)
  starting transfers between devices  31.6 us (16%)
  Pallas kernels  21.5 us (11%)
  waiting for transfers between devices  12.7 us (6%)
    all_to_all x6, blocking collectives, gather(): lax.all_to_all(copies, 'col', 0, 0, tiled=True, axis_index_groups=Z_GROUPS)  67.7 us
    all_to_all x6, blocking collectives, exchange(): lax.all_to_all(message, ('slab', 'row'), 0, 0, tiled=True, axis_index_gro...  53.1 us
    ppermute x7, starting transfers between devices, gather(): return (own, lax.ppermute(own, 'col', [(c, c ^ 1) for c in range(NCOL)]))  17.5 us
    all_to_all x1, blocking collectives, body(): return finish(section_blocks, lax.all_to_all(msg, 'row', 0, 0, tiled=True))  9.09 us
    all_to_all x1, starting transfers between devices, gather(): lax.all_to_all(copies, 'col', 0, 0, tiled=True, axis_index_groups=Z_GROUPS)  9.02 us
    ppermute x4, waiting for transfers between devices, from_next(): return lax.ppermute(value, ('slab', 'row'), pairs)  6.08 us
    all_to_all x1, waiting for transfers between devices, gather(): lax.all_to_all(copies, 'col', 0, 0, tiled=True, axis_index_groups=Z_GROUPS)  5.72 us
    pallas_call x5, Pallas kernels, own_apply(): pl.pallas_call(functools.partial(own_kernel, which=which, step=step), out...  5.45 us
  transfers between devices with their start and end apart: 12, of which 7 were waited for; matrix products, arithmetic and copies ran while one was open for 0% of the time, Pallas kernels for 5%

profile of v13, /device:TPU:1, one launch (start us, length us, event | category | flops | bytes accessed | tf_op | source)
XLA Modules:
  0.0 197.2 jit_solution(8184642520397394015)
XLA Ops:
  2.4 9.0 %all-to-all-start = ((bf16[8,8,32,128]{3,2,1,0:T(8,128)(2,1)}), bf16[8,8,32,128]{3,2,1,0:T(8,128)(2,1)S(1)}, u32[]{:S(2)}, u32[]{:S(2)}) async-start(bf16[8,8,32,128]{3,2,1,0:T(8,128)(2,1)} %get-tuple-element.31), calls=%async_computation | async-start | bytes 1048576 | tf_op jit(solution)/shard_map/all_to_all | solution.py:449
  17.8 3.2 %collective-permute-done.3 = f32[2,256]{1,0:T(2,128)S(1)} collective-permute-done((f32[2,256]{1,0:T(2,128)S(1)}, f32[2,256]{1,0:T(2,128)S(1)}, u32[]{:S(2)}, u32[]{:S(2)}) %collective-permute-start.3) | collective-permute-done | bytes 2080 | tf_op jit(solution)/shard_map/ppermute | solution.py:468
  23.6 5.7 %all-to-all-done = bf16[8,8,32,128]{3,2,1,0:T(8,128)(2,1)S(1)} async-done(((bf16[8,8,32,128]{3,2,1,0:T(8,128)(2,1)}), bf16[8,8,32,128]{3,2,1,0:T(8,128)(2,1)S(1)}, u32[]{:S(2)}, u32[]{:S(2)}) %all-to-all-start) | async-done | bytes 524320 | tf_op jit(solution)/shard_map/all_to_all | solution.py:449
  30.3 2.2 %load.1.tiles_ref = bf16[128,128,128]{2,1,0:T(8,128)(2,1)S(1)} custom-call(bf16[128,128,128]{2,1,0:T(8,128)(2,1)} %bitcast.38, bf16[64,32,128]{2,1,0:T(8,128)(2,1)S(1)} %bitcast.13), custom_call_target="tpu_custom_call" | custom-call | tf_op jit(solution)/shard_map/load/pallas_call | solution.py:123
  32.5 2.7 %first.1 = (f32[33,32,128]{2,1,0:T(8,128)S(1)}, bf16[8,2,32,128]{3,2,1,0:T(8,128)(2,1)S(1)}) custom-call(s32[16,128]{1,0:T(8,128)S(1)} %helper.1.lst, s32[1]{0:T(128)} %bitcast.5.row, bf16[64,32,128]{2,1,0:T(8,128)(2,1)S(1)} %bitcast.14, bf16[64,32,128]{2,1,0:T(8,128)(2,1)S(1)} %collective-permute-done.other_ref.other0, ...), custom_call_target="tpu_custom_call" | custom-call | tf_op jit(solution)/shard_map/first/pallas_call | solution.py:197
  35.3 10.7 %all_to_all.70.rcv_ref = bf16[8,2,32,128]{3,2,1,0:T(8,128)(2,1)S(1)} all-to-all(bf16[8,2,32,128]{3,2,1,0:T(8,128)(2,1)S(1)} %get-tuple-element.41), channel_id=1, replica_groups={{0,16,32,48,64,80,96,112},{128,144,160,176,192,208,224,240},{1,17,33,49..., dimensions={0} | all-to-all | bytes 262144 | tf_op jit(solution)/shard_map/all_to_all | solution.py:459
  46.0 10.3 %all_to_all.71 = bf16[8,2,32,128]{3,2,1,0:T(8,128)(2,1)S(1)} all-to-all(bf16[8,2,32,128]{3,2,1,0:T(8,128)(2,1)S(1)} %shard_map.73), channel_id=1, replica_groups={{0,2,4,6,8,10,12,14},{1,3,5,7,9,11,13,15},{16,18,20,22,24,26,28,30},{17..., dimensions={0} | all-to-all | bytes 262144 | tf_op jit(solution)/shard_map/all_to_all | solution.py:449
  56.4 2.7 %collective-permute-start.5 = (bf16[16,32,128]{2,1,0:T(8,128)(2,1)S(1)}, bf16[16,32,128]{2,1,0:T(8,128)(2,1)S(1)}, u32[]{:S(2)}, u32[]{:S(2)}) collective-permute-start(bf16[16,32,128]{2,1,0:T(8,128)(2,1)S(1)} %bitcast.33), channel_id=1, source_target_pairs={{0,1},{1,0},{2,3},{3,2},{4,5},{5,4},{6,7},{7,6},{8,9},{9,8},{10,11... | collective-permute-start | bytes 393224 | tf_op jit(solution)/shard_map/ppermute | solution.py:451
  61.4 8.8 %all_to_all.72.rcv_ref = bf16[8,2,32,128]{3,2,1,0:T(8,128)(2,1)S(1)} all-to-all(bf16[8,2,32,128]{3,2,1,0:T(8,128)(2,1)S(1)} %get-tuple-element.44), channel_id=1, replica_groups={{64,80,96,112,128,144,160,176},{192,208,224,240,0,16,32,48},{65,81,97,1..., dimensions={0} | all-to-all | bytes 262144 | tf_op jit(solution)/shard_map/all_to_all | solution.py:459
  70.2 10.4 %all_to_all.73 = bf16[8,2,32,128]{3,2,1,0:T(8,128)(2,1)S(1)} all-to-all(bf16[8,2,32,128]{3,2,1,0:T(8,128)(2,1)S(1)} %shard_map.74), channel_id=1, replica_groups={{0,2,4,6,8,10,12,14},{1,3,5,7,9,11,13,15},{16,18,20,22,24,26,28,30},{17..., dimensions={0} | all-to-all | bytes 262144 | tf_op jit(solution)/shard_map/all_to_all | solution.py:449
  80.6 2.4 %collective-permute-start.6 = (bf16[16,32,128]{2,1,0:T(8,128)(2,1)S(1)}, bf16[16,32,128]{2,1,0:T(8,128)(2,1)S(1)}, u32[]{:S(2)}, u32[]{:S(2)}) collective-permute-start(bf16[16,32,128]{2,1,0:T(8,128)(2,1)S(1)} %bitcast.27), channel_id=1, source_target_pairs={{0,1},{1,0},{2,3},{3,2},{4,5},{5,4},{6,7},{7,6},{8,9},{9,8},{10,11... | collective-permute-start | bytes 393224 | tf_op jit(solution)/shard_map/ppermute | solution.py:451
  85.3 7.9 %all_to_all.74.rcv_ref = bf16[8,2,32,128]{3,2,1,0:T(8,128)(2,1)S(1)} all-to-all(bf16[8,2,32,128]{3,2,1,0:T(8,128)(2,1)S(1)} %get-tuple-element.46), channel_id=1, replica_groups={{128,144,160,176,192,208,224,240},{0,16,32,48,64,80,96,112},{129,145,16..., dimensions={0} | all-to-all | bytes 262144 | tf_op jit(solution)/shard_map/all_to_all | solution.py:459
  93.2 10.3 %all_to_all.75 = bf16[8,2,32,128]{3,2,1,0:T(8,128)(2,1)S(1)} all-to-all(bf16[8,2,32,128]{3,2,1,0:T(8,128)(2,1)S(1)} %shard_map.75), channel_id=1, replica_groups={{0,2,4,6,8,10,12,14},{1,3,5,7,9,11,13,15},{16,18,20,22,24,26,28,30},{17..., dimensions={0} | all-to-all | bytes 262144 | tf_op jit(solution)/shard_map/all_to_all | solution.py:449
  103.6 2.8 %collective-permute-start.7 = (bf16[16,32,128]{2,1,0:T(8,128)(2,1)S(1)}, bf16[16,32,128]{2,1,0:T(8,128)(2,1)S(1)}, u32[]{:S(2)}, u32[]{:S(2)}) collective-permute-start(bf16[16,32,128]{2,1,0:T(8,128)(2,1)S(1)} %bitcast.30), channel_id=1, source_target_pairs={{0,1},{1,0},{2,3},{3,2},{4,5},{5,4},{6,7},{7,6},{8,9},{9,8},{10,11... | collective-permute-start | bytes 393224 | tf_op jit(solution)/shard_map/ppermute | solution.py:451
  108.4 7.8 %all_to_all.76.rcv_ref = bf16[8,2,32,128]{3,2,1,0:T(8,128)(2,1)S(1)} all-to-all(bf16[8,2,32,128]{3,2,1,0:T(8,128)(2,1)S(1)} %get-tuple-element.48), channel_id=1, replica_groups={{128,144,160,176,192,208,224,240},{0,16,32,48,64,80,96,112},{129,145,16..., dimensions={0} | all-to-all | bytes 262144 | tf_op jit(solution)/shard_map/all_to_all | solution.py:459
  116.4 12.6 %all_to_all.77 = bf16[8,4,32,128]{3,2,1,0:T(8,128)(2,1)S(1)} all-to-all(bf16[8,4,32,128]{3,2,1,0:T(8,128)(2,1)S(1)} %shard_map.76), channel_id=1, replica_groups={{0,2,4,6,8,10,12,14},{1,3,5,7,9,11,13,15},{16,18,20,22,24,26,28,30},{17..., dimensions={0} | all-to-all | bytes 524288 | tf_op jit(solution)/shard_map/all_to_all | solution.py:449
  129.0 2.7 %collective-permute-start.8 = (bf16[32,32,128]{2,1,0:T(8,128)(2,1)S(1)}, bf16[32,32,128]{2,1,0:T(8,128)(2,1)S(1)}, u32[]{:S(2)}, u32[]{:S(2)}) collective-permute-start(bf16[32,32,128]{2,1,0:T(8,128)(2,1)S(1)} %bitcast.21), channel_id=1, source_target_pairs={{0,1},{1,0},{2,3},{3,2},{4,5},{5,4},{6,7},{7,6},{8,9},{9,8},{10,11... | collective-permute-start | bytes 786440 | tf_op jit(solution)/shard_map/ppermute | solution.py:451
  133.5 8.8 %all_to_all.78.rcv_ref = bf16[8,2,32,128]{3,2,1,0:T(8,128)(2,1)S(1)} all-to-all(bf16[8,2,32,128]{3,2,1,0:T(8,128)(2,1)S(1)} %get-tuple-element.52), channel_id=1, replica_groups={{64,80,96,112,128,144,160,176},{192,208,224,240,0,16,32,48},{65,81,97,1..., dimensions={0} | all-to-all | bytes 262144 | tf_op jit(solution)/shard_map/all_to_all | solution.py:459
  142.5 12.0 %all_to_all.79 = bf16[8,4,32,128]{3,2,1,0:T(8,128)(2,1)S(1)} all-to-all(bf16[8,4,32,128]{3,2,1,0:T(8,128)(2,1)S(1)} %shard_map.77), channel_id=1, replica_groups={{0,2,4,6,8,10,12,14},{1,3,5,7,9,11,13,15},{16,18,20,22,24,26,28,30},{17..., dimensions={0} | all-to-all | bytes 524288 | tf_op jit(solution)/shard_map/all_to_all | solution.py:449
  154.5 3.2 %collective-permute-start.9 = (bf16[32,32,128]{2,1,0:T(8,128)(2,1)S(1)}, bf16[32,32,128]{2,1,0:T(8,128)(2,1)S(1)}, u32[]{:S(2)}, u32[]{:S(2)}) collective-permute-start(bf16[32,32,128]{2,1,0:T(8,128)(2,1)S(1)} %bitcast.24), channel_id=1, source_target_pairs={{0,1},{1,0},{2,3},{3,2},{4,5},{5,4},{6,7},{7,6},{8,9},{9,8},{10,11... | collective-permute-start | bytes 786440 | tf_op jit(solution)/shard_map/ppermute | solution.py:451
  159.6 9.1 %all_to_all.80.rcv_ref = bf16[8,2,32,128]{3,2,1,0:T(8,128)(2,1)S(1)} all-to-all(bf16[8,2,32,128]{3,2,1,0:T(8,128)(2,1)S(1)} %get-tuple-element.54), channel_id=1, replica_groups={{0,16,32,48,64,80,96,112},{128,144,160,176,192,208,224,240},{1,17,33,49..., dimensions={0} | all-to-all | bytes 262144 | tf_op jit(solution)/shard_map/all_to_all | solution.py:459
  168.9 12.0 %all_to_all.81 = bf16[8,4,32,128]{3,2,1,0:T(8,128)(2,1)S(1)} all-to-all(bf16[8,4,32,128]{3,2,1,0:T(8,128)(2,1)S(1)} %shard_map.78), channel_id=1, replica_groups={{0,2,4,6,8,10,12,14},{1,3,5,7,9,11,13,15},{16,18,20,22,24,26,28,30},{17..., dimensions={0} | all-to-all | bytes 524288 | tf_op jit(solution)/shard_map/all_to_all | solution.py:449
  180.9 3.2 %collective-permute-start.10 = (bf16[32,32,128]{2,1,0:T(8,128)(2,1)S(1)}, bf16[32,32,128]{2,1,0:T(8,128)(2,1)S(1)}, u32[]{:S(2)}, u32[]{:S(2)}) collective-permute-start(bf16[32,32,128]{2,1,0:T(8,128)(2,1)S(1)} %bitcast.36), channel_id=1, source_target_pairs={{0,1},{1,0},{2,3},{3,2},{4,5},{5,4},{6,7},{7,6},{8,9},{9,8},{10,11... | collective-permute-start | bytes 786440 | tf_op jit(solution)/shard_map/ppermute | solution.py:451
  187.4 9.1 %all_to_all.82.parts_ref = bf16[4,8,32,128]{3,2,1,0:T(8,128)(2,1)S(1)} all-to-all(bf16[4,8,32,128]{3,2,1,0:T(8,128)(2,1)S(1)} %get-tuple-element.56), channel_id=1, replica_groups=mesh['slab'=4,'row'=4,'col'=16] {'row'}, dimensions={0} | all-to-all | bytes 524288 | tf_op jit(solution)/shard_map/all_to_all | solution.py:509
  (46 shorter events, 26.5 us)
Async XLA Ops:
  2.4 27.0 %all-to-all-start = ((bf16[8,8,32,128]{3,2,1,0:T(8,128)(2,1)}), bf16[8,8,32,128]{3,2,1,0:T(8,128)(2,1)S(1)}, u32[]{:S(2)}, u32[]{:S(2)}) async-start(bf16[8,8,32,128]{3,2,1,0:T(8,128)(2,1)} %get-tuple-element.31), calls=%async_computation | async-start | bytes 1048576 | tf_op jit(solution)/shard_map/all_to_all | solution.py:449
  11.4 6.4 %collective-permute-start.4 = (f32[2,256]{1,0:T(2,128)S(1)}, f32[2,256]{1,0:T(2,128)S(1)}, u32[]{:S(2)}, u32[]{:S(2)}) collective-permute-start(f32[2,256]{1,0:T(2,128)S(1)} %get-tuple-element.32), channel_id=1, source_target_pairs={{112,0},{64,16},{80,32},{96,48},{176,64},{128,80},{144,96},{160,11... | collective-permute-start | bytes 6152 | tf_op jit(solution)/shard_map/ppermute | solution.py:468
  12.7 8.3 %collective-permute-start.3 = (f32[2,256]{1,0:T(2,128)S(1)}, f32[2,256]{1,0:T(2,128)S(1)}, u32[]{:S(2)}, u32[]{:S(2)}) collective-permute-start(f32[2,256]{1,0:T(2,128)S(1)} %get-tuple-element.32), channel_id=1, source_target_pairs={{96,0},{112,16},{64,32},{80,48},{160,64},{176,80},{128,96},{144,11... | collective-permute-start | bytes 6152 | tf_op jit(solution)/shard_map/ppermute | solution.py:468
  14.0 7.7 %collective-permute-start.2 = (f32[2,256]{1,0:T(2,128)S(1)}, f32[2,256]{1,0:T(2,128)S(1)}, u32[]{:S(2)}, u32[]{:S(2)}) collective-permute-start(f32[2,256]{1,0:T(2,128)S(1)} %get-tuple-element.32), channel_id=1, source_target_pairs={{80,0},{96,16},{112,32},{64,48},{144,64},{160,80},{176,96},{128,11... | collective-permute-start | bytes 6152 | tf_op jit(solution)/shard_map/ppermute | solution.py:468
  15.3 8.3 %collective-permute-start.1 = (f32[2,256]{1,0:T(2,128)S(1)}, f32[2,256]{1,0:T(2,128)S(1)}, u32[]{:S(2)}, u32[]{:S(2)}) collective-permute-start(f32[2,256]{1,0:T(2,128)S(1)} %get-tuple-element.32), channel_id=1, source_target_pairs={{64,0},{80,16},{96,32},{112,48},{128,64},{144,80},{160,96},{176,11... | collective-permute-start | bytes 6152 | tf_op jit(solution)/shard_map/ppermute | solution.py:468
  29.3 3.2 %collective-permute-start = (bf16[64,32,128]{2,1,0:T(8,128)(2,1)S(1)}, bf16[64,32,128]{2,1,0:T(8,128)(2,1)S(1)}, u32[]{:S(2)}, u32[]{:S(2)}) collective-permute-start(bf16[64,32,128]{2,1,0:T(8,128)(2,1)S(1)} %bitcast.12), channel_id=1, source_target_pairs={{0,1},{1,0},{2,3},{3,2},{4,5},{5,4},{6,7},{7,6},{8,9},{9,8},{10,11... | collective-permute-start | bytes 1572872 | tf_op jit(solution)/shard_map/ppermute | solution.py:451
  32.5 13.5 %copy-start = (f32[1,256]{1,0:T(1,128)S(1)}, f32[1,256]{1,0:T(1,128)}, u32[]{:S(2)}) copy-start(f32[1,256]{1,0:T(1,128)} %coef_ref.5) | copy-start | bytes 3076
  56.4 4.0 %collective-permute-start.5 = (bf16[16,32,128]{2,1,0:T(8,128)(2,1)S(1)}, bf16[16,32,128]{2,1,0:T(8,128)(2,1)S(1)}, u32[]{:S(2)}, u32[]{:S(2)}) collective-permute-start(bf16[16,32,128]{2,1,0:T(8,128)(2,1)S(1)} %bitcast.33), channel_id=1, source_target_pairs={{0,1},{1,0},{2,3},{3,2},{4,5},{5,4},{6,7},{7,6},{8,9},{9,8},{10,11... | collective-permute-start | bytes 393224 | tf_op jit(solution)/shard_map/ppermute | solution.py:451
  80.6 3.8 %collective-permute-start.6 = (bf16[16,32,128]{2,1,0:T(8,128)(2,1)S(1)}, bf16[16,32,128]{2,1,0:T(8,128)(2,1)S(1)}, u32[]{:S(2)}, u32[]{:S(2)}) collective-permute-start(bf16[16,32,128]{2,1,0:T(8,128)(2,1)S(1)} %bitcast.27), channel_id=1, source_target_pairs={{0,1},{1,0},{2,3},{3,2},{4,5},{5,4},{6,7},{7,6},{8,9},{9,8},{10,11... | collective-permute-start | bytes 393224 | tf_op jit(solution)/shard_map/ppermute | solution.py:451
  103.6 4.1 %collective-permute-start.7 = (bf16[16,32,128]{2,1,0:T(8,128)(2,1)S(1)}, bf16[16,32,128]{2,1,0:T(8,128)(2,1)S(1)}, u32[]{:S(2)}, u32[]{:S(2)}) collective-permute-start(bf16[16,32,128]{2,1,0:T(8,128)(2,1)S(1)} %bitcast.30), channel_id=1, source_target_pairs={{0,1},{1,0},{2,3},{3,2},{4,5},{5,4},{6,7},{7,6},{8,9},{9,8},{10,11... | collective-permute-start | bytes 393224 | tf_op jit(solution)/shard_map/ppermute | solution.py:451
  129.0 3.8 %collective-permute-start.8 = (bf16[32,32,128]{2,1,0:T(8,128)(2,1)S(1)}, bf16[32,32,128]{2,1,0:T(8,128)(2,1)S(1)}, u32[]{:S(2)}, u32[]{:S(2)}) collective-permute-start(bf16[32,32,128]{2,1,0:T(8,128)(2,1)S(1)} %bitcast.21), channel_id=1, source_target_pairs={{0,1},{1,0},{2,3},{3,2},{4,5},{5,4},{6,7},{7,6},{8,9},{9,8},{10,11... | collective-permute-start | bytes 786440 | tf_op jit(solution)/shard_map/ppermute | solution.py:451
  154.5 4.4 %collective-permute-start.9 = (bf16[32,32,128]{2,1,0:T(8,128)(2,1)S(1)}, bf16[32,32,128]{2,1,0:T(8,128)(2,1)S(1)}, u32[]{:S(2)}, u32[]{:S(2)}) collective-permute-start(bf16[32,32,128]{2,1,0:T(8,128)(2,1)S(1)} %bitcast.24), channel_id=1, source_target_pairs={{0,1},{1,0},{2,3},{3,2},{4,5},{5,4},{6,7},{7,6},{8,9},{9,8},{10,11... | collective-permute-start | bytes 786440 | tf_op jit(solution)/shard_map/ppermute | solution.py:451
  180.9 5.1 %collective-permute-start.10 = (bf16[32,32,128]{2,1,0:T(8,128)(2,1)S(1)}, bf16[32,32,128]{2,1,0:T(8,128)(2,1)S(1)}, u32[]{:S(2)}, u32[]{:S(2)}) collective-permute-start(bf16[32,32,128]{2,1,0:T(8,128)(2,1)S(1)} %bitcast.36), channel_id=1, source_target_pairs={{0,1},{1,0},{2,3},{3,2},{4,5},{5,4},{6,7},{7,6},{8,9},{9,8},{10,11... | collective-permute-start | bytes 786440 | tf_op jit(solution)/shard_map/ppermute | solution.py:451

commit v14 on v13

--- a/solution.py
+++ b/solution.py
@@ -35,6 +35,7 @@
 LISTS = 9
 V0AB, V0C, TC, TAB, LA, LBC = 0, 1, 2, 3, 5, 7
 CHUNK = 3
+EXTRA = 2
 ORDER = (1, 2, 3, 2, 1)
 HALF = NCOL // 2
 
@@ -163,7 +164,7 @@
         if 0 < j < NSLAB:
             busy = busy | (slab[0] == ORDER[j - 1])
         used = used - jnp.where(busy, jnp.int32(1), jnp.int32(0))
-    return used * CHUNK
+    return used * (CHUNK + EXTRA)
 
 
 def write_down(acc, row, hot_ref, msg_ref):
@@ -236,10 +237,19 @@
     )(lst, slab, *ins)
 
 
-def other_kernel(lst, slab, row, other_ref, hot_ref, tiles_ref, acc_in, acc, msg_ref, *, which, step):
-    @pl.when(slab[0] == ORDER[step])
+def other_kernel(
+    lst, slab, row, other_ref, own0, other0, hot_ref, tiles_ref, acc_in, acc, msg_ref, *, which, step
+):
+    active = slab[0] == ORDER[step]
+    after = slab[0] == ORDER[step - 1] if 0 < step < NSLAB else slab[0] < 0
+
+    @pl.when(active)
     def _():
         apply_list(lst, which + 1, (other_ref,), tiles_ref, acc)
+
+    @pl.when(jnp.logical_not(active | after))
+    def _():
+        apply_list(lst, V0C, (own0, other0), tiles_ref, acc, late_start(slab, step) + CHUNK, EXTRA)
 
     if step + 1 < len(ORDER) and ORDER[step] < ORDER[step + 1]:
         write_down(acc, row, hot_ref, msg_ref)
@@ -247,23 +257,23 @@
         write_up(acc, msg_ref)
 
 
-def other_apply(lst, slab, row, which, other, hots, tiles, acc, step):
+def other_apply(lst, slab, row, which, other, first_pair, hots, tiles, acc, step):
     return pl.pallas_call(
         functools.partial(other_kernel, which=which, step=step),
         out_shape=(jax.ShapeDtypeStruct(ACC, F32), MESSAGE),
-        in_specs=[smem(), smem(), smem()] + [vmem()] * 4,
+        in_specs=[smem(), smem(), smem()] + [vmem()] * 6,
         out_specs=(vmem(), vmem()),
-        input_output_aliases={6: 0},
+        input_output_aliases={8: 0},
         compiler_params=PARAMS,
         name="other",
-    )(lst, slab, row, other, hots, tiles, acc)
+    )(lst, slab, row, other, *first_pair, hots, tiles, acc)
 
 
 def step_apply(lst, slab, row, which, pairs, first_pair, hots, tiles, acc, step):
     own, other = pairs[-1]
     before = pairs[-2] if 0 < step < NSLAB else ()
     acc = own_apply(lst, slab, which, own, before, first_pair, tiles, acc, step)
-    return other_apply(lst, slab, row, which, other, hots, tiles, acc, step)
+    return other_apply(lst, slab, row, which, other, first_pair, hots, tiles, acc, step)
 
 
 def last_own_kernel(lst, slab, tiles_ref, own0, other0, *refs):

time: 198 us -> 198 us (level)
  transfers between devices with their start and end apart: 12 -> 12, of which waited for: 7 -> 8; matrix products, arithmetic and copies ran while one was open for 0% -> 0% of each run, Pallas kernels for 5% -> 5%
where the time goes in v14:
time: 198 us
  blocking collectives  130 us (66%)
  starting transfers between devices  31.2 us (16%)
  Pallas kernels  21.6 us (11%)
  waiting for transfers between devices  13 us (7%)
    all_to_all x6, blocking collectives, gather(): lax.all_to_all(copies, 'col', 0, 0, tiled=True, axis_index_groups=Z_GROUPS)  67.9 us
    all_to_all x6, blocking collectives, exchange(): lax.all_to_all(message, ('slab', 'row'), 0, 0, tiled=True, axis_index_gro...  53.4 us
    ppermute x7, starting transfers between devices, gather(): return (own, lax.ppermute(own, 'col', [(c, c ^ 1) for c in range(NCOL)]))  17 us
    all_to_all x1, blocking collectives, body(): return finish(section_blocks, lax.all_to_all(msg, 'row', 0, 0, tiled=True))  9.09 us
    all_to_all x1, starting transfers between devices, gather(): lax.all_to_all(copies, 'col', 0, 0, tiled=True, axis_index_groups=Z_GROUPS)  9.02 us
    ppermute x4, waiting for transfers between devices, from_next(): return lax.ppermute(value, ('slab', 'row'), pairs)  6.08 us
    all_to_all x1, waiting for transfers between devices, gather(): lax.all_to_all(copies, 'col', 0, 0, tiled=True, axis_index_groups=Z_GROUPS)  5.72 us
    ppermute x4, starting transfers between devices, from_next(): return lax.ppermute(value, ('slab', 'row'), pairs)  5.16 us
  transfers between devices with their start and end apart: 12, of which 8 were waited for; matrix products, arithmetic and copies ran while one was open for 0% of the time, Pallas kernels for 5%

profile of v14, /device:TPU:1, one launch (start us, length us, event | category | flops | bytes accessed | tf_op | source)
XLA Modules:
  0.0 197.6 jit_solution(6211519943294214156)
XLA Ops:
  2.4 9.0 %all-to-all-start = ((bf16[8,8,32,128]{3,2,1,0:T(8,128)(2,1)}), bf16[8,8,32,128]{3,2,1,0:T(8,128)(2,1)S(1)}, u32[]{:S(2)}, u32[]{:S(2)}) async-start(bf16[8,8,32,128]{3,2,1,0:T(8,128)(2,1)} %get-tuple-element.31), calls=%async_computation | async-start | bytes 1048576 | tf_op jit(solution)/shard_map/all_to_all | solution.py:459
  17.8 3.2 %collective-permute-done.3 = f32[2,256]{1,0:T(2,128)S(1)} collective-permute-done((f32[2,256]{1,0:T(2,128)S(1)}, f32[2,256]{1,0:T(2,128)S(1)}, u32[]{:S(2)}, u32[]{:S(2)}) %collective-permute-start.3) | collective-permute-done | bytes 2080 | tf_op jit(solution)/shard_map/ppermute | solution.py:478
  23.6 5.7 %all-to-all-done = bf16[8,8,32,128]{3,2,1,0:T(8,128)(2,1)S(1)} async-done(((bf16[8,8,32,128]{3,2,1,0:T(8,128)(2,1)}), bf16[8,8,32,128]{3,2,1,0:T(8,128)(2,1)S(1)}, u32[]{:S(2)}, u32[]{:S(2)}) %all-to-all-start) | async-done | bytes 524320 | tf_op jit(solution)/shard_map/all_to_all | solution.py:459
  30.3 2.2 %load.1.tiles_ref = bf16[128,128,128]{2,1,0:T(8,128)(2,1)S(1)} custom-call(bf16[128,128,128]{2,1,0:T(8,128)(2,1)} %bitcast.43, bf16[64,32,128]{2,1,0:T(8,128)(2,1)S(1)} %bitcast.13), custom_call_target="tpu_custom_call" | custom-call | tf_op jit(solution)/shard_map/load/pallas_call | solution.py:124
  32.5 2.7 %first.1 = (f32[33,32,128]{2,1,0:T(8,128)S(1)}, bf16[8,2,32,128]{3,2,1,0:T(8,128)(2,1)S(1)}) custom-call(s32[16,128]{1,0:T(8,128)S(1)} %helper.1.lst, s32[1]{0:T(128)} %bitcast.5.row, bf16[64,32,128]{2,1,0:T(8,128)(2,1)S(1)} %bitcast.14, bf16[64,32,128]{2,1,0:T(8,128)(2,1)S(1)} %collective-permute-done.other_ref.other0, ...), custom_call_target="tpu_custom_call" | custom-call | tf_op jit(solution)/shard_map/first/pallas_call | solution.py:198
  35.3 10.7 %all_to_all.70.rcv_ref = bf16[8,2,32,128]{3,2,1,0:T(8,128)(2,1)S(1)} all-to-all(bf16[8,2,32,128]{3,2,1,0:T(8,128)(2,1)S(1)} %get-tuple-element.41), channel_id=1, replica_groups={{0,16,32,48,64,80,96,112},{128,144,160,176,192,208,224,240},{1,17,33,49..., dimensions={0} | all-to-all | bytes 262144 | tf_op jit(solution)/shard_map/all_to_all | solution.py:469
  46.0 10.3 %all_to_all.71 = bf16[8,2,32,128]{3,2,1,0:T(8,128)(2,1)S(1)} all-to-all(bf16[8,2,32,128]{3,2,1,0:T(8,128)(2,1)S(1)} %shard_map.73), channel_id=1, replica_groups={{0,2,4,6,8,10,12,14},{1,3,5,7,9,11,13,15},{16,18,20,22,24,26,28,30},{17..., dimensions={0} | all-to-all | bytes 262144 | tf_op jit(solution)/shard_map/all_to_all | solution.py:459
  56.4 2.7 %collective-permute-start.5 = (bf16[16,32,128]{2,1,0:T(8,128)(2,1)S(1)}, bf16[16,32,128]{2,1,0:T(8,128)(2,1)S(1)}, u32[]{:S(2)}, u32[]{:S(2)}) collective-permute-start(bf16[16,32,128]{2,1,0:T(8,128)(2,1)S(1)} %bitcast.38), channel_id=1, source_target_pairs={{0,1},{1,0},{2,3},{3,2},{4,5},{5,4},{6,7},{7,6},{8,9},{9,8},{10,11... | collective-permute-start | bytes 393224 | tf_op jit(solution)/shard_map/ppermute | solution.py:461
  61.8 8.8 %all_to_all.72.rcv_ref = bf16[8,2,32,128]{3,2,1,0:T(8,128)(2,1)S(1)} all-to-all(bf16[8,2,32,128]{3,2,1,0:T(8,128)(2,1)S(1)} %get-tuple-element.44), channel_id=1, replica_groups={{64,80,96,112,128,144,160,176},{192,208,224,240,0,16,32,48},{65,81,97,1..., dimensions={0} | all-to-all | bytes 262144 | tf_op jit(solution)/shard_map/all_to_all | solution.py:469
  70.6 10.4 %all_to_all.73 = bf16[8,2,32,128]{3,2,1,0:T(8,128)(2,1)S(1)} all-to-all(bf16[8,2,32,128]{3,2,1,0:T(8,128)(2,1)S(1)} %shard_map.74), channel_id=1, replica_groups={{0,2,4,6,8,10,12,14},{1,3,5,7,9,11,13,15},{16,18,20,22,24,26,28,30},{17..., dimensions={0} | all-to-all | bytes 262144 | tf_op jit(solution)/shard_map/all_to_all | solution.py:459
  81.0 2.4 %collective-permute-start.6 = (bf16[16,32,128]{2,1,0:T(8,128)(2,1)S(1)}, bf16[16,32,128]{2,1,0:T(8,128)(2,1)S(1)}, u32[]{:S(2)}, u32[]{:S(2)}) collective-permute-start(bf16[16,32,128]{2,1,0:T(8,128)(2,1)S(1)} %bitcast.32), channel_id=1, source_target_pairs={{0,1},{1,0},{2,3},{3,2},{4,5},{5,4},{6,7},{7,6},{8,9},{9,8},{10,11... | collective-permute-start | bytes 393224 | tf_op jit(solution)/shard_map/ppermute | solution.py:461
  86.0 7.8 %all_to_all.74.rcv_ref = bf16[8,2,32,128]{3,2,1,0:T(8,128)(2,1)S(1)} all-to-all(bf16[8,2,32,128]{3,2,1,0:T(8,128)(2,1)S(1)} %get-tuple-element.46), channel_id=1, replica_groups={{128,144,160,176,192,208,224,240},{0,16,32,48,64,80,96,112},{129,145,16..., dimensions={0} | all-to-all | bytes 262144 | tf_op jit(solution)/shard_map/all_to_all | solution.py:469
  93.9 10.4 %all_to_all.75 = bf16[8,2,32,128]{3,2,1,0:T(8,128)(2,1)S(1)} all-to-all(bf16[8,2,32,128]{3,2,1,0:T(8,128)(2,1)S(1)} %shard_map.75), channel_id=1, replica_groups={{0,2,4,6,8,10,12,14},{1,3,5,7,9,11,13,15},{16,18,20,22,24,26,28,30},{17..., dimensions={0} | all-to-all | bytes 262144 | tf_op jit(solution)/shard_map/all_to_all | solution.py:459
  104.3 2.5 %collective-permute-start.7 = (bf16[16,32,128]{2,1,0:T(8,128)(2,1)S(1)}, bf16[16,32,128]{2,1,0:T(8,128)(2,1)S(1)}, u32[]{:S(2)}, u32[]{:S(2)}) collective-permute-start(bf16[16,32,128]{2,1,0:T(8,128)(2,1)S(1)} %bitcast.35), channel_id=1, source_target_pairs={{0,1},{1,0},{2,3},{3,2},{4,5},{5,4},{6,7},{7,6},{8,9},{9,8},{10,11... | collective-permute-start | bytes 393224 | tf_op jit(solution)/shard_map/ppermute | solution.py:461
  108.5 8.5 %all_to_all.76.rcv_ref = bf16[8,2,32,128]{3,2,1,0:T(8,128)(2,1)S(1)} all-to-all(bf16[8,2,32,128]{3,2,1,0:T(8,128)(2,1)S(1)} %get-tuple-element.48), channel_id=1, replica_groups={{128,144,160,176,192,208,224,240},{0,16,32,48,64,80,96,112},{129,145,16..., dimensions={0} | all-to-all | bytes 262144 | tf_op jit(solution)/shard_map/all_to_all | solution.py:469
  117.2 12.6 %all_to_all.77 = bf16[8,4,32,128]{3,2,1,0:T(8,128)(2,1)S(1)} all-to-all(bf16[8,4,32,128]{3,2,1,0:T(8,128)(2,1)S(1)} %shard_map.76), channel_id=1, replica_groups={{0,2,4,6,8,10,12,14},{1,3,5,7,9,11,13,15},{16,18,20,22,24,26,28,30},{17..., dimensions={0} | all-to-all | bytes 524288 | tf_op jit(solution)/shard_map/all_to_all | solution.py:459
  129.8 2.6 %collective-permute-start.8 = (bf16[32,32,128]{2,1,0:T(8,128)(2,1)S(1)}, bf16[32,32,128]{2,1,0:T(8,128)(2,1)S(1)}, u32[]{:S(2)}, u32[]{:S(2)}) collective-permute-start(bf16[32,32,128]{2,1,0:T(8,128)(2,1)S(1)} %bitcast.26), channel_id=1, source_target_pairs={{0,1},{1,0},{2,3},{3,2},{4,5},{5,4},{6,7},{7,6},{8,9},{9,8},{10,11... | collective-permute-start | bytes 786440 | tf_op jit(solution)/shard_map/ppermute | solution.py:461
  134.3 8.8 %all_to_all.78.rcv_ref = bf16[8,2,32,128]{3,2,1,0:T(8,128)(2,1)S(1)} all-to-all(bf16[8,2,32,128]{3,2,1,0:T(8,128)(2,1)S(1)} %get-tuple-element.52), channel_id=1, replica_groups={{64,80,96,112,128,144,160,176},{192,208,224,240,0,16,32,48},{65,81,97,1..., dimensions={0} | all-to-all | bytes 262144 | tf_op jit(solution)/shard_map/all_to_all | solution.py:469
  143.3 12.0 %all_to_all.79 = bf16[8,4,32,128]{3,2,1,0:T(8,128)(2,1)S(1)} all-to-all(bf16[8,4,32,128]{3,2,1,0:T(8,128)(2,1)S(1)} %shard_map.77), channel_id=1, replica_groups={{0,2,4,6,8,10,12,14},{1,3,5,7,9,11,13,15},{16,18,20,22,24,26,28,30},{17..., dimensions={0} | all-to-all | bytes 524288 | tf_op jit(solution)/shard_map/all_to_all | solution.py:459
  155.3 3.2 %collective-permute-start.9 = (bf16[32,32,128]{2,1,0:T(8,128)(2,1)S(1)}, bf16[32,32,128]{2,1,0:T(8,128)(2,1)S(1)}, u32[]{:S(2)}, u32[]{:S(2)}) collective-permute-start(bf16[32,32,128]{2,1,0:T(8,128)(2,1)S(1)} %bitcast.29), channel_id=1, source_target_pairs={{0,1},{1,0},{2,3},{3,2},{4,5},{5,4},{6,7},{7,6},{8,9},{9,8},{10,11... | collective-permute-start | bytes 786440 | tf_op jit(solution)/shard_map/ppermute | solution.py:461
  160.4 8.8 %all_to_all.80.rcv_ref = bf16[8,2,32,128]{3,2,1,0:T(8,128)(2,1)S(1)} all-to-all(bf16[8,2,32,128]{3,2,1,0:T(8,128)(2,1)S(1)} %get-tuple-element.54), channel_id=1, replica_groups={{0,16,32,48,64,80,96,112},{128,144,160,176,192,208,224,240},{1,17,33,49..., dimensions={0} | all-to-all | bytes 262144 | tf_op jit(solution)/shard_map/all_to_all | solution.py:469
  169.4 12.1 %all_to_all.81 = bf16[8,4,32,128]{3,2,1,0:T(8,128)(2,1)S(1)} all-to-all(bf16[8,4,32,128]{3,2,1,0:T(8,128)(2,1)S(1)} %shard_map.78), channel_id=1, replica_groups={{0,2,4,6,8,10,12,14},{1,3,5,7,9,11,13,15},{16,18,20,22,24,26,28,30},{17..., dimensions={0} | all-to-all | bytes 524288 | tf_op jit(solution)/shard_map/all_to_all | solution.py:459
  181.5 3.1 %collective-permute-start.10 = (bf16[32,32,128]{2,1,0:T(8,128)(2,1)S(1)}, bf16[32,32,128]{2,1,0:T(8,128)(2,1)S(1)}, u32[]{:S(2)}, u32[]{:S(2)}) collective-permute-start(bf16[32,32,128]{2,1,0:T(8,128)(2,1)S(1)} %bitcast.41), channel_id=1, source_target_pairs={{0,1},{1,0},{2,3},{3,2},{4,5},{5,4},{6,7},{7,6},{8,9},{9,8},{10,11... | collective-permute-start | bytes 786440 | tf_op jit(solution)/shard_map/ppermute | solution.py:461
  187.9 9.1 %all_to_all.82.parts_ref = bf16[4,8,32,128]{3,2,1,0:T(8,128)(2,1)S(1)} all-to-all(bf16[4,8,32,128]{3,2,1,0:T(8,128)(2,1)S(1)} %get-tuple-element.56), channel_id=1, replica_groups=mesh['slab'=4,'row'=4,'col'=16] {'row'}, dimensions={0} | all-to-all | bytes 524288 | tf_op jit(solution)/shard_map/all_to_all | solution.py:519
  (46 shorter events, 26.9 us)
Async XLA Ops:
  2.4 27.0 %all-to-all-start = ((bf16[8,8,32,128]{3,2,1,0:T(8,128)(2,1)}), bf16[8,8,32,128]{3,2,1,0:T(8,128)(2,1)S(1)}, u32[]{:S(2)}, u32[]{:S(2)}) async-start(bf16[8,8,32,128]{3,2,1,0:T(8,128)(2,1)} %get-tuple-element.31), calls=%async_computation | async-start | bytes 1048576 | tf_op jit(solution)/shard_map/all_to_all | solution.py:459
  11.4 6.4 %collective-permute-start.4 = (f32[2,256]{1,0:T(2,128)S(1)}, f32[2,256]{1,0:T(2,128)S(1)}, u32[]{:S(2)}, u32[]{:S(2)}) collective-permute-start(f32[2,256]{1,0:T(2,128)S(1)} %get-tuple-element.32), channel_id=1, source_target_pairs={{112,0},{64,16},{80,32},{96,48},{176,64},{128,80},{144,96},{160,11... | collective-permute-start | bytes 6152 | tf_op jit(solution)/shard_map/ppermute | solution.py:478
  12.7 8.3 %collective-permute-start.3 = (f32[2,256]{1,0:T(2,128)S(1)}, f32[2,256]{1,0:T(2,128)S(1)}, u32[]{:S(2)}, u32[]{:S(2)}) collective-permute-start(f32[2,256]{1,0:T(2,128)S(1)} %get-tuple-element.32), channel_id=1, source_target_pairs={{96,0},{112,16},{64,32},{80,48},{160,64},{176,80},{128,96},{144,11... | collective-permute-start | bytes 6152 | tf_op jit(solution)/shard_map/ppermute | solution.py:478
  14.0 7.7 %collective-permute-start.2 = (f32[2,256]{1,0:T(2,128)S(1)}, f32[2,256]{1,0:T(2,128)S(1)}, u32[]{:S(2)}, u32[]{:S(2)}) collective-permute-start(f32[2,256]{1,0:T(2,128)S(1)} %get-tuple-element.32), channel_id=1, source_target_pairs={{80,0},{96,16},{112,32},{64,48},{144,64},{160,80},{176,96},{128,11... | collective-permute-start | bytes 6152 | tf_op jit(solution)/shard_map/ppermute | solution.py:478
  15.3 8.3 %collective-permute-start.1 = (f32[2,256]{1,0:T(2,128)S(1)}, f32[2,256]{1,0:T(2,128)S(1)}, u32[]{:S(2)}, u32[]{:S(2)}) collective-permute-start(f32[2,256]{1,0:T(2,128)S(1)} %get-tuple-element.32), channel_id=1, source_target_pairs={{64,0},{80,16},{96,32},{112,48},{128,64},{144,80},{160,96},{176,11... | collective-permute-start | bytes 6152 | tf_op jit(solution)/shard_map/ppermute | solution.py:478
  29.3 3.2 %collective-permute-start = (bf16[64,32,128]{2,1,0:T(8,128)(2,1)S(1)}, bf16[64,32,128]{2,1,0:T(8,128)(2,1)S(1)}, u32[]{:S(2)}, u32[]{:S(2)}) collective-permute-start(bf16[64,32,128]{2,1,0:T(8,128)(2,1)S(1)} %bitcast.12), channel_id=1, source_target_pairs={{0,1},{1,0},{2,3},{3,2},{4,5},{5,4},{6,7},{7,6},{8,9},{9,8},{10,11... | collective-permute-start | bytes 1572872 | tf_op jit(solution)/shard_map/ppermute | solution.py:461
  32.5 13.5 %copy-start = (f32[1,256]{1,0:T(1,128)S(1)}, f32[1,256]{1,0:T(1,128)}, u32[]{:S(2)}) copy-start(f32[1,256]{1,0:T(1,128)} %coef_ref.5) | copy-start | bytes 3076
  56.4 4.0 %collective-permute-start.5 = (bf16[16,32,128]{2,1,0:T(8,128)(2,1)S(1)}, bf16[16,32,128]{2,1,0:T(8,128)(2,1)S(1)}, u32[]{:S(2)}, u32[]{:S(2)}) collective-permute-start(bf16[16,32,128]{2,1,0:T(8,128)(2,1)S(1)} %bitcast.38), channel_id=1, source_target_pairs={{0,1},{1,0},{2,3},{3,2},{4,5},{5,4},{6,7},{7,6},{8,9},{9,8},{10,11... | collective-permute-start | bytes 393224 | tf_op jit(solution)/shard_map/ppermute | solution.py:461
  81.0 3.8 %collective-permute-start.6 = (bf16[16,32,128]{2,1,0:T(8,128)(2,1)S(1)}, bf16[16,32,128]{2,1,0:T(8,128)(2,1)S(1)}, u32[]{:S(2)}, u32[]{:S(2)}) collective-permute-start(bf16[16,32,128]{2,1,0:T(8,128)(2,1)S(1)} %bitcast.32), channel_id=1, source_target_pairs={{0,1},{1,0},{2,3},{3,2},{4,5},{5,4},{6,7},{7,6},{8,9},{9,8},{10,11... | collective-permute-start | bytes 393224 | tf_op jit(solution)/shard_map/ppermute | solution.py:461
  104.3 3.5 %collective-permute-start.7 = (bf16[16,32,128]{2,1,0:T(8,128)(2,1)S(1)}, bf16[16,32,128]{2,1,0:T(8,128)(2,1)S(1)}, u32[]{:S(2)}, u32[]{:S(2)}) collective-permute-start(bf16[16,32,128]{2,1,0:T(8,128)(2,1)S(1)} %bitcast.35), channel_id=1, source_target_pairs={{0,1},{1,0},{2,3},{3,2},{4,5},{5,4},{6,7},{7,6},{8,9},{9,8},{10,11... | collective-permute-start | bytes 393224 | tf_op jit(solution)/shard_map/ppermute | solution.py:461
  129.8 3.8 %collective-permute-start.8 = (bf16[32,32,128]{2,1,0:T(8,128)(2,1)S(1)}, bf16[32,32,128]{2,1,0:T(8,128)(2,1)S(1)}, u32[]{:S(2)}, u32[]{:S(2)}) collective-permute-start(bf16[32,32,128]{2,1,0:T(8,128)(2,1)S(1)} %bitcast.26), channel_id=1, source_target_pairs={{0,1},{1,0},{2,3},{3,2},{4,5},{5,4},{6,7},{7,6},{8,9},{9,8},{10,11... | collective-permute-start | bytes 786440 | tf_op jit(solution)/shard_map/ppermute | solution.py:461
  155.3 4.4 %collective-permute-start.9 = (bf16[32,32,128]{2,1,0:T(8,128)(2,1)S(1)}, bf16[32,32,128]{2,1,0:T(8,128)(2,1)S(1)}, u32[]{:S(2)}, u32[]{:S(2)}) collective-permute-start(bf16[32,32,128]{2,1,0:T(8,128)(2,1)S(1)} %bitcast.29), channel_id=1, source_target_pairs={{0,1},{1,0},{2,3},{3,2},{4,5},{5,4},{6,7},{7,6},{8,9},{9,8},{10,11... | collective-permute-start | bytes 786440 | tf_op jit(solution)/shard_map/ppermute | solution.py:461
  181.5 5.0 %collective-permute-start.10 = (bf16[32,32,128]{2,1,0:T(8,128)(2,1)S(1)}, bf16[32,32,128]{2,1,0:T(8,128)(2,1)S(1)}, u32[]{:S(2)}, u32[]{:S(2)}) collective-permute-start(bf16[32,32,128]{2,1,0:T(8,128)(2,1)S(1)} %bitcast.41), channel_id=1, source_target_pairs={{0,1},{1,0},{2,3},{3,2},{4,5},{5,4},{6,7},{7,6},{8,9},{9,8},{10,11... | collective-permute-start | bytes 786440 | tf_op jit(solution)/shard_map/ppermute | solution.py:461

commit v15 on v13

--- a/solution.py
+++ b/solution.py
@@ -134,8 +134,12 @@
 def products(pairs):
     out = []
     for (va, ta), (vb, tb) in zip(pairs[::2], pairs[1::2]):
-        both = product(jnp.concatenate([va, vb], axis=0), jnp.concatenate([ta, tb], axis=0))
-        out += [both[:W, :B], both[W:, B:]]
+        zero = jnp.zeros_like(va)
+        left = jnp.concatenate(
+            [jnp.concatenate([va, zero], axis=1), jnp.concatenate([zero, vb], axis=1)], axis=0
+        )
+        both = product(left, jnp.concatenate([ta, tb], axis=1))
+        out += [both[:W], both[W:]]
     return out
 
 

time: 198 us -> 198 us (level)
  no operation moved by 1% of the time
where the time goes in v15:
time: 198 us; the launch traced here: 197 us
  blocking collectives  130 us (66%)
  starting transfers between devices  31.5 us (16%)
  Pallas kernels  21.6 us (11%)
  waiting for transfers between devices  12.7 us (6%)
    all_to_all x6, blocking collectives, gather(): lax.all_to_all(copies, 'col', 0, 0, tiled=True, axis_index_groups=Z_GROUPS)  67.8 us
    all_to_all x6, blocking collectives, exchange(): lax.all_to_all(message, ('slab', 'row'), 0, 0, tiled=True, axis_index_gro...  53.2 us
    ppermute x7, starting transfers between devices, gather(): return (own, lax.ppermute(own, 'col', [(c, c ^ 1) for c in range(NCOL)]))  17.3 us
    all_to_all x1, blocking collectives, body(): return finish(section_blocks, lax.all_to_all(msg, 'row', 0, 0, tiled=True))  9.11 us
    all_to_all x1, starting transfers between devices, gather(): lax.all_to_all(copies, 'col', 0, 0, tiled=True, axis_index_groups=Z_GROUPS)  9.02 us
    ppermute x4, waiting for transfers between devices, from_next(): return lax.ppermute(value, ('slab', 'row'), pairs)  6.08 us
    all_to_all x1, waiting for transfers between devices, gather(): lax.all_to_all(copies, 'col', 0, 0, tiled=True, axis_index_groups=Z_GROUPS)  5.72 us
    pallas_call x5, Pallas kernels, own_apply(): pl.pallas_call(functools.partial(own_kernel, which=which, step=step), out...  5.46 us
  transfers between devices with their start and end apart: 12, of which 7 were waited for; matrix products, arithmetic and copies ran while one was open for 0% of the time, Pallas kernels for 5%

profile of v15, /device:TPU:1, one launch (start us, length us, event | category | flops | bytes accessed | tf_op | source)
XLA Modules:
  0.0 197.2 jit_solution(16487973018717930546)
XLA Ops:
  2.4 9.0 %all-to-all-start = ((bf16[8,8,32,128]{3,2,1,0:T(8,128)(2,1)}), bf16[8,8,32,128]{3,2,1,0:T(8,128)(2,1)S(1)}, u32[]{:S(2)}, u32[]{:S(2)}) async-start(bf16[8,8,32,128]{3,2,1,0:T(8,128)(2,1)} %get-tuple-element.31), calls=%async_computation | async-start | bytes 1048576 | tf_op jit(solution)/shard_map/all_to_all | solution.py:453
  17.8 3.2 %collective-permute-done.3 = f32[2,256]{1,0:T(2,128)S(1)} collective-permute-done((f32[2,256]{1,0:T(2,128)S(1)}, f32[2,256]{1,0:T(2,128)S(1)}, u32[]{:S(2)}, u32[]{:S(2)}) %collective-permute-start.3) | collective-permute-done | bytes 2080 | tf_op jit(solution)/shard_map/ppermute | solution.py:472
  23.6 5.7 %all-to-all-done = bf16[8,8,32,128]{3,2,1,0:T(8,128)(2,1)S(1)} async-done(((bf16[8,8,32,128]{3,2,1,0:T(8,128)(2,1)}), bf16[8,8,32,128]{3,2,1,0:T(8,128)(2,1)S(1)}, u32[]{:S(2)}, u32[]{:S(2)}) %all-to-all-start) | async-done | bytes 524320 | tf_op jit(solution)/shard_map/all_to_all | solution.py:453
  30.3 2.2 %load.1.tiles_ref = bf16[128,128,128]{2,1,0:T(8,128)(2,1)S(1)} custom-call(bf16[128,128,128]{2,1,0:T(8,128)(2,1)} %bitcast.38, bf16[64,32,128]{2,1,0:T(8,128)(2,1)S(1)} %bitcast.13), custom_call_target="tpu_custom_call" | custom-call | tf_op jit(solution)/shard_map/load/pallas_call | solution.py:123
  32.5 2.8 %first.1 = (f32[33,32,128]{2,1,0:T(8,128)S(1)}, bf16[8,2,32,128]{3,2,1,0:T(8,128)(2,1)S(1)}) custom-call(s32[16,128]{1,0:T(8,128)S(1)} %helper.1.lst, s32[1]{0:T(128)} %bitcast.5.row, bf16[64,32,128]{2,1,0:T(8,128)(2,1)S(1)} %bitcast.14, bf16[64,32,128]{2,1,0:T(8,128)(2,1)S(1)} %collective-permute-done.other_ref.other0, ...), custom_call_target="tpu_custom_call" | custom-call | tf_op jit(solution)/shard_map/first/pallas_call | solution.py:201
  35.3 10.7 %all_to_all.70.rcv_ref = bf16[8,2,32,128]{3,2,1,0:T(8,128)(2,1)S(1)} all-to-all(bf16[8,2,32,128]{3,2,1,0:T(8,128)(2,1)S(1)} %get-tuple-element.41), channel_id=1, replica_groups={{0,16,32,48,64,80,96,112},{128,144,160,176,192,208,224,240},{1,17,33,49..., dimensions={0} | all-to-all | bytes 262144 | tf_op jit(solution)/shard_map/all_to_all | solution.py:463
  46.1 10.3 %all_to_all.71 = bf16[8,2,32,128]{3,2,1,0:T(8,128)(2,1)S(1)} all-to-all(bf16[8,2,32,128]{3,2,1,0:T(8,128)(2,1)S(1)} %shard_map.73), channel_id=1, replica_groups={{0,2,4,6,8,10,12,14},{1,3,5,7,9,11,13,15},{16,18,20,22,24,26,28,30},{17..., dimensions={0} | all-to-all | bytes 262144 | tf_op jit(solution)/shard_map/all_to_all | solution.py:453
  56.4 2.7 %collective-permute-start.5 = (bf16[16,32,128]{2,1,0:T(8,128)(2,1)S(1)}, bf16[16,32,128]{2,1,0:T(8,128)(2,1)S(1)}, u32[]{:S(2)}, u32[]{:S(2)}) collective-permute-start(bf16[16,32,128]{2,1,0:T(8,128)(2,1)S(1)} %bitcast.33), channel_id=1, source_target_pairs={{0,1},{1,0},{2,3},{3,2},{4,5},{5,4},{6,7},{7,6},{8,9},{9,8},{10,11... | collective-permute-start | bytes 393224 | tf_op jit(solution)/shard_map/ppermute | solution.py:455
  61.4 8.8 %all_to_all.72.rcv_ref = bf16[8,2,32,128]{3,2,1,0:T(8,128)(2,1)S(1)} all-to-all(bf16[8,2,32,128]{3,2,1,0:T(8,128)(2,1)S(1)} %get-tuple-element.44), channel_id=1, replica_groups={{64,80,96,112,128,144,160,176},{192,208,224,240,0,16,32,48},{65,81,97,1..., dimensions={0} | all-to-all | bytes 262144 | tf_op jit(solution)/shard_map/all_to_all | solution.py:463
  70.2 10.4 %all_to_all.73 = bf16[8,2,32,128]{3,2,1,0:T(8,128)(2,1)S(1)} all-to-all(bf16[8,2,32,128]{3,2,1,0:T(8,128)(2,1)S(1)} %shard_map.74), channel_id=1, replica_groups={{0,2,4,6,8,10,12,14},{1,3,5,7,9,11,13,15},{16,18,20,22,24,26,28,30},{17..., dimensions={0} | all-to-all | bytes 262144 | tf_op jit(solution)/shard_map/all_to_all | solution.py:453
  80.6 2.4 %collective-permute-start.6 = (bf16[16,32,128]{2,1,0:T(8,128)(2,1)S(1)}, bf16[16,32,128]{2,1,0:T(8,128)(2,1)S(1)}, u32[]{:S(2)}, u32[]{:S(2)}) collective-permute-start(bf16[16,32,128]{2,1,0:T(8,128)(2,1)S(1)} %bitcast.27), channel_id=1, source_target_pairs={{0,1},{1,0},{2,3},{3,2},{4,5},{5,4},{6,7},{7,6},{8,9},{9,8},{10,11... | collective-permute-start | bytes 393224 | tf_op jit(solution)/shard_map/ppermute | solution.py:455
  85.4 7.9 %all_to_all.74.rcv_ref = bf16[8,2,32,128]{3,2,1,0:T(8,128)(2,1)S(1)} all-to-all(bf16[8,2,32,128]{3,2,1,0:T(8,128)(2,1)S(1)} %get-tuple-element.46), channel_id=1, replica_groups={{128,144,160,176,192,208,224,240},{0,16,32,48,64,80,96,112},{129,145,16..., dimensions={0} | all-to-all | bytes 262144 | tf_op jit(solution)/shard_map/all_to_all | solution.py:463
  93.3 10.3 %all_to_all.75 = bf16[8,2,32,128]{3,2,1,0:T(8,128)(2,1)S(1)} all-to-all(bf16[8,2,32,128]{3,2,1,0:T(8,128)(2,1)S(1)} %shard_map.75), channel_id=1, replica_groups={{0,2,4,6,8,10,12,14},{1,3,5,7,9,11,13,15},{16,18,20,22,24,26,28,30},{17..., dimensions={0} | all-to-all | bytes 262144 | tf_op jit(solution)/shard_map/all_to_all | solution.py:453
  103.6 2.8 %collective-permute-start.7 = (bf16[16,32,128]{2,1,0:T(8,128)(2,1)S(1)}, bf16[16,32,128]{2,1,0:T(8,128)(2,1)S(1)}, u32[]{:S(2)}, u32[]{:S(2)}) collective-permute-start(bf16[16,32,128]{2,1,0:T(8,128)(2,1)S(1)} %bitcast.30), channel_id=1, source_target_pairs={{0,1},{1,0},{2,3},{3,2},{4,5},{5,4},{6,7},{7,6},{8,9},{9,8},{10,11... | collective-permute-start | bytes 393224 | tf_op jit(solution)/shard_map/ppermute | solution.py:455
  108.4 7.8 %all_to_all.76.rcv_ref = bf16[8,2,32,128]{3,2,1,0:T(8,128)(2,1)S(1)} all-to-all(bf16[8,2,32,128]{3,2,1,0:T(8,128)(2,1)S(1)} %get-tuple-element.48), channel_id=1, replica_groups={{128,144,160,176,192,208,224,240},{0,16,32,48,64,80,96,112},{129,145,16..., dimensions={0} | all-to-all | bytes 262144 | tf_op jit(solution)/shard_map/all_to_all | solution.py:463
  116.4 12.6 %all_to_all.77 = bf16[8,4,32,128]{3,2,1,0:T(8,128)(2,1)S(1)} all-to-all(bf16[8,4,32,128]{3,2,1,0:T(8,128)(2,1)S(1)} %shard_map.76), channel_id=1, replica_groups={{0,2,4,6,8,10,12,14},{1,3,5,7,9,11,13,15},{16,18,20,22,24,26,28,30},{17..., dimensions={0} | all-to-all | bytes 524288 | tf_op jit(solution)/shard_map/all_to_all | solution.py:453
  129.0 2.7 %collective-permute-start.8 = (bf16[32,32,128]{2,1,0:T(8,128)(2,1)S(1)}, bf16[32,32,128]{2,1,0:T(8,128)(2,1)S(1)}, u32[]{:S(2)}, u32[]{:S(2)}) collective-permute-start(bf16[32,32,128]{2,1,0:T(8,128)(2,1)S(1)} %bitcast.21), channel_id=1, source_target_pairs={{0,1},{1,0},{2,3},{3,2},{4,5},{5,4},{6,7},{7,6},{8,9},{9,8},{10,11... | collective-permute-start | bytes 786440 | tf_op jit(solution)/shard_map/ppermute | solution.py:455
  133.5 8.8 %all_to_all.78.rcv_ref = bf16[8,2,32,128]{3,2,1,0:T(8,128)(2,1)S(1)} all-to-all(bf16[8,2,32,128]{3,2,1,0:T(8,128)(2,1)S(1)} %get-tuple-element.52), channel_id=1, replica_groups={{64,80,96,112,128,144,160,176},{192,208,224,240,0,16,32,48},{65,81,97,1..., dimensions={0} | all-to-all | bytes 262144 | tf_op jit(solution)/shard_map/all_to_all | solution.py:463
  142.6 12.0 %all_to_all.79 = bf16[8,4,32,128]{3,2,1,0:T(8,128)(2,1)S(1)} all-to-all(bf16[8,4,32,128]{3,2,1,0:T(8,128)(2,1)S(1)} %shard_map.77), channel_id=1, replica_groups={{0,2,4,6,8,10,12,14},{1,3,5,7,9,11,13,15},{16,18,20,22,24,26,28,30},{17..., dimensions={0} | all-to-all | bytes 524288 | tf_op jit(solution)/shard_map/all_to_all | solution.py:453
  154.6 3.2 %collective-permute-start.9 = (bf16[32,32,128]{2,1,0:T(8,128)(2,1)S(1)}, bf16[32,32,128]{2,1,0:T(8,128)(2,1)S(1)}, u32[]{:S(2)}, u32[]{:S(2)}) collective-permute-start(bf16[32,32,128]{2,1,0:T(8,128)(2,1)S(1)} %bitcast.24), channel_id=1, source_target_pairs={{0,1},{1,0},{2,3},{3,2},{4,5},{5,4},{6,7},{7,6},{8,9},{9,8},{10,11... | collective-permute-start | bytes 786440 | tf_op jit(solution)/shard_map/ppermute | solution.py:455
  159.6 9.1 %all_to_all.80.rcv_ref = bf16[8,2,32,128]{3,2,1,0:T(8,128)(2,1)S(1)} all-to-all(bf16[8,2,32,128]{3,2,1,0:T(8,128)(2,1)S(1)} %get-tuple-element.54), channel_id=1, replica_groups={{0,16,32,48,64,80,96,112},{128,144,160,176,192,208,224,240},{1,17,33,49..., dimensions={0} | all-to-all | bytes 262144 | tf_op jit(solution)/shard_map/all_to_all | solution.py:463
  169.0 12.1 %all_to_all.81 = bf16[8,4,32,128]{3,2,1,0:T(8,128)(2,1)S(1)} all-to-all(bf16[8,4,32,128]{3,2,1,0:T(8,128)(2,1)S(1)} %shard_map.78), channel_id=1, replica_groups={{0,2,4,6,8,10,12,14},{1,3,5,7,9,11,13,15},{16,18,20,22,24,26,28,30},{17..., dimensions={0} | all-to-all | bytes 524288 | tf_op jit(solution)/shard_map/all_to_all | solution.py:453
  181.1 3.1 %collective-permute-start.10 = (bf16[32,32,128]{2,1,0:T(8,128)(2,1)S(1)}, bf16[32,32,128]{2,1,0:T(8,128)(2,1)S(1)}, u32[]{:S(2)}, u32[]{:S(2)}) collective-permute-start(bf16[32,32,128]{2,1,0:T(8,128)(2,1)S(1)} %bitcast.36), channel_id=1, source_target_pairs={{0,1},{1,0},{2,3},{3,2},{4,5},{5,4},{6,7},{7,6},{8,9},{9,8},{10,11... | collective-permute-start | bytes 786440 | tf_op jit(solution)/shard_map/ppermute | solution.py:455
  187.4 9.1 %all_to_all.82.parts_ref = bf16[4,8,32,128]{3,2,1,0:T(8,128)(2,1)S(1)} all-to-all(bf16[4,8,32,128]{3,2,1,0:T(8,128)(2,1)S(1)} %get-tuple-element.56), channel_id=1, replica_groups=mesh['slab'=4,'row'=4,'col'=16] {'row'}, dimensions={0} | all-to-all | bytes 524288 | tf_op jit(solution)/shard_map/all_to_all | solution.py:513
  (46 shorter events, 26.5 us)
Async XLA Ops:
  2.4 27.0 %all-to-all-start = ((bf16[8,8,32,128]{3,2,1,0:T(8,128)(2,1)}), bf16[8,8,32,128]{3,2,1,0:T(8,128)(2,1)S(1)}, u32[]{:S(2)}, u32[]{:S(2)}) async-start(bf16[8,8,32,128]{3,2,1,0:T(8,128)(2,1)} %get-tuple-element.31), calls=%async_computation | async-start | bytes 1048576 | tf_op jit(solution)/shard_map/all_to_all | solution.py:453
  11.4 6.4 %collective-permute-start.4 = (f32[2,256]{1,0:T(2,128)S(1)}, f32[2,256]{1,0:T(2,128)S(1)}, u32[]{:S(2)}, u32[]{:S(2)}) collective-permute-start(f32[2,256]{1,0:T(2,128)S(1)} %get-tuple-element.32), channel_id=1, source_target_pairs={{112,0},{64,16},{80,32},{96,48},{176,64},{128,80},{144,96},{160,11... | collective-permute-start | bytes 6152 | tf_op jit(solution)/shard_map/ppermute | solution.py:472
  12.7 8.3 %collective-permute-start.3 = (f32[2,256]{1,0:T(2,128)S(1)}, f32[2,256]{1,0:T(2,128)S(1)}, u32[]{:S(2)}, u32[]{:S(2)}) collective-permute-start(f32[2,256]{1,0:T(2,128)S(1)} %get-tuple-element.32), channel_id=1, source_target_pairs={{96,0},{112,16},{64,32},{80,48},{160,64},{176,80},{128,96},{144,11... | collective-permute-start | bytes 6152 | tf_op jit(solution)/shard_map/ppermute | solution.py:472
  14.0 7.7 %collective-permute-start.2 = (f32[2,256]{1,0:T(2,128)S(1)}, f32[2,256]{1,0:T(2,128)S(1)}, u32[]{:S(2)}, u32[]{:S(2)}) collective-permute-start(f32[2,256]{1,0:T(2,128)S(1)} %get-tuple-element.32), channel_id=1, source_target_pairs={{80,0},{96,16},{112,32},{64,48},{144,64},{160,80},{176,96},{128,11... | collective-permute-start | bytes 6152 | tf_op jit(solution)/shard_map/ppermute | solution.py:472
  15.3 8.3 %collective-permute-start.1 = (f32[2,256]{1,0:T(2,128)S(1)}, f32[2,256]{1,0:T(2,128)S(1)}, u32[]{:S(2)}, u32[]{:S(2)}) collective-permute-start(f32[2,256]{1,0:T(2,128)S(1)} %get-tuple-element.32), channel_id=1, source_target_pairs={{64,0},{80,16},{96,32},{112,48},{128,64},{144,80},{160,96},{176,11... | collective-permute-start | bytes 6152 | tf_op jit(solution)/shard_map/ppermute | solution.py:472
  29.3 3.2 %collective-permute-start = (bf16[64,32,128]{2,1,0:T(8,128)(2,1)S(1)}, bf16[64,32,128]{2,1,0:T(8,128)(2,1)S(1)}, u32[]{:S(2)}, u32[]{:S(2)}) collective-permute-start(bf16[64,32,128]{2,1,0:T(8,128)(2,1)S(1)} %bitcast.12), channel_id=1, source_target_pairs={{0,1},{1,0},{2,3},{3,2},{4,5},{5,4},{6,7},{7,6},{8,9},{9,8},{10,11... | collective-permute-start | bytes 1572872 | tf_op jit(solution)/shard_map/ppermute | solution.py:455
  32.5 13.5 %copy-start = (f32[1,256]{1,0:T(1,128)S(1)}, f32[1,256]{1,0:T(1,128)}, u32[]{:S(2)}) copy-start(f32[1,256]{1,0:T(1,128)} %coef_ref.5) | copy-start | bytes 3076
  56.4 4.0 %collective-permute-start.5 = (bf16[16,32,128]{2,1,0:T(8,128)(2,1)S(1)}, bf16[16,32,128]{2,1,0:T(8,128)(2,1)S(1)}, u32[]{:S(2)}, u32[]{:S(2)}) collective-permute-start(bf16[16,32,128]{2,1,0:T(8,128)(2,1)S(1)} %bitcast.33), channel_id=1, source_target_pairs={{0,1},{1,0},{2,3},{3,2},{4,5},{5,4},{6,7},{7,6},{8,9},{9,8},{10,11... | collective-permute-start | bytes 393224 | tf_op jit(solution)/shard_map/ppermute | solution.py:455
  80.6 3.8 %collective-permute-start.6 = (bf16[16,32,128]{2,1,0:T(8,128)(2,1)S(1)}, bf16[16,32,128]{2,1,0:T(8,128)(2,1)S(1)}, u32[]{:S(2)}, u32[]{:S(2)}) collective-permute-start(bf16[16,32,128]{2,1,0:T(8,128)(2,1)S(1)} %bitcast.27), channel_id=1, source_target_pairs={{0,1},{1,0},{2,3},{3,2},{4,5},{5,4},{6,7},{7,6},{8,9},{9,8},{10,11... | collective-permute-start | bytes 393224 | tf_op jit(solution)/shard_map/ppermute | solution.py:455
  103.6 4.1 %collective-permute-start.7 = (bf16[16,32,128]{2,1,0:T(8,128)(2,1)S(1)}, bf16[16,32,128]{2,1,0:T(8,128)(2,1)S(1)}, u32[]{:S(2)}, u32[]{:S(2)}) collective-permute-start(bf16[16,32,128]{2,1,0:T(8,128)(2,1)S(1)} %bitcast.30), channel_id=1, source_target_pairs={{0,1},{1,0},{2,3},{3,2},{4,5},{5,4},{6,7},{7,6},{8,9},{9,8},{10,11... | collective-permute-start | bytes 393224 | tf_op jit(solution)/shard_map/ppermute | solution.py:455
  129.0 3.8 %collective-permute-start.8 = (bf16[32,32,128]{2,1,0:T(8,128)(2,1)S(1)}, bf16[32,32,128]{2,1,0:T(8,128)(2,1)S(1)}, u32[]{:S(2)}, u32[]{:S(2)}) collective-permute-start(bf16[32,32,128]{2,1,0:T(8,128)(2,1)S(1)} %bitcast.21), channel_id=1, source_target_pairs={{0,1},{1,0},{2,3},{3,2},{4,5},{5,4},{6,7},{7,6},{8,9},{9,8},{10,11... | collective-permute-start | bytes 786440 | tf_op jit(solution)/shard_map/ppermute | solution.py:455
  154.6 4.4 %collective-permute-start.9 = (bf16[32,32,128]{2,1,0:T(8,128)(2,1)S(1)}, bf16[32,32,128]{2,1,0:T(8,128)(2,1)S(1)}, u32[]{:S(2)}, u32[]{:S(2)}) collective-permute-start(bf16[32,32,128]{2,1,0:T(8,128)(2,1)S(1)} %bitcast.24), channel_id=1, source_target_pairs={{0,1},{1,0},{2,3},{3,2},{4,5},{5,4},{6,7},{7,6},{8,9},{9,8},{10,11... | collective-permute-start | bytes 786440 | tf_op jit(solution)/shard_map/ppermute | solution.py:455
  181.1 5.0 %collective-permute-start.10 = (bf16[32,32,128]{2,1,0:T(8,128)(2,1)S(1)}, bf16[32,32,128]{2,1,0:T(8,128)(2,1)S(1)}, u32[]{:S(2)}, u32[]{:S(2)}) collective-permute-start(bf16[32,32,128]{2,1,0:T(8,128)(2,1)S(1)} %bitcast.36), channel_id=1, source_target_pairs={{0,1},{1,0},{2,3},{3,2},{4,5},{5,4},{6,7},{7,6},{8,9},{9,8},{10,11... | collective-permute-start | bytes 786440 | tf_op jit(solution)/shard_map/ppermute | solution.py:455
